TPU v7x, 32 devices: a whole 2x2x4 slice. The times are simulated.
32 devices in a mesh: dp: 2 (over core), row: 4 (over y, x), col: 4 (over z).
Axes of the slice: x: 2, y: 2, z: 4, core: 2. Of those that a mesh axis runs over, the one named last changes fastest.
Arguments:
- block_input: bfloat16 [8192, 2048], P(('dp', 'row')), may hold values from -6 to 6
- segment_ids: int32 [8192], P(('dp', 'row')), may hold values from 0 to 3, as said below
- positions: int32 [8192], P(('dp', 'row')), may hold values from 0 to 1023, as said below
- w_query: bfloat16 [2048, 2048], P('row', 'col'), as said below
- w_key: bfloat16 [2048, 2048], P('row', 'col'), as said below
- w_value: bfloat16 [2048, 2048], P('row', 'col'), may hold values from -0.125 to 0.125
- w_out: bfloat16 [2048, 2048], P('col', 'row'), may hold values from -0.125 to 0.125
- w_gate: bfloat16 [2048, 8192], P('row', 'col'), may hold values from -0.125 to 0.125
- w_up: bfloat16 [2048, 8192], P('row', 'col'), may hold values from -0.125 to 0.125
- w_down: bfloat16 [8192, 2048], P('col', 'row'), may hold values from -0.0625 to 0.0625
- query_gain: float32 [2048], P('col'), may hold values from 0.25 to 1.75
- key_gain: float32 [2048], P('col'), may hold values from 0.25 to 1.75
- attn_gain: float32 [2048], replicated, may hold values from 0.25 to 1.75
- mlp_gain: float32 [2048], replicated, may hold values from 0.25 to 1.75
- grad_output: bfloat16 [8192, 2048], P(('dp', 'row')), as said below
Outputs:
- block_output: bfloat16 [8192, 2048], P(('dp', 'row'))
- grad_input: float32 [8192, 2048], P(('dp', 'row'))
- grad_w_query: float32 [2048, 2048], P('row', 'col')
- grad_w_key: float32 [2048, 2048], P('row', 'col')
- grad_w_value: float32 [2048, 2048], P('row', 'col')
- grad_w_out: float32 [2048, 2048], P('col', 'row')
- grad_w_gate: float32 [2048, 8192], P('row', 'col')
- grad_w_up: float32 [2048, 8192], P('row', 'col')
- grad_w_down: float32 [8192, 2048], P('col', 'row')
- grad_query_gain: float32 [2048], P('col')
- grad_key_gain: float32 [2048], P('col')
- grad_attn_gain: float32 [2048], replicated
- grad_mlp_gain: float32 [2048], replicated
Inputs may be any that keep to these rules, and one draw needn't show every extreme that they name: `segment_ids`: within each sequence of 1024 tokens the ids never fall. `positions`: the index of a token counted from the first token with the same id in its sequence. `w_query`: scaled to the fan-in 2048. `w_key`: scaled to the fan-in 2048. `grad_output`: of order one in every row.
All inputs are finite; a program needn't handle non-finite values.
Results may differ from a plain program's by a relative error of at most 0.02.
Values may be sent and summed in bfloat16 or wider, within the bound.
No kernel may reach another device: no remote copies, remote signals or barrier semaphores. Data moves between devices by JAX's collectives and lax.ppermute only.
A program may use at most 320 MiB of HBM per device.

v0:
```python
import jax
import jax.numpy as jnp
from jax import lax
from jax.sharding import PartitionSpec as P

HD = 128
LEN = 1024


EPS = 1e-06
THETA = 500000.0
NEG_FILL = -1e30


def plain_dot(left_mat, right_mat):
    return jnp.dot(left_mat, right_mat, preferred_element_type=jnp.float32)


def times_transposed(left_mat, right_mat):
    return lax.dot_general(
        left_mat, right_mat, (((1,), (1,)), ((), ())), preferred_element_type=jnp.float32
    )


def left_transposed(left_mat, right_mat):
    return lax.dot_general(
        left_mat, right_mat, (((0,), (0,)), ((), ())), preferred_element_type=jnp.float32
    )


def rope_tables(positions):
    half_dim = HD // 2
    inv_freq = THETA ** (-(jnp.arange(half_dim, dtype=jnp.float32) * 2.0) / HD)
    angles = positions.astype(jnp.float32)[:, None] * inv_freq[None, :]
    cosine = jnp.concatenate([jnp.cos(angles), jnp.cos(angles)], axis=-1)
    sine_tab = jnp.concatenate([jnp.sin(angles), jnp.sin(angles)], axis=-1)
    return (cosine, sine_tab)


def rotate(values):
    first_half = values[..., : HD // 2]
    second_half = values[..., HD // 2 :]
    return jnp.concatenate([-second_half, first_half], axis=-1)


def rotate_back(values):
    first_half = values[..., : HD // 2]
    second_half = values[..., HD // 2 :]
    return jnp.concatenate([second_half, -first_half], axis=-1)


def block_mask(seg_seq, first_row, block_rows):
    length = seg_seq.shape[0]
    query_index = first_row + jnp.arange(block_rows)
    key_index = jnp.arange(length)
    query_seg = seg_seq[first_row : first_row + block_rows]
    return (
        (query_seg[:, None] == seg_seq[None, :]) & (key_index[None, :] <= query_index[:, None])
    )[None]


def attend_forward(packed):
    query_rot, key_rot, value_heads, seg_seq = packed
    length = query_rot.shape[0]
    block_rows = min(512, length)
    score_scale = HD ** (-0.5)
    output_list = []
    log_list = []
    for first_row in range(0, length, block_rows):
        query_blk = query_rot[first_row : first_row + block_rows]
        scores = (
            jnp.einsum("qhd,khd->hqk", query_blk, key_rot, preferred_element_type=jnp.float32)
            * score_scale
        )
        allowed = block_mask(seg_seq, first_row, block_rows)
        masked = jnp.where(allowed, scores, NEG_FILL)
        row_peak = jnp.max(masked, axis=-1, keepdims=True)
        row_total = jnp.sum(jnp.exp(masked - row_peak), axis=-1, keepdims=True)
        log_total = row_peak + jnp.log(row_total)
        probs_b = jnp.where(allowed, jnp.exp(scores - log_total), 0.0).astype(jnp.bfloat16)
        attended = jnp.einsum(
            "hqk,khd->qhd", probs_b, value_heads, preferred_element_type=jnp.float32
        ).astype(jnp.bfloat16)
        output_list.append(attended)
        log_list.append(log_total[..., 0])
    return (jnp.concatenate(output_list, axis=0), jnp.concatenate(log_list, axis=1))


def attend_backward(packed):
    query_rot, key_rot, value_heads, seg_seq, attended, log_total, grad_att = packed
    length = query_rot.shape[0]
    block_rows = min(512, length)
    score_scale = HD ** (-0.5)
    delta = jnp.sum(grad_att.astype(jnp.float32) * attended.astype(jnp.float32), axis=-1)
    grad_key = jnp.zeros(key_rot.shape, jnp.float32)
    grad_value = jnp.zeros(value_heads.shape, jnp.float32)
    grad_query_list = []
    for first_row in range(0, length, block_rows):
        query_blk = query_rot[first_row : first_row + block_rows]
        grad_blk = grad_att[first_row : first_row + block_rows]
        scores = (
            jnp.einsum("qhd,khd->hqk", query_blk, key_rot, preferred_element_type=jnp.float32)
            * score_scale
        )
        allowed = block_mask(seg_seq, first_row, block_rows)
        probs = jnp.where(
            allowed, jnp.exp(scores - log_total[:, first_row : first_row + block_rows, None]), 0.0
        )
        probs_b = probs.astype(jnp.bfloat16)
        grad_probs = jnp.einsum(
            "qhd,khd->hqk", grad_blk, value_heads, preferred_element_type=jnp.float32
        )
        delta_blk = jnp.transpose(delta[first_row : first_row + block_rows])[:, :, None]
        grad_scores = (probs * (grad_probs - delta_blk) * score_scale).astype(jnp.bfloat16)
        grad_query_list.append(
            jnp.einsum("hqk,khd->qhd", grad_scores, key_rot, preferred_element_type=jnp.float32)
        )
        grad_key = grad_key + jnp.einsum(
            "hqk,qhd->khd", grad_scores, query_blk, preferred_element_type=jnp.float32
        )
        grad_value = grad_value + jnp.einsum(
            "hqk,qhd->khd", probs_b, grad_blk, preferred_element_type=jnp.float32
        )
    return (jnp.concatenate(grad_query_list, axis=0), grad_key, grad_value)


def shards(
    block_input,
    segment_ids,
    positions,
    w_query,
    w_key,
    w_value,
    w_out,
    w_gate,
    w_up,
    w_down,
    query_gain,
    key_gain,
    attn_gain,
    mlp_gain,
    grad_output,
):
    tokens_here = block_input.shape[0]
    seq_count = tokens_here // LEN
    width = block_input.shape[1]
    local_width = w_query.shape[1]
    local_heads = local_width // HD
    gathered = (
        lax.all_gather(w_query, "row", axis=0, tiled=True),
        lax.all_gather(w_key, "row", axis=0, tiled=True),
        lax.all_gather(w_value, "row", axis=0, tiled=True),
        lax.all_gather(w_out, "row", axis=1, tiled=True),
        lax.all_gather(w_gate, "row", axis=0, tiled=True),
        lax.all_gather(w_up, "row", axis=0, tiled=True),
        lax.all_gather(w_down, "row", axis=1, tiled=True),
    )
    full_query, full_key, full_value, full_out, full_gate, full_up, full_down = gathered
    query_raw = plain_dot(block_input, full_query)
    key_raw = plain_dot(block_input, full_key)
    value_raw = plain_dot(block_input, full_value)
    query_sq, key_sq = lax.psum(
        (jnp.sum(query_raw * query_raw, axis=1), jnp.sum(key_raw * key_raw, axis=1)), "col"
    )
    query_scale = lax.rsqrt(query_sq / width + EPS)[:, None]
    key_scale = lax.rsqrt(key_sq / width + EPS)[:, None]
    query_unit = query_raw * query_scale
    key_unit = key_raw * key_scale
    cosine, sine_tab = rope_tables(positions)

    def turn(values):
        head_view = values.reshape(tokens_here, local_heads, HD)
        return head_view * cosine[:, None, :] + rotate(head_view) * sine_tab[:, None, :]

    def unturn(values):
        back = values * cosine[:, None, :] + rotate_back(values * sine_tab[:, None, :])
        return back.reshape(tokens_here, local_width)

    seq_shape = (seq_count, LEN, local_heads, HD)
    query_rot = turn(query_unit * query_gain).astype(jnp.bfloat16).reshape(seq_shape)
    key_rot = turn(key_unit * key_gain).astype(jnp.bfloat16).reshape(seq_shape)
    value_heads = value_raw.astype(jnp.bfloat16).reshape(seq_shape)
    seg_view = segment_ids.reshape(seq_count, LEN)
    attended, log_total = lax.map(attend_forward, (query_rot, key_rot, value_heads, seg_view))
    attended_flat = attended.reshape(tokens_here, local_width)
    attn_raw = lax.psum(plain_dot(attended_flat, full_out), "col")
    attn_scale = lax.rsqrt(jnp.mean(attn_raw * attn_raw, axis=1, keepdims=True) + EPS)
    attn_unit = attn_raw * attn_scale
    hidden = block_input.astype(jnp.float32) + attn_unit * attn_gain
    hidden_b = hidden.astype(jnp.bfloat16)
    gate_proj = plain_dot(hidden_b, full_gate)
    up_proj = plain_dot(hidden_b, full_up)
    gate_sig = jax.nn.sigmoid(gate_proj)
    gate_act = gate_proj * gate_sig
    mixed_act = (gate_act * up_proj).astype(jnp.bfloat16)
    down_raw = lax.psum(plain_dot(mixed_act, full_down), "col")
    down_scale = lax.rsqrt(jnp.mean(down_raw * down_raw, axis=1, keepdims=True) + EPS)
    down_unit = down_raw * down_scale
    block_output = (hidden + down_unit * mlp_gain).astype(jnp.bfloat16)
    regathered = (
        lax.all_gather(w_query, "row", axis=0, tiled=True),
        lax.all_gather(w_key, "row", axis=0, tiled=True),
        lax.all_gather(w_value, "row", axis=0, tiled=True),
        lax.all_gather(w_out, "row", axis=1, tiled=True),
        lax.all_gather(w_gate, "row", axis=0, tiled=True),
        lax.all_gather(w_up, "row", axis=0, tiled=True),
        lax.all_gather(w_down, "row", axis=1, tiled=True),
    )
    full_query, full_key, full_value, full_out, full_gate, full_up, full_down = regathered
    grad_y = grad_output.astype(jnp.float32)
    grad_mlp_gain = jnp.sum(grad_y * down_unit, axis=0)
    down_dz = grad_y * mlp_gain
    grad_down_in = (
        down_scale * (down_dz - down_unit * jnp.mean(down_dz * down_unit, axis=1, keepdims=True))
    ).astype(jnp.bfloat16)
    grad_w_down = left_transposed(mixed_act, grad_down_in)
    grad_mixed = times_transposed(grad_down_in, full_down)
    grad_gate_in = (grad_mixed * up_proj * gate_sig * (1.0 + gate_proj * (1.0 - gate_sig))).astype(
        jnp.bfloat16
    )
    grad_up_in = (grad_mixed * gate_act).astype(jnp.bfloat16)
    grad_w_gate = left_transposed(hidden_b, grad_gate_in)
    grad_w_up = left_transposed(hidden_b, grad_up_in)
    mlp_part = times_transposed(grad_gate_in, full_gate) + times_transposed(grad_up_in, full_up)
    grad_hidden = grad_y + lax.psum(mlp_part, "col")
    grad_attn_gain = jnp.sum(grad_hidden * attn_unit, axis=0)
    attn_dz = grad_hidden * attn_gain
    grad_attn_in = (
        attn_scale * (attn_dz - attn_unit * jnp.mean(attn_dz * attn_unit, axis=1, keepdims=True))
    ).astype(jnp.bfloat16)
    grad_w_out = left_transposed(attended_flat, grad_attn_in)
    grad_att = times_transposed(grad_attn_in, full_out).astype(jnp.bfloat16).reshape(seq_shape)
    grad_query_rot, grad_key_rot, grad_value_heads = lax.map(
        attend_backward, (query_rot, key_rot, value_heads, seg_view, attended, log_total, grad_att)
    )
    head_shape = (tokens_here, local_heads, HD)
    grad_query_norm = unturn(grad_query_rot.reshape(head_shape))
    grad_key_norm = unturn(grad_key_rot.reshape(head_shape))
    grad_query_gain = jnp.sum(grad_query_norm * query_unit, axis=0)
    grad_key_gain = jnp.sum(grad_key_norm * key_unit, axis=0)
    query_dz = grad_query_norm * query_gain
    key_dz = grad_key_norm * key_gain
    query_dot, key_dot = lax.psum(
        (jnp.sum(query_dz * query_unit, axis=1), jnp.sum(key_dz * key_unit, axis=1)), "col"
    )
    grad_query_in = (query_scale * (query_dz - query_unit * (query_dot / width)[:, None])).astype(
        jnp.bfloat16
    )
    grad_key_in = (key_scale * (key_dz - key_unit * (key_dot / width)[:, None])).astype(
        jnp.bfloat16
    )
    grad_value_in = grad_value_heads.reshape(tokens_here, local_width).astype(jnp.bfloat16)
    input_part = (
        times_transposed(grad_query_in, full_query)
        + times_transposed(grad_key_in, full_key)
        + times_transposed(grad_value_in, full_value)
    )
    grad_input = grad_hidden + lax.psum(input_part.astype(jnp.bfloat16), "col").astype(jnp.float32)
    grad_w_query = left_transposed(block_input, grad_query_in)
    grad_w_key = left_transposed(block_input, grad_key_in)
    grad_w_value = left_transposed(block_input, grad_value_in)
    row_grads = (
        lax.psum_scatter(
            grad_w_query.astype(jnp.bfloat16), "row", scatter_dimension=0, tiled=True
        ).astype(jnp.float32),
        lax.psum_scatter(
            grad_w_key.astype(jnp.bfloat16), "row", scatter_dimension=0, tiled=True
        ).astype(jnp.float32),
        lax.psum_scatter(
            grad_w_value.astype(jnp.bfloat16), "row", scatter_dimension=0, tiled=True
        ).astype(jnp.float32),
        lax.psum_scatter(
            grad_w_out.astype(jnp.bfloat16), "row", scatter_dimension=1, tiled=True
        ).astype(jnp.float32),
        lax.psum_scatter(
            grad_w_gate.astype(jnp.bfloat16), "row", scatter_dimension=0, tiled=True
        ).astype(jnp.float32),
        lax.psum_scatter(
            grad_w_up.astype(jnp.bfloat16), "row", scatter_dimension=0, tiled=True
        ).astype(jnp.float32),
        lax.psum_scatter(
            grad_w_down.astype(jnp.bfloat16), "row", scatter_dimension=1, tiled=True
        ).astype(jnp.float32),
    )
    data_grads = (
        lax.psum(row_grads[0].astype(jnp.bfloat16), "dp").astype(jnp.float32),
        lax.psum(row_grads[1].astype(jnp.bfloat16), "dp").astype(jnp.float32),
        lax.psum(row_grads[2].astype(jnp.bfloat16), "dp").astype(jnp.float32),
        lax.psum(row_grads[3].astype(jnp.bfloat16), "dp").astype(jnp.float32),
        lax.psum(row_grads[4].astype(jnp.bfloat16), "dp").astype(jnp.float32),
        lax.psum(row_grads[5].astype(jnp.bfloat16), "dp").astype(jnp.float32),
        lax.psum(row_grads[6].astype(jnp.bfloat16), "dp").astype(jnp.float32),
    )
    gain_grads = lax.psum(
        (grad_query_gain, grad_key_gain, grad_attn_gain, grad_mlp_gain), ("dp", "row")
    )
    return (
        block_output,
        grad_input,
        data_grads[0],
        data_grads[1],
        data_grads[2],
        data_grads[3],
        data_grads[4],
        data_grads[5],
        data_grads[6],
        gain_grads[0],
        gain_grads[1],
        gain_grads[2],
        gain_grads[3],
    )


def solution(mesh):
    in_specs = (
        P(("dp", "row"), None),
        P(("dp", "row")),
        P(("dp", "row")),
        P("row", "col"),
        P("row", "col"),
        P("row", "col"),
        P("col", "row"),
        P("row", "col"),
        P("row", "col"),
        P("col", "row"),
        P("col"),
        P("col"),
        P(),
        P(),
        P(("dp", "row"), None),
    )
    out_specs = (
        P(("dp", "row"), None),
        P(("dp", "row"), None),
        P("row", "col"),
        P("row", "col"),
        P("row", "col"),
        P("col", "row"),
        P("row", "col"),
        P("row", "col"),
        P("col", "row"),
        P("col"),
        P("col"),
        P(),
        P(),
    )
    return jax.shard_map(shards, mesh=mesh, in_specs=in_specs, out_specs=out_specs, check_vma=False)
```

profile of v0, /device:TPU:0, one launch (start us, length us, event | category | flops | bytes accessed | tf_op | source)
XLA Modules:
  0.0 2085.6 jit_solution(18045758009475935675)
XLA Ops:
  15.1 32.7 %all-gather.12.cloned.1.call-done = bf16[2048,512]{1,0:T(8,128)(2,1)} async-done(((bf16[512,512]{1,0:T(8,128)(2,1)}), bf16[2048,512]{1,0:T(8,128)(2,1)}) %all-gather.12.cloned.1.call-update) | async-done | bytes 2097168 | tf_op jit(solution)/shard_map/all_gather | solution.py:151
  54.4 30.5 %all-gather.10.cloned.1.call-done = bf16[2048,512]{1,0:T(8,128)(2,1)} async-done(((bf16[512,512]{1,0:T(8,128)(2,1)}), bf16[2048,512]{1,0:T(8,128)(2,1)}) %all-gather.10.cloned.1.call-update) | async-done | bytes 2097168 | tf_op jit(solution)/shard_map/all_gather | solution.py:150
  90.1 12.2 all-reduce.2
  134.5 13.8 fusion.22
  158.6 7.2 fusion.41
  168.0 288.9 %all-reduce.10.cloned.1.call-done = f32[1024,2048]{1,0:T(8,128)} async-done(((f32[1024,2048]{1,0:T(8,128)}), f32[1024,2048]{1,0:T(8,128)}) %all-reduce.10.cloned.1.call-update) | async-done | bytes 8388624 | tf_op jit(solution)/shard_map/psum | solution.py:186
  467.6 77.5 %all-gather.16.cloned.1.call-done = bf16[2048,2048]{1,0:T(8,128)(2,1)} async-done(((bf16[512,2048]{1,0:T(8,128)(2,1)}), bf16[2048,2048]{1,0:T(8,128)(2,1)}) %all-gather.16.cloned.1.call-update) | async-done | bytes 8388624 | tf_op jit(solution)/shard_map/all_gather | solution.py:154
  545.1 14.5 fusion.42
  559.7 74.8 %all-gather.18.cloned.1.call-done = bf16[2048,2048]{1,0:T(8,128)(2,1)} async-done(((bf16[512,2048]{1,0:T(8,128)(2,1)}), bf16[2048,2048]{1,0:T(8,128)(2,1)}) %all-gather.18.cloned.1.call-update) | async-done | bytes 8388624 | tf_op jit(solution)/shard_map/all_gather | solution.py:155
  634.5 17.0 multiply_convert_fusion.5
  651.4 72.3 %all-gather.20.cloned.1.call-done = bf16[2048,2048]{1,0:T(8,128)(2,1)} async-done(((bf16[2048,512]{1,0:T(8,128)(2,1)}), bf16[2048,2048]{1,0:T(8,128)(2,1)}) %all-gather.20.cloned.1.call-update) | async-done | bytes 8388624 | tf_op jit(solution)/shard_map/all_gather | solution.py:156
  723.7 14.5 fusion.43
  738.3 290.9 %all-reduce.12.cloned.1.call-done = f32[1024,2048]{1,0:T(8,128)} async-done(((f32[1024,2048]{1,0:T(8,128)}), f32[1024,2048]{1,0:T(8,128)}) %all-reduce.12.cloned.1.call-update) | async-done | bytes 8388624 | tf_op jit(solution)/shard_map/psum | solution.py:196
  1042.8 19.7 multiply_convert_fusion.3
  1062.5 12.7 fusion.44
  1075.2 13.6 convolution_add_fusion
  1090.9 288.0 %all-reduce.14.cloned.1.call-done = f32[1024,2048]{1,0:T(8,128)} async-done(((f32[1024,2048]{1,0:T(8,128)}), f32[1024,2048]{1,0:T(8,128)}) %all-reduce.14.cloned.1.call-update) | async-done | bytes 8388624 | tf_op jit(solution)/shard_map/psum | solution.py:225
  1378.9 10.6 multiply_reduce_fusion
  1389.5 13.4 multiply_convert_fusion.2
  1413.4 7.3 multiply_convert_fusion.1
  1469.9 9.6 all-reduce.1
  1499.9 14.4 convolution_convert_fusion
  1514.4 14.1 convolution_convert_fusion.2
  1528.5 14.6 convolution_convert_fusion.1
  1558.8 38.0 %reduce-scatter.8.cloned.1.call-done = bf16[512,512]{0,1:T(8,128)(2,1)} async-done(((bf16[2048,512]{0,1:T(8,128)(2,1)}), bf16[512,512]{0,1:T(8,128)(2,1)}) %reduce-scatter.8.cloned.1.call-update) | async-done | bytes 524304 | tf_op jit(solution)/shard_map/reduce_scatter | solution.py:263
  1596.8 89.2 %reduce-scatter.20.cloned.1.call-done = bf16[2048,512]{1,0:T(8,128)(2,1)} async-done(((bf16[2048,2048]{1,0:T(8,128)(2,1)}), bf16[2048,512]{1,0:T(8,128)(2,1)}) %reduce-scatter.20.cloned.1.call-update) | async-done | bytes 2097168 | tf_op jit(solution)/shard_map/reduce_scatter | solution.py:281
  1686.1 89.8 %reduce-scatter.16.cloned.1.call-done = bf16[512,2048]{1,0:T(8,128)(2,1)} async-done(((bf16[2048,2048]{1,0:T(8,128)(2,1)}), bf16[512,2048]{1,0:T(8,128)(2,1)}) %reduce-scatter.16.cloned.1.call-update) | async-done | bytes 2097168 | tf_op jit(solution)/shard_map/reduce_scatter | solution.py:275
  1775.9 89.2 %reduce-scatter.18.cloned.1.call-done = bf16[512,2048]{1,0:T(8,128)(2,1)} async-done(((bf16[2048,2048]{1,0:T(8,128)(2,1)}), bf16[512,2048]{1,0:T(8,128)(2,1)}) %reduce-scatter.18.cloned.1.call-update) | async-done | bytes 2097168 | tf_op jit(solution)/shard_map/reduce_scatter | solution.py:278
  1865.9 27.8 %all-reduce = (f32[512]{0:T(512)}, f32[512]{0:T(512)}, f32[2048]{0:T(1024)}, f32[2048]{0:T(1024)}) all-reduce(f32[512]{0:T(512)S(1)} %get-tuple-element.86, f32[512]{0:T(512)S(1)} %get-tuple-element.84, f32[2048]{0:T(1024)S(1)} %copy-done.64, f32[2048]{0:T(1024)S(1)} %copy-done.65), channel_id=1, replica_groups=mesh['dp'=2,'row'=4,'col'=4] {'dp','row'}, use_global_device_ids=true, to_apply=%region_36.37 | all-reduce | flops 5120 | bytes 40960 | tf_op jit(solution)/shard_map/psum | solution.py:294
  1893.7 129.3 %all-reduce.16.cloned.1.call-done = bf16[1024,2048]{1,0:T(8,128)(2,1)} async-done(((bf16[1024,2048]{1,0:T(8,128)(2,1)}), bf16[1024,2048]{1,0:T(8,128)(2,1)}) %all-reduce.16.cloned.1.call-update) | async-done | bytes 4194320 | tf_op jit(solution)/shard_map/psum | solution.py:258
  2023.0 12.0 convert_add_fusion.1
  2035.0 29.7 %all-reduce.18.cloned.1.call-done = (bf16[512,512]{0,1:T(8,128)(2,1)}, bf16[512,512]{0,1:T(8,128)(2,1)}, bf16[512,512]{0,1:T(8,128)(2,1)}, bf16[512,512]{1,0:T(8...) async-done(((bf16[512,512]{0,1:T(8,128)(2,1)}, bf16[512,512]{0,1:T(8,128)(2,1)}, bf16[512,512]{0,1:T(8,128)(2,1)}, ...) | async-done | bytes 8388624 | tf_op jit(solution)/shard_map/psum | solution.py:286
  (283 shorter events, 200.3 us)
Async XLA Ops:
  7.2 40.6 %all-gather.12.cloned.1.call-start = ((), (), s32[]{:S(2)}) async-start(), calls=%async_computation.9 | async-start | bytes 2621440 | tf_op jit(solution)/shard_map/all_gather | solution.py:151
  7.9 76.9 %all-gather.10.cloned.1.call-start = ((), (), s32[]{:S(2)}) async-start(), calls=%async_computation.8 | async-start | bytes 2621440 | tf_op jit(solution)/shard_map/all_gather | solution.py:150
  8.7 119.9 %all-gather.8.cloned.1.call-start = ((), (), s32[]{:S(2)}) async-start(), calls=%async_computation.7 | async-start | bytes 2621440 | tf_op jit(solution)/shard_map/all_gather | solution.py:152
  9.4 149.2 %all-gather.14.cloned.1.call-start = ((), (), s32[]{:S(2)}) async-start(), calls=%async_computation.10 | async-start | bytes 2621440 | tf_op jit(solution)/shard_map/all_gather | solution.py:153
  10.0 446.9 %all-reduce.10.cloned.1.call-start = ((), (), s32[]{:S(2)}) async-start(), calls=%async_computation.11 | async-start | bytes 16777216 | tf_op jit(solution)/shard_map/psum | solution.py:186
  12.8 103.2 %copy-start.22 = (f32[1024,128]{1,0:T(8,128)}, f32[1024,128]{1,0:T(8,128)S(1)}, u32[]{:S(2)}) copy-start(f32[1024,128]{1,0:T(8,128)S(1)} %pad_maximum_fusion.2) | copy-start | bytes 1572868
  13.1 103.0 %copy-start.27 = (f32[1024,128]{1,0:T(8,128)}, f32[1024,128]{1,0:T(8,128)S(1)}, u32[]{:S(2)}) copy-start(f32[1024,128]{1,0:T(8,128)S(1)} %pad_maximum_fusion.3) | copy-start | bytes 1572868
  54.3 48.0 %copy-start.68 = (f32[512]{0:T(512)S(1)}, f32[512]{0:T(512)}, u32[]{:S(2)}) copy-start(f32[512]{0:T(512)} %param.25) | copy-start | bytes 6148
  90.1 13.8 copy-start.9
  128.5 19.8 copy-start.71
  134.3 14.0 copy-start.77
  134.5 13.8 copy-start.6
  151.7 14.1 copy-start.46
  165.9 379.2 %all-gather.16.cloned.1.call-start = ((), (), s32[]{:S(2)}) async-start(), calls=%async_computation.12 | async-start | bytes 10485760 | tf_op jit(solution)/shard_map/all_gather | solution.py:154
  166.5 468.0 %all-gather.18.cloned.1.call-start = ((), (), s32[]{:S(2)}) async-start(), calls=%async_computation.13 | async-start | bytes 10485760 | tf_op jit(solution)/shard_map/all_gather | solution.py:155
  167.2 556.4 %all-gather.20.cloned.1.call-start = ((), (), s32[]{:S(2)}) async-start(), calls=%async_computation.14 | async-start | bytes 10485760 | tf_op jit(solution)/shard_map/all_gather | solution.py:156
  168.0 293.7 %copy-start.56 = (f32[2048]{0:T(1024)S(1)}, f32[2048]{0:T(1024)}, u32[]{:S(2)}) copy-start(f32[2048]{0:T(1024)} %param.27) | copy-start | bytes 24580
  168.0 861.2 %all-reduce.12.cloned.1.call-start = ((), (), s32[]{:S(2)}) async-start(), calls=%async_computation.15 | async-start | bytes 16777216 | tf_op jit(solution)/shard_map/psum | solution.py:196
  738.2 295.2 %copy-start.55 = (f32[2048]{0:T(1024)S(1)}, f32[2048]{0:T(1024)}, u32[]{:S(2)}) copy-start(f32[2048]{0:T(1024)} %param.28) | copy-start | bytes 24580
  738.2 640.6 %all-reduce.14.cloned.1.call-start = ((), (), s32[]{:S(2)}) async-start(), calls=%async_computation.16 | async-start | bytes 16777216 | tf_op jit(solution)/shard_map/psum | solution.py:225
  1042.8 19.7 copy-start.34
  1088.9 290.0 %copy-start.57 = (f32[2048]{0:T(1024)S(1)}, f32[2048]{0:T(1024)}, u32[]{:S(2)}) copy-start(f32[2048]{0:T(1024)} %param.27) | copy-start | bytes 24580
  1088.9 290.0 %copy-start.63 = (f32[1024]{0:T(1024)S(1)}, f32[1024]{0:T(1024)}, u32[]{:S(2)}) copy-start(f32[1024]{0:T(1024)} %copy-done.62) | copy-start | bytes 12292
  1088.9 466.6 %reduce-scatter.12.cloned.1.call-start = ((), (), s32[]{:S(2)}) async-start(), calls=%async_computation.20 | async-start | bytes 2621440 | tf_op jit(solution)/shard_map/reduce_scatter | solution.py:269
  1433.7 121.8 %reduce-scatter.10.cloned.1.call-start = ((), (), s32[]{:S(2)}) async-start(), calls=%async_computation.19 | async-start | bytes 2621440 | tf_op jit(solution)/shard_map/reduce_scatter | solution.py:266
  1486.7 72.1 %reduce-scatter.14.cloned.1.call-start = ((), (), s32[]{:S(2)}) async-start(), calls=%async_computation.21 | async-start | bytes 2621440 | tf_op jit(solution)/shard_map/reduce_scatter | solution.py:272
  1493.0 103.9 %reduce-scatter.8.cloned.1.call-start = ((), (), s32[]{:S(2)}) async-start(), calls=%async_computation.18 | async-start | bytes 2621440 | tf_op jit(solution)/shard_map/reduce_scatter | solution.py:263
  1499.9 186.2 %reduce-scatter.20.cloned.1.call-start = ((), (), s32[]{:S(2)}) async-start(), calls=%async_computation.24 | async-start | bytes 10485760 | tf_op jit(solution)/shard_map/reduce_scatter | solution.py:281
  1514.4 261.6 %reduce-scatter.16.cloned.1.call-start = ((), (), s32[]{:S(2)}) async-start(), calls=%async_computation.22 | async-start | bytes 10485760 | tf_op jit(solution)/shard_map/reduce_scatter | solution.py:275
  1528.5 336.7 %reduce-scatter.18.cloned.1.call-start = ((), (), s32[]{:S(2)}) async-start(), calls=%async_computation.23 | async-start | bytes 10485760 | tf_op jit(solution)/shard_map/reduce_scatter | solution.py:278
  1543.2 479.8 %all-reduce.16.cloned.1.call-start = ((), (), s32[]{:S(2)}) async-start(), calls=%async_computation.17 | async-start | bytes 8388608 | tf_op jit(solution)/shard_map/psum | solution.py:258
  1555.4 509.2 %all-reduce.18.cloned.1.call-start = ((), (), s32[]{:S(2)}) async-start(), calls=%async_computation.25 | async-start | bytes 16777216 | tf_op jit(solution)/shard_map/psum | solution.py:286
  (69 other events, 309.0 us)
Sparse Core Ops, SparseCore 0:
  9.8 37.8 all-gather.11
  49.6 35.1 all-gather.9
  86.7 35.1 all-gather.7
  123.6 35.0 all-gather.13
  166.0 290.8 all-reduce.9
  458.6 86.4 all-gather.15
  547.0 87.4 all-gather.17
  636.3 87.3 all-gather.19
  738.3 290.8 all-reduce.11
  1089.0 289.8 all-reduce.13
  1433.8 34.1 reduce-scatter.11
  1486.8 33.7 reduce-scatter.9
  1523.6 35.1 reduce-scatter.13
  1561.6 35.1 reduce-scatter.7
  1599.7 86.2 reduce-scatter.19
  1689.6 86.3 reduce-scatter.15
  1778.8 86.2 reduce-scatter.17
  1867.9 154.9 all-reduce.15
  2026.3 38.3 all-reduce.17
where the time goes:
time: 2090 us
  waiting for transfers between devices  1640 us (78%)
  matrix products  247 us (12%)
  other arithmetic  103 us (5%)
  blocking collectives  49.7 us (2%)
  local copies, waits for them, and re-layouts  34 us (2%)
    psum x1, waiting for transfers between devices, shards(): down_raw = lax.psum(plain_dot(mixed_act, full_down), 'col')  291 us
    psum x1, waiting for transfers between devices, shards(): attn_raw = lax.psum(plain_dot(attended_flat, full_out), 'col')  289 us
    psum x1, waiting for transfers between devices, shards(): grad_hidden = grad_y + lax.psum(mlp_part, 'col')  288 us
    psum x1, waiting for transfers between devices, shards(): lax.psum(input_part.astype(jnp.bfloat16), 'col').astype(jnp.float32)  129 us
    reduce_scatter x1, waiting for transfers between devices, shards(): lax.psum_scatter(grad_w_gate.astype(jnp.bfloat16), 'row', scatter_dimensi...  89.8 us
    reduce_scatter x1, waiting for transfers between devices, shards(): lax.psum_scatter(grad_w_down.astype(jnp.bfloat16), 'row', scatter_dimensi...  89.2 us
    reduce_scatter x1, waiting for transfers between devices, shards(): lax.psum_scatter(grad_w_up.astype(jnp.bfloat16), 'row', scatter_dimension...  89.2 us
    all_gather x1, waiting for transfers between devices, shards(): lax.all_gather(w_gate, 'row', axis=0, tiled=True)  77.5 us
  transfers between devices with their start and end apart: 19, of which 16 were waited for; matrix products, arithmetic and copies ran while one was open for 11% of the time, Pallas kernels for 0%

commit v1 on v0

v1 whole, which is shorter than its diff:
```python
import functools

import jax
import jax.numpy as jnp
from jax import lax
from jax.experimental import pallas as pl
from jax.experimental.pallas import tpu as pltpu
from jax.sharding import PartitionSpec as P

HD = 128
LEN = 1024
BQ = 256

EPS = 1e-06
THETA = 500000.0
NEG_FILL = -1e30
SCORE_SCALE = HD ** (-0.5)
F32 = jnp.float32
BF16 = jnp.bfloat16


def plain_dot(left_mat, right_mat):
    return jnp.dot(left_mat, right_mat, preferred_element_type=F32)


def times_transposed(left_mat, right_mat):
    return lax.dot_general(
        left_mat, right_mat, (((1,), (1,)), ((), ())), preferred_element_type=F32
    )


def left_transposed(left_mat, right_mat):
    return lax.dot_general(
        left_mat, right_mat, (((0,), (0,)), ((), ())), preferred_element_type=F32
    )


def rope_tables(positions):
    half_dim = HD // 2
    inv_freq = THETA ** (-(jnp.arange(half_dim, dtype=F32) * 2.0) / HD)
    angles = positions.astype(F32)[:, None] * inv_freq[None, :]
    cos_half, sin_half = jnp.cos(angles), jnp.sin(angles)
    cosine = jnp.concatenate([cos_half, cos_half], axis=-1)
    sine_signed = jnp.concatenate([-sin_half, sin_half], axis=-1)
    return cosine, sine_signed


def allowed_block(seg_col_ref, seg_row_ref, first, keys):
    rows = seg_col_ref[pl.ds(first, BQ), :]
    cols = seg_row_ref[:, :keys]
    query_index = first + lax.broadcasted_iota(jnp.int32, (BQ, keys), 0)
    key_index = lax.broadcasted_iota(jnp.int32, (BQ, keys), 1)
    return (rows == cols) & (key_index <= query_index)


def attend_forward_kernel(
    q_ref, k_ref, v_ref, qs_ref, ks_ref, qg_ref, kg_ref, cos_ref, sin_ref, segc_ref, segr_ref,
    qrot_ref, krot_ref, vb_ref, att_ref, log_ref,
):
    cosine, sine = cos_ref[...], sin_ref[...]

    def turned(raw, scale, gain):
        norm = raw * scale * gain
        return (norm * cosine + pltpu.roll(norm, HD // 2, 1) * sine).astype(BF16)

    qrot_ref[...] = turned(q_ref[...], qs_ref[...], qg_ref[...])
    krot_ref[...] = turned(k_ref[...], ks_ref[...], kg_ref[...])
    vb_ref[...] = v_ref[...].astype(BF16)
    for first in range(0, LEN, BQ):
        keys = first + BQ
        scores = times_transposed(qrot_ref[first:keys, :], krot_ref[:keys, :]) * SCORE_SCALE
        allowed = allowed_block(segc_ref, segr_ref, first, keys)
        masked = jnp.where(allowed, scores, NEG_FILL)
        peak = jnp.max(masked, axis=1, keepdims=True)
        weight = jnp.exp(masked - peak)
        total = jnp.sum(weight, axis=1, keepdims=True)
        probs = (weight * (1.0 / total)).astype(BF16)
        att_ref[first:keys, :] = plain_dot(probs, vb_ref[:keys, :]).astype(BF16)
        log_ref[0, first:keys, :] = peak + jnp.log(total)


def attend_backward_kernel(
    q_ref, k_ref, qs_ref, ks_ref, qg_ref, kg_ref, cos_ref, sin_ref, segc_ref, segr_ref,
    qrot_ref, krot_ref, vb_ref, att_ref, log_ref, grad_ref,
    dzq_ref, dzk_ref, gv_ref, dotq_ref, dotk_ref, gainq_ref, gaink_ref,
    dq_acc, dk_acc, dv_acc,
):
    dk_acc[...] = jnp.zeros_like(dk_acc)
    dv_acc[...] = jnp.zeros_like(dv_acc)
    for first in range(0, LEN, BQ):
        keys = first + BQ
        queries = qrot_ref[first:keys, :]
        grads = grad_ref[first:keys, :]
        scores = times_transposed(queries, krot_ref[:keys, :]) * SCORE_SCALE
        allowed = allowed_block(segc_ref, segr_ref, first, keys)
        probs = jnp.where(allowed, jnp.exp(scores - log_ref[0, first:keys, :]), 0.0)
        delta = jnp.sum(
            grads.astype(F32) * att_ref[first:keys, :].astype(F32), axis=1, keepdims=True
        )
        grad_probs = times_transposed(grads, vb_ref[:keys, :])
        grad_scores = (probs * (grad_probs - delta) * SCORE_SCALE).astype(BF16)
        dq_acc[first:keys, :] = plain_dot(grad_scores, krot_ref[:keys, :])
        dk_acc[:keys, :] += left_transposed(grad_scores, queries)
        dv_acc[:keys, :] += left_transposed(probs.astype(BF16), grads)
    gv_ref[...] = dv_acc[...].astype(BF16)
    cosine, sine = cos_ref[...], sin_ref[...]

    def finish(acc, raw_ref, scale_ref, gain_ref, dz_ref, dot_ref, gain_grad_ref):
        grad_rot = acc[...]
        grad_norm = grad_rot * cosine - pltpu.roll(grad_rot, HD // 2, 1) * sine
        unit = raw_ref[...] * scale_ref[...]
        gain_grad_ref[...] = jnp.sum(grad_norm * unit, axis=0, keepdims=True)
        grad_unit = grad_norm * gain_ref[...]
        dz_ref[...] = grad_unit
        part = jnp.sum(grad_unit * unit, axis=1, keepdims=True)

        @pl.when(pl.program_id(0) == 0)
        def _():
            dot_ref[...] = part

        @pl.when(pl.program_id(0) > 0)
        def _():
            dot_ref[...] += part

    finish(dq_acc, q_ref, qs_ref, qg_ref, dzq_ref, dotq_ref, gainq_ref)
    finish(dk_acc, k_ref, ks_ref, kg_ref, dzk_ref, dotk_ref, gaink_ref)


def head_spec(offset):
    return pl.BlockSpec((LEN, HD), lambda h: (0, offset + h))


def whole_spec(shape):
    return pl.BlockSpec(shape, lambda h: (0,) * len(shape))


def gain_spec():
    return pl.BlockSpec((1, HD), lambda h: (0, h))


LOG_SPEC = pl.BlockSpec((1, LEN, 1), lambda h: (h, 0, 0))
COLUMN = (LEN, 1)
TABLE = (LEN, HD)


def attend_forward(qkv, scales, gains, tables, seg_col, seg_row, heads):
    width = heads * HD
    piece = jax.ShapeDtypeStruct((LEN, width), BF16)
    return pl.pallas_call(
        attend_forward_kernel,
        grid=(heads,),
        in_specs=[
            head_spec(0), head_spec(heads), head_spec(2 * heads),
            whole_spec(COLUMN), whole_spec(COLUMN), gain_spec(), gain_spec(),
            whole_spec(TABLE), whole_spec(TABLE), whole_spec(COLUMN), whole_spec((1, LEN)),
        ],
        out_specs=[head_spec(0)] * 4 + [LOG_SPEC],
        out_shape=[piece] * 4 + [jax.ShapeDtypeStruct((heads, LEN, 1), F32)],
        compiler_params=pltpu.CompilerParams(vmem_limit_bytes=48 << 20),
        cost_estimate=pl.CostEstimate(
            flops=heads * 4 * LEN * LEN * HD, bytes_accessed=LEN * width * 20, transcendentals=0
        ),
        name="attend_forward",
    )(qkv, qkv, qkv, *scales, *gains, *tables, seg_col, seg_row)


def attend_backward(qkv, scales, gains, tables, seg_col, seg_row, saved, grad_att, heads):
    width = heads * HD
    full = jax.ShapeDtypeStruct((LEN, width), F32)
    column = jax.ShapeDtypeStruct(COLUMN, F32)
    gain_row = jax.ShapeDtypeStruct((1, width), F32)
    return pl.pallas_call(
        attend_backward_kernel,
        grid=(heads,),
        in_specs=[
            head_spec(0), head_spec(heads),
            whole_spec(COLUMN), whole_spec(COLUMN), gain_spec(), gain_spec(),
            whole_spec(TABLE), whole_spec(TABLE), whole_spec(COLUMN), whole_spec((1, LEN)),
            head_spec(0), head_spec(0), head_spec(0), head_spec(0), LOG_SPEC, head_spec(0),
        ],
        out_specs=[
            head_spec(0), head_spec(0), head_spec(0),
            whole_spec(COLUMN), whole_spec(COLUMN), gain_spec(), gain_spec(),
        ],
        out_shape=[
            full, full, jax.ShapeDtypeStruct((LEN, width), BF16), column, column, gain_row, gain_row,
        ],
        scratch_shapes=[pltpu.VMEM((LEN, HD), F32)] * 3,
        compiler_params=pltpu.CompilerParams(vmem_limit_bytes=48 << 20),
        cost_estimate=pl.CostEstimate(
            flops=heads * 10 * LEN * LEN * HD, bytes_accessed=LEN * width * 40, transcendentals=0
        ),
        name="attend_backward",
    )(qkv, qkv, *scales, *gains, *tables, seg_col, seg_row, *saved, grad_att)


def shards(
    sizes,
    block_input,
    segment_ids,
    positions,
    w_query,
    w_key,
    w_value,
    w_out,
    w_gate,
    w_up,
    w_down,
    query_gain,
    key_gain,
    attn_gain,
    mlp_gain,
    grad_output,
):
    cores, rows, cols = sizes
    tokens_here, width = block_input.shape
    assert tokens_here == LEN and cores == 2
    local_width = w_query.shape[1]
    heads = local_width // HD
    core = lax.axis_index("dp")
    swap = [(0, 1), (1, 0)]

    def own_half(array, axis):
        half = array.shape[axis] // 2
        return lax.dynamic_slice_in_dim(array, core * half, half, axis)

    def other_half(array, axis):
        half = array.shape[axis] // 2
        return lax.dynamic_slice_in_dim(array, (1 - core) * half, half, axis)

    def gather(weight, axis):
        return lax.all_gather(own_half(weight, axis), ("row", "dp"), axis=axis, tiled=True)

    def sum_over_col(partial):
        piece = lax.psum_scatter(partial.astype(BF16), "col", scatter_dimension=0, tiled=True)
        whole = lax.all_gather(piece, ("dp", "col"), axis=0, tiled=True)
        return lax.dynamic_slice_in_dim(whole, core * tokens_here, tokens_here, 0).astype(F32)

    def both_cores(half, axis):
        other = lax.ppermute(half, "dp", swap)
        first = jnp.where(core == 0, half, other)
        second = jnp.where(core == 0, other, half)
        return jnp.concatenate([first, second], axis=axis).astype(F32)

    def summed(left_mat, right_own, right_other):
        sent = left_transposed(left_mat, right_other).astype(BF16)
        got = lax.ppermute(sent, "dp", swap)
        total = (left_transposed(left_mat, right_own) + got.astype(F32)).astype(BF16)
        return lax.psum_scatter(total, "row", scatter_dimension=0, tiled=True)

    full_qkv = gather(jnp.concatenate([w_query, w_key, w_value], axis=1), 0)
    full_out = gather(w_out, 1)
    full_gate = gather(w_gate, 0)
    full_up = gather(w_up, 0)
    full_down = gather(w_down, 1)

    qkv = plain_dot(block_input, full_qkv)
    query_raw, key_raw = qkv[:, :local_width], qkv[:, local_width : 2 * local_width]
    query_sq, key_sq = lax.psum(
        (jnp.sum(query_raw * query_raw, axis=1), jnp.sum(key_raw * key_raw, axis=1)), "col"
    )
    query_scale = lax.rsqrt(query_sq / width + EPS)[:, None]
    key_scale = lax.rsqrt(key_sq / width + EPS)[:, None]
    scales = (query_scale, key_scale)
    gains = (query_gain[None, :], key_gain[None, :])
    tables = rope_tables(positions)
    seg_col, seg_row = segment_ids[:, None], segment_ids[None, :]
    query_rot, key_rot, value_heads, attended, log_total = attend_forward(
        qkv, scales, gains, tables, seg_col, seg_row, heads
    )
    attn_raw = sum_over_col(plain_dot(attended, full_out))
    attn_scale = lax.rsqrt(jnp.mean(attn_raw * attn_raw, axis=1, keepdims=True) + EPS)
    attn_unit = attn_raw * attn_scale
    hidden = block_input.astype(F32) + attn_unit * attn_gain
    hidden_b = hidden.astype(BF16)
    gate_proj = plain_dot(hidden_b, full_gate)
    up_proj = plain_dot(hidden_b, full_up)
    gate_sig = jax.nn.sigmoid(gate_proj)
    gate_act = gate_proj * gate_sig
    mixed_act = (gate_act * up_proj).astype(BF16)
    down_raw = sum_over_col(plain_dot(mixed_act, full_down))
    down_scale = lax.rsqrt(jnp.mean(down_raw * down_raw, axis=1, keepdims=True) + EPS)
    down_unit = down_raw * down_scale
    block_output = (hidden + down_unit * mlp_gain).astype(BF16)

    grad_y = grad_output.astype(F32)
    grad_mlp_gain = jnp.sum(grad_y * down_unit, axis=0)
    down_dz = grad_y * mlp_gain
    grad_down_in = (
        down_scale * (down_dz - down_unit * jnp.mean(down_dz * down_unit, axis=1, keepdims=True))
    ).astype(BF16)
    grad_mixed = times_transposed(grad_down_in, full_down)
    grad_gate_in = (grad_mixed * up_proj * gate_sig * (1.0 + gate_proj * (1.0 - gate_sig))).astype(BF16)
    grad_up_in = (grad_mixed * gate_act).astype(BF16)
    mlp_part = times_transposed(grad_gate_in, full_gate) + times_transposed(grad_up_in, full_up)
    grad_hidden = grad_y + sum_over_col(mlp_part)
    down_block = summed(grad_down_in, own_half(mixed_act, 1), other_half(mixed_act, 1))
    gate_block = summed(hidden_b, own_half(grad_gate_in, 1), other_half(grad_gate_in, 1))
    up_block = summed(hidden_b, own_half(grad_up_in, 1), other_half(grad_up_in, 1))

    grad_attn_gain = jnp.sum(grad_hidden * attn_unit, axis=0)
    attn_dz = grad_hidden * attn_gain
    grad_attn_in = (
        attn_scale * (attn_dz - attn_unit * jnp.mean(attn_dz * attn_unit, axis=1, keepdims=True))
    ).astype(BF16)
    grad_att = times_transposed(grad_attn_in, full_out).astype(BF16)
    query_dz, key_dz, grad_value_in, query_dot, key_dot, grad_query_gain, grad_key_gain = attend_backward(
        qkv, scales, gains, tables, seg_col, seg_row,
        (query_rot, key_rot, value_heads, attended, log_total), grad_att, heads,
    )
    query_dot, key_dot = lax.psum((query_dot[:, 0], key_dot[:, 0]), "col")
    grad_query_in = (
        query_scale * (query_dz - query_raw * query_scale * (query_dot / width)[:, None])
    ).astype(BF16)
    grad_key_in = (
        key_scale * (key_dz - key_raw * key_scale * (key_dot / width)[:, None])
    ).astype(BF16)
    grad_qkv = jnp.concatenate([grad_query_in, grad_key_in, grad_value_in], axis=1)
    grad_input = grad_hidden + sum_over_col(times_transposed(grad_qkv, full_qkv))

    def interleaved(picker):
        return jnp.concatenate(
            [picker(one, 1) for one in (grad_query_in, grad_key_in, grad_value_in)], axis=1
        )

    qkv_block = summed(block_input, interleaved(own_half), interleaved(other_half))
    out_block = summed(grad_attn_in, own_half(attended, 1), other_half(attended, 1))
    qkv_pair = both_cores(qkv_block[None], 0)
    quarter = local_width // 2

    def projection(index):
        part = qkv_pair[:, :, index * quarter : (index + 1) * quarter]
        return jnp.concatenate([part[0], part[1]], axis=1)

    gain_grads = lax.psum(
        (grad_query_gain[0], grad_key_gain[0], grad_attn_gain, grad_mlp_gain), ("dp", "row")
    )
    return (
        block_output,
        grad_input,
        projection(0),
        projection(1),
        projection(2),
        jnp.transpose(both_cores(out_block, 1)),
        both_cores(gate_block, 1),
        both_cores(up_block, 1),
        jnp.transpose(both_cores(down_block, 1)),
        gain_grads[0],
        gain_grads[1],
        gain_grads[2],
        gain_grads[3],
    )


def solution(mesh):
    in_specs = (
        P(("dp", "row"), None),
        P(("dp", "row")),
        P(("dp", "row")),
        P("row", "col"),
        P("row", "col"),
        P("row", "col"),
        P("col", "row"),
        P("row", "col"),
        P("row", "col"),
        P("col", "row"),
        P("col"),
        P("col"),
        P(),
        P(),
        P(("dp", "row"), None),
    )
    out_specs = (
        P(("dp", "row"), None),
        P(("dp", "row"), None),
        P("row", "col"),
        P("row", "col"),
        P("row", "col"),
        P("col", "row"),
        P("row", "col"),
        P("row", "col"),
        P("col", "row"),
        P("col"),
        P("col"),
        P(),
        P(),
    )
    sizes = (mesh.shape["dp"], mesh.shape["row"], mesh.shape["col"])
    return jax.shard_map(
        functools.partial(shards, sizes), mesh=mesh, in_specs=in_specs, out_specs=out_specs, check_vma=False
    )
```

time: 2090 us -> 1340 us (0.64)
  waiting for transfers between devices: 1640 us -> 939 us
  matrix products: 247 us -> 181 us
  Pallas kernels: 0 us -> 33.6 us
  other arithmetic: 103 us -> 75.2 us
    psum x5 -> x0, waiting for transfers between devices: 1030 us -> none  [the longest x1 291 us: shards(): down_raw = lax.psum(plain_dot(mixed_act, full_down), 'col')]
    all_gather x7 -> x9, waiting for transfers between devices: 295 us -> 465 us  [the longest x4 293 us: sum_over_col(): whole = lax.all_gather(piece, ('dp', 'col'), axis=0, tiled=True)]
    reduce_scatter x7 -> x9, waiting for transfers between devices: 310 us -> 444 us  [the longest x4 226 us: sum_over_col(): lax.psum_scatter(partial.astype(BF16), 'col', scatter_dimension=0, tiled=...]
    dot_general x19 -> x5, matrix products: 125 us -> 63.1 us  [plain_dot(): return jnp.dot(left_mat, right_mat, preferred_element_type=F32)]
    pallas_call x0 -> x2, Pallas kernels: none -> 33.6 us  [the longest x1 17.5 us: attend_forward(): pl.pallas_call(attend_forward_kernel, grid=(heads,), in_specs=[head_spec(...]
    ppermute x0 -> x10, waiting for transfers between devices: none -> 29.2 us  [the longest x5 29.2 us: summed(): got = lax.ppermute(sent, 'dp', swap)]
    dot_general x7 -> x10, matrix products: 60.3 us -> 57.4 us  [left_transposed(): lax.dot_general(left_mat, right_mat, (((0,), (0,)), ((), ())), preferred_...]
    dot_general x7 -> x5, matrix products: 61.9 us -> 60.6 us  [times_transposed(): lax.dot_general(left_mat, right_mat, (((1,), (1,)), ((), ())), preferred_...]
  transfers between devices with their start and end apart: 19 -> 28, of which waited for: 16 -> 21; matrix products, arithmetic and copies ran while one was open for 11% -> 11% of each run, Pallas kernels for 0% -> 1%
where the time goes in v1:
time: 1340 us; the launch traced here: 1330 us
  waiting for transfers between devices  939 us (70%)
  matrix products  181 us (14%)
  other arithmetic  75.2 us (6%)
  blocking collectives  48.4 us (4%)
  Pallas kernels  33.6 us (3%)
  local copies, waits for them, and re-layouts  31.2 us (2%)
  between operations  15.1 us (1%)
    all_gather x4, waiting for transfers between devices, sum_over_col(): whole = lax.all_gather(piece, ('dp', 'col'), axis=0, tiled=True)  293 us
    reduce_scatter x4, waiting for transfers between devices, sum_over_col(): lax.psum_scatter(partial.astype(BF16), 'col', scatter_dimension=0, tiled=...  226 us
    reduce_scatter x5, waiting for transfers between devices, summed(): return lax.psum_scatter(total, 'row', scatter_dimension=0, tiled=True)  218 us
    all_gather x5, waiting for transfers between devices, gather(): lax.all_gather(own_half(weight, axis), ('row', 'dp'), axis=axis, tiled=True)  172 us
    dot_general x5, matrix products, plain_dot(): return jnp.dot(left_mat, right_mat, preferred_element_type=F32)  63.1 us
    dot_general x5, matrix products, times_transposed(): lax.dot_general(left_mat, right_mat, (((1,), (1,)), ((), ())), preferred_...  60.6 us
    dot_general x10, matrix products, left_transposed(): lax.dot_general(left_mat, right_mat, (((0,), (0,)), ((), ())), preferred_...  57.4 us
    ppermute x5, waiting for transfers between devices, summed(): got = lax.ppermute(sent, 'dp', swap)  29.2 us
  transfers between devices with their start and end apart: 28, of which 21 were waited for; matrix products, arithmetic and copies ran while one was open for 11% of the time, Pallas kernels for 1%

profile of v1, /device:TPU:0, one launch (start us, length us, event | category | flops | bytes accessed | tf_op | source)
XLA Modules:
  0.0 1326.9 jit_solution(17923103392816720231)
XLA Ops:
  16.0 42.6 %all-gather.10.cloned.1.call-done = bf16[2048,1536]{1,0:T(8,128)(2,1)} async-done(((bf16[256,1536]{1,0:T(8,128)(2,1)}), bf16[2048,1536]{1,0:T(8,128)(2,1)}) %all-gather.10.cloned.1.call-update) | async-done | bytes 6291472 | tf_op jit(solution)/shard_map/all_gather | solution.py:232
  58.6 11.7 convolution_bitcast_fusion.q_ref.k_ref.v_ref
  73.0 11.9 all-reduce.2
  90.1 17.5 %attend_forward.1 = (bf16[1024,512]{1,0:T(8,128)(2,1)S(1)}, bf16[1024,512]{1,0:T(8,128)(2,1)S(1)}, bf16[1024,512]{1,0:T(8,128)(2,1)S(1)}, bf16[1024,512]{1,0:T(8,128)(2,1)}, f32[4,1024,1]{2,1,0:T(8,128)}) custom-call(f32[1024,1536]{1,0:T(8,128)} %convolution_bitcast_fusion.q_ref.k_ref.v_ref, f32[1024,1536]{1,0:T(8,128)} %convolution_bitcast_fusion.q_ref.k_ref.v_ref, ...), custom_call_target="tpu_custom_call" | custom-call | flops 2147483648 | bytes 10485760 | tf_op jit(solution)/shard_map/attend_forward/pallas_call | solution.py:149
  116.9 74.1 %reduce-scatter.10.cloned.1.call-done = bf16[256,2048]{1,0:T(8,128)(2,1)} async-done(((bf16[1024,2048]{1,0:T(8,128)(2,1)}), bf16[256,2048]{1,0:T(8,128)(2,1)}) %reduce-scatter.10.cloned.1.call-update) | async-done | bytes 1048592 | tf_op jit(solution)/shard_map/reduce_scatter | solution.py:235
  196.1 79.0 %all-gather.14.cloned.1.call-done = bf16[2048,2048]{1,0:T(8,128)(2,1)} async-done(((bf16[256,2048]{1,0:T(8,128)(2,1)}), bf16[2048,2048]{1,0:T(8,128)(2,1)}) %all-gather.14.cloned.1.call-update) | async-done | bytes 8388624 | tf_op jit(solution)/shard_map/all_gather | solution.py:236
  284.1 46.0 %all-gather.16.cloned.1.call-done = bf16[2048,2048]{1,0:T(8,128)(2,1)} async-done(((bf16[256,2048]{1,0:T(8,128)(2,1)}), bf16[2048,2048]{1,0:T(8,128)(2,1)}) %all-gather.16.cloned.1.call-update) | async-done | bytes 8388624 | tf_op jit(solution)/shard_map/all_gather | solution.py:232
  330.2 14.5 %fusion.75 = f32[1024,2048]{1,0:T(8,128)} fusion(bf16[1024,2048]{1,0:T(8,128)(2,1)} %fusion.23, bf16[2048,2048]{1,0:T(8,128)(2,1)} %all-gather.16.cloned.1.call-done), kind=kOutput, calls=%fused_computation.149 | convolution fusion | flops 8589934592 | bytes 20971520 | tf_op jit(solution)/shard_map/dot_general | solution.py:23
  344.6 42.1 %all-gather.18.cloned.1.call-done = bf16[2048,2048]{1,0:T(8,128)(2,1)} async-done(((bf16[256,2048]{1,0:T(8,128)(2,1)}), bf16[2048,2048]{1,0:T(8,128)(2,1)}) %all-gather.18.cloned.1.call-update) | async-done | bytes 8388624 | tf_op jit(solution)/shard_map/all_gather | solution.py:232
  386.8 16.9 %multiply_convert_fusion.2 = (bf16[1024,2048]{1,0:T(8,128)(2,1)}, f32[1024,2048]{1,0:T(8,128)}) fusion(f32[1024,2048]{1,0:T(8,128)} %fusion.75, bf16[1024,2048]{1,0:T(8,128)(2,1)} %fusion.23, bf16[2048,2048]{1,0:T(8,128)(2,1)} %all-gather.18.cloned.1.call-done), kind=kOutput, calls=%fused_computation.36 | convolution fusion | flops 8602517504 | bytes 33554432 | tf_op jit(solution)/shard_map/dot_general | solution.py:23
  403.7 41.5 %all-gather.20.cloned.1.call-done = bf16[2048,2048]{1,0:T(8,128)(2,1)} async-done(((bf16[2048,256]{1,0:T(8,128)(2,1)}), bf16[2048,2048]{1,0:T(8,128)(2,1)}) %all-gather.20.cloned.1.call-update) | async-done | bytes 8388624 | tf_op jit(solution)/shard_map/all_gather | solution.py:232
  445.1 13.8 %convolution_convert_fusion.1 = bf16[1024,2048]{1,0:T(8,128)(2,1)} fusion(bf16[1024,2048]{1,0:T(8,128)(2,1)} %get-tuple-element.108, bf16[2048,2048]{1,0:T(8,128)(2,1)} %all-gather.20.cloned.1.call-done), kind=kOutput, calls=%fused_computation.45 | convolution fusion | flops 8592031744 | bytes 16777216 | tf_op jit(solution)/shard_map/dot_general | solution.py:23
  459.0 76.9 %reduce-scatter.12.cloned.1.call-done = bf16[256,2048]{1,0:T(8,128)(2,1)} async-done(((bf16[1024,2048]{1,0:T(8,128)(2,1)}), bf16[256,2048]{1,0:T(8,128)(2,1)}) %reduce-scatter.12.cloned.1.call-update) | async-done | bytes 1048592 | tf_op jit(solution)/shard_map/reduce_scatter | solution.py:235
  536.4 83.7 %all-gather.22.cloned.1.call-done = bf16[2048,2048]{1,0:T(8,128)(2,1)} async-done(((bf16[256,2048]{1,0:T(8,128)(2,1)}), bf16[2048,2048]{1,0:T(8,128)(2,1)}) %all-gather.22.cloned.1.call-update) | async-done | bytes 8388624 | tf_op jit(solution)/shard_map/all_gather | solution.py:236
  632.4 20.5 %multiply_convert_fusion = (bf16[1024,2048]{1,0:T(8,128)(2,1)}, bf16[1024,2048]{1,0:T(8,128)(2,1)}) fusion(f32[1024,2048]{1,0:T(8,128)} %fusion.75, f32[1024,2048]{1,0:T(8,128)} %get-tuple-element.109, bf16[1024,2048]{1,0:T(8,128)(2,1)} %fusion.9, bf16[2048,2048]{1,0:T(8,128)(2,1)} %all-gather.20.cloned.1.call-done), kind=kOutput, calls=%fused_computation.34 | convolution fusion | flops 8617197568 | bytes 37748736 | tf_op jit(solution)/shard_map/dot_general | solution.py:27
  652.9 12.7 fusion.76
  665.6 13.0 add_convert_fusion.3
  678.7 75.4 %reduce-scatter.14.cloned.1.call-done = bf16[256,2048]{1,0:T(8,128)(2,1)} async-done(((bf16[1024,2048]{1,0:T(8,128)(2,1)}), bf16[256,2048]{1,0:T(8,128)(2,1)}) %reduce-scatter.14.cloned.1.call-update) | async-done | bytes 1048592 | tf_op jit(solution)/shard_map/reduce_scatter | solution.py:235
  754.2 84.1 %all-gather.24.cloned.1.call-done = bf16[2048,2048]{1,0:T(8,128)(2,1)} async-done(((bf16[256,2048]{1,0:T(8,128)(2,1)}), bf16[2048,2048]{1,0:T(8,128)(2,1)}) %all-gather.24.cloned.1.call-update) | async-done | bytes 8388624 | tf_op jit(solution)/shard_map/all_gather | solution.py:236
  846.6 11.5 fusion.14
  861.5 16.2 %attend_backward.1 = (f32[1024,512]{1,0:T(8,128)}, f32[1024,512]{1,0:T(8,128)}, bf16[1024,512]{1,0:T(8,128)(2,1)S(1)}, f32[1024,1]{1,0:T(8,128)S(1)}, f32[1024,1...) custom-call(f32[1024,1536]{1,0:T(8,128)} %convolution_bitcast_fusion.q_ref.k_ref.v_ref, ...), custom_call_target="tpu_custom_call" | custom-call | flops 5368709120 | bytes 20971520 | tf_op jit(solution)/shard_map/attend_backward/pallas_call | solution.py:172
  878.1 9.1 all-reduce.1
  891.4 11.0 convolution_convert_fusion
  945.8 7.6 convolution_convert_fusion.5
  994.1 41.0 %reduce-scatter.26.cloned.1.call-done = bf16[512,1024]{1,0:T(8,128)(2,1)} async-done(((bf16[2048,1024]{1,0:T(8,128)(2,1)}), bf16[512,1024]{1,0:T(8,128)(2,1)}) %reduce-scatter.26.cloned.1.call-update) | async-done | bytes 1048592 | tf_op jit(solution)/shard_map/reduce_scatter | solution.py:249
  1035.1 56.0 %reduce-scatter.24.cloned.1.call-done = bf16[512,1024]{1,0:T(8,128)(2,1)} async-done(((bf16[2048,1024]{1,0:T(8,128)(2,1)}), bf16[512,1024]{1,0:T(8,128)(2,1)}) %reduce-scatter.24.cloned.1.call-update) | async-done | bytes 1048592 | tf_op jit(solution)/shard_map/reduce_scatter | solution.py:249
  1091.1 56.0 %reduce-scatter.22.cloned.1.call-done = bf16[512,1024]{1,0:T(8,128)(2,1)} async-done(((bf16[2048,1024]{1,0:T(8,128)(2,1)}), bf16[512,1024]{1,0:T(8,128)(2,1)}) %reduce-scatter.22.cloned.1.call-update) | async-done | bytes 1048592 | tf_op jit(solution)/shard_map/reduce_scatter | solution.py:249
  1153.8 40.1 %reduce-scatter.18.cloned.1.call-done = bf16[512,768]{0,1:T(8,128)(2,1)} async-done(((bf16[2048,768]{0,1:T(8,128)(2,1)}), bf16[512,768]{0,1:T(8,128)(2,1)}) %reduce-scatter.18.cloned.1.call-update) | async-done | bytes 786448 | tf_op jit(solution)/shard_map/reduce_scatter | solution.py:249
  1200.7 24.6 %reduce-scatter.20.cloned.1.call-done = bf16[512,256]{1,0:T(8,128)(2,1)} async-done(((bf16[2048,256]{1,0:T(8,128)(2,1)}), bf16[512,256]{1,0:T(8,128)(2,1)}) %reduce-scatter.20.cloned.1.call-update) | async-done | bytes 262160 | tf_op jit(solution)/shard_map/reduce_scatter | solution.py:249
  1227.8 27.5 %all-reduce = (f32[512]{0:T(512)}, f32[512]{0:T(512)}, f32[2048]{0:T(1024)}, f32[2048]{0:T(1024)}) all-reduce(f32[512]{0:T(512)S(1)} %bitcast.71, f32[512]{0:T(512)S(1)} %bitcast.72, f32[2048]{0:T(1024)S(1)} %get-tuple-element.63, f32[2048]{0:T(1024)S(1)} %copy-done.41), channel_id=1, replica_groups=mesh['dp'=2,'row'=4,'col'=4] {'dp','row'}, use_global_device_ids=true, to_apply=%region_19.0 | all-reduce | flops 5120 | bytes 40960 | tf_op jit(solution)/shard_map/psum | solution.py:335
  1262.7 46.1 %all-gather.26.cloned.1.call-done = bf16[2048,2048]{1,0:T(8,128)(2,1)} async-done(((bf16[256,2048]{1,0:T(8,128)(2,1)}), bf16[2048,2048]{1,0:T(8,128)(2,1)}) %all-gather.26.cloned.1.call-update) | async-done | bytes 8388624 | tf_op jit(solution)/shard_map/all_gather | solution.py:236
  1308.8 11.1 convert_add_fusion.1
  (215 shorter events, 176.2 us)
Async XLA Ops:
  7.2 183.9 %copy-start = (bf16[512,2048]{1,0:T(8,128)(2,1)S(1)}, bf16[512,2048]{1,0:T(8,128)(2,1)}, u32[]{:S(2)}) copy-start(bf16[512,2048]{1,0:T(8,128)(2,1)} %param.22) | copy-start | bytes 6291460
  7.2 51.4 %all-gather.10.cloned.1.call-start = ((), (), s32[]{:S(2)}) async-start(), calls=%async_computation.9 | async-start | bytes 7077888 | tf_op jit(solution)/shard_map/all_gather | solution.py:232
  9.5 101.1 %all-gather.12.cloned.1.call-start = ((), (), s32[]{:S(2)}) async-start(), calls=%async_computation.10 | async-start | bytes 2359296 | tf_op jit(solution)/shard_map/all_gather | solution.py:232
  11.2 179.8 %reduce-scatter.10.cloned.1.call-start = ((), (), s32[]{:S(2)}) async-start(), calls=%async_computation.11 | async-start | bytes 5242880 | tf_op jit(solution)/shard_map/reduce_scatter | solution.py:235
  116.9 158.2 %all-gather.14.cloned.1.call-start = ((), (), s32[]{:S(2)}) async-start(), calls=%async_computation.12 | async-start | bytes 9437184 | tf_op jit(solution)/shard_map/all_gather | solution.py:236
  191.1 139.1 %all-gather.16.cloned.1.call-start = ((), (), s32[]{:S(2)}) async-start(), calls=%async_computation.13 | async-start | bytes 9437184 | tf_op jit(solution)/shard_map/all_gather | solution.py:232
  192.2 194.6 %all-gather.18.cloned.1.call-start = ((), (), s32[]{:S(2)}) async-start(), calls=%async_computation.14 | async-start | bytes 9437184 | tf_op jit(solution)/shard_map/all_gather | solution.py:232
  194.7 250.4 %all-gather.20.cloned.1.call-start = ((), (), s32[]{:S(2)}) async-start(), calls=%async_computation.15 | async-start | bytes 9437184 | tf_op jit(solution)/shard_map/all_gather | solution.py:232
  195.8 340.0 %reduce-scatter.12.cloned.1.call-start = ((), (), s32[]{:S(2)}) async-start(), calls=%async_computation.16 | async-start | bytes 5242880 | tf_op jit(solution)/shard_map/reduce_scatter | solution.py:235
  458.9 164.4 %copy-start.32 = (f32[2048]{0:T(1024)S(1)}, f32[2048]{0:T(1024)}, u32[]{:S(2)}) copy-start(f32[2048]{0:T(1024)} %param.28) | copy-start | bytes 24580
  458.9 161.1 %all-gather.22.cloned.1.call-start = ((), (), s32[]{:S(2)}) async-start(), calls=%async_computation.17 | async-start | bytes 9437184 | tf_op jit(solution)/shard_map/all_gather | solution.py:236
  535.9 218.2 %reduce-scatter.14.cloned.1.call-start = ((), (), s32[]{:S(2)}) async-start(), calls=%async_computation.18 | async-start | bytes 5242880 | tf_op jit(solution)/shard_map/reduce_scatter | solution.py:235
  678.6 159.7 %copy-start.34 = (f32[2048]{0:T(1024)S(1)}, f32[2048]{0:T(1024)}, u32[]{:S(2)}) copy-start(f32[2048]{0:T(1024)} %param.27) | copy-start | bytes 24580
  678.6 159.7 %copy-start.36 = (f32[1024]{0:T(1024)S(1)}, f32[1024]{0:T(1024)}, u32[]{:S(2)}) copy-start(f32[1024]{0:T(1024)} %copy-done.35) | copy-start | bytes 12292
  678.7 159.6 %all-gather.24.cloned.1.call-start = ((), (), s32[]{:S(2)}) async-start(), calls=%async_computation.19 | async-start | bytes 9437184 | tf_op jit(solution)/shard_map/all_gather | solution.py:236
  754.1 239.4 %reduce-scatter.16.cloned.1.call-start = ((), (), s32[]{:S(2)}) async-start(), calls=%async_computation.20 | async-start | bytes 5242880 | tf_op jit(solution)/shard_map/reduce_scatter | solution.py:235
  902.4 132.7 %reduce-scatter.26.cloned.1.call-start = ((), (), s32[]{:S(2)}) async-start(), calls=%async_computation.26 | async-start | bytes 5242880 | tf_op jit(solution)/shard_map/reduce_scatter | solution.py:249
  910.1 7.2 collective-permute-start.8
  923.8 167.4 %reduce-scatter.24.cloned.1.call-start = ((), (), s32[]{:S(2)}) async-start(), calls=%async_computation.25 | async-start | bytes 5242880 | tf_op jit(solution)/shard_map/reduce_scatter | solution.py:249
  931.8 7.2 collective-permute-start.6
  945.5 201.6 %reduce-scatter.22.cloned.1.call-start = ((), (), s32[]{:S(2)}) async-start(), calls=%async_computation.24 | async-start | bytes 5242880 | tf_op jit(solution)/shard_map/reduce_scatter | solution.py:249
  953.4 7.2 collective-permute-start.4
  967.1 226.8 %reduce-scatter.18.cloned.1.call-start = ((), (), s32[]{:S(2)}) async-start(), calls=%async_computation.22 | async-start | bytes 3932160 | tf_op jit(solution)/shard_map/reduce_scatter | solution.py:249
  973.4 5.7 collective-permute-start
  984.4 240.9 %reduce-scatter.20.cloned.1.call-start = ((), (), s32[]{:S(2)}) async-start(), calls=%async_computation.23 | async-start | bytes 1310720 | tf_op jit(solution)/shard_map/reduce_scatter | solution.py:249
  988.3 2.7 collective-permute-start.2
  993.5 315.3 %all-gather.26.cloned.1.call-start = ((), (), s32[]{:S(2)}) async-start(), calls=%async_computation.21 | async-start | bytes 9437184 | tf_op jit(solution)/shard_map/all_gather | solution.py:236
  1035.1 112.1 %collective-permute-start.9 = (bf16[512,1024]{1,0:T(8,128)(2,1)}, bf16[512,1024]{1,0:T(8,128)(2,1)S(1)}, u32[]{:S(2)}, u32[]{:S(2)}) collective-permute-start(bf16[512,1024]{1,0:T(8,128)(2,1)} %reduce-scatter.26.cloned.1.call-done), channel_id=1, source_target_pairs={{0,16},{16,0},{1,17},{17,1},{2,18},{18,2},{3,19},{19,3},{4,20},{20... | collective-permute-start | bytes 3145736 | tf_op jit(solution)/shard_map/ppermute | solution.py:240
  1091.1 60.0 %collective-permute-start.7 = (bf16[512,1024]{1,0:T(8,128)(2,1)}, bf16[512,1024]{1,0:T(8,128)(2,1)S(1)}, u32[]{:S(2)}, u32[]{:S(2)}) collective-permute-start(bf16[512,1024]{1,0:T(8,128)(2,1)} %reduce-scatter.24.cloned.1.call-done), channel_id=1, source_target_pairs={{0,16},{16,0},{1,17},{17,1},{2,18},{18,2},{3,19},{19,3},{4,20},{20... | collective-permute-start | bytes 3145736 | tf_op jit(solution)/shard_map/ppermute | solution.py:240
  1147.2 46.8 %collective-permute-start.5 = (bf16[512,1024]{1,0:T(8,128)(2,1)}, bf16[512,1024]{1,0:T(8,128)(2,1)}, u32[]{:S(2)}, u32[]{:S(2)}) collective-permute-start(bf16[512,1024]{1,0:T(8,128)(2,1)} %reduce-scatter.22.cloned.1.call-done), channel_id=1, source_target_pairs={{0,16},{16,0},{1,17},{17,1},{2,18},{18,2},{3,19},{19,3},{4,20},{20... | collective-permute-start | bytes 3145736 | tf_op jit(solution)/shard_map/ppermute | solution.py:240
  1193.9 62.8 %collective-permute-start.1 = (bf16[1,512,768]{1,2,0:T(8,128)(2,1)}, bf16[1,512,768]{1,2,0:T(8,128)(2,1)}, u32[]{:S(2)}, u32[]{:S(2)}) collective-permute-start(bf16[1,512,768]{1,2,0:T(8,128)(2,1)} %bitcast.73), channel_id=1, source_target_pairs={{0,16},{16,0},{1,17},{17,1},{2,18},{18,2},{3,19},{19,3},{4,20},{20... | collective-permute-start | bytes 2359304 | tf_op jit(solution)/shard_map/ppermute | solution.py:240
  1225.3 30.0 %collective-permute-start.3 = (bf16[512,256]{1,0:T(8,128)(2,1)}, bf16[512,256]{1,0:T(8,128)(2,1)S(1)}, u32[]{:S(2)}, u32[]{:S(2)}) collective-permute-start(bf16[512,256]{1,0:T(8,128)(2,1)} %reduce-scatter.20.cloned.1.call-done), channel_id=1, source_target_pairs={{0,16},{16,0},{1,17},{17,1},{2,18},{18,2},{3,19},{19,3},{4,20},{20... | collective-permute-start | bytes 786440 | tf_op jit(solution)/shard_map/ppermute | solution.py:240
  (43 other events, 556.0 us)
Sparse Core Ops, SparseCore 0:
  10.5 48.1 all-gather.9
  61.1 28.0 all-gather.11
  117.0 73.9 reduce-scatter.9
  192.5 82.5 all-gather.13
  277.4 52.7 all-gather.15
  332.5 54.2 all-gather.17
  389.2 55.8 all-gather.19
  459.0 76.7 reduce-scatter.11
  537.5 82.5 all-gather.21
  678.8 75.2 reduce-scatter.13
  755.7 82.5 all-gather.23
  902.6 75.8 reduce-scatter.15
  982.0 53.0 reduce-scatter.25
  1038.5 52.5 reduce-scatter.23
  1094.5 52.5 reduce-scatter.21
  1150.0 43.8 reduce-scatter.17
  1197.3 27.9 reduce-scatter.19
  1226.7 82.0 all-gather.25

commit v2 on v1

--- a/solution.py
+++ b/solution.py
@@ -214,10 +214,12 @@
 ):
     cores, rows, cols = sizes
     tokens_here, width = block_input.shape
-    assert tokens_here == LEN and cores == 2
+    assert tokens_here == LEN and cores == 2 and cols == 4
     local_width = w_query.shape[1]
     heads = local_width // HD
+    chunk = tokens_here // cols
     core = lax.axis_index("dp")
+    col = lax.axis_index("col")
     swap = [(0, 1), (1, 0)]
 
     def own_half(array, axis):
@@ -231,10 +233,58 @@
     def gather(weight, axis):
         return lax.all_gather(own_half(weight, axis), ("row", "dp"), axis=axis, tiled=True)
 
-    def sum_over_col(partial):
-        piece = lax.psum_scatter(partial.astype(BF16), "col", scatter_dimension=0, tiled=True)
-        whole = lax.all_gather(piece, ("dp", "col"), axis=0, tiled=True)
-        return lax.dynamic_slice_in_dim(whole, core * tokens_here, tokens_here, 0).astype(F32)
+    def line_step(from_left, from_right, step):
+        from_left = lax.ppermute(from_left, "col", [(i, i + 1) for i in range(step - 1, cols - 1)])
+        from_right = lax.ppermute(from_right, "col", [(i + 1, i) for i in range(cols - step)])
+        return from_left, from_right
+
+    def line_gather(own):
+        lefts, rights = [own], [own]
+        for step in range(1, cols):
+            left, right = line_step(lefts[-1], rights[-1], step)
+            lefts.append(left)
+            rights.append(right)
+        return lefts, rights
+
+    def pick(at_zero, at_one, at_two, at_three):
+        low = jnp.where(col == 0, at_zero, at_one)
+        high = jnp.where(col == 2, at_two, at_three)
+        return jnp.where(col < 2, low, high)
+
+    slot_chunk = (
+        pick(3, 3, 0, 0),
+        pick(2, 2, 1, 1),
+        pick(1, 0, 3, 2),
+        col,
+    )
+
+    def slot_rows(array, slot):
+        return lax.dynamic_slice_in_dim(array, slot_chunk[slot] * chunk, chunk, 0)
+
+    def place(whole, slot, rows_of):
+        return lax.dynamic_update_slice_in_dim(whole, rows_of, slot_chunk[slot] * chunk, 0)
+
+    def gather_slots(own):
+        lefts, rights = line_gather(own)
+        return (
+            pick(rights[3], rights[2], lefts[2], lefts[3]),
+            pick(rights[2], rights[1], lefts[1], lefts[2]),
+            jnp.where(col % 2 == 0, rights[1], lefts[1]),
+            own,
+        )
+
+    def sum_slots(parts):
+        up = lax.ppermute(parts[0], "col", [(0, 1)])
+        down = lax.ppermute(parts[0], "col", [(3, 2)])
+        up = jnp.where(col == 0, parts[1], parts[0]) + up
+        down = jnp.where(col == 3, parts[1], parts[0]) + down
+        up = lax.ppermute(up, "col", [(0, 1), (1, 2)])
+        down = lax.ppermute(down, "col", [(3, 2), (2, 1)])
+        up = jnp.where(col == 1, parts[1], parts[2]) + up
+        down = jnp.where(col == 2, parts[1], parts[2]) + down
+        up = lax.ppermute(up, "col", [(0, 1), (1, 2), (2, 3)])
+        down = lax.ppermute(down, "col", [(3, 2), (2, 1), (1, 0)])
+        return parts[3].astype(F32) + up.astype(F32) + down.astype(F32)
 
     def both_cores(half, axis):
         other = lax.ppermute(half, "dp", swap)
@@ -249,7 +299,14 @@
         return lax.psum_scatter(total, "row", scatter_dimension=0, tiled=True)
 
     full_qkv = gather(jnp.concatenate([w_query, w_key, w_value], axis=1), 0)
-    full_out = gather(w_out, 1)
+    out_half = own_half(w_out, 0)
+    out_pieces = [out_half] + [
+        lax.ppermute(out_half, "col", [(i, (i - step) % cols) for i in range(cols)])
+        for step in range(1, cols)
+    ]
+    full_out = lax.all_gather(jnp.stack(out_pieces), ("row", "dp"), axis=0, tiled=False)
+    full_out = full_out.reshape(rows, cores, cols, local_width // 2, width // rows)
+    full_out = jnp.transpose(full_out, (2, 1, 3, 0, 4)).reshape(cols * local_width, width)
     full_gate = gather(w_gate, 0)
     full_up = gather(w_up, 0)
     full_down = gather(w_down, 1)
@@ -268,42 +325,86 @@
     query_rot, key_rot, value_heads, attended, log_total = attend_forward(
         qkv, scales, gains, tables, seg_col, seg_row, heads
     )
-    attn_raw = sum_over_col(plain_dot(attended, full_out))
-    attn_scale = lax.rsqrt(jnp.mean(attn_raw * attn_raw, axis=1, keepdims=True) + EPS)
-    attn_unit = attn_raw * attn_scale
-    hidden = block_input.astype(F32) + attn_unit * attn_gain
-    hidden_b = hidden.astype(BF16)
-    gate_proj = plain_dot(hidden_b, full_gate)
-    up_proj = plain_dot(hidden_b, full_up)
-    gate_sig = jax.nn.sigmoid(gate_proj)
-    gate_act = gate_proj * gate_sig
-    mixed_act = (gate_act * up_proj).astype(BF16)
-    down_raw = sum_over_col(plain_dot(mixed_act, full_down))
-    down_scale = lax.rsqrt(jnp.mean(down_raw * down_raw, axis=1, keepdims=True) + EPS)
-    down_unit = down_raw * down_scale
-    block_output = (hidden + down_unit * mlp_gain).astype(BF16)
-
-    grad_y = grad_output.astype(F32)
-    grad_mlp_gain = jnp.sum(grad_y * down_unit, axis=0)
-    down_dz = grad_y * mlp_gain
-    grad_down_in = (
-        down_scale * (down_dz - down_unit * jnp.mean(down_dz * down_unit, axis=1, keepdims=True))
-    ).astype(BF16)
-    grad_mixed = times_transposed(grad_down_in, full_down)
-    grad_gate_in = (grad_mixed * up_proj * gate_sig * (1.0 + gate_proj * (1.0 - gate_sig))).astype(BF16)
-    grad_up_in = (grad_mixed * gate_act).astype(BF16)
-    mlp_part = times_transposed(grad_gate_in, full_gate) + times_transposed(grad_up_in, full_up)
-    grad_hidden = grad_y + sum_over_col(mlp_part)
-    down_block = summed(grad_down_in, own_half(mixed_act, 1), other_half(mixed_act, 1))
-    gate_block = summed(hidden_b, own_half(grad_gate_in, 1), other_half(grad_gate_in, 1))
-    up_block = summed(hidden_b, own_half(grad_up_in, 1), other_half(grad_up_in, 1))
-
-    grad_attn_gain = jnp.sum(grad_hidden * attn_unit, axis=0)
-    attn_dz = grad_hidden * attn_gain
-    grad_attn_in = (
-        attn_scale * (attn_dz - attn_unit * jnp.mean(attn_dz * attn_unit, axis=1, keepdims=True))
-    ).astype(BF16)
-    grad_att = times_transposed(grad_attn_in, full_out).astype(BF16)
+    lefts, rights = line_gather(attended)
+    attended_all = jnp.concatenate(
+        [attended] + [rights[step] + lefts[cols - step] for step in range(1, cols)], axis=1
+    )
+
+    saved = []
+    down_parts = []
+    for slot in range(cols):
+        attn_raw = plain_dot(slot_rows(attended_all, slot), full_out)
+        attn_scale = lax.rsqrt(jnp.mean(attn_raw * attn_raw, axis=1, keepdims=True) + EPS)
+        attn_unit = attn_raw * attn_scale
+        hidden = slot_rows(block_input, slot).astype(F32) + attn_unit * attn_gain
+        hidden_b = hidden.astype(BF16)
+        gate_proj = plain_dot(hidden_b, full_gate)
+        up_proj = plain_dot(hidden_b, full_up)
+        gate_sig = jax.nn.sigmoid(gate_proj)
+        gate_act = gate_proj * gate_sig
+        mixed_act = (gate_act * up_proj).astype(BF16)
+        down_parts.append(plain_dot(mixed_act, full_down).astype(BF16))
+        saved.append((attn_scale, attn_raw, hidden, hidden_b, gate_proj, up_proj, mixed_act))
+    down_slots = gather_slots(sum_slots(down_parts).astype(BF16))
+
+    block_output = jnp.zeros((tokens_here, width), BF16)
+    grad_mlp_gain = 0.0
+    mlp_parts = [None] * cols
+    grads = [None] * cols
+    for slot in reversed(range(cols)):
+        attn_scale, attn_raw, hidden, hidden_b, gate_proj, up_proj, mixed_act = saved[slot]
+        down_raw = down_slots[slot].astype(F32)
+        down_scale = lax.rsqrt(jnp.mean(down_raw * down_raw, axis=1, keepdims=True) + EPS)
+        down_unit = down_raw * down_scale
+        block_output = place(block_output, slot, (hidden + down_unit * mlp_gain).astype(BF16))
+        grad_y = slot_rows(grad_output, slot).astype(F32)
+        grad_mlp_gain = grad_mlp_gain + jnp.sum(grad_y * down_unit, axis=0)
+        down_dz = grad_y * mlp_gain
+        grad_down_in = (
+            down_scale * (down_dz - down_unit * jnp.mean(down_dz * down_unit, axis=1, keepdims=True))
+        ).astype(BF16)
+        grad_mixed = times_transposed(grad_down_in, full_down)
+        gate_sig = jax.nn.sigmoid(gate_proj)
+        grad_gate_in = (
+            grad_mixed * up_proj * gate_sig * (1.0 + gate_proj * (1.0 - gate_sig))
+        ).astype(BF16)
+        grad_up_in = (grad_mixed * (gate_proj * gate_sig)).astype(BF16)
+        mlp_parts[slot] = (
+            times_transposed(grad_gate_in, full_gate) + times_transposed(grad_up_in, full_up)
+        ).astype(BF16)
+        grads[slot] = (grad_down_in, grad_gate_in, grad_up_in)
+    mlp_slots = gather_slots(sum_slots(mlp_parts).astype(BF16))
+
+    def stacked(pieces):
+        return jnp.concatenate(pieces, axis=0)
+
+    hidden_all = stacked([one[3] for one in saved])
+    mixed_all = stacked([one[6] for one in saved])
+    grad_down_all, grad_gate_all, grad_up_all = (stacked([one[i] for one in grads]) for i in range(3))
+    down_block = summed(grad_down_all, own_half(mixed_all, 1), other_half(mixed_all, 1))
+    gate_block = summed(hidden_all, own_half(grad_gate_all, 1), other_half(grad_gate_all, 1))
+    up_block = summed(hidden_all, own_half(grad_up_all, 1), other_half(grad_up_all, 1))
+
+    grad_attn_gain = 0.0
+    grad_att = jnp.zeros((tokens_here, local_width), BF16)
+    attn_ins = [None] * cols
+    for slot in reversed(range(cols)):
+        attn_scale, attn_raw = saved[slot][:2]
+        attn_unit = attn_raw * attn_scale
+        grad_hidden = slot_rows(grad_output, slot).astype(F32) + mlp_slots[slot].astype(F32)
+        grad_attn_gain = grad_attn_gain + jnp.sum(grad_hidden * attn_unit, axis=0)
+        attn_dz = grad_hidden * attn_gain
+        grad_attn_in = (
+            attn_scale * (attn_dz - attn_unit * jnp.mean(attn_dz * attn_unit, axis=1, keepdims=True))
+        ).astype(BF16)
+        grad_att = place(
+            grad_att, slot, times_transposed(grad_attn_in, full_out[:local_width]).astype(BF16)
+        )
+        attn_ins[slot] = grad_attn_in
+    own_grad_hidden = (
+        slot_rows(grad_output, 3).astype(F32) + mlp_slots[3].astype(F32)
+    )
+
     query_dz, key_dz, grad_value_in, query_dot, key_dot, grad_query_gain, grad_key_gain = attend_backward(
         qkv, scales, gains, tables, seg_col, seg_row,
         (query_rot, key_rot, value_heads, attended, log_total), grad_att, heads,
@@ -316,7 +417,13 @@
         key_scale * (key_dz - key_raw * key_scale * (key_dot / width)[:, None])
     ).astype(BF16)
     grad_qkv = jnp.concatenate([grad_query_in, grad_key_in, grad_value_in], axis=1)
-    grad_input = grad_hidden + sum_over_col(times_transposed(grad_qkv, full_qkv))
+    input_parts = [
+        times_transposed(slot_rows(grad_qkv, slot), full_qkv).astype(BF16) for slot in range(cols)
+    ]
+    input_slots = gather_slots((own_grad_hidden + sum_slots(input_parts)).astype(BF16))
+    grad_input = jnp.zeros((tokens_here, width), F32)
+    for slot in reversed(range(cols)):
+        grad_input = place(grad_input, slot, input_slots[slot].astype(F32))
 
     def interleaved(picker):
         return jnp.concatenate(
@@ -324,7 +431,10 @@
         )
 
     qkv_block = summed(block_input, interleaved(own_half), interleaved(other_half))
-    out_block = summed(grad_attn_in, own_half(attended, 1), other_half(attended, 1))
+    attended_slots = stacked([slot_rows(attended, slot) for slot in range(cols)])
+    out_block = summed(
+        stacked(attn_ins), own_half(attended_slots, 1), other_half(attended_slots, 1)
+    )
     qkv_pair = both_cores(qkv_block[None], 0)
     quarter = local_width // 2
 
@@ -332,9 +442,9 @@
         part = qkv_pair[:, :, index * quarter : (index + 1) * quarter]
         return jnp.concatenate([part[0], part[1]], axis=1)
 
-    gain_grads = lax.psum(
-        (grad_query_gain[0], grad_key_gain[0], grad_attn_gain, grad_mlp_gain), ("dp", "row")
-    )
+    gain_grads = (grad_query_gain[0], grad_key_gain[0], grad_attn_gain, grad_mlp_gain)
+    for axis in ("dp", "row"):
+        gain_grads = lax.psum(gain_grads, axis)
     return (
         block_output,
         grad_input,

time: 1340 us -> 970 us (0.72)
  waiting for transfers between devices: 939 us -> 387 us
  starting transfers between devices: 3.05 us -> 97.5 us
  matrix products: 181 us -> 228 us
  local copies, waits for them, and re-layouts: 31.2 us -> 71 us
    ppermute x0 -> x45, waiting for transfers between devices: none -> 315 us  [the longest x12 151 us: line_step(): lax.ppermute(from_right, 'col', [(i + 1, i) for i in range(cols - step)])]
    all_gather x4 -> x1, waiting for transfers between devices: 293 us -> 0.01 us  [shards(): lax.all_gather(jnp.stack(out_pieces), ('row', 'dp'), axis=0, tiled=False)]
    reduce_scatter x4 -> x0, waiting for transfers between devices: 226 us -> none  [sum_over_col(): lax.psum_scatter(partial.astype(BF16), 'col', scatter_dimension=0, tiled=...]
    reduce_scatter x5, waiting for transfers between devices: 218 us -> 0.03 us  [summed(): return lax.psum_scatter(total, 'row', scatter_dimension=0, tiled=True)]
    all_gather x5 -> x4, waiting for transfers between devices: 172 us -> 59 us  [gather(): lax.all_gather(own_half(weight, axis), ('row', 'dp'), axis=axis, tiled=True)]
    ppermute x0 -> x45, starting transfers between devices: none -> 95.4 us  [the longest x12 24.2 us: line_step(): lax.ppermute(from_left, 'col', [(i, i + 1) for i in range(step - 1, cols...]
    dot_general x5 -> x20, matrix products: 60.6 us -> 96.8 us  [times_transposed(): lax.dot_general(left_mat, right_mat, (((1,), (1,)), ((), ())), preferred_...]
    unnamed x99 -> x303, local copies, waits for them, and re-layouts: 21.5 us -> 44.9 us
  transfers between devices with their start and end apart: 28 -> 65, of which waited for: 21 -> 32; matrix products, arithmetic and copies ran while one was open for 11% -> 32% of each run, Pallas kernels for 1% -> 3%
where the time goes in v2:
time: 970 us; the launch traced here: 961 us
  waiting for transfers between devices  387 us (40%)
  matrix products  228 us (24%)
  starting transfers between devices  97.5 us (10%)
  other arithmetic  86.4 us (9%)
  local copies, waits for them, and re-layouts  71 us (7%)
  blocking collectives  40.2 us (4%)
  Pallas kernels  33.5 us (3%)
  between operations  16.9 us (2%)
    ppermute x12, waiting for transfers between devices, line_step(): lax.ppermute(from_right, 'col', [(i + 1, i) for i in range(cols - step)])  151 us
    dot_general x20, matrix products, times_transposed(): lax.dot_general(left_mat, right_mat, (((1,), (1,)), ((), ())), preferred_...  96.8 us
    dot_general x17, matrix products, plain_dot(): return jnp.dot(left_mat, right_mat, preferred_element_type=F32)  74.3 us
    all_gather x4, waiting for transfers between devices, gather(): lax.all_gather(own_half(weight, axis), ('row', 'dp'), axis=axis, tiled=True)  59 us
    dot_general x10, matrix products, left_transposed(): lax.dot_general(left_mat, right_mat, (((0,), (0,)), ((), ())), preferred_...  57.2 us
    ppermute x12, waiting for transfers between devices, line_step(): lax.ppermute(from_left, 'col', [(i, i + 1) for i in range(step - 1, cols...  52 us
    unnamed x303, local copies, waits for them, and re-layouts  44.9 us
    ppermute x3, waiting for transfers between devices, sum_slots(): up = lax.ppermute(up, 'col', [(0, 1), (1, 2)])  35.7 us
  transfers between devices with their start and end apart: 65, of which 32 were waited for; matrix products, arithmetic and copies ran while one was open for 32% of the time, Pallas kernels for 3%

profile of v2, /device:TPU:0, one launch (start us, length us, event | category | flops | bytes accessed | tf_op | source)
XLA Modules:
  0.0 960.7 jit_solution(4684043368291244847)
XLA Ops:
  15.8 11.6 %collective-permute-done.7 = bf16[256,512]{1,0:T(8,128)(2,1)S(1)} collective-permute-done((bf16[256,512]{1,0:T(8,128)(2,1)S(1)}, bf16[256,512]{1,0:T(8,128)(2,1)S(1)}, u32[]{:S(2)}, u32[]{:S(2)}) %collective-permute-start.7) | collective-permute-done | bytes 262176 | tf_op jit(solution)/shard_map/ppermute | solution.py:304
  41.1 17.5 %all-gather.7.cloned.1.call-done = bf16[2048,1536]{1,0:T(8,128)(2,1)} async-done(((bf16[256,1536]{1,0:T(8,128)(2,1)}), bf16[2048,1536]{1,0:T(8,128)(2,1)}) %all-gather.7.cloned.1.call-update) | async-done | bytes 6291472 | tf_op jit(solution)/shard_map/all_gather | solution.py:234
  58.6 10.0 %convolution_bitcast_fusion.q_ref.k_ref.v_ref = f32[1024,1536]{1,0:T(8,128)S(1)} fusion(bf16[1024,2048]{1,0:T(8,128)(2,1)} %param.15, bf16[2048,1536]{1,0:T(8,128)(2,1)} %all-gather.7.cloned.1.call-done), kind=kOutput, calls=%fused_computation.5 | convolution fusion | flops 6442450944 | bytes 16777216 | tf_op jit(solution)/shard_map/dot_general | solution.py:23
  71.7 11.9 %all-reduce.1 = (f32[1024]{0:T(1024)S(1)}, f32[1024]{0:T(1024)S(1)}) all-reduce(f32[1024]{0:T(1024)S(1)} %get-tuple-element.85, f32[1024]{0:T(1024)S(1)} %get-tuple-element.84), channel_id=1, replica_groups=mesh['dp'=2,'row'=4,'col'=4] {'col'}, use_global_device_ids=true, to_apply=%region_1.2 | all-reduce | flops 2048 | bytes 16384 | tf_op jit(solution)/shard_map/psum | solution.py:316
  84.4 17.4 %attend_forward.1 = (bf16[1024,512]{1,0:T(8,128)(2,1)S(1)}, bf16[1024,512]{1,0:T(8,128)(2,1)S(1)}, bf16[1024,512]{1,0:T(8,128)(2,1)S(1)}, bf16[1024,512]{1,0:T(8,128)(2,1)}, f32[4,1024,1]{2,1,0:T(8,128)}) custom-call(f32[1024,1536]{1,0:T(8,128)} %copy-done.15, f32[1024,1536]{1,0:T(8,128)} %copy-done.15, f32[1024,1536]{1,0:T(8,128)} %copy-done.15, ...), custom_call_target="tpu_custom_call" | custom-call | flops 2147483648 | bytes 10485760 | tf_op jit(solution)/shard_map/attend_forward/pallas_call | solution.py:149
  107.4 20.0 %collective-permute-done.1 = bf16[1024,512]{1,0:T(8,128)(2,1)S(1)} collective-permute-done((bf16[1024,512]{1,0:T(8,128)(2,1)}, bf16[1024,512]{1,0:T(8,128)(2,1)S(1)}, u32[]{:S(2)}, u32[]{:S(2)}) %collective-permute-start.1) | collective-permute-done | bytes 1048608 | tf_op jit(solution)/shard_map/ppermute | solution.py:237
  134.5 23.7 %collective-permute-done.4 = bf16[1024,512]{1,0:T(8,128)(2,1)} collective-permute-done((bf16[1024,512]{1,0:T(8,128)(2,1)S(1)}, bf16[1024,512]{1,0:T(8,128)(2,1)}, u32[]{:S(2)}, u32[]{:S(2)}) %collective-permute-start.4) | collective-permute-done | bytes 1048608 | tf_op jit(solution)/shard_map/ppermute | solution.py:238
  163.3 19.4 %collective-permute-done.5 = bf16[1024,512]{1,0:T(8,128)(2,1)} collective-permute-done((bf16[1024,512]{1,0:T(8,128)(2,1)}, bf16[1024,512]{1,0:T(8,128)(2,1)}, u32[]{:S(2)}, u32[]{:S(2)}) %collective-permute-start.5) | collective-permute-done | bytes 1048608 | tf_op jit(solution)/shard_map/ppermute | solution.py:238
  186.7 12.2 %copy.65 = bf16[4,2,4,256,512]{4,0,3,1,2:T(4,128)(2,1)} copy(bf16[4,2,4,256,512]{4,3,2,1,0:T(8,128)(2,1)} %bitcast.129) | data formatting | bytes 16777216 | tf_op jit(solution)/shard_map/reshape | solution.py:308
  198.8 10.3 %copy.61 = bf16[256,8,4,512]{3,1,2,0:T(8,128)(2,1)} copy(bf16[256,8,4,512]{3,2,1,0:T(4,128)(2,1)} %bitcast.127) | data formatting | bytes 16777216
  235.5 9.4 multiply_convert_fusion.14
  244.9 41.5 %all-gather.13.cloned.1.call-done = bf16[2048,2048]{1,0:T(8,128)(2,1)} async-done(((bf16[2048,256]{1,0:T(8,128)(2,1)}), bf16[2048,2048]{1,0:T(8,128)(2,1)}) %all-gather.13.cloned.1.call-update) | async-done | bytes 8388624 | tf_op jit(solution)/shard_map/all_gather | solution.py:234
  311.2 8.3 collective-permute-done.9
  333.2 16.5 %collective-permute-done.10 = bf16[256,2048]{1,0:T(8,128)(2,1)S(1)} collective-permute-done((bf16[256,2048]{1,0:T(8,128)(2,1)}, bf16[256,2048]{1,0:T(8,128)(2,1)S(1)}, u32[]{:S(2)}, u32[]{:S(2)}) %collective-permute-start.10) | collective-permute-done | bytes 1048608 | tf_op jit(solution)/shard_map/ppermute | solution.py:281
  364.4 12.9 %collective-permute-done.11 = bf16[256,2048]{1,0:T(8,128)(2,1)S(1)} collective-permute-done((bf16[256,2048]{1,0:T(8,128)(2,1)S(1)}, bf16[256,2048]{1,0:T(8,128)(2,1)S(1)}, u32[]{:S(2)}, u32[]{:S(2)}) %collective-permute-start.11) | collective-permute-done | bytes 1048608 | tf_op jit(solution)/shard_map/ppermute | solution.py:285
  385.6 18.6 %collective-permute-done.16 = bf16[256,2048]{1,0:T(8,128)(2,1)S(1)} collective-permute-done((bf16[256,2048]{1,0:T(8,128)(2,1)S(1)}, bf16[256,2048]{1,0:T(8,128)(2,1)S(1)}, u32[]{:S(2)}, u32[]{:S(2)}) %collective-permute-start.16) | collective-permute-done | bytes 1048608 | tf_op jit(solution)/shard_map/ppermute | solution.py:237
  411.4 20.4 %collective-permute-done.17 = bf16[256,2048]{1,0:T(8,128)(2,1)} collective-permute-done((bf16[256,2048]{1,0:T(8,128)(2,1)S(1)}, bf16[256,2048]{1,0:T(8,128)(2,1)}, u32[]{:S(2)}, u32[]{:S(2)}) %collective-permute-start.17) | collective-permute-done | bytes 1048608 | tf_op jit(solution)/shard_map/ppermute | solution.py:238
  433.1 21.3 %collective-permute-done.19 = bf16[256,2048]{1,0:T(8,128)(2,1)} collective-permute-done((bf16[256,2048]{1,0:T(8,128)(2,1)}, bf16[256,2048]{1,0:T(8,128)(2,1)}, u32[]{:S(2)}, u32[]{:S(2)}) %collective-permute-start.19) | collective-permute-done | bytes 1048608 | tf_op jit(solution)/shard_map/ppermute | solution.py:238
  467.2 7.9 multiply_convert_fusion.6
  514.0 7.8 select_add_fusion.6
  531.4 9.6 %collective-permute-done.22 = bf16[256,2048]{1,0:T(8,128)(2,1)S(1)} collective-permute-done((bf16[256,2048]{1,0:T(8,128)(2,1)}, bf16[256,2048]{1,0:T(8,128)(2,1)S(1)}, u32[]{:S(2)}, u32[]{:S(2)}) %collective-permute-start.22) | collective-permute-done | bytes 1048608 | tf_op jit(solution)/shard_map/ppermute | solution.py:281
  572.2 13.4 %collective-permute-done.28 = bf16[256,2048]{1,0:T(8,128)(2,1)} collective-permute-done((bf16[256,2048]{1,0:T(8,128)(2,1)S(1)}, bf16[256,2048]{1,0:T(8,128)(2,1)}, u32[]{:S(2)}, u32[]{:S(2)}) %collective-permute-start.28) | collective-permute-done | bytes 1048608 | tf_op jit(solution)/shard_map/ppermute | solution.py:237
  599.4 17.9 %collective-permute-done.29 = bf16[256,2048]{1,0:T(8,128)(2,1)} collective-permute-done((bf16[256,2048]{1,0:T(8,128)(2,1)}, bf16[256,2048]{1,0:T(8,128)(2,1)}, u32[]{:S(2)}, u32[]{:S(2)}) %collective-permute-start.29) | collective-permute-done | bytes 1048608 | tf_op jit(solution)/shard_map/ppermute | solution.py:238
  619.1 8.3 convolution_convert_fusion
  651.7 10.8 %add_convert_fusion = bf16[2048,1024]{1,0:T(8,128)(2,1)} fusion(bf16[2048,1024]{1,0:T(8,128)(2,1)} %collective-permute-done.53, bf16[1024,2048]{1,0:T(8,128)(2,1)} %copy-done.50, s32[]{:T(128)S(6)} %select_n.360, bf16[256,2048]{1,0:T(8,128)(2,1)} %copy-done.87, bf16[256,2048]{1,0:T(8,128)(2,1)} %copy-done.91, bf16[256,2048]{1,0:T(8,128)(2,1)} %copy-done.89, ...), kind=kOutput, calls=%fused_computation | convolution fusion | flops 4318035968 | bytes 14680068 | tf_op jit(solution)/shard_map/dot_general | solution.py:33
  714.8 16.1 %attend_backward.1 = (f32[1024,512]{1,0:T(8,128)}, f32[1024,512]{1,0:T(8,128)}, bf16[1024,512]{1,0:T(8,128)(2,1)S(1)}, f32[1024,1]{1,0:T(8,128)S(1)}, f32[1024,1...) custom-call(f32[1024,1536]{1,0:T(8,128)} %copy-done.15, f32[1024,1536]{1,0:T(8,128)} %copy-done.15, ...), custom_call_target="tpu_custom_call" | custom-call | flops 5368709120 | bytes 20971520 | tf_op jit(solution)/shard_map/attend_backward/pallas_call | solution.py:172
  734.2 8.5 all-reduce
  768.8 12.5 %collective-permute-done.33 = bf16[256,2048]{1,0:T(8,128)(2,1)} collective-permute-done((bf16[256,2048]{1,0:T(8,128)(2,1)}, bf16[256,2048]{1,0:T(8,128)(2,1)}, u32[]{:S(2)}, u32[]{:S(2)}) %collective-permute-start.33) | collective-permute-done | bytes 1048608 | tf_op jit(solution)/shard_map/ppermute | solution.py:277
  802.6 9.6 collective-permute-done.34
  860.5 13.1 %collective-permute-done.39 = bf16[256,2048]{1,0:T(8,128)(2,1)} collective-permute-done((bf16[256,2048]{1,0:T(8,128)(2,1)S(1)}, bf16[256,2048]{1,0:T(8,128)(2,1)}, u32[]{:S(2)}, u32[]{:S(2)}) %collective-permute-start.39) | collective-permute-done | bytes 1048608 | tf_op jit(solution)/shard_map/ppermute | solution.py:238
  882.0 16.1 %all-reduce.2 = (f32[512]{0:T(512)}, f32[512]{0:T(512)}, f32[2048]{0:T(1024)}, f32[2048]{0:T(1024)}) all-reduce(f32[512]{0:T(512)S(1)} %get-tuple-element.114, f32[512]{0:T(512)S(1)} %get-tuple-element.115, f32[2048]{0:T(1024)S(1)} %get-tuple-element.116, ...), channel_id=1, replica_groups=mesh['dp'=2,'row'=4,'col'=4] {'row'}, use_global_device_ids=true, to_apply=%region_28.29 | all-reduce | flops 5120 | bytes 40960 | tf_op jit(solution)/shard_map/psum | solution.py:447
  909.9 16.8 %collective-permute-done.43 = bf16[256,2048]{1,0:T(8,128)(2,1)S(1)} collective-permute-done((bf16[256,2048]{1,0:T(8,128)(2,1)}, bf16[256,2048]{1,0:T(8,128)(2,1)S(1)}, u32[]{:S(2)}, u32[]{:S(2)}) %collective-permute-start.43) | collective-permute-done | bytes 1048608 | tf_op jit(solution)/shard_map/ppermute | solution.py:238
  (558 shorter events, 472.3 us)
Async XLA Ops:
  7.2 51.4 %all-gather.7.cloned.1.call-start = ((), (), s32[]{:S(2)}) async-start(), calls=%async_computation.5 | async-start | bytes 7077888 | tf_op jit(solution)/shard_map/all_gather | solution.py:234
  9.5 177.2 %all-gather.15.cloned.1.call-start = ((), (), s32[]{:S(2)}) async-start(), calls=%async_computation.14 | async-start | bytes 9437184 | tf_op jit(solution)/shard_map/all_gather | solution.py:307
  33.6 194.5 %all-gather.9.cloned.1.call-start = ((), (), s32[]{:S(2)}) async-start(), calls=%async_computation.6 | async-start | bytes 9437184 | tf_op jit(solution)/shard_map/all_gather | solution.py:234
  34.8 200.7 %all-gather.11.cloned.1.call-start = ((), (), s32[]{:S(2)}) async-start(), calls=%async_computation.7 | async-start | bytes 9437184 | tf_op jit(solution)/shard_map/all_gather | solution.py:234
  37.3 249.1 %all-gather.13.cloned.1.call-start = ((), (), s32[]{:S(2)}) async-start(), calls=%async_computation.8 | async-start | bytes 9437184 | tf_op jit(solution)/shard_map/all_gather | solution.py:234
  38.5 839.8 %reduce-scatter.8.cloned.1.call-start = ((), (), s32[]{:S(2)}) async-start(), calls=%async_computation.10 | async-start | bytes 1310720 | tf_op jit(solution)/shard_map/reduce_scatter | solution.py:299
  106.1 25.4 %collective-permute-start = (bf16[1024,512]{1,0:T(8,128)(2,1)}, bf16[1024,512]{1,0:T(8,128)(2,1)S(1)}, u32[]{:S(2)}, u32[]{:S(2)}) collective-permute-start(bf16[1024,512]{1,0:T(8,128)(2,1)} %get-tuple-element.25.att_ref), channel_id=1, source_target_pairs={{1,0},{2,1},{3,2},{5,4},{6,5},{7,6},{9,8},{10,9},{11,10},{13,12},{... | collective-permute-start | bytes 3145736 | tf_op jit(solution)/shard_map/ppermute | solution.py:238
  131.5 26.6 %collective-permute-start.4 = (bf16[1024,512]{1,0:T(8,128)(2,1)S(1)}, bf16[1024,512]{1,0:T(8,128)(2,1)}, u32[]{:S(2)}, u32[]{:S(2)}) collective-permute-start(bf16[1024,512]{1,0:T(8,128)(2,1)S(1)} %collective-permute-done), channel_id=1, source_target_pairs={{1,0},{2,1},{5,4},{6,5},{9,8},{10,9},{13,12},{14,13},{17,16},{18,1... | collective-permute-start | bytes 3145736 | tf_op jit(solution)/shard_map/ppermute | solution.py:238
  132.8 28.9 %collective-permute-start.3 = (bf16[1024,512]{1,0:T(8,128)(2,1)}, bf16[1024,512]{1,0:T(8,128)(2,1)}, u32[]{:S(2)}, u32[]{:S(2)}) collective-permute-start(bf16[1024,512]{1,0:T(8,128)(2,1)} %collective-permute-done.2), channel_id=1, source_target_pairs={{2,3},{6,7},{10,11},{14,15},{18,19},{22,23},{26,27},{30,31}} | collective-permute-start | bytes 3145736 | tf_op jit(solution)/shard_map/ppermute | solution.py:237
  158.2 24.6 %collective-permute-start.5 = (bf16[1024,512]{1,0:T(8,128)(2,1)}, bf16[1024,512]{1,0:T(8,128)(2,1)}, u32[]{:S(2)}, u32[]{:S(2)}) collective-permute-start(bf16[1024,512]{1,0:T(8,128)(2,1)} %collective-permute-done.4), channel_id=1, source_target_pairs={{1,0},{5,4},{9,8},{13,12},{17,16},{21,20},{25,24},{29,28}} | collective-permute-start | bytes 3145736 | tf_op jit(solution)/shard_map/ppermute | solution.py:238
  293.3 26.2 %collective-permute-start.9 = (bf16[256,2048]{1,0:T(8,128)(2,1)S(1)}, bf16[256,2048]{1,0:T(8,128)(2,1)S(1)}, u32[]{:S(2)}, u32[]{:S(2)}) collective-permute-start(bf16[256,2048]{1,0:T(8,128)(2,1)S(1)} %convolution_convert_fusion.9), channel_id=1, source_target_pairs={{0,1},{4,5},{8,9},{12,13},{16,17},{20,21},{24,25},{28,29}} | collective-permute-start | bytes 3145736 | tf_op jit(solution)/shard_map/ppermute | solution.py:277
  323.0 26.7 %collective-permute-start.10 = (bf16[256,2048]{1,0:T(8,128)(2,1)}, bf16[256,2048]{1,0:T(8,128)(2,1)S(1)}, u32[]{:S(2)}, u32[]{:S(2)}) collective-permute-start(bf16[256,2048]{1,0:T(8,128)(2,1)} %get-tuple-element.180), channel_id=1, source_target_pairs={{0,1},{1,2},{4,5},{5,6},{8,9},{9,10},{12,13},{13,14},{16,17},{17,1... | collective-permute-start | bytes 3145736 | tf_op jit(solution)/shard_map/ppermute | solution.py:281
  350.0 27.3 %collective-permute-start.11 = (bf16[256,2048]{1,0:T(8,128)(2,1)S(1)}, bf16[256,2048]{1,0:T(8,128)(2,1)S(1)}, u32[]{:S(2)}, u32[]{:S(2)}) collective-permute-start(bf16[256,2048]{1,0:T(8,128)(2,1)S(1)} %get-tuple-element.178), channel_id=1, source_target_pairs={{0,1},{1,2},{2,3},{4,5},{5,6},{6,7},{8,9},{9,10},{10,11},{12,13},{... | collective-permute-start | bytes 3145736 | tf_op jit(solution)/shard_map/ppermute | solution.py:285
  356.5 24.9 %collective-permute-start.14 = (bf16[256,2048]{1,0:T(8,128)(2,1)S(1)}, bf16[256,2048]{1,0:T(8,128)(2,1)S(1)}, u32[]{:S(2)}, u32[]{:S(2)}) collective-permute-start(bf16[256,2048]{1,0:T(8,128)(2,1)S(1)} %get-tuple-element.179), channel_id=1, source_target_pairs={{3,2},{2,1},{1,0},{7,6},{6,5},{5,4},{11,10},{10,9},{9,8},{15,14},{... | collective-permute-start | bytes 3145736 | tf_op jit(solution)/shard_map/ppermute | solution.py:286
  483.5 30.5 %collective-permute-start.24 = (bf16[256,2048]{1,0:T(8,128)(2,1)S(1)}, bf16[256,2048]{1,0:T(8,128)(2,1)S(1)}, u32[]{:S(2)}, u32[]{:S(2)}) collective-permute-start(bf16[256,2048]{1,0:T(8,128)(2,1)S(1)} %fusion.18), channel_id=1, source_target_pairs={{3,2},{7,6},{11,10},{15,14},{19,18},{23,22},{27,26},{31,30}} | collective-permute-start | bytes 3145736 | tf_op jit(solution)/shard_map/ppermute | solution.py:278
  484.2 29.7 %collective-permute-start.21 = (bf16[256,2048]{1,0:T(8,128)(2,1)S(1)}, bf16[256,2048]{1,0:T(8,128)(2,1)S(1)}, u32[]{:S(2)}, u32[]{:S(2)}) collective-permute-start(bf16[256,2048]{1,0:T(8,128)(2,1)S(1)} %fusion.18), channel_id=1, source_target_pairs={{0,1},{4,5},{8,9},{12,13},{16,17},{20,21},{24,25},{28,29}} | collective-permute-start | bytes 3145736 | tf_op jit(solution)/shard_map/ppermute | solution.py:277
  598.6 28.8 %collective-permute-start.32 = (bf16[256,2048]{1,0:T(8,128)(2,1)}, bf16[256,2048]{1,0:T(8,128)(2,1)S(1)}, u32[]{:S(2)}, u32[]{:S(2)}) collective-permute-start(bf16[256,2048]{1,0:T(8,128)(2,1)} %collective-permute-done.30), channel_id=1, source_target_pairs={{2,3},{6,7},{10,11},{14,15},{18,19},{22,23},{26,27},{30,31}} | collective-permute-start | bytes 3145736 | tf_op jit(solution)/shard_map/ppermute | solution.py:237
  627.4 24.3 %collective-permute-start.53 = (bf16[2048,1024]{1,0:T(8,128)(2,1)}, bf16[2048,1024]{1,0:T(8,128)(2,1)}, u32[]{:S(2)}, u32[]{:S(2)}) collective-permute-start(bf16[2048,1024]{1,0:T(8,128)(2,1)} %convolution_convert_fusion), channel_id=1, source_target_pairs={{0,16},{16,0},{1,17},{17,1},{2,18},{18,2},{3,19},{19,3},{4,20},{20... | collective-permute-start | bytes 12582920 | tf_op jit(solution)/shard_map/ppermute | solution.py:297
  651.4 254.4 %reduce-scatter.14.cloned.1.call-start = ((), (), s32[]{:S(2)}) async-start(), calls=%async_computation.13 | async-start | bytes 5242880 | tf_op jit(solution)/shard_map/reduce_scatter | solution.py:299
  662.5 246.8 %reduce-scatter.12.cloned.1.call-start = ((), (), s32[]{:S(2)}) async-start(), calls=%async_computation.12 | async-start | bytes 5242880 | tf_op jit(solution)/shard_map/reduce_scatter | solution.py:299
  684.6 225.3 %reduce-scatter.10.cloned.1.call-start = ((), (), s32[]{:S(2)}) async-start(), calls=%async_computation.11 | async-start | bytes 5242880 | tf_op jit(solution)/shard_map/reduce_scatter | solution.py:299
  707.2 227.2 %reduce-scatter.6.cloned.1.call-start = ((), (), s32[]{:S(2)}) async-start(), calls=%async_computation.9 | async-start | bytes 3932160 | tf_op jit(solution)/shard_map/reduce_scatter | solution.py:299
  755.9 25.4 %collective-permute-start.33 = (bf16[256,2048]{1,0:T(8,128)(2,1)}, bf16[256,2048]{1,0:T(8,128)(2,1)}, u32[]{:S(2)}, u32[]{:S(2)}) collective-permute-start(bf16[256,2048]{1,0:T(8,128)(2,1)} %convolution_convert_fusion.5), channel_id=1, source_target_pairs={{0,1},{4,5},{8,9},{12,13},{16,17},{20,21},{24,25},{28,29}} | collective-permute-start | bytes 3145736 | tf_op jit(solution)/shard_map/ppermute | solution.py:277
  768.8 53.2 %collective-permute-start.45 = (bf16[2048,768]{0,1:T(8,128)(2,1)}, bf16[2048,768]{0,1:T(8,128)(2,1)}, u32[]{:S(2)}, u32[]{:S(2)}) collective-permute-start(bf16[2048,768]{0,1:T(8,128)(2,1)} %fusion.1), channel_id=1, source_target_pairs={{0,16},{16,0},{1,17},{17,1},{2,18},{18,2},{3,19},{19,3},{4,20},{20... | collective-permute-start | bytes 9437192 | tf_op jit(solution)/shard_map/ppermute | solution.py:297
  787.3 24.9 %collective-permute-start.34 = (bf16[256,2048]{1,0:T(8,128)(2,1)S(1)}, bf16[256,2048]{1,0:T(8,128)(2,1)S(1)}, u32[]{:S(2)}, u32[]{:S(2)}) collective-permute-start(bf16[256,2048]{1,0:T(8,128)(2,1)S(1)} %get-tuple-element.168), channel_id=1, source_target_pairs={{0,1},{1,2},{4,5},{5,6},{8,9},{9,10},{12,13},{13,14},{16,17},{17,1... | collective-permute-start | bytes 3145736 | tf_op jit(solution)/shard_map/ppermute | solution.py:281
  813.9 26.9 %collective-permute-start.35 = (bf16[256,2048]{1,0:T(8,128)(2,1)}, bf16[256,2048]{1,0:T(8,128)(2,1)S(1)}, u32[]{:S(2)}, u32[]{:S(2)}) collective-permute-start(bf16[256,2048]{1,0:T(8,128)(2,1)} %get-tuple-element.166), channel_id=1, source_target_pairs={{0,1},{1,2},{2,3},{4,5},{5,6},{6,7},{8,9},{9,10},{10,11},{12,13},{... | collective-permute-start | bytes 3145736 | tf_op jit(solution)/shard_map/ppermute | solution.py:285
  820.8 24.1 %collective-permute-start.38 = (bf16[256,2048]{1,0:T(8,128)(2,1)}, bf16[256,2048]{1,0:T(8,128)(2,1)S(1)}, u32[]{:S(2)}, u32[]{:S(2)}) collective-permute-start(bf16[256,2048]{1,0:T(8,128)(2,1)} %get-tuple-element.167), channel_id=1, source_target_pairs={{3,2},{2,1},{1,0},{7,6},{6,5},{5,4},{11,10},{10,9},{9,8},{15,14},{... | collective-permute-start | bytes 3145736 | tf_op jit(solution)/shard_map/ppermute | solution.py:286
  873.6 27.0 %collective-permute-start.41 = (bf16[256,2048]{1,0:T(8,128)(2,1)}, bf16[256,2048]{1,0:T(8,128)(2,1)}, u32[]{:S(2)}, u32[]{:S(2)}) collective-permute-start(bf16[256,2048]{1,0:T(8,128)(2,1)} %collective-permute-done.39), channel_id=1, source_target_pairs={{1,0},{2,1},{5,4},{6,5},{9,8},{10,9},{13,12},{14,13},{17,16},{18,1... | collective-permute-start | bytes 3145736 | tf_op jit(solution)/shard_map/ppermute | solution.py:238
  874.9 27.0 %collective-permute-start.42 = (bf16[256,2048]{1,0:T(8,128)(2,1)}, bf16[256,2048]{1,0:T(8,128)(2,1)}, u32[]{:S(2)}, u32[]{:S(2)}) collective-permute-start(bf16[256,2048]{1,0:T(8,128)(2,1)} %collective-permute-done.40), channel_id=1, source_target_pairs={{1,2},{2,3},{5,6},{6,7},{9,10},{10,11},{13,14},{14,15},{17,18},{18... | collective-permute-start | bytes 3145736 | tf_op jit(solution)/shard_map/ppermute | solution.py:237
  900.6 26.1 %collective-permute-start.43 = (bf16[256,2048]{1,0:T(8,128)(2,1)}, bf16[256,2048]{1,0:T(8,128)(2,1)S(1)}, u32[]{:S(2)}, u32[]{:S(2)}) collective-permute-start(bf16[256,2048]{1,0:T(8,128)(2,1)} %collective-permute-done.41), channel_id=1, source_target_pairs={{1,0},{5,4},{9,8},{13,12},{17,16},{21,20},{25,24},{29,28}} | collective-permute-start | bytes 3145736 | tf_op jit(solution)/shard_map/ppermute | solution.py:238
  901.9 24.8 %collective-permute-start.44 = (bf16[256,2048]{1,0:T(8,128)(2,1)}, bf16[256,2048]{1,0:T(8,128)(2,1)S(1)}, u32[]{:S(2)}, u32[]{:S(2)}) collective-permute-start(bf16[256,2048]{1,0:T(8,128)(2,1)} %collective-permute-done.42), channel_id=1, source_target_pairs={{2,3},{6,7},{10,11},{14,15},{18,19},{22,23},{26,27},{30,31}} | collective-permute-start | bytes 3145736 | tf_op jit(solution)/shard_map/ppermute | solution.py:237
  909.8 32.5 %collective-permute-start.50 = (bf16[512,1024]{1,0:T(8,128)(2,1)}, bf16[512,1024]{1,0:T(8,128)(2,1)}, u32[]{:S(2)}, u32[]{:S(2)}) collective-permute-start(bf16[512,1024]{1,0:T(8,128)(2,1)} %reduce-scatter.10.cloned.1.call-done), channel_id=1, source_target_pairs={{0,16},{16,0},{1,17},{17,1},{2,18},{18,2},{3,19},{19,3},{4,20},{20... | collective-permute-start | bytes 3145736 | tf_op jit(solution)/shard_map/ppermute | solution.py:290
  (181 other events, 2119.9 us)
Sparse Core Ops, SparseCore 0:
  10.5 48.1 all-gather.6
  61.1 54.2 all-gather.14
  117.9 54.2 all-gather.8
  174.5 54.2 all-gather.10
  230.5 55.8 all-gather.12
  651.5 25.1 reduce-scatter.7
  680.3 52.5 reduce-scatter.13
  736.5 52.5 reduce-scatter.11
  792.7 52.5 reduce-scatter.9
  848.1 44.4 reduce-scatter.5

commit v3 on v2

--- a/solution.py
+++ b/solution.py
@@ -45,18 +45,24 @@
     return cosine, sine_signed
 
 
-def allowed_block(seg_col_ref, seg_row_ref, first, keys):
-    rows = seg_col_ref[pl.ds(first, BQ), :]
-    cols = seg_row_ref[:, :keys]
-    query_index = first + lax.broadcasted_iota(jnp.int32, (BQ, keys), 0)
-    key_index = lax.broadcasted_iota(jnp.int32, (BQ, keys), 1)
-    return (rows == cols) & (key_index <= query_index)
+def fill_mask(bias_ref, seg_col_ref, seg_row_ref):
+    @pl.when(pl.program_id(0) == 0)
+    def _():
+        for first in range(0, LEN, BQ):
+            keys = first + BQ
+            rows = seg_col_ref[first:keys, :]
+            cols = seg_row_ref[:, :keys]
+            query_index = first + lax.broadcasted_iota(jnp.int32, (BQ, keys), 0)
+            key_index = lax.broadcasted_iota(jnp.int32, (BQ, keys), 1)
+            allowed = (rows == cols) & (key_index <= query_index)
+            bias_ref[first:keys, :keys] = jnp.where(allowed, 0.0, NEG_FILL)
 
 
 def attend_forward_kernel(
     q_ref, k_ref, v_ref, qs_ref, ks_ref, qg_ref, kg_ref, cos_ref, sin_ref, segc_ref, segr_ref,
-    qrot_ref, krot_ref, vb_ref, att_ref, log_ref,
+    qrot_ref, krot_ref, vb_ref, att_ref, log_ref, bias_ref,
 ):
+    fill_mask(bias_ref, segc_ref, segr_ref)
     cosine, sine = cos_ref[...], sin_ref[...]
 
     def turned(raw, scale, gain):
@@ -69,8 +75,7 @@
     for first in range(0, LEN, BQ):
         keys = first + BQ
         scores = times_transposed(qrot_ref[first:keys, :], krot_ref[:keys, :]) * SCORE_SCALE
-        allowed = allowed_block(segc_ref, segr_ref, first, keys)
-        masked = jnp.where(allowed, scores, NEG_FILL)
+        masked = scores + bias_ref[first:keys, :keys]
         peak = jnp.max(masked, axis=1, keepdims=True)
         weight = jnp.exp(masked - peak)
         total = jnp.sum(weight, axis=1, keepdims=True)
@@ -83,8 +88,9 @@
     q_ref, k_ref, qs_ref, ks_ref, qg_ref, kg_ref, cos_ref, sin_ref, segc_ref, segr_ref,
     qrot_ref, krot_ref, vb_ref, att_ref, log_ref, grad_ref,
     dzq_ref, dzk_ref, gv_ref, dotq_ref, dotk_ref, gainq_ref, gaink_ref,
-    dq_acc, dk_acc, dv_acc,
+    dq_acc, dk_acc, dv_acc, bias_ref,
 ):
+    fill_mask(bias_ref, segc_ref, segr_ref)
     dk_acc[...] = jnp.zeros_like(dk_acc)
     dv_acc[...] = jnp.zeros_like(dv_acc)
     for first in range(0, LEN, BQ):
@@ -92,8 +98,7 @@
         queries = qrot_ref[first:keys, :]
         grads = grad_ref[first:keys, :]
         scores = times_transposed(queries, krot_ref[:keys, :]) * SCORE_SCALE
-        allowed = allowed_block(segc_ref, segr_ref, first, keys)
-        probs = jnp.where(allowed, jnp.exp(scores - log_ref[0, first:keys, :]), 0.0)
+        probs = jnp.exp(scores + bias_ref[first:keys, :keys] - log_ref[0, first:keys, :])
         delta = jnp.sum(
             grads.astype(F32) * att_ref[first:keys, :].astype(F32), axis=1, keepdims=True
         )
@@ -156,6 +161,7 @@
         ],
         out_specs=[head_spec(0)] * 4 + [LOG_SPEC],
         out_shape=[piece] * 4 + [jax.ShapeDtypeStruct((heads, LEN, 1), F32)],
+        scratch_shapes=[pltpu.VMEM((LEN, LEN), F32)],
         compiler_params=pltpu.CompilerParams(vmem_limit_bytes=48 << 20),
         cost_estimate=pl.CostEstimate(
             flops=heads * 4 * LEN * LEN * HD, bytes_accessed=LEN * width * 20, transcendentals=0
@@ -185,13 +191,64 @@
         out_shape=[
             full, full, jax.ShapeDtypeStruct((LEN, width), BF16), column, column, gain_row, gain_row,
         ],
-        scratch_shapes=[pltpu.VMEM((LEN, HD), F32)] * 3,
+        scratch_shapes=[pltpu.VMEM((LEN, HD), F32)] * 3 + [pltpu.VMEM((LEN, LEN), F32)],
         compiler_params=pltpu.CompilerParams(vmem_limit_bytes=48 << 20),
         cost_estimate=pl.CostEstimate(
             flops=heads * 10 * LEN * LEN * HD, bytes_accessed=LEN * width * 40, transcendentals=0
         ),
         name="attend_backward",
     )(qkv, qkv, *scales, *gains, *tables, seg_col, seg_row, *saved, grad_att)
+
+
+def project_out_kernel(slot_ref, att_ref, w_ref, x_ref, gain_ref, raw_ref, hidden_ref, hidden_b_ref, scale_ref):
+    block = w_ref.shape[2]
+    step = pl.program_id(0)
+    raw_ref[:, pl.ds(pl.multiple_of(step * block, block), block)] = plain_dot(att_ref[...], w_ref[0])
+
+    @pl.when(step == pl.num_programs(0) - 1)
+    def _():
+        raw = raw_ref[...]
+        scale = lax.rsqrt(jnp.mean(raw * raw, axis=1, keepdims=True) + EPS)
+        scale_ref[...] = scale
+        hidden = x_ref[...].astype(F32) + raw * scale * gain_ref[...]
+        hidden_ref[...] = hidden
+        hidden_b_ref[...] = hidden.astype(BF16)
+
+
+def project_out(slot_index, attended, weight, block_input, gain, chunk):
+    blocks, depth, block = weight.shape
+    width = blocks * block
+    rows = pl.BlockSpec((chunk, width), lambda j, idx: (idx[0], 0))
+    out = pl.BlockSpec((chunk, width), lambda j, idx: (0, 0))
+    return pl.pallas_call(
+        project_out_kernel,
+        grid_spec=pltpu.PrefetchScalarGridSpec(
+            num_scalar_prefetch=1,
+            grid=(blocks,),
+            in_specs=[
+                pl.BlockSpec((chunk, depth), lambda j, idx: (idx[0], 0)),
+                pl.BlockSpec((1, depth, block), lambda j, idx: (j, 0, 0)),
+                rows,
+                pl.BlockSpec((1, width), lambda j, idx: (0, 0)),
+            ],
+            out_specs=[out, out, out, pl.BlockSpec((chunk, 1), lambda j, idx: (0, 0))],
+        ),
+        out_shape=[
+            jax.ShapeDtypeStruct((chunk, width), F32),
+            jax.ShapeDtypeStruct((chunk, width), F32),
+            jax.ShapeDtypeStruct((chunk, width), BF16),
+            jax.ShapeDtypeStruct((chunk, 1), F32),
+        ],
+        compiler_params=pltpu.CompilerParams(vmem_limit_bytes=40 << 20),
+        cost_estimate=pl.CostEstimate(
+            flops=2 * chunk * depth * width, bytes_accessed=2 * depth * width + 16 * chunk * width, transcendentals=0
+        ),
+        name="project_out",
+    )(slot_index, attended, weight, block_input, gain)
+
+
+def after(value, *tokens):
+    return lax.optimization_barrier((value, tokens))[0]
 
 
 def shards(
@@ -264,27 +321,39 @@
     def place(whole, slot, rows_of):
         return lax.dynamic_update_slice_in_dim(whole, rows_of, slot_chunk[slot] * chunk, 0)
 
-    def gather_slots(own):
-        lefts, rights = line_gather(own)
-        return (
-            pick(rights[3], rights[2], lefts[2], lefts[3]),
-            pick(rights[2], rights[1], lefts[1], lefts[2]),
-            jnp.where(col % 2 == 0, rights[1], lefts[1]),
-            own,
-        )
-
-    def sum_slots(parts):
-        up = lax.ppermute(parts[0], "col", [(0, 1)])
-        down = lax.ppermute(parts[0], "col", [(3, 2)])
-        up = jnp.where(col == 0, parts[1], parts[0]) + up
-        down = jnp.where(col == 3, parts[1], parts[0]) + down
+    def gather_slots(own, work):
+        left1, right1 = line_step(own, own, 1)
+        token = work(3, own)
+        left1, right1 = after((left1, right1), token)
+        left2, right2 = line_step(left1, right1, 2)
+        token = work(2, jnp.where(col % 2 == 0, right1, left1))
+        left2, right2 = after((left2, right2), token)
+        left3, right3 = line_step(left2, right2, 3)
+        token = work(1, pick(right2, right1, left1, left2))
+        left3, right3 = after((left3, right3), token)
+        return work(0, pick(right3, right2, left2, left3))
+
+    def sum_slots(make, window=lambda step, gate: ()):
+        first = make(0, ())
+        up = lax.ppermute(first, "col", [(0, 1)])
+        down = lax.ppermute(first, "col", [(3, 2)])
+        second = make(1, first)
+        up, down = after((up, down), second, window(1, first))
+        up = jnp.where(col == 0, second, first) + up
+        down = jnp.where(col == 3, second, first) + down
+        gate = (up, down)
         up = lax.ppermute(up, "col", [(0, 1), (1, 2)])
         down = lax.ppermute(down, "col", [(3, 2), (2, 1)])
-        up = jnp.where(col == 1, parts[1], parts[2]) + up
-        down = jnp.where(col == 2, parts[1], parts[2]) + down
+        third = make(2, gate)
+        up, down = after((up, down), third, window(2, gate))
+        up = jnp.where(col == 1, second, third) + up
+        down = jnp.where(col == 2, second, third) + down
+        gate = (up, down)
         up = lax.ppermute(up, "col", [(0, 1), (1, 2), (2, 3)])
         down = lax.ppermute(down, "col", [(3, 2), (2, 1), (1, 0)])
-        return parts[3].astype(F32) + up.astype(F32) + down.astype(F32)
+        fourth = make(3, gate)
+        up, down = after((up, down), fourth, window(3, gate))
+        return fourth.astype(F32) + up.astype(F32) + down.astype(F32)
 
     def both_cores(half, axis):
         other = lax.ppermute(half, "dp", swap)
@@ -296,7 +365,7 @@
         sent = left_transposed(left_mat, right_other).astype(BF16)
         got = lax.ppermute(sent, "dp", swap)
         total = (left_transposed(left_mat, right_own) + got.astype(F32)).astype(BF16)
-        return lax.psum_scatter(total, "row", scatter_dimension=0, tiled=True)
+        return total, lax.psum_scatter(total, "row", scatter_dimension=0, tiled=True)
 
     full_qkv = gather(jnp.concatenate([w_query, w_key, w_value], axis=1), 0)
     out_half = own_half(w_out, 0)
@@ -304,9 +373,11 @@
         lax.ppermute(out_half, "col", [(i, (i - step) % cols) for i in range(cols)])
         for step in range(1, cols)
     ]
-    full_out = lax.all_gather(jnp.stack(out_pieces), ("row", "dp"), axis=0, tiled=False)
-    full_out = full_out.reshape(rows, cores, cols, local_width // 2, width // rows)
-    full_out = jnp.transpose(full_out, (2, 1, 3, 0, 4)).reshape(cols * local_width, width)
+    half_width = local_width // 2
+    gathered_out = lax.all_gather(jnp.stack(out_pieces), ("row", "dp"), axis=0, tiled=False)
+    gathered_out = gathered_out.reshape(rows, cores, cols, half_width, width // rows)
+    full_out = gathered_out.reshape(rows, cols * local_width, width // rows)
+    own_out = jnp.transpose(gathered_out[:, :, 0], (1, 2, 0, 3)).reshape(local_width, width)
     full_gate = gather(w_gate, 0)
     full_up = gather(w_up, 0)
     full_down = gather(w_down, 1)
@@ -326,39 +397,50 @@
         qkv, scales, gains, tables, seg_col, seg_row, heads
     )
     lefts, rights = line_gather(attended)
+    pieces = [attended] + [rights[step] + lefts[cols - step] for step in range(1, cols)]
     attended_all = jnp.concatenate(
-        [attended] + [rights[step] + lefts[cols - step] for step in range(1, cols)], axis=1
-    )
-
-    saved = []
-    down_parts = []
-    for slot in range(cols):
-        attn_raw = plain_dot(slot_rows(attended_all, slot), full_out)
-        attn_scale = lax.rsqrt(jnp.mean(attn_raw * attn_raw, axis=1, keepdims=True) + EPS)
-        attn_unit = attn_raw * attn_scale
-        hidden = slot_rows(block_input, slot).astype(F32) + attn_unit * attn_gain
-        hidden_b = hidden.astype(BF16)
+        [one[:, half * half_width : (half + 1) * half_width] for half in range(cores) for one in pieces],
+        axis=1,
+    )
+
+    saved = [None] * cols
+    down_parts = [None] * cols
+
+    def forward_chunk(slot, gate):
+        rows_in = after(attended_all, gate)
+        attn_raw, hidden, hidden_b, attn_scale = project_out(
+            slot_chunk[slot].astype(jnp.int32)[None],
+            rows_in, full_out, block_input, attn_gain[None, :], chunk,
+        )
         gate_proj = plain_dot(hidden_b, full_gate)
         up_proj = plain_dot(hidden_b, full_up)
-        gate_sig = jax.nn.sigmoid(gate_proj)
-        gate_act = gate_proj * gate_sig
-        mixed_act = (gate_act * up_proj).astype(BF16)
-        down_parts.append(plain_dot(mixed_act, full_down).astype(BF16))
-        saved.append((attn_scale, attn_raw, hidden, hidden_b, gate_proj, up_proj, mixed_act))
-    down_slots = gather_slots(sum_slots(down_parts).astype(BF16))
-
-    block_output = jnp.zeros((tokens_here, width), BF16)
-    grad_mlp_gain = 0.0
+        mixed_act = (gate_proj * jax.nn.sigmoid(gate_proj) * up_proj).astype(BF16)
+        down_parts[slot] = plain_dot(mixed_act, full_down).astype(BF16)
+        saved[slot] = (attn_scale, attn_raw, hidden, hidden_b, gate_proj, up_proj, mixed_act)
+        return down_parts[slot]
+
+    down_own = sum_slots(forward_chunk).astype(BF16)
+
+    state = dict(
+        block_output=jnp.zeros((tokens_here, width), BF16),
+        grad_att=jnp.zeros((tokens_here, local_width), BF16),
+        grad_input=jnp.zeros((tokens_here, width), F32),
+        mlp_gain=0.0,
+        attn_gain=0.0,
+    )
+    grads = [None] * cols
     mlp_parts = [None] * cols
-    grads = [None] * cols
-    for slot in reversed(range(cols)):
+
+    def backward_chunk(slot, down_rows):
         attn_scale, attn_raw, hidden, hidden_b, gate_proj, up_proj, mixed_act = saved[slot]
-        down_raw = down_slots[slot].astype(F32)
+        down_raw = down_rows.astype(F32)
         down_scale = lax.rsqrt(jnp.mean(down_raw * down_raw, axis=1, keepdims=True) + EPS)
         down_unit = down_raw * down_scale
-        block_output = place(block_output, slot, (hidden + down_unit * mlp_gain).astype(BF16))
+        state["block_output"] = place(
+            state["block_output"], slot, (hidden + down_unit * mlp_gain).astype(BF16)
+        )
         grad_y = slot_rows(grad_output, slot).astype(F32)
-        grad_mlp_gain = grad_mlp_gain + jnp.sum(grad_y * down_unit, axis=0)
+        state["mlp_gain"] = state["mlp_gain"] + jnp.sum(grad_y * down_unit, axis=0)
         down_dz = grad_y * mlp_gain
         grad_down_in = (
             down_scale * (down_dz - down_unit * jnp.mean(down_dz * down_unit, axis=1, keepdims=True))
@@ -373,41 +455,54 @@
             times_transposed(grad_gate_in, full_gate) + times_transposed(grad_up_in, full_up)
         ).astype(BF16)
         grads[slot] = (grad_down_in, grad_gate_in, grad_up_in)
-    mlp_slots = gather_slots(sum_slots(mlp_parts).astype(BF16))
+        return mlp_parts[slot]
+
+    gather_slots(down_own, backward_chunk)
 
     def stacked(pieces):
         return jnp.concatenate(pieces, axis=0)
 
-    hidden_all = stacked([one[3] for one in saved])
-    mixed_all = stacked([one[6] for one in saved])
-    grad_down_all, grad_gate_all, grad_up_all = (stacked([one[i] for one in grads]) for i in range(3))
-    down_block = summed(grad_down_all, own_half(mixed_all, 1), other_half(mixed_all, 1))
-    gate_block = summed(hidden_all, own_half(grad_gate_all, 1), other_half(grad_gate_all, 1))
-    up_block = summed(hidden_all, own_half(grad_up_all, 1), other_half(grad_up_all, 1))
-
-    grad_attn_gain = 0.0
-    grad_att = jnp.zeros((tokens_here, local_width), BF16)
+    blocks = {}
+
+    def mlp_window(step, gate):
+        if step == 1:
+            left_all, right_all = after(
+                (stacked([one[0] for one in grads]), stacked([one[6] for one in saved])), gate
+            )
+            blocks["down"] = summed(left_all, own_half(right_all, 1), other_half(right_all, 1))
+            return blocks["down"][0]
+        kind = ("gate", "up")[step - 2]
+        grad_all, hidden_all = after(
+            (stacked([one[step - 1] for one in grads]), stacked([one[3] for one in saved])), gate
+        )
+        blocks[kind] = summed(hidden_all, own_half(grad_all, 1), other_half(grad_all, 1))
+        return blocks[kind][0]
+
+    mlp_own = sum_slots(lambda slot, gate: mlp_parts[slot], mlp_window).astype(BF16)
+
     attn_ins = [None] * cols
-    for slot in reversed(range(cols)):
+
+    def attention_chunk(slot, mlp_rows):
         attn_scale, attn_raw = saved[slot][:2]
         attn_unit = attn_raw * attn_scale
-        grad_hidden = slot_rows(grad_output, slot).astype(F32) + mlp_slots[slot].astype(F32)
-        grad_attn_gain = grad_attn_gain + jnp.sum(grad_hidden * attn_unit, axis=0)
+        grad_hidden = slot_rows(grad_output, slot).astype(F32) + mlp_rows.astype(F32)
+        state["attn_gain"] = state["attn_gain"] + jnp.sum(grad_hidden * attn_unit, axis=0)
         attn_dz = grad_hidden * attn_gain
         grad_attn_in = (
             attn_scale * (attn_dz - attn_unit * jnp.mean(attn_dz * attn_unit, axis=1, keepdims=True))
         ).astype(BF16)
-        grad_att = place(
-            grad_att, slot, times_transposed(grad_attn_in, full_out[:local_width]).astype(BF16)
+        state["grad_att"] = place(
+            state["grad_att"], slot, times_transposed(grad_attn_in, own_out).astype(BF16)
         )
         attn_ins[slot] = grad_attn_in
-    own_grad_hidden = (
-        slot_rows(grad_output, 3).astype(F32) + mlp_slots[3].astype(F32)
-    )
+        return state["grad_att"]
+
+    gather_slots(mlp_own, attention_chunk)
+    own_grad_hidden = slot_rows(grad_output, 3).astype(F32) + mlp_own.astype(F32)
 
     query_dz, key_dz, grad_value_in, query_dot, key_dot, grad_query_gain, grad_key_gain = attend_backward(
         qkv, scales, gains, tables, seg_col, seg_row,
-        (query_rot, key_rot, value_heads, attended, log_total), grad_att, heads,
+        (query_rot, key_rot, value_heads, attended, log_total), state["grad_att"], heads,
     )
     query_dot, key_dot = lax.psum((query_dot[:, 0], key_dot[:, 0]), "col")
     grad_query_in = (
@@ -417,48 +512,72 @@
         key_scale * (key_dz - key_raw * key_scale * (key_dot / width)[:, None])
     ).astype(BF16)
     grad_qkv = jnp.concatenate([grad_query_in, grad_key_in, grad_value_in], axis=1)
-    input_parts = [
-        times_transposed(slot_rows(grad_qkv, slot), full_qkv).astype(BF16) for slot in range(cols)
-    ]
-    input_slots = gather_slots((own_grad_hidden + sum_slots(input_parts)).astype(BF16))
-    grad_input = jnp.zeros((tokens_here, width), F32)
-    for slot in reversed(range(cols)):
-        grad_input = place(grad_input, slot, input_slots[slot].astype(F32))
 
     def interleaved(picker):
         return jnp.concatenate(
             [picker(one, 1) for one in (grad_query_in, grad_key_in, grad_value_in)], axis=1
         )
 
-    qkv_block = summed(block_input, interleaved(own_half), interleaved(other_half))
-    attended_slots = stacked([slot_rows(attended, slot) for slot in range(cols)])
-    out_block = summed(
-        stacked(attn_ins), own_half(attended_slots, 1), other_half(attended_slots, 1)
-    )
-    qkv_pair = both_cores(qkv_block[None], 0)
+    def input_window(step, gate):
+        if step == 1:
+            own, other, tokens_in = after(
+                (interleaved(own_half), interleaved(other_half), block_input), gate
+            )
+            blocks["qkv"] = summed(tokens_in, own, other)
+            return blocks["qkv"][0]
+        if step == 2:
+            attended_slots, left_all = after(
+                (stacked([slot_rows(attended, slot) for slot in range(cols)]), stacked(attn_ins)), gate
+            )
+            blocks["out"] = summed(left_all, own_half(attended_slots, 1), other_half(attended_slots, 1))
+            return blocks["out"][0]
+        gain_grads = after(
+            (grad_query_gain[0], grad_key_gain[0], state["attn_gain"], state["mlp_gain"]), gate
+        )
+        for axis in ("dp", "row"):
+            gain_grads = lax.psum(gain_grads, axis)
+        blocks["gains"] = gain_grads
+        return gain_grads
+
+    input_own = sum_slots(
+        lambda slot, gate: times_transposed(after(slot_rows(grad_qkv, slot), gate), full_qkv).astype(BF16),
+        input_window,
+    )
+
+    results = {}
+
+    def output_chunk(slot, rows_in):
+        state["grad_input"] = place(state["grad_input"], slot, rows_in.astype(F32))
+        if slot == 3:
+            results["down"] = jnp.transpose(both_cores(blocks["down"][1], 1))
+            results["gate"] = both_cores(blocks["gate"][1], 1)
+            return state["grad_input"], results["down"], results["gate"]
+        if slot == 2:
+            results["up"] = both_cores(blocks["up"][1], 1)
+            return state["grad_input"], results["up"]
+        if slot == 1:
+            results["out"] = jnp.transpose(both_cores(blocks["out"][1], 1))
+            results["qkv"] = [projection(index) for index in range(3)]
+            return state["grad_input"], results["out"], results["qkv"]
+        return state["grad_input"]
+
     quarter = local_width // 2
 
     def projection(index):
-        part = qkv_pair[:, :, index * quarter : (index + 1) * quarter]
-        return jnp.concatenate([part[0], part[1]], axis=1)
-
-    gain_grads = (grad_query_gain[0], grad_key_gain[0], grad_attn_gain, grad_mlp_gain)
-    for axis in ("dp", "row"):
-        gain_grads = lax.psum(gain_grads, axis)
+        pair = both_cores(blocks["qkv"][1][None, :, index * quarter : (index + 1) * quarter], 0)
+        return jnp.concatenate([pair[0], pair[1]], axis=1)
+
+    gather_slots((own_grad_hidden + input_own).astype(BF16), output_chunk)
+    gain_grads = blocks["gains"]
     return (
-        block_output,
-        grad_input,
-        projection(0),
-        projection(1),
-        projection(2),
-        jnp.transpose(both_cores(out_block, 1)),
-        both_cores(gate_block, 1),
-        both_cores(up_block, 1),
-        jnp.transpose(both_cores(down_block, 1)),
-        gain_grads[0],
-        gain_grads[1],
-        gain_grads[2],
-        gain_grads[3],
+        state["block_output"],
+        state["grad_input"],
+        *results["qkv"],
+        results["out"],
+        results["gate"],
+        results["up"],
+        results["down"],
+        *gain_grads,
     )
 
 

time: 970 us -> 1020 us (1.052)
  Pallas kernels: 33.5 us -> 57.4 us
  matrix products: 228 us -> 246 us
  other arithmetic: 86.4 us -> 97.3 us
    pallas_call x0 -> x4, Pallas kernels: none -> 25.2 us  [project_out(): pl.pallas_call(project_out_kernel, grid_spec=pltpu.PrefetchScalarGridSpec...]
    all_gather x4, waiting for transfers between devices: 59 us -> 79.8 us  [gather(): lax.all_gather(own_half(weight, axis), ('row', 'dp'), axis=axis, tiled=True)]
    ppermute x3, waiting for transfers between devices: 26.8 us -> 10.4 us  [sum_slots(): up = lax.ppermute(up, 'col', [(0, 1), (1, 2), (2, 3)])]
    ppermute x12, waiting for transfers between devices: 151 us -> 139 us  [line_step(): lax.ppermute(from_right, 'col', [(i + 1, i) for i in range(cols - step)])]
    dot_general x17 -> x13, matrix products: 74.3 us -> 86.5 us  [plain_dot(): return jnp.dot(left_mat, right_mat, preferred_element_type=F32)]
    reshape x1 -> x0, local copies, waits for them, and re-layouts: 12.2 us -> none  [shards(): full_out.reshape(rows, cores, cols, local_width // 2, width // rows)]
    unnamed x303 -> x302, local copies, waits for them, and re-layouts: 44.9 us -> 43.9 us
  transfers between devices with their start and end apart: 65 -> 67, of which waited for: 32 -> 30; matrix products, arithmetic and copies ran while one was open for 32% -> 32% of each run, Pallas kernels for 3% -> 6%
where the time goes in v3:
time: 1020 us; the launch traced here: 1010 us
  waiting for transfers between devices  382 us (37%)
  matrix products  246 us (24%)
  starting transfers between devices  104 us (10%)
  other arithmetic  97.3 us (10%)
  local copies, waits for them, and re-layouts  62.9 us (6%)
  Pallas kernels  57.4 us (6%)
  blocking collectives  41.1 us (4%)
  between operations  17 us (2%)
    ppermute x12, waiting for transfers between devices, line_step(): lax.ppermute(from_right, 'col', [(i + 1, i) for i in range(cols - step)])  139 us
    dot_general x20, matrix products, times_transposed(): lax.dot_general(left_mat, right_mat, (((1,), (1,)), ((), ())), preferred_...  101 us
    dot_general x13, matrix products, plain_dot(): return jnp.dot(left_mat, right_mat, preferred_element_type=F32)  86.5 us
    all_gather x4, waiting for transfers between devices, gather(): lax.all_gather(own_half(weight, axis), ('row', 'dp'), axis=axis, tiled=True)  79.8 us
    dot_general x10, matrix products, left_transposed(): lax.dot_general(left_mat, right_mat, (((0,), (0,)), ((), ())), preferred_...  58.1 us
    ppermute x12, waiting for transfers between devices, line_step(): lax.ppermute(from_left, 'col', [(i, i + 1) for i in range(step - 1, cols...  44.3 us
    unnamed x302, local copies, waits for them, and re-layouts  43.9 us
    ppermute x3, waiting for transfers between devices, sum_slots(): up = lax.ppermute(up, 'col', [(0, 1), (1, 2)])  34.3 us
  transfers between devices with their start and end apart: 67, of which 30 were waited for; matrix products, arithmetic and copies ran while one was open for 32% of the time, Pallas kernels for 6%

profile of v3, /device:TPU:0, one launch (start us, length us, event | category | flops | bytes accessed | tf_op | source)
XLA Modules:
  0.0 1007.2 jit_solution(10822489129022906760)
XLA Ops:
  21.5 15.6 %collective-permute-done.7 = bf16[256,512]{1,0:T(8,128)(2,1)S(1)} collective-permute-done((bf16[256,512]{1,0:T(8,128)(2,1)S(1)}, bf16[256,512]{1,0:T(8,128)(2,1)S(1)}, u32[]{:S(2)}, u32[]{:S(2)}) %collective-permute-start.7) | collective-permute-done | bytes 262176 | tf_op jit(solution)/shard_map/ppermute | solution.py:373
  46.5 12.1 %all-gather.7.cloned.1.call-done = bf16[2048,1536]{1,0:T(8,128)(2,1)} async-done(((bf16[256,1536]{1,0:T(8,128)(2,1)}), bf16[2048,1536]{1,0:T(8,128)(2,1)}) %all-gather.7.cloned.1.call-update) | async-done | bytes 6291472 | tf_op jit(solution)/shard_map/all_gather | solution.py:291
  58.6 10.0 convolution_bitcast_fusion.q_ref.k_ref.v_ref
  71.7 11.8 %all-reduce.1 = (f32[1024]{0:T(1024)S(1)}, f32[1024]{0:T(1024)S(1)}) all-reduce(f32[1024]{0:T(1024)S(1)} %get-tuple-element.231, f32[1024]{0:T(1024)S(1)} %get-tuple-element.230), channel_id=1, replica_groups=mesh['dp'=2,'row'=4,'col'=4] {'col'}, use_global_device_ids=true, to_apply=%region_1.2 | all-reduce | flops 2048 | bytes 16384 | tf_op jit(solution)/shard_map/psum | solution.py:387
  88.8 16.1 %attend_forward.1 = (bf16[1024,512]{1,0:T(8,128)(2,1)S(1)}, bf16[1024,512]{1,0:T(8,128)(2,1)S(1)}, bf16[1024,512]{1,0:T(8,128)(2,1)S(1)}, bf16[1024,512]{1,0:T(8,128)(2,1)}, f32[4,1024,1]{2,1,0:T(8,128)}) custom-call(f32[1024,1536]{1,0:T(8,128)} %copy-done.48, f32[1024,1536]{1,0:T(8,128)} %copy-done.48, f32[1024,1536]{1,0:T(8,128)} %copy-done.48, ...), custom_call_target="tpu_custom_call" | custom-call | flops 2147483648 | bytes 10485760 | tf_op jit(solution)/shard_map/attend_forward/pallas_call | solution.py:154
  108.5 19.5 %collective-permute-done.1 = bf16[1024,512]{1,0:T(8,128)(2,1)S(1)} collective-permute-done((bf16[1024,512]{1,0:T(8,128)(2,1)}, bf16[1024,512]{1,0:T(8,128)(2,1)S(1)}, u32[]{:S(2)}, u32[]{:S(2)}) %collective-permute-start.1) | collective-permute-done | bytes 1048608 | tf_op jit(solution)/shard_map/ppermute | solution.py:294
  135.1 23.7 %collective-permute-done.4 = bf16[1024,512]{1,0:T(8,128)(2,1)} collective-permute-done((bf16[1024,512]{1,0:T(8,128)(2,1)S(1)}, bf16[1024,512]{1,0:T(8,128)(2,1)}, u32[]{:S(2)}, u32[]{:S(2)}) %collective-permute-start.4) | collective-permute-done | bytes 1048608 | tf_op jit(solution)/shard_map/ppermute | solution.py:295
  165.3 18.1 %collective-permute-done.5 = bf16[1024,512]{1,0:T(8,128)(2,1)} collective-permute-done((bf16[1024,512]{1,0:T(8,128)(2,1)}, bf16[1024,512]{1,0:T(8,128)(2,1)}, u32[]{:S(2)}, u32[]{:S(2)}) %collective-permute-start.5) | collective-permute-done | bytes 1048608 | tf_op jit(solution)/shard_map/ppermute | solution.py:295
  201.6 8.8 fusion.94
  210.4 18.3 %all-gather.11.cloned.1.call-done = bf16[2048,2048]{1,0:T(8,128)(2,1)} async-done(((bf16[256,2048]{1,0:T(8,128)(2,1)}), bf16[2048,2048]{1,0:T(8,128)(2,1)}) %all-gather.11.cloned.1.call-update) | async-done | bytes 8388624 | tf_op jit(solution)/shard_map/all_gather | solution.py:291
  228.7 8.2 multiply_convert_fusion.17
  237.0 49.4 %all-gather.13.cloned.1.call-done = bf16[2048,2048]{1,0:T(8,128)(2,1)} async-done(((bf16[2048,256]{1,0:T(8,128)(2,1)}), bf16[2048,2048]{1,0:T(8,128)(2,1)}) %all-gather.13.cloned.1.call-update) | async-done | bytes 8388624 | tf_op jit(solution)/shard_map/all_gather | solution.py:291
  310.7 8.1 multiply_convert_fusion.16
  339.0 8.1 multiply_convert_fusion.15
  368.4 8.2 multiply_convert_fusion.14
  506.4 10.7 %add_convert_fusion.2 = bf16[2048,1024]{1,0:T(8,128)(2,1)} fusion(bf16[2048,1024]{1,0:T(8,128)(2,1)} %collective-permute-done.23, bf16[1024,2048]{1,0:T(8,128)(2,1)} %copy-done.65, bf16[1024,2048]{1,0:T(8,128)(2,1)} %copy-done.62, s32[]{:T(128)S(6)} %select_n.340), kind=kOutput, calls=%fused_computation.2 | convolution fusion | flops 4301258752 | bytes 14680068 | tf_op jit(solution)/shard_map/dot_general | solution.py:33
  527.0 19.1 %collective-permute-done.21 = bf16[256,2048]{1,0:T(8,128)(2,1)S(1)} collective-permute-done((bf16[256,2048]{1,0:T(8,128)(2,1)}, bf16[256,2048]{1,0:T(8,128)(2,1)S(1)}, u32[]{:S(2)}, u32[]{:S(2)}) %collective-permute-start.21) | collective-permute-done | bytes 1048608 | tf_op jit(solution)/shard_map/ppermute | solution.py:338
  574.2 19.6 %collective-permute-done.24 = bf16[256,2048]{1,0:T(8,128)(2,1)S(1)} collective-permute-done((bf16[256,2048]{1,0:T(8,128)(2,1)}, bf16[256,2048]{1,0:T(8,128)(2,1)S(1)}, u32[]{:S(2)}, u32[]{:S(2)}) %collective-permute-start.24) | collective-permute-done | bytes 1048608 | tf_op jit(solution)/shard_map/ppermute | solution.py:345
  608.5 9.7 collective-permute-start.27
  619.5 10.7 %add_convert_fusion = bf16[2048,1024]{1,0:T(8,128)(2,1)} fusion(bf16[2048,1024]{1,0:T(8,128)(2,1)} %collective-permute-done.29, bf16[1024,2048]{1,0:T(8,128)(2,1)} %copy-done.110, bf16[1024,2048]{1,0:T(8,128)(2,1)} %copy-done.63, s32[]{:T(128)S(6)} %select_n.340), kind=kOutput, calls=%fused_computation | convolution fusion | flops 4301258752 | bytes 14680068 | tf_op jit(solution)/shard_map/dot_general | solution.py:33
  630.2 10.4 %collective-permute-done.27 = bf16[256,2048]{1,0:T(8,128)(2,1)} collective-permute-done((bf16[256,2048]{1,0:T(8,128)(2,1)}, bf16[256,2048]{1,0:T(8,128)(2,1)}, u32[]{:S(2)}, u32[]{:S(2)}) %collective-permute-start.27) | collective-permute-done | bytes 1048608 | tf_op jit(solution)/shard_map/ppermute | solution.py:352
  657.4 16.2 %collective-permute-done.30 = bf16[256,2048]{1,0:T(8,128)(2,1)} collective-permute-done((bf16[256,2048]{1,0:T(8,128)(2,1)}, bf16[256,2048]{1,0:T(8,128)(2,1)}, u32[]{:S(2)}, u32[]{:S(2)}) %collective-permute-start.30) | collective-permute-done | bytes 1048608 | tf_op jit(solution)/shard_map/ppermute | solution.py:294
  684.6 20.3 %collective-permute-done.33 = bf16[256,2048]{1,0:T(8,128)(2,1)S(1)} collective-permute-done((bf16[256,2048]{1,0:T(8,128)(2,1)}, bf16[256,2048]{1,0:T(8,128)(2,1)S(1)}, u32[]{:S(2)}, u32[]{:S(2)}) %collective-permute-start.33) | collective-permute-done | bytes 1048608 | tf_op jit(solution)/shard_map/ppermute | solution.py:295
  709.9 20.3 %collective-permute-done.35 = bf16[256,2048]{1,0:T(8,128)(2,1)S(1)} collective-permute-done((bf16[256,2048]{1,0:T(8,128)(2,1)S(1)}, bf16[256,2048]{1,0:T(8,128)(2,1)S(1)}, u32[]{:S(2)}, u32[]{:S(2)}) %collective-permute-start.35) | collective-permute-done | bytes 1048608 | tf_op jit(solution)/shard_map/ppermute | solution.py:295
  734.6 16.2 %attend_backward.1 = (f32[1024,512]{1,0:T(8,128)}, f32[1024,512]{1,0:T(8,128)}, bf16[1024,512]{1,0:T(8,128)(2,1)S(1)}, f32[1024,1]{1,0:T(8,128)S(1)}, f32[1024,1...) custom-call(f32[1024,1536]{1,0:T(8,128)} %copy-done.48, f32[1024,1536]{1,0:T(8,128)} %copy-done.48, ...), custom_call_target="tpu_custom_call" | custom-call | flops 5368709120 | bytes 20971520 | tf_op jit(solution)/shard_map/attend_backward/pallas_call | solution.py:178
  755.0 8.7 all-reduce
  795.7 11.1 %collective-permute-done.36 = bf16[256,2048]{1,0:T(8,128)(2,1)} collective-permute-done((bf16[256,2048]{1,0:T(8,128)(2,1)}, bf16[256,2048]{1,0:T(8,128)(2,1)}, u32[]{:S(2)}, u32[]{:S(2)}) %collective-permute-start.36) | collective-permute-done | bytes 1048608 | tf_op jit(solution)/shard_map/ppermute | solution.py:338
  840.4 14.8 %collective-permute-done.39 = bf16[256,2048]{1,0:T(8,128)(2,1)S(1)} collective-permute-done((bf16[256,2048]{1,0:T(8,128)(2,1)}, bf16[256,2048]{1,0:T(8,128)(2,1)S(1)}, u32[]{:S(2)}, u32[]{:S(2)}) %collective-permute-start.39) | collective-permute-done | bytes 1048608 | tf_op jit(solution)/shard_map/ppermute | solution.py:345
  871.1 16.7 %all-reduce.2 = (f32[512]{0:T(512)}, f32[512]{0:T(512)}, f32[2048]{0:T(1024)}, f32[2048]{0:T(1024)}) all-reduce(f32[512]{0:T(512)S(1)} %get-tuple-element.248, f32[512]{0:T(512)S(1)} %get-tuple-element.249, f32[2048]{0:T(1024)S(1)} %get-tuple-element.250, ...), channel_id=1, replica_groups=mesh['dp'=2,'row'=4,'col'=4] {'row'}, use_global_device_ids=true, to_apply=%region_27.28 | all-reduce | flops 5120 | bytes 40960 | tf_op jit(solution)/shard_map/psum | solution.py:538
  921.8 8.5 collective-permute-done.44
  944.4 18.3 %collective-permute-done.49 = bf16[256,2048]{1,0:T(8,128)(2,1)} collective-permute-done((bf16[256,2048]{1,0:T(8,128)(2,1)}, bf16[256,2048]{1,0:T(8,128)(2,1)}, u32[]{:S(2)}, u32[]{:S(2)}) %collective-permute-start.49) | collective-permute-done | bytes 1048608 | tf_op jit(solution)/shard_map/ppermute | solution.py:295
  974.7 22.2 %collective-permute-done.52 = bf16[256,2048]{1,0:T(8,128)(2,1)S(1)} collective-permute-done((bf16[256,2048]{1,0:T(8,128)(2,1)}, bf16[256,2048]{1,0:T(8,128)(2,1)S(1)}, u32[]{:S(2)}, u32[]{:S(2)}) %collective-permute-start.52) | collective-permute-done | bytes 1048608 | tf_op jit(solution)/shard_map/ppermute | solution.py:295
  (585 shorter events, 500.7 us)
Async XLA Ops:
  7.2 51.4 %all-gather.7.cloned.1.call-start = ((), (), s32[]{:S(2)}) async-start(), calls=%async_computation.5 | async-start | bytes 7077888 | tf_op jit(solution)/shard_map/all_gather | solution.py:291
  9.5 179.1 %all-gather.15.cloned.1.call-start = ((), (), s32[]{:S(2)}) async-start(), calls=%async_computation.14 | async-start | bytes 9437184 | tf_op jit(solution)/shard_map/all_gather | solution.py:377
  38.2 163.4 %all-gather.9.cloned.1.call-start = ((), (), s32[]{:S(2)}) async-start(), calls=%async_computation.6 | async-start | bytes 9437184 | tf_op jit(solution)/shard_map/all_gather | solution.py:291
  39.4 189.4 %all-gather.11.cloned.1.call-start = ((), (), s32[]{:S(2)}) async-start(), calls=%async_computation.7 | async-start | bytes 9437184 | tf_op jit(solution)/shard_map/all_gather | solution.py:291
  41.9 244.5 %all-gather.13.cloned.1.call-start = ((), (), s32[]{:S(2)}) async-start(), calls=%async_computation.8 | async-start | bytes 9437184 | tf_op jit(solution)/shard_map/all_gather | solution.py:291
  43.0 792.3 %reduce-scatter.6.cloned.1.call-start = ((), (), s32[]{:S(2)}) async-start(), calls=%async_computation.9 | async-start | bytes 5242880 | tf_op jit(solution)/shard_map/reduce_scatter | solution.py:368
  132.1 26.6 %collective-permute-start.4 = (bf16[1024,512]{1,0:T(8,128)(2,1)S(1)}, bf16[1024,512]{1,0:T(8,128)(2,1)}, u32[]{:S(2)}, u32[]{:S(2)}) collective-permute-start(bf16[1024,512]{1,0:T(8,128)(2,1)S(1)} %collective-permute-done), channel_id=1, source_target_pairs={{1,0},{2,1},{5,4},{6,5},{9,8},{10,9},{13,12},{14,13},{17,16},{18,1... | collective-permute-start | bytes 3145736 | tf_op jit(solution)/shard_map/ppermute | solution.py:295
  133.4 30.2 %collective-permute-start.3 = (bf16[1024,512]{1,0:T(8,128)(2,1)}, bf16[1024,512]{1,0:T(8,128)(2,1)}, u32[]{:S(2)}, u32[]{:S(2)}) collective-permute-start(bf16[1024,512]{1,0:T(8,128)(2,1)} %collective-permute-done.2), channel_id=1, source_target_pairs={{2,3},{6,7},{10,11},{14,15},{18,19},{22,23},{26,27},{30,31}} | collective-permute-start | bytes 3145736 | tf_op jit(solution)/shard_map/ppermute | solution.py:294
  292.2 28.9 %collective-permute-start.10 = (bf16[256,2048]{1,0:T(8,128)(2,1)S(1)}, bf16[256,2048]{1,0:T(8,128)(2,1)S(1)}, u32[]{:S(2)}, u32[]{:S(2)}) collective-permute-start(bf16[256,2048]{1,0:T(8,128)(2,1)S(1)} %convolution_convert_fusion.12), channel_id=1, source_target_pairs={{3,2},{7,6},{11,10},{15,14},{19,18},{23,22},{27,26},{31,30}} | collective-permute-start | bytes 3145736 | tf_op jit(solution)/shard_map/ppermute | solution.py:339
  293.0 28.1 %collective-permute-start.9 = (bf16[256,2048]{1,0:T(8,128)(2,1)S(1)}, bf16[256,2048]{1,0:T(8,128)(2,1)S(1)}, u32[]{:S(2)}, u32[]{:S(2)}) collective-permute-start(bf16[256,2048]{1,0:T(8,128)(2,1)S(1)} %convolution_convert_fusion.12), channel_id=1, source_target_pairs={{0,1},{4,5},{8,9},{12,13},{16,17},{20,21},{24,25},{28,29}} | collective-permute-start | bytes 3145736 | tf_op jit(solution)/shard_map/ppermute | solution.py:338
  321.5 27.9 %collective-permute-start.11 = (bf16[256,2048]{1,0:T(8,128)(2,1)S(1)}, bf16[256,2048]{1,0:T(8,128)(2,1)S(1)}, u32[]{:S(2)}, u32[]{:S(2)}) collective-permute-start(bf16[256,2048]{1,0:T(8,128)(2,1)S(1)} %get-tuple-element.297), channel_id=1, source_target_pairs={{0,1},{1,2},{4,5},{5,6},{8,9},{9,10},{12,13},{13,14},{16,17},{17,1... | collective-permute-start | bytes 3145736 | tf_op jit(solution)/shard_map/ppermute | solution.py:345
  349.8 29.9 %collective-permute-start.13 = (bf16[256,2048]{1,0:T(8,128)(2,1)S(1)}, bf16[256,2048]{1,0:T(8,128)(2,1)S(1)}, u32[]{:S(2)}, u32[]{:S(2)}) collective-permute-start(bf16[256,2048]{1,0:T(8,128)(2,1)S(1)} %get-tuple-element.295), channel_id=1, source_target_pairs={{0,1},{1,2},{2,3},{4,5},{5,6},{6,7},{8,9},{9,10},{10,11},{12,13},{... | collective-permute-start | bytes 3145736 | tf_op jit(solution)/shard_map/ppermute | solution.py:352
  380.4 30.0 %collective-permute-start.15 = (bf16[256,2048]{1,0:T(8,128)(2,1)S(1)}, bf16[256,2048]{1,0:T(8,128)(2,1)S(1)}, u32[]{:S(2)}, u32[]{:S(2)}) collective-permute-start(bf16[256,2048]{1,0:T(8,128)(2,1)S(1)} %get-tuple-element.265), channel_id=1, source_target_pairs={{0,1},{1,2},{2,3},{4,5},{5,6},{6,7},{8,9},{9,10},{10,11},{12,13},{... | collective-permute-start | bytes 3145736 | tf_op jit(solution)/shard_map/ppermute | solution.py:294
  411.7 28.3 %collective-permute-start.18 = (bf16[256,2048]{1,0:T(8,128)(2,1)S(1)}, bf16[256,2048]{1,0:T(8,128)(2,1)S(1)}, u32[]{:S(2)}, u32[]{:S(2)}) collective-permute-start(bf16[256,2048]{1,0:T(8,128)(2,1)S(1)} %collective-permute-done.16), channel_id=1, source_target_pairs={{1,0},{2,1},{5,4},{6,5},{9,8},{10,9},{13,12},{14,13},{17,16},{18,1... | collective-permute-start | bytes 3145736 | tf_op jit(solution)/shard_map/ppermute | solution.py:295
  517.1 350.1 %reduce-scatter.8.cloned.1.call-start = ((), (), s32[]{:S(2)}) async-start(), calls=%async_computation.10 | async-start | bytes 5242880 | tf_op jit(solution)/shard_map/reduce_scatter | solution.py:368
  518.7 27.4 %collective-permute-start.21 = (bf16[256,2048]{1,0:T(8,128)(2,1)}, bf16[256,2048]{1,0:T(8,128)(2,1)S(1)}, u32[]{:S(2)}, u32[]{:S(2)}) collective-permute-start(bf16[256,2048]{1,0:T(8,128)(2,1)} %fusion.15), channel_id=1, source_target_pairs={{0,1},{4,5},{8,9},{12,13},{16,17},{20,21},{24,25},{28,29}} | collective-permute-start | bytes 3145736 | tf_op jit(solution)/shard_map/ppermute | solution.py:338
  566.3 326.5 %reduce-scatter.10.cloned.1.call-start = ((), (), s32[]{:S(2)}) async-start(), calls=%async_computation.11 | async-start | bytes 5242880 | tf_op jit(solution)/shard_map/reduce_scatter | solution.py:368
  566.3 27.4 %collective-permute-start.24 = (bf16[256,2048]{1,0:T(8,128)(2,1)}, bf16[256,2048]{1,0:T(8,128)(2,1)S(1)}, u32[]{:S(2)}, u32[]{:S(2)}) collective-permute-start(bf16[256,2048]{1,0:T(8,128)(2,1)} %get-tuple-element.293), channel_id=1, source_target_pairs={{0,1},{1,2},{4,5},{5,6},{8,9},{9,10},{12,13},{13,14},{16,17},{17,1... | collective-permute-start | bytes 3145736 | tf_op jit(solution)/shard_map/ppermute | solution.py:345
  608.5 32.1 %collective-permute-start.27 = (bf16[256,2048]{1,0:T(8,128)(2,1)}, bf16[256,2048]{1,0:T(8,128)(2,1)}, u32[]{:S(2)}, u32[]{:S(2)}) collective-permute-start(bf16[256,2048]{1,0:T(8,128)(2,1)} %get-tuple-element.291), channel_id=1, source_target_pairs={{0,1},{1,2},{2,3},{4,5},{5,6},{6,7},{8,9},{9,10},{10,11},{12,13},{... | collective-permute-start | bytes 3145736 | tf_op jit(solution)/shard_map/ppermute | solution.py:352
  618.2 27.5 %collective-permute-start.28 = (bf16[256,2048]{1,0:T(8,128)(2,1)}, bf16[256,2048]{1,0:T(8,128)(2,1)}, u32[]{:S(2)}, u32[]{:S(2)}) collective-permute-start(bf16[256,2048]{1,0:T(8,128)(2,1)} %get-tuple-element.290), channel_id=1, source_target_pairs={{3,2},{2,1},{1,0},{7,6},{6,5},{5,4},{11,10},{10,9},{9,8},{15,14},{... | collective-permute-start | bytes 3145736 | tf_op jit(solution)/shard_map/ppermute | solution.py:353
  653.6 286.3 %reduce-scatter.12.cloned.1.call-start = ((), (), s32[]{:S(2)}) async-start(), calls=%async_computation.12 | async-start | bytes 1310720 | tf_op jit(solution)/shard_map/reduce_scatter | solution.py:368
  779.6 27.2 %collective-permute-start.36 = (bf16[256,2048]{1,0:T(8,128)(2,1)}, bf16[256,2048]{1,0:T(8,128)(2,1)}, u32[]{:S(2)}, u32[]{:S(2)}) collective-permute-start(bf16[256,2048]{1,0:T(8,128)(2,1)} %convolution_convert_fusion.8), channel_id=1, source_target_pairs={{0,1},{4,5},{8,9},{12,13},{16,17},{20,21},{24,25},{28,29}} | collective-permute-start | bytes 3145736 | tf_op jit(solution)/shard_map/ppermute | solution.py:338
  816.7 147.6 %reduce-scatter.14.cloned.1.call-start = ((), (), s32[]{:S(2)}) async-start(), calls=%async_computation.13 | async-start | bytes 3932160 | tf_op jit(solution)/shard_map/reduce_scatter | solution.py:368
  827.7 27.5 %collective-permute-start.39 = (bf16[256,2048]{1,0:T(8,128)(2,1)}, bf16[256,2048]{1,0:T(8,128)(2,1)S(1)}, u32[]{:S(2)}, u32[]{:S(2)}) collective-permute-start(bf16[256,2048]{1,0:T(8,128)(2,1)} %get-tuple-element.289), channel_id=1, source_target_pairs={{0,1},{1,2},{4,5},{5,6},{8,9},{9,10},{12,13},{13,14},{16,17},{17,1... | collective-permute-start | bytes 3145736 | tf_op jit(solution)/shard_map/ppermute | solution.py:345
  835.3 31.7 %collective-permute-start.46 = (bf16[512,1024]{1,0:T(8,128)(2,1)}, bf16[512,1024]{1,0:T(8,128)(2,1)S(1)}, u32[]{:S(2)}, u32[]{:S(2)}) collective-permute-start(bf16[512,1024]{1,0:T(8,128)(2,1)} %reduce-scatter.6.cloned.1.call-done), channel_id=1, source_target_pairs={{0,16},{16,0},{1,17},{17,1},{2,18},{18,2},{3,19},{19,3},{4,20},{20... | collective-permute-start | bytes 3145736 | tf_op jit(solution)/shard_map/ppermute | solution.py:359
  857.9 35.0 %collective-permute-start.42 = (bf16[256,2048]{1,0:T(8,128)(2,1)}, bf16[256,2048]{1,0:T(8,128)(2,1)}, u32[]{:S(2)}, u32[]{:S(2)}) collective-permute-start(bf16[256,2048]{1,0:T(8,128)(2,1)} %get-tuple-element.287), channel_id=1, source_target_pairs={{0,1},{1,2},{2,3},{4,5},{5,6},{6,7},{8,9},{9,10},{10,11},{12,13},{... | collective-permute-start | bytes 3145736 | tf_op jit(solution)/shard_map/ppermute | solution.py:352
  865.5 27.4 %collective-permute-start.43 = (bf16[256,2048]{1,0:T(8,128)(2,1)}, bf16[256,2048]{1,0:T(8,128)(2,1)}, u32[]{:S(2)}, u32[]{:S(2)}) collective-permute-start(bf16[256,2048]{1,0:T(8,128)(2,1)} %get-tuple-element.286), channel_id=1, source_target_pairs={{3,2},{2,1},{1,0},{7,6},{6,5},{5,4},{11,10},{10,9},{9,8},{15,14},{... | collective-permute-start | bytes 3145736 | tf_op jit(solution)/shard_map/ppermute | solution.py:353
  867.2 41.9 %collective-permute-start.47 = (bf16[512,1024]{1,0:T(8,128)(2,1)}, bf16[512,1024]{1,0:T(8,128)(2,1)}, u32[]{:S(2)}, u32[]{:S(2)}) collective-permute-start(bf16[512,1024]{1,0:T(8,128)(2,1)} %reduce-scatter.8.cloned.1.call-done), channel_id=1, source_target_pairs={{0,16},{16,0},{1,17},{17,1},{2,18},{18,2},{3,19},{19,3},{4,20},{20... | collective-permute-start | bytes 3145736 | tf_op jit(solution)/shard_map/ppermute | solution.py:359
  892.8 27.6 %collective-permute-start.50 = (bf16[512,1024]{1,0:T(8,128)(2,1)}, bf16[512,1024]{1,0:T(8,128)(2,1)}, u32[]{:S(2)}, u32[]{:S(2)}) collective-permute-start(bf16[512,1024]{1,0:T(8,128)(2,1)} %reduce-scatter.10.cloned.1.call-done), channel_id=1, source_target_pairs={{0,16},{16,0},{1,17},{17,1},{2,18},{18,2},{3,19},{19,3},{4,20},{20... | collective-permute-start | bytes 3145736 | tf_op jit(solution)/shard_map/ppermute | solution.py:359
  902.3 27.9 %collective-permute-start.44 = (bf16[256,2048]{1,0:T(8,128)(2,1)}, bf16[256,2048]{1,0:T(8,128)(2,1)}, u32[]{:S(2)}, u32[]{:S(2)}) collective-permute-start(bf16[256,2048]{1,0:T(8,128)(2,1)} %get-tuple-element.253), channel_id=1, source_target_pairs={{0,1},{1,2},{2,3},{4,5},{5,6},{6,7},{8,9},{9,10},{10,11},{12,13},{... | collective-permute-start | bytes 3145736 | tf_op jit(solution)/shard_map/ppermute | solution.py:294
  907.9 27.5 %collective-permute-start.45 = (bf16[256,2048]{1,0:T(8,128)(2,1)}, bf16[256,2048]{1,0:T(8,128)(2,1)}, u32[]{:S(2)}, u32[]{:S(2)}) collective-permute-start(bf16[256,2048]{1,0:T(8,128)(2,1)} %get-tuple-element.253), channel_id=1, source_target_pairs={{1,0},{2,1},{3,2},{5,4},{6,5},{7,6},{9,8},{10,9},{11,10},{13,12},{... | collective-permute-start | bytes 3145736 | tf_op jit(solution)/shard_map/ppermute | solution.py:295
  969.4 27.5 %collective-permute-start.52 = (bf16[256,2048]{1,0:T(8,128)(2,1)}, bf16[256,2048]{1,0:T(8,128)(2,1)S(1)}, u32[]{:S(2)}, u32[]{:S(2)}) collective-permute-start(bf16[256,2048]{1,0:T(8,128)(2,1)} %collective-permute-done.49), channel_id=1, source_target_pairs={{1,0},{5,4},{9,8},{13,12},{17,16},{21,20},{25,24},{29,28}} | collective-permute-start | bytes 3145736 | tf_op jit(solution)/shard_map/ppermute | solution.py:295
  (179 other events, 1930.4 us)
Sparse Core Ops, SparseCore 0:
  10.5 48.1 all-gather.6
  61.1 54.2 all-gather.14
  117.8 54.2 all-gather.8
  174.5 54.2 all-gather.10
  230.5 55.8 all-gather.12
  517.2 53.1 reduce-scatter.5
  574.0 52.5 reduce-scatter.7
  653.7 51.8 reduce-scatter.9
  816.8 27.0 reduce-scatter.11
  846.8 44.2 reduce-scatter.13

commit v4 on v1

--- a/solution.py
+++ b/solution.py
@@ -6,6 +6,7 @@
 from jax.experimental import pallas as pl
 from jax.experimental.pallas import tpu as pltpu
 from jax.sharding import PartitionSpec as P
+
 
 HD = 128
 LEN = 1024
@@ -45,18 +46,24 @@
     return cosine, sine_signed
 
 
-def allowed_block(seg_col_ref, seg_row_ref, first, keys):
-    rows = seg_col_ref[pl.ds(first, BQ), :]
-    cols = seg_row_ref[:, :keys]
-    query_index = first + lax.broadcasted_iota(jnp.int32, (BQ, keys), 0)
-    key_index = lax.broadcasted_iota(jnp.int32, (BQ, keys), 1)
-    return (rows == cols) & (key_index <= query_index)
+def fill_mask(bias_ref, seg_col_ref, seg_row_ref):
+    @pl.when(pl.program_id(0) == 0)
+    def _():
+        for first in range(0, LEN, BQ):
+            keys = first + BQ
+            rows = seg_col_ref[first:keys, :]
+            cols = seg_row_ref[:, :keys]
+            query_index = first + lax.broadcasted_iota(jnp.int32, (BQ, keys), 0)
+            key_index = lax.broadcasted_iota(jnp.int32, (BQ, keys), 1)
+            allowed = (rows == cols) & (key_index <= query_index)
+            bias_ref[first:keys, :keys] = jnp.where(allowed, 0.0, NEG_FILL)
 
 
 def attend_forward_kernel(
     q_ref, k_ref, v_ref, qs_ref, ks_ref, qg_ref, kg_ref, cos_ref, sin_ref, segc_ref, segr_ref,
-    qrot_ref, krot_ref, vb_ref, att_ref, log_ref,
+    qrot_ref, krot_ref, vb_ref, att_ref, log_ref, bias_ref,
 ):
+    fill_mask(bias_ref, segc_ref, segr_ref)
     cosine, sine = cos_ref[...], sin_ref[...]
 
     def turned(raw, scale, gain):
@@ -69,8 +76,7 @@
     for first in range(0, LEN, BQ):
         keys = first + BQ
         scores = times_transposed(qrot_ref[first:keys, :], krot_ref[:keys, :]) * SCORE_SCALE
-        allowed = allowed_block(segc_ref, segr_ref, first, keys)
-        masked = jnp.where(allowed, scores, NEG_FILL)
+        masked = scores + bias_ref[first:keys, :keys]
         peak = jnp.max(masked, axis=1, keepdims=True)
         weight = jnp.exp(masked - peak)
         total = jnp.sum(weight, axis=1, keepdims=True)
@@ -83,8 +89,9 @@
     q_ref, k_ref, qs_ref, ks_ref, qg_ref, kg_ref, cos_ref, sin_ref, segc_ref, segr_ref,
     qrot_ref, krot_ref, vb_ref, att_ref, log_ref, grad_ref,
     dzq_ref, dzk_ref, gv_ref, dotq_ref, dotk_ref, gainq_ref, gaink_ref,
-    dq_acc, dk_acc, dv_acc,
+    dq_acc, dk_acc, dv_acc, bias_ref,
 ):
+    fill_mask(bias_ref, segc_ref, segr_ref)
     dk_acc[...] = jnp.zeros_like(dk_acc)
     dv_acc[...] = jnp.zeros_like(dv_acc)
     for first in range(0, LEN, BQ):
@@ -92,8 +99,7 @@
         queries = qrot_ref[first:keys, :]
         grads = grad_ref[first:keys, :]
         scores = times_transposed(queries, krot_ref[:keys, :]) * SCORE_SCALE
-        allowed = allowed_block(segc_ref, segr_ref, first, keys)
-        probs = jnp.where(allowed, jnp.exp(scores - log_ref[0, first:keys, :]), 0.0)
+        probs = jnp.exp(scores + bias_ref[first:keys, :keys] - log_ref[0, first:keys, :])
         delta = jnp.sum(
             grads.astype(F32) * att_ref[first:keys, :].astype(F32), axis=1, keepdims=True
         )
@@ -156,7 +162,8 @@
         ],
         out_specs=[head_spec(0)] * 4 + [LOG_SPEC],
         out_shape=[piece] * 4 + [jax.ShapeDtypeStruct((heads, LEN, 1), F32)],
-        compiler_params=pltpu.CompilerParams(vmem_limit_bytes=48 << 20),
+        scratch_shapes=[pltpu.VMEM((LEN, LEN), F32)],
+        compiler_params=pltpu.CompilerParams(vmem_limit_bytes=28 << 20),
         cost_estimate=pl.CostEstimate(
             flops=heads * 4 * LEN * LEN * HD, bytes_accessed=LEN * width * 20, transcendentals=0
         ),
@@ -185,13 +192,321 @@
         out_shape=[
             full, full, jax.ShapeDtypeStruct((LEN, width), BF16), column, column, gain_row, gain_row,
         ],
-        scratch_shapes=[pltpu.VMEM((LEN, HD), F32)] * 3,
-        compiler_params=pltpu.CompilerParams(vmem_limit_bytes=48 << 20),
+        scratch_shapes=[pltpu.VMEM((LEN, HD), F32)] * 3 + [pltpu.VMEM((LEN, LEN), F32)],
+        compiler_params=pltpu.CompilerParams(vmem_limit_bytes=28 << 20),
         cost_estimate=pl.CostEstimate(
             flops=heads * 10 * LEN * LEN * HD, bytes_accessed=LEN * width * 40, transcendentals=0
         ),
         name="attend_backward",
     )(qkv, qkv, *scales, *gains, *tables, seg_col, seg_row, *saved, grad_att)
+
+
+def half_tile(step, core, tiles):
+    per_half = tiles // 2
+    return ((core + step // per_half) % 2) * per_half + step % per_half
+
+
+def forward_chunk_kernel(
+    idx_ref, att_ref, wo_own_ref, wo_oth_ref, x_ref, gain_ref, wg_ref, wu_ref, wd_own_ref, wd_oth_ref, *refs,
+    blocks, tiles,
+):
+    raw_ref, scale_ref, hb_ref, gate_ref, up_ref, mixed_ref, part_ref, acc_ref = refs[-8:]
+    block = wo_own_ref.shape[2]
+    depth = wo_own_ref.shape[1]
+    step = pl.program_id(0)
+    core = idx_ref[1]
+
+    @pl.when(step < blocks)
+    def _():
+        own = att_ref[:, pl.ds(pl.multiple_of(core * depth, depth), depth)]
+        other = att_ref[:, pl.ds(pl.multiple_of((1 - core) * depth, depth), depth)]
+        raw_ref[:, pl.ds(pl.multiple_of(step * block, block), block)] = plain_dot(
+            own, wo_own_ref[0]
+        ) + plain_dot(other, wo_oth_ref[0])
+
+    @pl.when(step == blocks - 1)
+    def _():
+        raw = raw_ref[...]
+        scale = lax.rsqrt(jnp.mean(raw * raw, axis=1, keepdims=True) + EPS)
+        scale_ref[...] = scale
+        hb_ref[...] = (x_ref[...].astype(F32) + raw * scale * gain_ref[...]).astype(BF16)
+        acc_ref[...] = jnp.zeros_like(acc_ref)
+
+    def tile_work(wd_ref):
+        hidden_b = hb_ref[...]
+        gate = plain_dot(hidden_b, wg_ref[...])
+        up = plain_dot(hidden_b, wu_ref[...])
+        mixed = (gate * jax.nn.sigmoid(gate) * up).astype(BF16)
+        gate_ref[...] = gate.astype(BF16)
+        up_ref[...] = up.astype(BF16)
+        mixed_ref[...] = mixed
+        for j in range(blocks):
+            acc_ref[:, j * block : (j + 1) * block] += plain_dot(mixed, wd_ref[j])
+
+    @pl.when((step >= blocks) & (step < blocks + tiles // 2))
+    def _():
+        tile_work(wd_own_ref)
+
+    @pl.when(step >= blocks + tiles // 2)
+    def _():
+        tile_work(wd_oth_ref)
+
+    @pl.when(step == blocks + tiles - 1)
+    def _():
+        part_ref[...] = acc_ref[...].astype(BF16)
+
+
+TILE = 256
+
+
+def forward_chunk(index, attended, out_halves, block_input, gain, w_gate, w_up, down_halves, chunk, before):
+    tokens, width = block_input.shape
+    hidden = w_gate.shape[1]
+    blocks, depth, block = out_halves[0].shape
+    tiles = hidden // TILE
+
+    def tile_of(j, idx):
+        return half_tile(jnp.maximum(j - blocks, 0), idx[1], tiles)
+
+    rows = pl.BlockSpec((chunk, width), lambda j, idx: (idx[0], 0))
+    out_half = pl.BlockSpec((1, depth, block), lambda j, idx: (jnp.minimum(j, blocks - 1), 0, 0))
+    up_tile = pl.BlockSpec((width, TILE), lambda j, idx: (0, tile_of(j, idx)))
+    down_own = pl.BlockSpec(
+        (blocks, TILE, block), lambda j, idx: (0, jnp.clip(j - blocks, 0, tiles // 2 - 1), 0)
+    )
+    down_oth = pl.BlockSpec(
+        (blocks, TILE, block), lambda j, idx: (0, jnp.maximum(j - blocks - tiles // 2, 0), 0)
+    )
+    act_tile = pl.BlockSpec((chunk, TILE), lambda j, idx: (idx[0], tile_of(j, idx)))
+    before = tuple(before)
+    return pl.pallas_call(
+        functools.partial(forward_chunk_kernel, blocks=blocks, tiles=tiles),
+        grid_spec=pltpu.PrefetchScalarGridSpec(
+            num_scalar_prefetch=1,
+            grid=(blocks + tiles,),
+            in_specs=[
+                pl.BlockSpec((chunk, attended.shape[1]), lambda j, idx: (idx[0], 0)),
+                out_half, out_half, rows, pl.BlockSpec((1, width), lambda j, idx: (0, 0)),
+                up_tile, up_tile, down_own, down_oth,
+            ] + [pl.BlockSpec(memory_space=pl.ANY)] * len(before),
+            out_specs=[
+                rows, pl.BlockSpec((chunk, 1), lambda j, idx: (idx[0], 0)), rows, act_tile, act_tile, act_tile,
+                pl.BlockSpec((chunk, width), lambda j, idx: (0, 0)),
+            ],
+            scratch_shapes=[pltpu.VMEM((chunk, width), F32)],
+        ),
+        out_shape=[
+            jax.ShapeDtypeStruct((tokens, width), F32),
+            jax.ShapeDtypeStruct((tokens, 1), F32),
+            jax.ShapeDtypeStruct((tokens, width), BF16),
+            jax.ShapeDtypeStruct((tokens, hidden), BF16),
+            jax.ShapeDtypeStruct((tokens, hidden), BF16),
+            jax.ShapeDtypeStruct((tokens, hidden), BF16),
+            jax.ShapeDtypeStruct((chunk, width), BF16),
+        ],
+        input_output_aliases={10 + i: i for i in range(len(before))},
+        compiler_params=pltpu.CompilerParams(vmem_limit_bytes=40 << 20),
+        cost_estimate=pl.CostEstimate(
+            flops=2 * chunk * width * (width + 3 * hidden),
+            bytes_accessed=2 * width * (width + 3 * hidden),
+            transcendentals=0,
+        ),
+        name="forward_chunk",
+    )(index, attended, *out_halves, block_input, gain, w_gate, w_up, *down_halves, *before)
+
+
+def backward_chunk_kernel(
+    idx_ref, down_ref, raw_ref, scale_ref, x_ref, grad_ref, attn_gain_ref, mlp_gain_ref,
+    gate_ref, up_ref, wg_ref, wu_ref, wd_own_ref, wd_oth_ref, *refs, blocks, tiles,
+):
+    out_ref, gdi_ref, gg_ref, gu_ref, part_ref, gain_grad_ref, acc_ref = refs[-7:]
+    block = wd_own_ref.shape[2]
+    step = pl.program_id(0)
+
+    @pl.when(step == 0)
+    def _():
+        down_raw = down_ref[...].astype(F32)
+        down_scale = lax.rsqrt(jnp.mean(down_raw * down_raw, axis=1, keepdims=True) + EPS)
+        unit = down_raw * down_scale
+        mlp_gain = mlp_gain_ref[...]
+        hidden = x_ref[...].astype(F32) + raw_ref[...] * scale_ref[...] * attn_gain_ref[...]
+        out_ref[...] = (hidden + unit * mlp_gain).astype(BF16)
+        grad_y = grad_ref[...].astype(F32)
+        gain_grad_ref[...] = jnp.sum(grad_y * unit, axis=0, keepdims=True)
+        grad_unit = grad_y * mlp_gain
+        mean = jnp.mean(grad_unit * unit, axis=1, keepdims=True)
+        gdi_ref[...] = (down_scale * (grad_unit - unit * mean)).astype(BF16)
+        acc_ref[...] = jnp.zeros_like(acc_ref)
+
+    def tile_work(wd_ref):
+        grad_mixed = times_transposed(gdi_ref[:, :block], wd_ref[0])
+        for j in range(1, blocks):
+            grad_mixed += times_transposed(gdi_ref[:, j * block : (j + 1) * block], wd_ref[j])
+        gate = gate_ref[...].astype(F32)
+        sig = jax.nn.sigmoid(gate)
+        grad_gate = (grad_mixed * up_ref[...].astype(F32) * sig * (1.0 + gate * (1.0 - sig))).astype(BF16)
+        grad_up = (grad_mixed * (gate * sig)).astype(BF16)
+        gg_ref[...] = grad_gate
+        gu_ref[...] = grad_up
+        acc_ref[...] += times_transposed(grad_gate, wg_ref[...]) + times_transposed(grad_up, wu_ref[...])
+
+    @pl.when(step < tiles // 2)
+    def _():
+        tile_work(wd_own_ref)
+
+    @pl.when(step >= tiles // 2)
+    def _():
+        tile_work(wd_oth_ref)
+
+    @pl.when(step == tiles - 1)
+    def _():
+        part_ref[...] = acc_ref[...].astype(BF16)
+
+
+def backward_chunk(
+    index, down_rows, raw, scale, block_input, grad_output, attn_gain, mlp_gain, gate, up, w_gate, w_up,
+    down_halves, chunk, before,
+):
+    tokens, width = block_input.shape
+    hidden = w_gate.shape[1]
+    blocks, _, block = down_halves[0].shape
+    tiles = hidden // TILE
+
+    def tile_of(j, idx):
+        return half_tile(j, idx[1], tiles)
+
+    rows = pl.BlockSpec((chunk, width), lambda j, idx: (idx[0], 0))
+    fixed = pl.BlockSpec((chunk, width), lambda j, idx: (0, 0))
+    gain_row = pl.BlockSpec((1, width), lambda j, idx: (0, 0))
+    up_tile = pl.BlockSpec((width, TILE), lambda j, idx: (0, tile_of(j, idx)))
+    act_tile = pl.BlockSpec((chunk, TILE), lambda j, idx: (idx[0], tile_of(j, idx)))
+    before = tuple(before)
+    return pl.pallas_call(
+        functools.partial(backward_chunk_kernel, blocks=blocks, tiles=tiles),
+        grid_spec=pltpu.PrefetchScalarGridSpec(
+            num_scalar_prefetch=1,
+            grid=(tiles,),
+            in_specs=[
+                fixed, rows, pl.BlockSpec((chunk, 1), lambda j, idx: (idx[0], 0)), rows, rows, gain_row, gain_row,
+                act_tile, act_tile, up_tile, up_tile,
+                pl.BlockSpec((blocks, TILE, block), lambda j, idx: (0, jnp.minimum(j, tiles // 2 - 1), 0)),
+                pl.BlockSpec((blocks, TILE, block), lambda j, idx: (0, jnp.maximum(j - tiles // 2, 0), 0)),
+            ] + [pl.BlockSpec(memory_space=pl.ANY)] * len(before),
+            out_specs=[rows, rows, act_tile, act_tile, fixed, gain_row],
+            scratch_shapes=[pltpu.VMEM((chunk, width), F32)],
+        ),
+        out_shape=[
+            jax.ShapeDtypeStruct((tokens, width), BF16),
+            jax.ShapeDtypeStruct((tokens, width), BF16),
+            jax.ShapeDtypeStruct((tokens, hidden), BF16),
+            jax.ShapeDtypeStruct((tokens, hidden), BF16),
+            jax.ShapeDtypeStruct((chunk, width), BF16),
+            jax.ShapeDtypeStruct((1, width), F32),
+        ],
+        input_output_aliases={14 + i: i for i in range(len(before))},
+        compiler_params=pltpu.CompilerParams(vmem_limit_bytes=40 << 20),
+        cost_estimate=pl.CostEstimate(
+            flops=6 * chunk * width * hidden, bytes_accessed=6 * width * hidden, transcendentals=0
+        ),
+        name="backward_chunk",
+    )(
+        index, down_rows, raw, scale, block_input, grad_output, attn_gain, mlp_gain, gate, up, w_gate, w_up,
+        *down_halves, *before,
+    )
+
+
+def attention_chunk_kernel(
+    idx_ref, mlp_ref, grad_ref, raw_ref, scale_ref, gain_ref, wo_own_ref, wo_oth_ref, *refs, blocks,
+):
+    gai_ref, gatt_ref, gain_grad_ref = refs[-3:]
+    half, block = wo_own_ref.shape[1:]
+    core = idx_ref[1]
+    scale = scale_ref[...]
+    unit = raw_ref[...] * scale
+    grad_hidden = grad_ref[...].astype(F32) + mlp_ref[...].astype(F32)
+    gain_grad_ref[...] = jnp.sum(grad_hidden * unit, axis=0, keepdims=True)
+    grad_unit = grad_hidden * gain_ref[...]
+    mean = jnp.mean(grad_unit * unit, axis=1, keepdims=True)
+    gai_ref[...] = (scale * (grad_unit - unit * mean)).astype(BF16)
+    for place, w_ref in ((core, wo_own_ref), (1 - core, wo_oth_ref)):
+        total = times_transposed(gai_ref[:, :block], w_ref[0])
+        for j in range(1, blocks):
+            total += times_transposed(gai_ref[:, j * block : (j + 1) * block], w_ref[j])
+        gatt_ref[:, pl.ds(pl.multiple_of(place * half, half), half)] = total.astype(BF16)
+
+
+def attention_chunk(index, mlp_rows, grad_output, raw, scale, gain, out_halves, half, chunk, before):
+    tokens, width = grad_output.shape
+    blocks, _, block = out_halves[0].shape
+    rows = pl.BlockSpec((chunk, width), lambda j, idx: (idx[0], 0))
+    fixed = pl.BlockSpec((chunk, width), lambda j, idx: (0, 0))
+    gain_row = pl.BlockSpec((1, width), lambda j, idx: (0, 0))
+    own_heads = pl.BlockSpec((blocks, half, block), lambda j, idx: (0, 0, 0))
+    before = tuple(before)
+    return pl.pallas_call(
+        functools.partial(attention_chunk_kernel, blocks=blocks),
+        grid_spec=pltpu.PrefetchScalarGridSpec(
+            num_scalar_prefetch=1,
+            grid=(1,),
+            in_specs=[
+                fixed, rows, rows, pl.BlockSpec((chunk, 1), lambda j, idx: (idx[0], 0)), gain_row,
+                own_heads, own_heads,
+            ] + [pl.BlockSpec(memory_space=pl.ANY)] * len(before),
+            out_specs=[rows, pl.BlockSpec((chunk, 2 * half), lambda j, idx: (idx[0], 0)), gain_row],
+        ),
+        out_shape=[
+            jax.ShapeDtypeStruct((tokens, width), BF16),
+            jax.ShapeDtypeStruct((tokens, 2 * half), BF16),
+            jax.ShapeDtypeStruct((1, width), F32),
+        ],
+        input_output_aliases={8 + i: i for i in range(len(before))},
+        compiler_params=pltpu.CompilerParams(vmem_limit_bytes=32 << 20),
+        cost_estimate=pl.CostEstimate(
+            flops=4 * chunk * width * half, bytes_accessed=16 * chunk * width, transcendentals=0
+        ),
+        name="attention_chunk",
+    )(index, mlp_rows, grad_output, raw, scale, gain, *out_halves, *before)
+
+
+def place_rows_kernel(idx_ref, rows_ref, *refs):
+    refs[-1][...] = rows_ref[...].astype(refs[-1].dtype)
+
+
+def place_rows(index, rows_in, tokens, dtype, before):
+    chunk, width = rows_in.shape
+    before = tuple(before)
+    return pl.pallas_call(
+        place_rows_kernel,
+        grid_spec=pltpu.PrefetchScalarGridSpec(
+            num_scalar_prefetch=1,
+            grid=(2,),
+            in_specs=[pl.BlockSpec((chunk // 2, width), lambda j, idx: (j, 0))]
+            + [pl.BlockSpec(memory_space=pl.ANY)] * len(before),
+            out_specs=pl.BlockSpec((chunk // 2, width), lambda j, idx: (2 * idx[0] + j, 0)),
+        ),
+        out_shape=jax.ShapeDtypeStruct((tokens, width), dtype),
+        input_output_aliases={2: 0} if before else {},
+        compiler_params=pltpu.CompilerParams(vmem_limit_bytes=16 << 20),
+        cost_estimate=pl.CostEstimate(flops=0, bytes_accessed=6 * chunk * width, transcendentals=0),
+        name="place_rows",
+    )(index, rows_in, *before)
+
+
+def after(value, *tokens):
+    return lax.optimization_barrier((value, tokens))[0]
+
+
+def unset_kernel(out_ref):
+    pass
+
+
+def unset(shape, dtype):
+    return pl.pallas_call(
+        unset_kernel,
+        out_specs=pl.BlockSpec(memory_space=pl.ANY),
+        out_shape=jax.ShapeDtypeStruct(shape, dtype),
+        name="unset",
+    )()
 
 
 def shards(
@@ -214,11 +529,16 @@
 ):
     cores, rows, cols = sizes
     tokens_here, width = block_input.shape
-    assert tokens_here == LEN and cores == 2
+    assert tokens_here == LEN and cores == 2 and cols == 4
     local_width = w_query.shape[1]
+    half_width = local_width // 2
     heads = local_width // HD
+    chunk = tokens_here // cols
     core = lax.axis_index("dp")
+    row = lax.axis_index("row")
+    col = lax.axis_index("col")
     swap = [(0, 1), (1, 0)]
+    attn_row, mlp_row = attn_gain[None, :], mlp_gain[None, :]
 
     def own_half(array, axis):
         half = array.shape[axis] // 2
@@ -231,10 +551,57 @@
     def gather(weight, axis):
         return lax.all_gather(own_half(weight, axis), ("row", "dp"), axis=axis, tiled=True)
 
-    def sum_over_col(partial):
-        piece = lax.psum_scatter(partial.astype(BF16), "col", scatter_dimension=0, tiled=True)
-        whole = lax.all_gather(piece, ("dp", "col"), axis=0, tiled=True)
-        return lax.dynamic_slice_in_dim(whole, core * tokens_here, tokens_here, 0).astype(F32)
+    def line_step(from_left, from_right, step):
+        from_left = lax.ppermute(from_left, "col", [(i, i + 1) for i in range(step - 1, cols - 1)])
+        from_right = lax.ppermute(from_right, "col", [(i + 1, i) for i in range(cols - step)])
+        return from_left, from_right
+
+    def sum_step(up, down, step):
+        up = lax.ppermute(up, "col", [(i, i + 1) for i in range(step)])
+        down = lax.ppermute(down, "col", [(cols - 1 - i, cols - 2 - i) for i in range(step)])
+        return up, down
+
+    def pick(at_zero, at_one, at_two, at_three):
+        low = jnp.where(col == 0, at_zero, at_one)
+        high = jnp.where(col == 2, at_two, at_three)
+        return jnp.where(col < 2, low, high)
+
+    slot_chunk = [pick(3, 3, 0, 0), pick(2, 2, 1, 1), pick(1, 0, 3, 2), col]
+    slot_index = [jnp.stack([one, core]).astype(jnp.int32) for one in slot_chunk]
+
+    def slot_rows(array, slot):
+        return lax.dynamic_slice_in_dim(array, slot_chunk[slot] * chunk, chunk, 0)
+
+    def gather_slots(own, work):
+        left1, right1 = line_step(own, own, 1)
+        left1, right1 = after((left1, right1), work(3, own))
+        left2, right2 = line_step(left1, right1, 2)
+        left2, right2 = after((left2, right2), work(2, jnp.where(col % 2 == 0, right1, left1)))
+        left3, right3 = line_step(left2, right2, 3)
+        left3, right3 = after((left3, right3), work(1, pick(right2, right1, left1, left2)))
+        return work(0, pick(right3, right2, left2, left3))
+
+    def sum_slots(make, window=lambda step, gate: ()):
+        def at(step, gate):
+            return make(step, gate), window(step, gate)
+
+        first = make(0, ())
+        up, down = sum_step(first, first, 1)
+        second, extra = at(1, first)
+        up, down = after((up, down), second, extra)
+        up = jnp.where(col == 0, second, first) + up
+        down = jnp.where(col == 3, second, first) + down
+        gate = (up, down)
+        up, down = sum_step(up, down, 2)
+        third, extra = at(2, gate)
+        up, down = after((up, down), third, extra)
+        up = jnp.where(col == 1, second, third) + up
+        down = jnp.where(col == 2, second, third) + down
+        gate = (up, down)
+        up, down = sum_step(up, down, 3)
+        fourth, extra = at(3, gate)
+        up, down = after((up, down), fourth, extra)
+        return fourth.astype(F32) + up.astype(F32) + down.astype(F32)
 
     def both_cores(half, axis):
         other = lax.ppermute(half, "dp", swap)
@@ -242,19 +609,63 @@
         second = jnp.where(core == 0, other, half)
         return jnp.concatenate([first, second], axis=axis).astype(F32)
 
-    def summed(left_mat, right_own, right_other):
-        sent = left_transposed(left_mat, right_other).astype(BF16)
-        got = lax.ppermute(sent, "dp", swap)
+    def sum_sent(left_mat, right_other):
+        return lax.ppermute(left_transposed(left_mat, right_other).astype(BF16), "dp", swap)
+
+    def sum_kept(left_mat, right_own, got):
         total = (left_transposed(left_mat, right_own) + got.astype(F32)).astype(BF16)
-        return lax.psum_scatter(total, "row", scatter_dimension=0, tiled=True)
+        return total, lax.psum_scatter(total, "row", scatter_dimension=0, tiled=True)
+
+    by_x = [(0, 1), (1, 0), (2, 3), (3, 2)]
+    by_y = [(0, 2), (2, 0), (1, 3), (3, 1)]
+
+    def row_first(half):
+        if rows != 4:
+            return (half,)
+        return half, lax.ppermute(half, "row", by_x), lax.ppermute(half, "row", by_y)
+
+    def row_second(pieces):
+        if rows != 4:
+            return pieces
+        middle = pieces[0].shape[0] // 2
+        return (
+            *pieces,
+            lax.ppermute(pieces[1][:middle], "row", by_y),
+            lax.ppermute(pieces[2][middle:], "row", by_x),
+        )
+
+    def row_blocks(pieces):
+        if rows != 4:
+            whole = lax.all_gather(pieces[0], ("row", "dp"), axis=0, tiled=False)
+            whole = whole.reshape(rows, cores, *pieces[0].shape)
+            return tuple(lax.dynamic_index_in_dim(whole, one, 1, keepdims=False) for one in (core, 1 - core))
+        own, by_one, by_two, corner_top, corner_low = pieces
+        middle = own.shape[0] // 2
+        held = unset((rows, *own.shape), own.dtype)
+        for piece, block, start in (
+            (own, row, 0), (by_one, row ^ 1, 0), (by_two, row ^ 2, 0),
+            (corner_top, row ^ 3, 0), (corner_low, row ^ 3, middle),
+        ):
+            held = lax.dynamic_update_slice(held, piece[None], (block, start, 0))
+        return held, lax.ppermute(held, "dp", swap)
 
     full_qkv = gather(jnp.concatenate([w_query, w_key, w_value], axis=1), 0)
-    full_out = gather(w_out, 1)
     full_gate = gather(w_gate, 0)
     full_up = gather(w_up, 0)
-    full_down = gather(w_down, 1)
-
-    qkv = plain_dot(block_input, full_qkv)
+    down_pieces = row_first(own_half(w_down, 0))
+    out_half = own_half(w_out, 0)
+    out_stack = jnp.concatenate(
+        [out_half]
+        + [
+            lax.ppermute(out_half, "col", [(i, (i - step) % cols) for i in range(cols)])
+            for step in range(1, cols)
+        ],
+        axis=0,
+    )
+
+    qkv = plain_dot(after(block_input, down_pieces, out_stack), full_qkv)
+    out_pieces = row_first(out_stack)
+    down_pieces = row_second(down_pieces)
     query_raw, key_raw = qkv[:, :local_width], qkv[:, local_width : 2 * local_width]
     query_sq, key_sq = lax.psum(
         (jnp.sum(query_raw * query_raw, axis=1), jnp.sum(key_raw * key_raw, axis=1)), "col"
@@ -266,44 +677,85 @@
     tables = rope_tables(positions)
     seg_col, seg_row = segment_ids[:, None], segment_ids[None, :]
     query_rot, key_rot, value_heads, attended, log_total = attend_forward(
-        qkv, scales, gains, tables, seg_col, seg_row, heads
-    )
-    attn_raw = sum_over_col(plain_dot(attended, full_out))
-    attn_scale = lax.rsqrt(jnp.mean(attn_raw * attn_raw, axis=1, keepdims=True) + EPS)
-    attn_unit = attn_raw * attn_scale
-    hidden = block_input.astype(F32) + attn_unit * attn_gain
-    hidden_b = hidden.astype(BF16)
-    gate_proj = plain_dot(hidden_b, full_gate)
-    up_proj = plain_dot(hidden_b, full_up)
-    gate_sig = jax.nn.sigmoid(gate_proj)
-    gate_act = gate_proj * gate_sig
-    mixed_act = (gate_act * up_proj).astype(BF16)
-    down_raw = sum_over_col(plain_dot(mixed_act, full_down))
-    down_scale = lax.rsqrt(jnp.mean(down_raw * down_raw, axis=1, keepdims=True) + EPS)
-    down_unit = down_raw * down_scale
-    block_output = (hidden + down_unit * mlp_gain).astype(BF16)
-
-    grad_y = grad_output.astype(F32)
-    grad_mlp_gain = jnp.sum(grad_y * down_unit, axis=0)
-    down_dz = grad_y * mlp_gain
-    grad_down_in = (
-        down_scale * (down_dz - down_unit * jnp.mean(down_dz * down_unit, axis=1, keepdims=True))
-    ).astype(BF16)
-    grad_mixed = times_transposed(grad_down_in, full_down)
-    grad_gate_in = (grad_mixed * up_proj * gate_sig * (1.0 + gate_proj * (1.0 - gate_sig))).astype(BF16)
-    grad_up_in = (grad_mixed * gate_act).astype(BF16)
-    mlp_part = times_transposed(grad_gate_in, full_gate) + times_transposed(grad_up_in, full_up)
-    grad_hidden = grad_y + sum_over_col(mlp_part)
-    down_block = summed(grad_down_in, own_half(mixed_act, 1), other_half(mixed_act, 1))
-    gate_block = summed(hidden_b, own_half(grad_gate_in, 1), other_half(grad_gate_in, 1))
-    up_block = summed(hidden_b, own_half(grad_up_in, 1), other_half(grad_up_in, 1))
-
-    grad_attn_gain = jnp.sum(grad_hidden * attn_unit, axis=0)
-    attn_dz = grad_hidden * attn_gain
-    grad_attn_in = (
-        attn_scale * (attn_dz - attn_unit * jnp.mean(attn_dz * attn_unit, axis=1, keepdims=True))
-    ).astype(BF16)
-    grad_att = times_transposed(grad_attn_in, full_out).astype(BF16)
+        after(qkv, out_pieces, down_pieces), scales, gains, tables, seg_col, seg_row, heads
+    )
+
+    left1, right1 = line_step(attended, attended, 1)
+    out_pieces = row_second(out_pieces)
+    down_halves = row_blocks(down_pieces)
+    left1, right1 = after((left1, right1), out_pieces, down_halves[0])
+    left2, right2 = line_step(left1, right1, 2)
+    out_halves = row_blocks(out_pieces)
+    left2, right2 = after((left2, right2), out_halves[0], down_halves[1])
+    left3, right3 = line_step(left2, right2, 3)
+    pieces = [attended, right1 + left3, right2 + left2, right3 + left1]
+    attended_all = jnp.concatenate(
+        [one[:, half * half_width : (half + 1) * half_width] for half in range(cores) for one in pieces],
+        axis=1,
+    )
+
+    held = dict(forward=(), backward=(), attention=(), output=())
+    gain_sums = dict(mlp=0.0, attn=0.0)
+
+    def forward_work(slot, gate):
+        results = forward_chunk(
+            slot_index[slot], after(attended_all, gate), out_halves, block_input, attn_row, full_gate, full_up,
+            down_halves, chunk, held["forward"],
+        )
+        held["forward"] = results[:6]
+        return results[6]
+
+    down_own = sum_slots(forward_work).astype(BF16)
+    attn_raw, attn_scale, hidden_b, gate_proj, up_proj, mixed_act = held["forward"]
+    mlp_parts = [None] * cols
+
+    def backward_work(slot, down_rows):
+        results = backward_chunk(
+            slot_index[slot], down_rows, attn_raw, attn_scale, block_input, grad_output, attn_row, mlp_row,
+            gate_proj, up_proj, full_gate, full_up, down_halves, chunk, held["backward"],
+        )
+        held["backward"] = results[:4]
+        mlp_parts[slot] = results[4]
+        gain_sums["mlp"] = gain_sums["mlp"] + results[5]
+        return results[4]
+
+    gather_slots(down_own, backward_work)
+    block_output, grad_down_in, grad_gate_in, grad_up_in = held["backward"]
+
+    blocks = {}
+    got = {}
+
+    def mlp_window(step, gate):
+        down_left, down_right, hidden_left, gate_right, up_right = after(
+            (grad_down_in, mixed_act, hidden_b, grad_gate_in, grad_up_in), gate
+        )
+        if step == 1:
+            got["down"] = sum_sent(down_left, other_half(down_right, 1))
+            got["gate"] = sum_sent(hidden_left, other_half(gate_right, 1))
+            return got["down"], got["gate"]
+        if step == 2:
+            blocks["down"] = sum_kept(down_left, own_half(down_right, 1), got["down"])
+            got["up"] = sum_sent(hidden_left, other_half(up_right, 1))
+            return blocks["down"][0], got["up"]
+        blocks["gate"] = sum_kept(hidden_left, own_half(gate_right, 1), got["gate"])
+        blocks["up"] = sum_kept(hidden_left, own_half(up_right, 1), got["up"])
+        return blocks["gate"][0], blocks["up"][0]
+
+    mlp_own = sum_slots(lambda slot, gate: mlp_parts[slot], mlp_window).astype(BF16)
+
+    def attention_work(slot, mlp_rows):
+        results = attention_chunk(
+            slot_index[slot], mlp_rows, grad_output, attn_raw, attn_scale, attn_row, out_halves, half_width,
+            chunk, held["attention"],
+        )
+        held["attention"] = results[:2]
+        gain_sums["attn"] = gain_sums["attn"] + results[2]
+        return results[1]
+
+    gather_slots(mlp_own, attention_work)
+    grad_attn_in, grad_att = held["attention"]
+    own_grad_hidden = slot_rows(grad_output, 3).astype(F32) + mlp_own.astype(F32)
+
     query_dz, key_dz, grad_value_in, query_dot, key_dot, grad_query_gain, grad_key_gain = attend_backward(
         qkv, scales, gains, tables, seg_col, seg_row,
         (query_rot, key_rot, value_heads, attended, log_total), grad_att, heads,
@@ -316,40 +768,73 @@
         key_scale * (key_dz - key_raw * key_scale * (key_dot / width)[:, None])
     ).astype(BF16)
     grad_qkv = jnp.concatenate([grad_query_in, grad_key_in, grad_value_in], axis=1)
-    grad_input = grad_hidden + sum_over_col(times_transposed(grad_qkv, full_qkv))
-
-    def interleaved(picker):
-        return jnp.concatenate(
-            [picker(one, 1) for one in (grad_query_in, grad_key_in, grad_value_in)], axis=1
+    gain_pack = jnp.concatenate([grad_query_gain, grad_key_gain, gain_sums["attn"], gain_sums["mlp"]], axis=1)
+
+    def interleaved(picker, pieces_in):
+        return jnp.concatenate([picker(one, 1) for one in pieces_in], axis=1)
+
+    def input_window(step, gate):
+        nonlocal gain_pack
+        pack, *pieces_in, tokens_in, left_out, right_out = after(
+            (gain_pack, grad_query_in, grad_key_in, grad_value_in, block_input, grad_attn_in, attended), gate
         )
-
-    qkv_block = summed(block_input, interleaved(own_half), interleaved(other_half))
-    out_block = summed(grad_attn_in, own_half(attended, 1), other_half(attended, 1))
-    qkv_pair = both_cores(qkv_block[None], 0)
+        if step == 1:
+            got["qkv"] = sum_sent(tokens_in, interleaved(other_half, pieces_in))
+            got["out"] = sum_sent(left_out, other_half(right_out, 1))
+            gain_pack = pack + lax.ppermute(pack, "dp", swap)
+            return got["qkv"], got["out"], gain_pack
+        if step == 2:
+            blocks["qkv"] = sum_kept(tokens_in, interleaved(own_half, pieces_in), got["qkv"])
+            if rows == 4:
+                gain_pack = pack + lax.ppermute(pack, "row", by_x)
+            return blocks["qkv"][0], gain_pack
+        blocks["out"] = sum_kept(left_out, own_half(right_out, 1), got["out"])
+        gain_pack = pack + lax.ppermute(pack, "row", by_y) if rows == 4 else lax.psum(pack, "row")
+        return blocks["out"][0], gain_pack
+
+    input_own = sum_slots(
+        lambda slot, gate: times_transposed(after(slot_rows(grad_qkv, slot), gate), full_qkv).astype(BF16), input_window
+    )
+
+    results = {}
     quarter = local_width // 2
 
     def projection(index):
-        part = qkv_pair[:, :, index * quarter : (index + 1) * quarter]
-        return jnp.concatenate([part[0], part[1]], axis=1)
-
-    gain_grads = lax.psum(
-        (grad_query_gain[0], grad_key_gain[0], grad_attn_gain, grad_mlp_gain), ("dp", "row")
-    )
+        pair = both_cores(blocks["qkv"][1][None, :, index * quarter : (index + 1) * quarter], 0)
+        return jnp.concatenate([pair[0], pair[1]], axis=1)
+
+    def output_work(slot, rows_in):
+        held["output"] = (place_rows(slot_index[slot], rows_in, tokens_here, F32, held["output"]),)
+        if slot == 3:
+            results["down"] = jnp.transpose(both_cores(blocks["down"][1], 1))
+            results["gate"] = both_cores(blocks["gate"][1], 1)
+            return held["output"], results["down"], results["gate"]
+        if slot == 2:
+            results["up"] = both_cores(blocks["up"][1], 1)
+            return held["output"], results["up"]
+        if slot == 1:
+            results["out"] = jnp.transpose(both_cores(blocks["out"][1], 1))
+            results["qkv"] = [projection(index) for index in range(3)]
+            return held["output"], results["out"], results["qkv"]
+        return held["output"]
+
+    gather_slots((own_grad_hidden + input_own).astype(BF16), output_work)
+    ends = (local_width, 2 * local_width, 2 * local_width + width)
+    gain_grads = jnp.split(gain_pack[0], ends)
     return (
         block_output,
-        grad_input,
-        projection(0),
-        projection(1),
-        projection(2),
-        jnp.transpose(both_cores(out_block, 1)),
-        both_cores(gate_block, 1),
-        both_cores(up_block, 1),
-        jnp.transpose(both_cores(down_block, 1)),
-        gain_grads[0],
-        gain_grads[1],
-        gain_grads[2],
-        gain_grads[3],
-    )
+        held["output"][0],
+        *results["qkv"],
+        results["out"],
+        results["gate"],
+        results["up"],
+        results["down"],
+        *gain_grads,
+    )
+
+
+def layer(sizes, *arrays):
+    return shards(sizes, *arrays)
 
 
 def solution(mesh):
@@ -387,5 +872,5 @@
     )
     sizes = (mesh.shape["dp"], mesh.shape["row"], mesh.shape["col"])
     return jax.shard_map(
-        functools.partial(shards, sizes), mesh=mesh, in_specs=in_specs, out_specs=out_specs, check_vma=False
-    )
+        functools.partial(layer, sizes), mesh=mesh, in_specs=in_specs, out_specs=out_specs, check_vma=False
+    )

time: 1340 us -> 972 us (0.73)
  waiting for transfers between devices: 939 us -> 319 us
  Pallas kernels: 33.6 us -> 242 us
  starting transfers between devices: 3.05 us -> 121 us
  matrix products: 181 us -> 78 us
  local copies, waits for them, and re-layouts: 31.2 us -> 103 us
  blocking collectives: 48.4 us -> 20.8 us
  other arithmetic: 75.2 us -> 60.5 us
    reduce_scatter x9 -> x5, waiting for transfers between devices: 444 us -> 0.05 us  [sum_kept(): lax.psum_scatter(total, 'row', scatter_dimension=0, tiled=True)]
    all_gather x4 -> x0, waiting for transfers between devices: 293 us -> none  [sum_over_col(): whole = lax.all_gather(piece, ('dp', 'col'), axis=0, tiled=True)]
    ppermute x5 -> x63, waiting for transfers between devices: 29.2 us -> 316 us  [the longest x12 128 us: line_step(): lax.ppermute(from_right, 'col', [(i + 1, i) for i in range(cols - step)])]
    pallas_call x0 -> x18, Pallas kernels: none -> 212 us  [the longest x4 93.3 us: forward_chunk(): pl.pallas_call(functools.partial(forward_chunk_kernel, blocks=blocks, til...]
    all_gather x5 -> x3, waiting for transfers between devices: 172 us -> 0.01 us  [gather(): lax.all_gather(own_half(weight, axis), ('row', 'dp'), axis=axis, tiled=True)]
    ppermute x5 -> x63, starting transfers between devices: 0.92 us -> 119 us  [the longest x9 45.5 us: sum_step(): up = lax.ppermute(up, 'col', [(i, i + 1) for i in range(step)])]
    unnamed x99 -> x221, local copies, waits for them, and re-layouts: 21.5 us -> 74.9 us
    dot_general x5 -> x1, matrix products: 63.1 us -> 10 us  [plain_dot(): return jnp.dot(left_mat, right_mat, preferred_element_type=F32)]
  transfers between devices with their start and end apart: 28 -> 78, of which waited for: 21 -> 27; matrix products, arithmetic and copies ran while one was open for 11% -> 16% of each run, Pallas kernels for 1% -> 20%
where the time goes in v4:
time: 972 us; the launch traced here: 960 us
  waiting for transfers between devices  319 us (33%)
  Pallas kernels  242 us (25%)
  starting transfers between devices  121 us (12%)
  local copies, waits for them, and re-layouts  103 us (11%)
  matrix products  78 us (8%)
  other arithmetic  60.5 us (6%)
  blocking collectives  20.8 us (2%)
  between operations  16.2 us (2%)
    ppermute x12, waiting for transfers between devices, line_step(): lax.ppermute(from_right, 'col', [(i + 1, i) for i in range(cols - step)])  128 us
    pallas_call x4, Pallas kernels, forward_chunk(): pl.pallas_call(functools.partial(forward_chunk_kernel, blocks=blocks, til...  93.3 us
    pallas_call x4, Pallas kernels, backward_chunk(): pl.pallas_call(functools.partial(backward_chunk_kernel, blocks=blocks, ti...  91.9 us
    ppermute x9, waiting for transfers between devices, sum_step(): up = lax.ppermute(up, 'col', [(i, i + 1) for i in range(step)])  86.7 us
    unnamed x221, local copies, waits for them, and re-layouts  74.9 us
    dot_general x10, matrix products, left_transposed(): lax.dot_general(left_mat, right_mat, (((0,), (0,)), ((), ())), preferred_...  55 us
    ppermute x9, starting transfers between devices, sum_step(): up = lax.ppermute(up, 'col', [(i, i + 1) for i in range(step)])  45.5 us
    ppermute x2, waiting for transfers between devices, row_first(): lax.ppermute(half, 'row', by_x)  27.9 us
  transfers between devices with their start and end apart: 78, of which 27 were waited for; matrix products, arithmetic and copies ran while one was open for 16% of the time, Pallas kernels for 20%

profile of v4, /device:TPU:0, one launch (start us, length us, event | category | flops | bytes accessed | tf_op | source)
XLA Modules:
  0.0 960.3 jit_solution(12461782642009833444)
XLA Ops:
  30.6 15.0 %collective-permute-done.3 = bf16[256,512]{1,0:T(8,128)(2,1)S(1)} collective-permute-done((bf16[256,512]{1,0:T(8,128)(2,1)S(1)}, bf16[256,512]{1,0:T(8,128)(2,1)S(1)}, u32[]{:S(2)}, u32[]{:S(2)}) %collective-permute-start.3) | collective-permute-done | bytes 262176 | tf_op jit(solution)/shard_map/ppermute | solution.py:660
  63.6 26.0 %collective-permute-done.5 = bf16[1024,512]{1,0:T(8,128)(2,1)S(1)} collective-permute-done((bf16[1024,512]{1,0:T(8,128)(2,1)S(1)}, bf16[1024,512]{1,0:T(8,128)(2,1)S(1)}, u32[]{:S(2)}, u32[]{:S(2)}) %collective-permute-start.5) | collective-permute-done | bytes 1048608 | tf_op jit(solution)/shard_map/ppermute | solution.py:625
  95.9 12.5 %collective-permute-done.7 = bf16[512,512]{1,0:T(8,128)(2,1)S(1)} collective-permute-done((bf16[512,512]{1,0:T(8,128)(2,1)S(1)}, bf16[512,512]{1,0:T(8,128)(2,1)S(1)}, u32[]{:S(2)}, u32[]{:S(2)}) %collective-permute-start.7) | collective-permute-done | bytes 524320 | tf_op jit(solution)/shard_map/ppermute | solution.py:633
  110.1 10.0 %fusion.43.q_ref.k_ref.v_ref = f32[1024,1536]{1,0:T(8,128)S(1)} fusion(bf16[1024,2048]{1,0:T(8,128)(2,1)} %x_ref.15, bf16[2048,1536]{1,0:T(8,128)(2,1)} %all-gather.4.cloned.1.call-done), kind=kOutput, calls=%fused_computation.165 | convolution fusion | flops 6442450944 | bytes 16777216 | tf_op jit(solution)/shard_map/dot_general | solution.py:24
  123.2 12.1 %all-reduce.1 = (f32[1024]{0:T(1024)S(1)}, f32[1024]{0:T(1024)S(1)}) all-reduce(f32[1024]{0:T(1024)S(1)} %get-tuple-element.340, f32[1024]{0:T(1024)S(1)} %get-tuple-element.339), channel_id=1, replica_groups=mesh['dp'=2,'row'=4,'col'=4] {'col'}, use_global_device_ids=true, to_apply=%region_1.2 | all-reduce | flops 2048 | bytes 16384 | tf_op jit(solution)/shard_map/psum | solution.py:670
  143.4 14.3 %attend_forward.1 = (bf16[1024,512]{1,0:T(8,128)(2,1)S(1)}, bf16[1024,512]{1,0:T(8,128)(2,1)S(1)}, bf16[1024,512]{1,0:T(8,128)(2,1)S(1)}, bf16[1024,512]{1,0:T(8,128)(2,1)S(1)}, f32[4,1024,1]{2,1,0:T(8,128)S(1)}) custom-call(f32[1024,1536]{1,0:T(8,128)S(1)} %copy-done.6, f32[1024,1536]{1,0:T(8,128)S(1)} %copy-done.6, f32[1024,1536]{1,0:T(8,128)S(1)} %copy-done.6, ...), custom_call_target="tpu_custom_call" | custom-call | flops 2147483648 | bytes 10485760 | tf_op jit(solution)/shard_map/attend_forward/pallas_call | solution.py:155
  170.2 14.3 %collective-permute-done.10 = bf16[1024,512]{1,0:T(8,128)(2,1)S(1)} collective-permute-done((bf16[1024,512]{1,0:T(8,128)(2,1)S(1)}, bf16[1024,512]{1,0:T(8,128)(2,1)S(1)}, u32[]{:S(2)}, u32[]{:S(2)}) %collective-permute-start.10) | collective-permute-done | bytes 1048608 | tf_op jit(solution)/shard_map/ppermute | solution.py:556
  188.7 25.4 %collective-permute-done.14 = bf16[1024,512]{1,0:T(8,128)(2,1)} collective-permute-done((bf16[1024,512]{1,0:T(8,128)(2,1)S(1)}, bf16[1024,512]{1,0:T(8,128)(2,1)}, u32[]{:S(2)}, u32[]{:S(2)}) %collective-permute-start.14) | collective-permute-done | bytes 1048608 | tf_op jit(solution)/shard_map/ppermute | solution.py:556
  219.8 18.4 %collective-permute-done.17 = bf16[1024,512]{1,0:T(8,128)(2,1)} collective-permute-done((bf16[1024,512]{1,0:T(8,128)(2,1)}, bf16[1024,512]{1,0:T(8,128)(2,1)}, u32[]{:S(2)}, u32[]{:S(2)}) %collective-permute-start.17) | collective-permute-done | bytes 1048608 | tf_op jit(solution)/shard_map/ppermute | solution.py:556
  247.1 23.6 %forward_chunk.4 = (f32[1024,2048]{1,0:T(8,128)}, f32[1024,1]{1,0:T(8,128)S(1)}, bf16[1024,2048]{1,0:T(8,128)(2,1)S(1)}, bf16[1024,2048]{1,0:T(8,128)(2,1)S(1)},...) custom-call(s32[2]{0:T(128)S(1)} %get-tuple-element.399.idx_ref, ...), custom_call_target="tpu_custom_call" | custom-call | flops 8589934592 | bytes 33554432 | tf_op jit(solution)/shard_map/forward_chunk/pallas_call | solution.py:282
  287.3 23.2 %forward_chunk.5 = (f32[1024,2048]{1,0:T(8,128)}, f32[1024,1]{1,0:T(8,128)S(1)}, bf16[1024,2048]{1,0:T(8,128)(2,1)S(1)}, bf16[1024,2048]{1,0:T(8,128)(2,1)S(1)},...) custom-call(s32[2]{0:T(128)S(1)} %get-tuple-element.400.idx_ref, ...), custom_call_target="tpu_custom_call", output_to_operand_aliasing={{0}: (10, {}), {1}: (11, {}), {2}: (12, {}), {3}: (13, {}),... | custom-call | flops 8589934592 | bytes 33554432 | tf_op jit(solution)/shard_map/forward_chunk/pallas_call | solution.py:282
  330.7 23.2 %forward_chunk.6 = (f32[1024,2048]{1,0:T(8,128)}, f32[1024,1]{1,0:T(8,128)S(1)}, bf16[1024,2048]{1,0:T(8,128)(2,1)S(1)}, bf16[1024,2048]{1,0:T(8,128)(2,1)S(1)},...) custom-call(s32[2]{0:T(128)S(1)} %pad_add_fusion.3.idx_ref, ...), custom_call_target="tpu_custom_call", output_to_operand_aliasing={{0}: (10, {}), {1}: (11, {}), {2}: (12, {}), {3}: (13, {}),... | custom-call | flops 8589934592 | bytes 33554432 | tf_op jit(solution)/shard_map/forward_chunk/pallas_call | solution.py:282
  358.5 23.2 %forward_chunk.7 = (f32[1024,2048]{1,0:T(8,128)}, f32[1024,1]{1,0:T(8,128)S(1)}, bf16[1024,2048]{1,0:T(8,128)(2,1)S(1)}, bf16[1024,2048]{1,0:T(8,128)(2,1)S(1)},...) custom-call(s32[2]{0:T(128)S(1)} %pad_add_fusion.1.idx_ref, ...), custom_call_target="tpu_custom_call", output_to_operand_aliasing={{0}: (10, {}), {1}: (11, {}), {2}: (12, {}), {3}: (13, {}),... | custom-call | flops 8589934592 | bytes 33554432 | tf_op jit(solution)/shard_map/forward_chunk/pallas_call | solution.py:282
  395.3 22.9 %backward_chunk.4 = (bf16[1024,2048]{1,0:T(8,128)(2,1)}, bf16[1024,2048]{1,0:T(8,128)(2,1)S(1)}, bf16[1024,2048]{1,0:T(8,128)(2,1)S(1)}, bf16[1024,2048]{1,0:T(8...) custom-call(s32[2]{0:T(128)S(1)} %pad_add_fusion.1.idx_ref, ...), custom_call_target="tpu_custom_call" | custom-call | flops 6442450944 | bytes 25165824 | tf_op jit(solution)/shard_map/backward_chunk/pallas_call | solution.py:384
  421.6 22.9 %backward_chunk.5 = (bf16[1024,2048]{1,0:T(8,128)(2,1)}, bf16[1024,2048]{1,0:T(8,128)(2,1)S(1)}, bf16[1024,2048]{1,0:T(8,128)(2,1)S(1)}, bf16[1024,2048]{1,0:T(8...) custom-call(s32[2]{0:T(128)S(1)} %pad_add_fusion.3.idx_ref, ...), custom_call_target="tpu_custom_call", output_to_operand_aliasing={{0}: (14, {}), {1}: (15, {}), {2}: (16, {}), {3}: (17, {})} | custom-call | flops 6442450944 | bytes 25165824 | tf_op jit(solution)/shard_map/backward_chunk/pallas_call | solution.py:384
  448.1 22.9 %backward_chunk.6 = (bf16[1024,2048]{1,0:T(8,128)(2,1)}, bf16[1024,2048]{1,0:T(8,128)(2,1)S(1)}, bf16[1024,2048]{1,0:T(8,128)(2,1)S(1)}, bf16[1024,2048]{1,0:T(8...) custom-call(s32[2]{0:T(128)S(1)} %get-tuple-element.400.idx_ref, ...), custom_call_target="tpu_custom_call", output_to_operand_aliasing={{0}: (14, {}), {1}: (15, {}), {2}: (16, {}), {3}: (17, {})} | custom-call | flops 6442450944 | bytes 25165824 | tf_op jit(solution)/shard_map/backward_chunk/pallas_call | solution.py:384
  471.3 23.2 %backward_chunk.7 = (bf16[1024,2048]{1,0:T(8,128)(2,1)}, bf16[1024,2048]{1,0:T(8,128)(2,1)S(1)}, bf16[1024,2048]{1,0:T(8,128)(2,1)S(1)}, bf16[1024,2048]{1,0:T(8...) custom-call(s32[2]{0:T(128)S(1)} %get-tuple-element.399.idx_ref, ...), custom_call_target="tpu_custom_call", output_to_operand_aliasing={{0}: (14, {}), {1}: (15, {}), {2}: (16, {}), {3}: (17, {})} | custom-call | flops 6442450944 | bytes 25165824 | tf_op jit(solution)/shard_map/backward_chunk/pallas_call | solution.py:384
  514.7 21.8 %collective-permute-done.31 = bf16[256,2048]{1,0:T(8,128)(2,1)S(1)} collective-permute-done((bf16[256,2048]{1,0:T(8,128)(2,1)S(1)}, bf16[256,2048]{1,0:T(8,128)(2,1)S(1)}, u32[]{:S(2)}, u32[]{:S(2)}) %collective-permute-start.31) | collective-permute-done | bytes 1048608 | tf_op jit(solution)/shard_map/ppermute | solution.py:560
  559.0 22.0 %collective-permute-done.35 = bf16[256,2048]{1,0:T(8,128)(2,1)S(1)} collective-permute-done((bf16[256,2048]{1,0:T(8,128)(2,1)S(1)}, bf16[256,2048]{1,0:T(8,128)(2,1)S(1)}, u32[]{:S(2)}, u32[]{:S(2)}) %collective-permute-start.35) | collective-permute-done | bytes 1048608 | tf_op jit(solution)/shard_map/ppermute | solution.py:560
  589.1 10.4 %collective-permute-start.38 = (bf16[256,2048]{1,0:T(8,128)(2,1)}, bf16[256,2048]{1,0:T(8,128)(2,1)}, u32[]{:S(2)}, u32[]{:S(2)}) collective-permute-start(bf16[256,2048]{1,0:T(8,128)(2,1)} %get-tuple-element.364), channel_id=1, source_target_pairs={{0,1},{1,2},{2,3},{4,5},{5,6},{6,7},{8,9},{9,10},{10,11},{12,13},{... | collective-permute-start | bytes 3145736 | tf_op jit(solution)/shard_map/ppermute | solution.py:560
  601.0 10.7 %add_convert_fusion.1 = bf16[2048,1024]{1,0:T(8,128)(2,1)} fusion(bf16[2048,1024]{1,0:T(8,128)(2,1)} %copy-done.99, bf16[1024,2048]{1,0:T(8,128)(2,1)} %copy-done.29, bf16[1024,2048]{1,0:T(8,128)(2,1)} %copy-done.17, s32[]{:T(128)S(6)} %select_n.307), kind=kOutput, calls=%fused_computation.1 | convolution fusion | flops 4301258752 | bytes 14680068 | tf_op jit(solution)/shard_map/dot_general | solution.py:34
  611.7 8.9 collective-permute-done.38
  637.9 12.2 %collective-permute-done.40 = bf16[256,2048]{1,0:T(8,128)(2,1)} collective-permute-done((bf16[256,2048]{1,0:T(8,128)(2,1)S(1)}, bf16[256,2048]{1,0:T(8,128)(2,1)}, u32[]{:S(2)}, u32[]{:S(2)}) %collective-permute-start.40) | collective-permute-done | bytes 1048608 | tf_op jit(solution)/shard_map/ppermute | solution.py:555
  670.3 11.1 %collective-permute-done.43 = bf16[256,2048]{1,0:T(8,128)(2,1)} collective-permute-done((bf16[256,2048]{1,0:T(8,128)(2,1)}, bf16[256,2048]{1,0:T(8,128)(2,1)}, u32[]{:S(2)}, u32[]{:S(2)}) %collective-permute-start.43) | collective-permute-done | bytes 1048608 | tf_op jit(solution)/shard_map/ppermute | solution.py:556
  695.2 11.4 %collective-permute-done.45 = bf16[256,2048]{1,0:T(8,128)(2,1)} collective-permute-done((bf16[256,2048]{1,0:T(8,128)(2,1)}, bf16[256,2048]{1,0:T(8,128)(2,1)}, u32[]{:S(2)}, u32[]{:S(2)}) %collective-permute-start.45) | collective-permute-done | bytes 1048608 | tf_op jit(solution)/shard_map/ppermute | solution.py:556
  716.6 15.6 %attend_backward.1 = (f32[1024,512]{1,0:T(8,128)S(1)}, f32[1024,512]{1,0:T(8,128)S(1)}, bf16[1024,512]{1,0:T(8,128)(2,1)S(1)}, f32[1024,1]{1,0:T(8,128)S(1)}, f3...) custom-call(f32[1024,1536]{1,0:T(8,128)S(1)} %bitcast.92, f32[1024,1536]{1,0:T(8,128)S(1)} %bitcast.92, ...), custom_call_target="tpu_custom_call" | custom-call | flops 5368709120 | bytes 20971520 | tf_op jit(solution)/shard_map/attend_backward/pallas_call | solution.py:179
  738.0 8.7 all-reduce
  767.6 19.8 %collective-permute-done.46 = bf16[256,2048]{1,0:T(8,128)(2,1)S(1)} collective-permute-done((bf16[256,2048]{1,0:T(8,128)(2,1)S(1)}, bf16[256,2048]{1,0:T(8,128)(2,1)S(1)}, u32[]{:S(2)}, u32[]{:S(2)}) %collective-permute-start.46) | collective-permute-done | bytes 1048608 | tf_op jit(solution)/shard_map/ppermute | solution.py:560
  806.2 9.1 collective-permute-done.51
  872.7 14.0 %collective-permute-done.57 = bf16[256,2048]{1,0:T(8,128)(2,1)} collective-permute-done((bf16[256,2048]{1,0:T(8,128)(2,1)S(1)}, bf16[256,2048]{1,0:T(8,128)(2,1)}, u32[]{:S(2)}, u32[]{:S(2)}) %collective-permute-start.57) | collective-permute-done | bytes 1048608 | tf_op jit(solution)/shard_map/ppermute | solution.py:555
  902.2 16.7 %collective-permute-done.62 = bf16[256,2048]{1,0:T(8,128)(2,1)} collective-permute-done((bf16[256,2048]{1,0:T(8,128)(2,1)}, bf16[256,2048]{1,0:T(8,128)(2,1)}, u32[]{:S(2)}, u32[]{:S(2)}) %collective-permute-start.62) | collective-permute-done | bytes 1048608 | tf_op jit(solution)/shard_map/ppermute | solution.py:556
  930.6 20.4 %collective-permute-done.65 = bf16[256,2048]{1,0:T(8,128)(2,1)S(1)} collective-permute-done((bf16[256,2048]{1,0:T(8,128)(2,1)}, bf16[256,2048]{1,0:T(8,128)(2,1)S(1)}, u32[]{:S(2)}, u32[]{:S(2)}) %collective-permute-start.65) | collective-permute-done | bytes 1048608 | tf_op jit(solution)/shard_map/ppermute | solution.py:556
  (485 shorter events, 398.2 us)
Async XLA Ops:
  7.2 102.9 %all-gather.4.cloned.1.call-start = ((), (), s32[]{:S(2)}) async-start(), calls=%async_computation.5 | async-start | bytes 7077888 | tf_op jit(solution)/shard_map/all_gather | solution.py:552
  9.5 237.6 %all-gather.6.cloned.1.call-start = ((), (), s32[]{:S(2)}) async-start(), calls=%async_computation.6 | async-start | bytes 9437184 | tf_op jit(solution)/shard_map/all_gather | solution.py:552
  10.6 236.5 %all-gather.8.cloned.1.call-start = ((), (), s32[]{:S(2)}) async-start(), calls=%async_computation.7 | async-start | bytes 9437184 | tf_op jit(solution)/shard_map/all_gather | solution.py:552
  13.1 808.4 %reduce-scatter.6.cloned.1.call-start = ((), (), s32[]{:S(2)}) async-start(), calls=%async_computation.8 | async-start | bytes 5242880 | tf_op jit(solution)/shard_map/reduce_scatter | solution.py:617
  14.7 38.8 %collective-permute-start = (bf16[1024,512]{1,0:T(8,128)(2,1)}, bf16[1024,512]{1,0:T(8,128)(2,1)S(1)}, u32[]{:S(2)}, u32[]{:S(2)}) collective-permute-start(bf16[1024,512]{1,0:T(8,128)(2,1)} %get-tuple-element.346), channel_id=1, source_target_pairs={{0,4},{4,0},{8,12},{12,8},{1,5},{5,1},{9,13},{13,9},{2,6},{6,2},{1... | collective-permute-start | bytes 3145736 | tf_op jit(solution)/shard_map/ppermute | solution.py:625
  17.7 38.9 %collective-permute-start.1 = (bf16[1024,512]{1,0:T(8,128)(2,1)}, bf16[1024,512]{1,0:T(8,128)(2,1)}, u32[]{:S(2)}, u32[]{:S(2)}) collective-permute-start(bf16[1024,512]{1,0:T(8,128)(2,1)} %get-tuple-element.346), channel_id=1, source_target_pairs={{0,8},{8,0},{4,12},{12,4},{1,9},{9,1},{5,13},{13,5},{2,10},{10,2},... | collective-permute-start | bytes 3145736 | tf_op jit(solution)/shard_map/ppermute | solution.py:625
  45.7 44.0 %collective-permute-start.5 = (bf16[1024,512]{1,0:T(8,128)(2,1)S(1)}, bf16[1024,512]{1,0:T(8,128)(2,1)S(1)}, u32[]{:S(2)}, u32[]{:S(2)}) collective-permute-start(bf16[1024,512]{1,0:T(8,128)(2,1)S(1)} %pad_maximum_fusion.1), channel_id=1, source_target_pairs={{0,4},{4,0},{8,12},{12,8},{1,5},{5,1},{9,13},{13,9},{2,6},{6,2},{1... | collective-permute-start | bytes 3145736 | tf_op jit(solution)/shard_map/ppermute | solution.py:625
  46.3 46.3 %collective-permute-start.6 = (bf16[1024,512]{1,0:T(8,128)(2,1)S(1)}, bf16[1024,512]{1,0:T(8,128)(2,1)S(1)}, u32[]{:S(2)}, u32[]{:S(2)}) collective-permute-start(bf16[1024,512]{1,0:T(8,128)(2,1)S(1)} %pad_maximum_fusion.1), channel_id=1, source_target_pairs={{0,8},{8,0},{4,12},{12,4},{1,9},{9,1},{5,13},{13,5},{2,10},{10,2},... | collective-permute-start | bytes 3145736 | tf_op jit(solution)/shard_map/ppermute | solution.py:625
  56.6 51.9 %collective-permute-start.7 = (bf16[512,512]{1,0:T(8,128)(2,1)S(1)}, bf16[512,512]{1,0:T(8,128)(2,1)S(1)}, u32[]{:S(2)}, u32[]{:S(2)}) collective-permute-start(bf16[512,512]{1,0:T(8,128)(2,1)S(1)} %slice.96), channel_id=1, source_target_pairs={{0,8},{8,0},{4,12},{12,4},{1,9},{9,1},{5,13},{13,5},{2,10},{10,2},... | collective-permute-start | bytes 1572872 | tf_op jit(solution)/shard_map/ppermute | solution.py:633
  60.2 49.1 %collective-permute-start.8 = (bf16[512,512]{1,0:T(8,128)(2,1)S(1)}, bf16[512,512]{1,0:T(8,128)(2,1)S(1)}, u32[]{:S(2)}, u32[]{:S(2)}) collective-permute-start(bf16[512,512]{1,0:T(8,128)(2,1)S(1)} %slice.97), channel_id=1, source_target_pairs={{0,4},{4,0},{8,12},{12,8},{1,5},{5,1},{9,13},{13,9},{2,6},{6,2},{1... | collective-permute-start | bytes 1572872 | tf_op jit(solution)/shard_map/ppermute | solution.py:634
  90.5 76.0 %collective-permute-start.11 = (bf16[512,512]{1,0:T(8,128)(2,1)}, bf16[512,512]{1,0:T(8,128)(2,1)}, u32[]{:S(2)}, u32[]{:S(2)}) collective-permute-start(bf16[512,512]{1,0:T(8,128)(2,1)} %slice.100), channel_id=1, source_target_pairs={{0,8},{8,0},{4,12},{12,4},{1,9},{9,1},{5,13},{13,5},{2,10},{10,2},... | collective-permute-start | bytes 1572872 | tf_op jit(solution)/shard_map/ppermute | solution.py:633
  93.4 74.9 %collective-permute-start.12 = (bf16[512,512]{1,0:T(8,128)(2,1)}, bf16[512,512]{1,0:T(8,128)(2,1)}, u32[]{:S(2)}, u32[]{:S(2)}) collective-permute-start(bf16[512,512]{1,0:T(8,128)(2,1)} %slice.101), channel_id=1, source_target_pairs={{0,4},{4,0},{8,12},{12,8},{1,5},{5,1},{9,13},{13,9},{2,6},{6,2},{1... | collective-permute-start | bytes 1572872 | tf_op jit(solution)/shard_map/ppermute | solution.py:634
  110.1 78.6 %collective-permute-start.15 = (bf16[4,1024,512]{2,1,0:T(8,128)(2,1)}, bf16[4,1024,512]{2,1,0:T(8,128)(2,1)}, u32[]{:S(2)}, u32[]{:S(2)}) collective-permute-start(bf16[4,1024,512]{2,1,0:T(8,128)(2,1)} %bitcast_dynamic-update-slice_fusion.8.wd_own_ref), channel_id=1, source_target_pairs={{0,16},{16,0},{1,17},{17,1},{2,18},{18,2},{3,19},{19,3},{4,20},{20... | collective-permute-start | bytes 12582920 | tf_op jit(solution)/shard_map/ppermute | solution.py:650
  170.2 76.9 %collective-permute-start.18 = (bf16[4,1024,512]{2,1,0:T(8,128)(2,1)}, bf16[4,1024,512]{2,1,0:T(8,128)(2,1)}, u32[]{:S(2)}, u32[]{:S(2)}) collective-permute-start(bf16[4,1024,512]{2,1,0:T(8,128)(2,1)} %bitcast_dynamic-update-slice_fusion.6.wo_own_ref), channel_id=1, source_target_pairs={{0,16},{16,0},{1,17},{17,1},{2,18},{18,2},{3,19},{19,3},{4,20},{20... | collective-permute-start | bytes 12582920 | tf_op jit(solution)/shard_map/ppermute | solution.py:650
  276.7 39.9 %collective-permute-start.19 = (bf16[256,2048]{1,0:T(8,128)(2,1)}, bf16[256,2048]{1,0:T(8,128)(2,1)}, u32[]{:S(2)}, u32[]{:S(2)}) collective-permute-start(bf16[256,2048]{1,0:T(8,128)(2,1)} %get-tuple-element.170), channel_id=1, source_target_pairs={{0,1},{4,5},{8,9},{12,13},{16,17},{20,21},{24,25},{28,29}} | collective-permute-start | bytes 3145736 | tf_op jit(solution)/shard_map/ppermute | solution.py:560
  279.1 37.5 %collective-permute-start.20 = (bf16[256,2048]{1,0:T(8,128)(2,1)}, bf16[256,2048]{1,0:T(8,128)(2,1)}, u32[]{:S(2)}, u32[]{:S(2)}) collective-permute-start(bf16[256,2048]{1,0:T(8,128)(2,1)} %get-tuple-element.170), channel_id=1, source_target_pairs={{3,2},{7,6},{11,10},{15,14},{19,18},{23,22},{27,26},{31,30}} | collective-permute-start | bytes 3145736 | tf_op jit(solution)/shard_map/ppermute | solution.py:561
  319.9 34.0 %collective-permute-start.21 = (bf16[256,2048]{1,0:T(8,128)(2,1)}, bf16[256,2048]{1,0:T(8,128)(2,1)}, u32[]{:S(2)}, u32[]{:S(2)}) collective-permute-start(bf16[256,2048]{1,0:T(8,128)(2,1)} %get-tuple-element.370), channel_id=1, source_target_pairs={{0,1},{1,2},{4,5},{5,6},{8,9},{9,10},{12,13},{13,14},{16,17},{17,1... | collective-permute-start | bytes 3145736 | tf_op jit(solution)/shard_map/ppermute | solution.py:560
  322.2 31.7 %collective-permute-start.22 = (bf16[256,2048]{1,0:T(8,128)(2,1)}, bf16[256,2048]{1,0:T(8,128)(2,1)}, u32[]{:S(2)}, u32[]{:S(2)}) collective-permute-start(bf16[256,2048]{1,0:T(8,128)(2,1)} %get-tuple-element.369), channel_id=1, source_target_pairs={{3,2},{2,1},{7,6},{6,5},{11,10},{10,9},{15,14},{14,13},{19,18},{18... | collective-permute-start | bytes 3145736 | tf_op jit(solution)/shard_map/ppermute | solution.py:561
  355.7 32.0 %collective-permute-start.23 = (bf16[256,2048]{1,0:T(8,128)(2,1)S(1)}, bf16[256,2048]{1,0:T(8,128)(2,1)S(1)}, u32[]{:S(2)}, u32[]{:S(2)}) collective-permute-start(bf16[256,2048]{1,0:T(8,128)(2,1)S(1)} %get-tuple-element.368), channel_id=1, source_target_pairs={{0,1},{1,2},{2,3},{4,5},{5,6},{6,7},{8,9},{9,10},{10,11},{12,13},{... | collective-permute-start | bytes 3145736 | tf_op jit(solution)/shard_map/ppermute | solution.py:560
  357.1 30.6 %collective-permute-start.24 = (bf16[256,2048]{1,0:T(8,128)(2,1)S(1)}, bf16[256,2048]{1,0:T(8,128)(2,1)S(1)}, u32[]{:S(2)}, u32[]{:S(2)}) collective-permute-start(bf16[256,2048]{1,0:T(8,128)(2,1)S(1)} %get-tuple-element.367), channel_id=1, source_target_pairs={{3,2},{2,1},{1,0},{7,6},{6,5},{5,4},{11,10},{10,9},{9,8},{15,14},{... | collective-permute-start | bytes 3145736 | tf_op jit(solution)/shard_map/ppermute | solution.py:561
  388.3 30.0 %collective-permute-start.25 = (bf16[256,2048]{1,0:T(8,128)(2,1)S(1)}, bf16[256,2048]{1,0:T(8,128)(2,1)}, u32[]{:S(2)}, u32[]{:S(2)}) collective-permute-start(bf16[256,2048]{1,0:T(8,128)(2,1)S(1)} %add_convert_fusion.6.down_ref), channel_id=1, source_target_pairs={{0,1},{1,2},{2,3},{4,5},{5,6},{6,7},{8,9},{9,10},{10,11},{12,13},{... | collective-permute-start | bytes 3145736 | tf_op jit(solution)/shard_map/ppermute | solution.py:555
  500.8 35.7 %collective-permute-start.34 = (bf16[2048,1024]{1,0:T(8,128)(2,1)}, bf16[2048,1024]{1,0:T(8,128)(2,1)S(1)}, u32[]{:S(2)}, u32[]{:S(2)}) collective-permute-start(bf16[2048,1024]{1,0:T(8,128)(2,1)} %convolution_convert_fusion.1), channel_id=1, source_target_pairs={{0,16},{16,0},{1,17},{17,1},{2,18},{18,2},{3,19},{19,3},{4,20},{20... | collective-permute-start | bytes 12582920 | tf_op jit(solution)/shard_map/ppermute | solution.py:613
  505.7 30.8 %collective-permute-start.33 = (bf16[2048,1024]{1,0:T(8,128)(2,1)S(1)}, bf16[2048,1024]{1,0:T(8,128)(2,1)S(1)}, u32[]{:S(2)}, u32[]{:S(2)}) collective-permute-start(bf16[2048,1024]{1,0:T(8,128)(2,1)S(1)} %convolution_convert_fusion.2), channel_id=1, source_target_pairs={{0,16},{16,0},{1,17},{17,1},{2,18},{18,2},{3,19},{19,3},{4,20},{20... | collective-permute-start | bytes 12582920 | tf_op jit(solution)/shard_map/ppermute | solution.py:613
  506.2 30.3 %collective-permute-start.31 = (bf16[256,2048]{1,0:T(8,128)(2,1)S(1)}, bf16[256,2048]{1,0:T(8,128)(2,1)S(1)}, u32[]{:S(2)}, u32[]{:S(2)}) collective-permute-start(bf16[256,2048]{1,0:T(8,128)(2,1)S(1)} %get-tuple-element.227), channel_id=1, source_target_pairs={{0,1},{4,5},{8,9},{12,13},{16,17},{20,21},{24,25},{28,29}} | collective-permute-start | bytes 3145736 | tf_op jit(solution)/shard_map/ppermute | solution.py:560
  545.5 297.1 %reduce-scatter.10.cloned.1.call-start = ((), (), s32[]{:S(2)}) async-start(), calls=%async_computation.10 | async-start | bytes 5242880 | tf_op jit(solution)/shard_map/reduce_scatter | solution.py:617
  589.1 253.5 %reduce-scatter.8.cloned.1.call-start = ((), (), s32[]{:S(2)}) async-start(), calls=%async_computation.9 | async-start | bytes 5242880 | tf_op jit(solution)/shard_map/reduce_scatter | solution.py:617
  589.1 31.5 %collective-permute-start.38 = (bf16[256,2048]{1,0:T(8,128)(2,1)}, bf16[256,2048]{1,0:T(8,128)(2,1)}, u32[]{:S(2)}, u32[]{:S(2)}) collective-permute-start(bf16[256,2048]{1,0:T(8,128)(2,1)} %get-tuple-element.364), channel_id=1, source_target_pairs={{0,1},{1,2},{2,3},{4,5},{5,6},{6,7},{8,9},{9,10},{10,11},{12,13},{... | collective-permute-start | bytes 3145736 | tf_op jit(solution)/shard_map/ppermute | solution.py:560
  684.4 213.0 %reduce-scatter.12.cloned.1.call-start = ((), (), s32[]{:S(2)}) async-start(), calls=%async_computation.11 | async-start | bytes 1310720 | tf_op jit(solution)/shard_map/reduce_scatter | solution.py:617
  758.9 28.5 %collective-permute-start.48 = (bf16[2048,768]{1,0:T(8,128)(2,1)S(1)}, bf16[2048,768]{1,0:T(8,128)(2,1)S(1)}, u32[]{:S(2)}, u32[]{:S(2)}) collective-permute-start(bf16[2048,768]{1,0:T(8,128)(2,1)S(1)} %convolution_convert_fusion.3), channel_id=1, source_target_pairs={{0,16},{16,0},{1,17},{17,1},{2,18},{18,2},{3,19},{19,3},{4,20},{20... | collective-permute-start | bytes 9437192 | tf_op jit(solution)/shard_map/ppermute | solution.py:613
  820.8 98.8 %reduce-scatter.14.cloned.1.call-start = ((), (), s32[]{:S(2)}) async-start(), calls=%async_computation.12 | async-start | bytes 3932160 | tf_op jit(solution)/shard_map/reduce_scatter | solution.py:617
  825.9 29.3 %collective-permute-start.54 = (bf16[256,2048]{1,0:T(8,128)(2,1)}, bf16[256,2048]{1,0:T(8,128)(2,1)}, u32[]{:S(2)}, u32[]{:S(2)}) collective-permute-start(bf16[256,2048]{1,0:T(8,128)(2,1)} %get-tuple-element.360), channel_id=1, source_target_pairs={{0,1},{1,2},{2,3},{4,5},{5,6},{6,7},{8,9},{9,10},{10,11},{12,13},{... | collective-permute-start | bytes 3145736 | tf_op jit(solution)/shard_map/ppermute | solution.py:560
  842.6 28.0 %collective-permute-start.63 = (bf16[512,1024]{1,0:T(8,128)(2,1)}, bf16[512,1024]{1,0:T(8,128)(2,1)S(1)}, u32[]{:S(2)}, u32[]{:S(2)}) collective-permute-start(bf16[512,1024]{1,0:T(8,128)(2,1)} %reduce-scatter.10.cloned.1.call-done), channel_id=1, source_target_pairs={{0,16},{16,0},{1,17},{17,1},{2,18},{18,2},{3,19},{19,3},{4,20},{20... | collective-permute-start | bytes 3145736 | tf_op jit(solution)/shard_map/ppermute | solution.py:607
  (152 other events, 2027.4 us)
Sparse Core Ops, SparseCore 0:
  10.5 73.5 all-gather.3
  86.5 65.5 all-gather.5
  154.6 54.2 all-gather.7
  545.6 55.5 reduce-scatter.5
  604.1 52.5 reduce-scatter.9
  684.5 53.4 reduce-scatter.7
  820.9 29.3 reduce-scatter.11
  853.4 43.6 reduce-scatter.13

commit v5 on v4

--- a/solution.py
+++ b/solution.py
@@ -11,6 +11,7 @@
 HD = 128
 LEN = 1024
 BQ = 256
+VMEM = 60 << 20
 
 EPS = 1e-06
 THETA = 500000.0
@@ -163,7 +164,7 @@
         out_specs=[head_spec(0)] * 4 + [LOG_SPEC],
         out_shape=[piece] * 4 + [jax.ShapeDtypeStruct((heads, LEN, 1), F32)],
         scratch_shapes=[pltpu.VMEM((LEN, LEN), F32)],
-        compiler_params=pltpu.CompilerParams(vmem_limit_bytes=28 << 20),
+        compiler_params=pltpu.CompilerParams(vmem_limit_bytes=VMEM),
         cost_estimate=pl.CostEstimate(
             flops=heads * 4 * LEN * LEN * HD, bytes_accessed=LEN * width * 20, transcendentals=0
         ),
@@ -193,7 +194,7 @@
             full, full, jax.ShapeDtypeStruct((LEN, width), BF16), column, column, gain_row, gain_row,
         ],
         scratch_shapes=[pltpu.VMEM((LEN, HD), F32)] * 3 + [pltpu.VMEM((LEN, LEN), F32)],
-        compiler_params=pltpu.CompilerParams(vmem_limit_bytes=28 << 20),
+        compiler_params=pltpu.CompilerParams(vmem_limit_bytes=VMEM),
         cost_estimate=pl.CostEstimate(
             flops=heads * 10 * LEN * LEN * HD, bytes_accessed=LEN * width * 40, transcendentals=0
         ),
@@ -305,7 +306,7 @@
             jax.ShapeDtypeStruct((chunk, width), BF16),
         ],
         input_output_aliases={10 + i: i for i in range(len(before))},
-        compiler_params=pltpu.CompilerParams(vmem_limit_bytes=40 << 20),
+        compiler_params=pltpu.CompilerParams(vmem_limit_bytes=VMEM),
         cost_estimate=pl.CostEstimate(
             flops=2 * chunk * width * (width + 3 * hidden),
             bytes_accessed=2 * width * (width + 3 * hidden),
@@ -404,7 +405,7 @@
             jax.ShapeDtypeStruct((1, width), F32),
         ],
         input_output_aliases={14 + i: i for i in range(len(before))},
-        compiler_params=pltpu.CompilerParams(vmem_limit_bytes=40 << 20),
+        compiler_params=pltpu.CompilerParams(vmem_limit_bytes=VMEM),
         cost_estimate=pl.CostEstimate(
             flops=6 * chunk * width * hidden, bytes_accessed=6 * width * hidden, transcendentals=0
         ),
@@ -460,7 +461,7 @@
             jax.ShapeDtypeStruct((1, width), F32),
         ],
         input_output_aliases={8 + i: i for i in range(len(before))},
-        compiler_params=pltpu.CompilerParams(vmem_limit_bytes=32 << 20),
+        compiler_params=pltpu.CompilerParams(vmem_limit_bytes=VMEM),
         cost_estimate=pl.CostEstimate(
             flops=4 * chunk * width * half, bytes_accessed=16 * chunk * width, transcendentals=0
         ),
@@ -486,7 +487,7 @@
         ),
         out_shape=jax.ShapeDtypeStruct((tokens, width), dtype),
         input_output_aliases={2: 0} if before else {},
-        compiler_params=pltpu.CompilerParams(vmem_limit_bytes=16 << 20),
+        compiler_params=pltpu.CompilerParams(vmem_limit_bytes=VMEM),
         cost_estimate=pl.CostEstimate(flops=0, bytes_accessed=6 * chunk * width, transcendentals=0),
         name="place_rows",
     )(index, rows_in, *before)
@@ -581,6 +582,33 @@
         left3, right3 = after((left3, right3), work(1, pick(right2, right1, left1, left2)))
         return work(0, pick(right3, right2, left2, left3))
 
+    def gather_halves(own, work):
+        half = own.shape[1] // 2
+        left, right, token = {}, {}, ()
+        for part in range(2):
+            left[part, 0] = right[part, 0] = own[:, part * half : (part + 1) * half]
+        arrived = (
+            lambda lefts, rights: lefts[0],
+            lambda lefts, rights: jnp.where(col % 2 == 0, rights[1], lefts[1]),
+            lambda lefts, rights: pick(rights[2], rights[1], lefts[1], lefts[2]),
+            lambda lefts, rights: pick(rights[3], rights[2], lefts[2], lefts[3]),
+        )
+
+        def slot_of(step, token):
+            halves = []
+            for part in range(2):
+                seen = tuple((left[part, k], right[part, k]) for k in range(step))
+                seen = after(seen, token)
+                halves.append(arrived[step - 1]([one[0] for one in seen], [one[1] for one in seen]))
+            return jnp.concatenate(halves, axis=1)
+
+        for step in range(1, cols):
+            for part in range(2):
+                sent = (left[part, step - 1], right[part, step - 1])
+                left[part, step], right[part, step] = line_step(*sent, step)
+            token = work(cols - step, slot_of(step, token))
+        return work(0, slot_of(cols, token))
+
     def sum_slots(make, window=lambda step, gate: ()):
         def at(step, gate):
             return make(step, gate), window(step, gate)
@@ -652,7 +680,6 @@
     full_qkv = gather(jnp.concatenate([w_query, w_key, w_value], axis=1), 0)
     full_gate = gather(w_gate, 0)
     full_up = gather(w_up, 0)
-    down_pieces = row_first(own_half(w_down, 0))
     out_half = own_half(w_out, 0)
     out_stack = jnp.concatenate(
         [out_half]
@@ -662,10 +689,11 @@
         ],
         axis=0,
     )
-
-    qkv = plain_dot(after(block_input, down_pieces, out_stack), full_qkv)
-    out_pieces = row_first(out_stack)
-    down_pieces = row_second(down_pieces)
+    down_start, out_start = after((own_half(w_down, 0), out_stack), full_qkv)
+    down_pieces = row_first(down_start)
+    out_pieces = row_first(out_start)
+
+    qkv = plain_dot(block_input, full_qkv)
     query_raw, key_raw = qkv[:, :local_width], qkv[:, local_width : 2 * local_width]
     query_sq, key_sq = lax.psum(
         (jnp.sum(query_raw * query_raw, axis=1), jnp.sum(key_raw * key_raw, axis=1)), "col"
@@ -677,20 +705,28 @@
     tables = rope_tables(positions)
     seg_col, seg_row = segment_ids[:, None], segment_ids[None, :]
     query_rot, key_rot, value_heads, attended, log_total = attend_forward(
-        after(qkv, out_pieces, down_pieces), scales, gains, tables, seg_col, seg_row, heads
-    )
-
-    left1, right1 = line_step(attended, attended, 1)
-    out_pieces = row_second(out_pieces)
-    down_halves = row_blocks(down_pieces)
-    left1, right1 = after((left1, right1), out_pieces, down_halves[0])
-    left2, right2 = line_step(left1, right1, 2)
-    out_halves = row_blocks(out_pieces)
-    left2, right2 = after((left2, right2), out_halves[0], down_halves[1])
-    left3, right3 = line_step(left2, right2, 3)
-    pieces = [attended, right1 + left3, right2 + left2, right3 + left1]
+        qkv, scales, gains, tables, seg_col, seg_row, heads
+    )
+
+    steps_from = {}
+    for part in range(cores):
+        steps_from[part] = [(attended[:, part * half_width : (part + 1) * half_width],) * 2]
+    for step in range(1, cols):
+        for part in range(cores):
+            sent = steps_from[part][-1]
+            steps_from[part].append(line_step(*sent, step))
+        if step == 1:
+            down_pieces = row_second(after(down_pieces, attended))
+            out_pieces = row_second(after(out_pieces, attended))
+            down_halves = row_blocks(down_pieces)
+        if step == 2:
+            out_halves = row_blocks(out_pieces)
     attended_all = jnp.concatenate(
-        [one[:, half * half_width : (half + 1) * half_width] for half in range(cores) for one in pieces],
+        [
+            steps_from[part][0][0] if step == 0 else steps_from[part][step][1] + steps_from[part][cols - step][0]
+            for part in range(cores)
+            for step in range(cols)
+        ],
         axis=1,
     )
 
@@ -752,7 +788,7 @@
         gain_sums["attn"] = gain_sums["attn"] + results[2]
         return results[1]
 
-    gather_slots(mlp_own, attention_work)
+    gather_halves(mlp_own, attention_work)
     grad_attn_in, grad_att = held["attention"]
     own_grad_hidden = slot_rows(grad_output, 3).astype(F32) + mlp_own.astype(F32)
 
@@ -818,7 +854,7 @@
             return held["output"], results["out"], results["qkv"]
         return held["output"]
 
-    gather_slots((own_grad_hidden + input_own).astype(BF16), output_work)
+    gather_halves((own_grad_hidden + input_own).astype(BF16), output_work)
     ends = (local_width, 2 * local_width, 2 * local_width + width)
     gain_grads = jnp.split(gain_pack[0], ends)
     return (

time: 972 us -> 984 us (1.012)
  local copies, waits for them, and re-layouts: 103 us -> 47.9 us
  other arithmetic: 60.5 us -> 87.5 us
  starting transfers between devices: 121 us -> 145 us
  Pallas kernels: 242 us -> 265 us
  waiting for transfers between devices: 319 us -> 305 us
    unnamed x221 -> x105, local copies, waits for them, and re-layouts: 74.9 us -> 16.5 us
    ppermute x12 -> x21, waiting for transfers between devices: 128 us -> 77.9 us  [line_step(): lax.ppermute(from_right, 'col', [(i + 1, i) for i in range(cols - step)])]
    reduce_scatter x5, waiting for transfers between devices: 0.05 us -> 45.7 us  [sum_kept(): lax.psum_scatter(total, 'row', scatter_dimension=0, tiled=True)]
    ppermute x12 -> x21, starting transfers between devices: 26.2 us -> 44.2 us  [line_step(): lax.ppermute(from_left, 'col', [(i, i + 1) for i in range(step - 1, cols...]
    all_gather x3, waiting for transfers between devices: 0.01 us -> 17.9 us  [gather(): lax.all_gather(own_half(weight, axis), ('row', 'dp'), axis=axis, tiled=True)]
    ppermute x12 -> x21, starting transfers between devices: 16.1 us -> 28.2 us  [line_step(): lax.ppermute(from_right, 'col', [(i + 1, i) for i in range(cols - step)])]
    concatenate x0 -> x9, other arithmetic: none -> 11.6 us  [the longest x8 10.7 us: slot_of(): return jnp.concatenate(halves, axis=1)]
    ppermute x12 -> x21, waiting for transfers between devices: 27.4 us -> 20.3 us  [line_step(): lax.ppermute(from_left, 'col', [(i, i + 1) for i in range(step - 1, cols...]
  transfers between devices with their start and end apart: 78 -> 96, of which waited for: 27 -> 37; matrix products, arithmetic and copies ran while one was open for 16% -> 19% of each run, Pallas kernels for 20% -> 22%
where the time goes in v5:
time: 984 us; the launch traced here: 972 us
  waiting for transfers between devices  305 us (31%)
  Pallas kernels  265 us (27%)
  starting transfers between devices  145 us (15%)
  other arithmetic  87.5 us (9%)
  matrix products  84.5 us (9%)
  local copies, waits for them, and re-layouts  47.9 us (5%)
  blocking collectives  21.4 us (2%)
  between operations  16.1 us (2%)
    pallas_call x4, Pallas kernels, forward_chunk(): pl.pallas_call(functools.partial(forward_chunk_kernel, blocks=blocks, til...  97.3 us
    pallas_call x4, Pallas kernels, backward_chunk(): pl.pallas_call(functools.partial(backward_chunk_kernel, blocks=blocks, ti...  97.1 us
    ppermute x21, waiting for transfers between devices, line_step(): lax.ppermute(from_right, 'col', [(i + 1, i) for i in range(cols - step)])  77.9 us
    ppermute x9, waiting for transfers between devices, sum_step(): up = lax.ppermute(up, 'col', [(i, i + 1) for i in range(step)])  77.4 us
    dot_general x10, matrix products, left_transposed(): lax.dot_general(left_mat, right_mat, (((0,), (0,)), ((), ())), preferred_...  61.2 us
    reduce_scatter x5, waiting for transfers between devices, sum_kept(): lax.psum_scatter(total, 'row', scatter_dimension=0, tiled=True)  45.7 us
    ppermute x21, starting transfers between devices, line_step(): lax.ppermute(from_left, 'col', [(i, i + 1) for i in range(step - 1, cols...  44.2 us
    ppermute x9, starting transfers between devices, sum_step(): up = lax.ppermute(up, 'col', [(i, i + 1) for i in range(step)])  43.3 us
  transfers between devices with their start and end apart: 96, of which 37 were waited for; matrix products, arithmetic and copies ran while one was open for 19% of the time, Pallas kernels for 22%

profile of v5, /device:TPU:0, one launch (start us, length us, event | category | flops | bytes accessed | tf_op | source)
XLA Modules:
  0.0 971.9 jit_solution(10301386294125435422)
XLA Ops:
  25.0 15.6 %collective-permute-done.13 = bf16[256,512]{1,0:T(8,128)(2,1)S(1)} collective-permute-done((bf16[256,512]{1,0:T(8,128)(2,1)S(1)}, bf16[256,512]{1,0:T(8,128)(2,1)S(1)}, u32[]{:S(2)}, u32[]{:S(2)}) %collective-permute-start.13) | collective-permute-done | bytes 262176 | tf_op jit(solution)/shard_map/ppermute | solution.py:687
  40.7 17.9 %all-gather.4.cloned.1.call-done = bf16[2048,1536]{1,0:T(8,128)(2,1)} async-done(((bf16[256,1536]{1,0:T(8,128)(2,1)}), bf16[2048,1536]{1,0:T(8,128)(2,1)}) %all-gather.4.cloned.1.call-update) | async-done | bytes 6291472 | tf_op jit(solution)/shard_map/all_gather | solution.py:553
  62.7 10.0 %convolution_bitcast_fusion.q_ref.k_ref.v_ref = f32[1024,1536]{1,0:T(8,128)S(1)} fusion(bf16[1024,2048]{1,0:T(8,128)(2,1)} %x_ref.15, bf16[2048,1536]{1,0:T(8,128)(2,1)} %all-gather.4.cloned.1.call-done), kind=kOutput, calls=%fused_computation.4 | convolution fusion | flops 6442450944 | bytes 16777216 | tf_op jit(solution)/shard_map/dot_general | solution.py:25
  75.7 11.9 %all-reduce.1 = (f32[1024]{0:T(1024)S(1)}, f32[1024]{0:T(1024)S(1)}) all-reduce(f32[1024]{0:T(1024)S(1)} %get-tuple-element.408, f32[1024]{0:T(1024)S(1)} %get-tuple-element.407), channel_id=1, replica_groups=mesh['dp'=2,'row'=4,'col'=4] {'col'}, use_global_device_ids=true, to_apply=%region_1.2 | all-reduce | flops 2048 | bytes 16384 | tf_op jit(solution)/shard_map/psum | solution.py:698
  89.7 16.1 %attend_forward.1 = (bf16[1024,512]{1,0:T(8,128)(2,1)}, bf16[1024,512]{1,0:T(8,128)(2,1)}, bf16[1024,512]{1,0:T(8,128)(2,1)}, bf16[1024,512]{1,0:T(8,128)(2,1)}, f32[4,1024,1]{2,1,0:T(8,128)}) custom-call(f32[1024,1536]{1,0:T(8,128)} %copy-done.3, f32[1024,1536]{1,0:T(8,128)} %copy-done.3, f32[1024,1536]{1,0:T(8,128)} %copy-done.3, f32[1024,1]{1,0:T(8,128)} %copy.71.qs_ref, ...), custom_call_target="tpu_custom_call" | custom-call | flops 2147483648 | bytes 10485760 | tf_op jit(solution)/shard_map/attend_forward/pallas_call | solution.py:156
  109.1 25.4 %collective-permute-done.15 = bf16[1024,512]{1,0:T(8,128)(2,1)} collective-permute-done((bf16[1024,512]{1,0:T(8,128)(2,1)S(1)}, bf16[1024,512]{1,0:T(8,128)(2,1)}, u32[]{:S(2)}, u32[]{:S(2)}) %collective-permute-start.15) | collective-permute-done | bytes 1048608 | tf_op jit(solution)/shard_map/ppermute | solution.py:653
  155.2 10.4 %collective-permute-done.17 = bf16[512,512]{1,0:T(8,128)(2,1)S(1)} collective-permute-done((bf16[512,512]{1,0:T(8,128)(2,1)S(1)}, bf16[512,512]{1,0:T(8,128)(2,1)S(1)}, u32[]{:S(2)}, u32[]{:S(2)}) %collective-permute-start.17) | collective-permute-done | bytes 524320 | tf_op jit(solution)/shard_map/ppermute | solution.py:661
  202.4 9.6 collective-permute-done.4
  245.7 24.2 %forward_chunk.4 = (f32[1024,2048]{1,0:T(8,128)}, f32[1024,1]{1,0:T(8,128)}, bf16[1024,2048]{1,0:T(8,128)(2,1)}, bf16[1024,2048]{1,0:T(8,128)(2,1)}, bf16[1024,2...) custom-call(s32[2]{0:T(128)} %pad_add_fusion.idx_ref, ...), custom_call_target="tpu_custom_call" | custom-call | flops 8589934592 | bytes 33554432 | tf_op jit(solution)/shard_map/forward_chunk/pallas_call | solution.py:283
  273.0 24.4 %forward_chunk.5 = (f32[1024,2048]{1,0:T(8,128)}, f32[1024,1]{1,0:T(8,128)}, bf16[1024,2048]{1,0:T(8,128)(2,1)}, bf16[1024,2048]{1,0:T(8,128)(2,1)}, bf16[1024,2...) custom-call(s32[2]{0:T(128)} %get-tuple-element.472.idx_ref, ...), custom_call_target="tpu_custom_call", output_to_operand_aliasing={{0}: (10, {}), {1}: (11, {}), {2}: (12, {}), {3}: (13, {}),... | custom-call | flops 8589934592 | bytes 33554432 | tf_op jit(solution)/shard_map/forward_chunk/pallas_call | solution.py:283
  302.5 24.4 %forward_chunk.6 = (f32[1024,2048]{1,0:T(8,128)}, f32[1024,1]{1,0:T(8,128)}, bf16[1024,2048]{1,0:T(8,128)(2,1)}, bf16[1024,2048]{1,0:T(8,128)(2,1)}, bf16[1024,2...) custom-call(s32[2]{0:T(128)} %get-tuple-element.473.idx_ref, ...), custom_call_target="tpu_custom_call", output_to_operand_aliasing={{0}: (10, {}), {1}: (11, {}), {2}: (12, {}), {3}: (13, {}),... | custom-call | flops 8589934592 | bytes 33554432 | tf_op jit(solution)/shard_map/forward_chunk/pallas_call | solution.py:283
  336.9 24.2 %forward_chunk.7 = (f32[1024,2048]{1,0:T(8,128)}, f32[1024,1]{1,0:T(8,128)}, bf16[1024,2048]{1,0:T(8,128)(2,1)}, bf16[1024,2048]{1,0:T(8,128)(2,1)}, bf16[1024,2...) custom-call(s32[2]{0:T(128)} %pad_add_fusion.1.idx_ref, ...), custom_call_target="tpu_custom_call", output_to_operand_aliasing={{0}: (10, {}), {1}: (11, {}), {2}: (12, {}), {3}: (13, {}),... | custom-call | flops 8589934592 | bytes 33554432 | tf_op jit(solution)/shard_map/forward_chunk/pallas_call | solution.py:283
  371.0 24.2 %backward_chunk.4 = (bf16[1024,2048]{1,0:T(8,128)(2,1)}, bf16[1024,2048]{1,0:T(8,128)(2,1)}, bf16[1024,2048]{1,0:T(8,128)(2,1)}, bf16[1024,2048]{1,0:T(8,128)(2,...) custom-call(s32[2]{0:T(128)} %pad_add_fusion.1.idx_ref, bf16[256,2048]{1,0:T(8,128)(2,1)} %copy-done.11, ...), custom_call_target="tpu_custom_call" | custom-call | flops 6442450944 | bytes 25165824 | tf_op jit(solution)/shard_map/backward_chunk/pallas_call | solution.py:385
  398.4 24.2 %backward_chunk.5 = (bf16[1024,2048]{1,0:T(8,128)(2,1)}, bf16[1024,2048]{1,0:T(8,128)(2,1)}, bf16[1024,2048]{1,0:T(8,128)(2,1)}, bf16[1024,2048]{1,0:T(8,128)(2,...) custom-call(s32[2]{0:T(128)} %get-tuple-element.473.idx_ref, ...), custom_call_target="tpu_custom_call", output_to_operand_aliasing={{0}: (14, {}), {1}: (15, {}), {2}: (16, {}), {3}: (17, {})} | custom-call | flops 6442450944 | bytes 25165824 | tf_op jit(solution)/shard_map/backward_chunk/pallas_call | solution.py:385
  429.9 24.2 %backward_chunk.6 = (bf16[1024,2048]{1,0:T(8,128)(2,1)}, bf16[1024,2048]{1,0:T(8,128)(2,1)}, bf16[1024,2048]{1,0:T(8,128)(2,1)}, bf16[1024,2048]{1,0:T(8,128)(2,...) custom-call(s32[2]{0:T(128)} %get-tuple-element.472.idx_ref, ...), custom_call_target="tpu_custom_call", output_to_operand_aliasing={{0}: (14, {}), {1}: (15, {}), {2}: (16, {}), {3}: (17, {})} | custom-call | flops 6442450944 | bytes 25165824 | tf_op jit(solution)/shard_map/backward_chunk/pallas_call | solution.py:385
  456.9 24.5 %backward_chunk.7 = (bf16[1024,2048]{1,0:T(8,128)(2,1)}, bf16[1024,2048]{1,0:T(8,128)(2,1)}, bf16[1024,2048]{1,0:T(8,128)(2,1)}, bf16[1024,2048]{1,0:T(8,128)(2,...) custom-call(s32[2]{0:T(128)} %pad_add_fusion.idx_ref, ...), custom_call_target="tpu_custom_call", output_to_operand_aliasing={{0}: (14, {}), {1}: (15, {}), {2}: (16, {}), {3}: (17, {})} | custom-call | flops 6442450944 | bytes 25165824 | tf_op jit(solution)/shard_map/backward_chunk/pallas_call | solution.py:385
  481.4 7.6 convolution_convert_fusion.1
  501.7 21.8 %collective-permute-done.37 = bf16[256,2048]{1,0:T(8,128)(2,1)S(1)} collective-permute-done((bf16[256,2048]{1,0:T(8,128)(2,1)S(1)}, bf16[256,2048]{1,0:T(8,128)(2,1)S(1)}, u32[]{:S(2)}, u32[]{:S(2)}) %collective-permute-start.37) | collective-permute-done | bytes 1048608 | tf_op jit(solution)/shard_map/ppermute | solution.py:561
  532.5 9.5 convolution_convert_fusion
  549.0 20.7 %collective-permute-done.41 = bf16[256,2048]{1,0:T(8,128)(2,1)} collective-permute-done((bf16[256,2048]{1,0:T(8,128)(2,1)}, bf16[256,2048]{1,0:T(8,128)(2,1)}, u32[]{:S(2)}, u32[]{:S(2)}) %collective-permute-start.41) | collective-permute-done | bytes 1048608 | tf_op jit(solution)/shard_map/ppermute | solution.py:561
  572.5 9.3 collective-permute-start.44
  583.3 9.2 add_convert_fusion
  592.5 10.7 %add_convert_fusion.1 = bf16[2048,1024]{1,0:T(8,128)(2,1)} fusion(bf16[2048,1024]{1,0:T(8,128)(2,1)} %copy-done.46, bf16[1024,2048]{1,0:T(8,128)(2,1)} %get-tuple-element.281, bf16[1024,2048]{1,0:T(8,128)(2,1)} %get-tuple-element.282, s32[]{:T(128)S(6)} %select_n.380), kind=kOutput, calls=%fused_computation.1 | convolution fusion | flops 4301258752 | bytes 14680068 | tf_op jit(solution)/shard_map/dot_general | solution.py:35
  656.2 8.0 collective-permute-done.55
  683.0 7.3 collective-permute-done.57
  698.6 17.9 %attend_backward.1 = (f32[1024,512]{1,0:T(8,128)}, f32[1024,512]{1,0:T(8,128)}, bf16[1024,512]{1,0:T(8,128)(2,1)}, f32[1024,1]{1,0:T(8,128)}, f32[1024,1]{1,0:T(...) custom-call(f32[1024,1536]{1,0:T(8,128)} %copy-done.3, f32[1024,1536]{1,0:T(8,128)} %copy-done.3, f32[1024,1]{1,0:T(8,128)} %copy.71.qs_ref, ...), custom_call_target="tpu_custom_call" | custom-call | flops 5368709120 | bytes 20971520 | tf_op jit(solution)/shard_map/attend_backward/pallas_call | solution.py:180
  719.0 9.5 all-reduce
  749.0 19.8 %collective-permute-done.58 = bf16[256,2048]{1,0:T(8,128)(2,1)S(1)} collective-permute-done((bf16[256,2048]{1,0:T(8,128)(2,1)S(1)}, bf16[256,2048]{1,0:T(8,128)(2,1)S(1)}, u32[]{:S(2)}, u32[]{:S(2)}) %collective-permute-start.58) | collective-permute-done | bytes 1048608 | tf_op jit(solution)/shard_map/ppermute | solution.py:561
  788.7 8.0 collective-permute-done.63
  867.0 20.7 %reduce-scatter.10.cloned.1.call-done = bf16[512,1024]{1,0:T(8,128)(2,1)} async-done(((bf16[2048,1024]{1,0:T(8,128)(2,1)}), bf16[512,1024]{1,0:T(8,128)(2,1)}) %reduce-scatter.10.cloned.1.call-update) | async-done | bytes 1048592 | tf_op jit(solution)/shard_map/reduce_scatter | solution.py:645
  909.7 24.9 %reduce-scatter.14.cloned.1.call-done = bf16[512,768]{1,0:T(8,128)(2,1)} async-done(((bf16[2048,768]{1,0:T(8,128)(2,1)}), bf16[512,768]{1,0:T(8,128)(2,1)}) %reduce-scatter.14.cloned.1.call-update) | async-done | bytes 786448 | tf_op jit(solution)/shard_map/reduce_scatter | solution.py:645
  948.0 11.1 %collective-permute-done.87 = bf16[256,1024]{1,0:T(8,128)(2,1)S(1)} collective-permute-done((bf16[256,1024]{1,0:T(8,128)(2,1)}, bf16[256,1024]{1,0:T(8,128)(2,1)S(1)}, u32[]{:S(2)}, u32[]{:S(2)}) %collective-permute-start.87) | collective-permute-done | bytes 524320 | tf_op jit(solution)/shard_map/ppermute | solution.py:557
  (424 shorter events, 428.5 us)
Async XLA Ops:
  7.2 51.4 %all-gather.4.cloned.1.call-start = ((), (), s32[]{:S(2)}) async-start(), calls=%async_computation.5 | async-start | bytes 7077888 | tf_op jit(solution)/shard_map/all_gather | solution.py:553
  9.5 236.2 %all-gather.6.cloned.1.call-start = ((), (), s32[]{:S(2)}) async-start(), calls=%async_computation.6 | async-start | bytes 9437184 | tf_op jit(solution)/shard_map/all_gather | solution.py:553
  10.7 235.0 %all-gather.8.cloned.1.call-start = ((), (), s32[]{:S(2)}) async-start(), calls=%async_computation.7 | async-start | bytes 9437184 | tf_op jit(solution)/shard_map/all_gather | solution.py:553
  13.0 790.0 %reduce-scatter.6.cloned.1.call-start = ((), (), s32[]{:S(2)}) async-start(), calls=%async_computation.8 | async-start | bytes 5242880 | tf_op jit(solution)/shard_map/reduce_scatter | solution.py:645
  58.6 47.2 %collective-permute-start.20 = (bf16[1024,512]{1,0:T(8,128)(2,1)S(1)}, bf16[1024,512]{1,0:T(8,128)(2,1)}, u32[]{:S(2)}, u32[]{:S(2)}) collective-permute-start(bf16[1024,512]{1,0:T(8,128)(2,1)S(1)} %constant_dynamic-slice_fusion.13), channel_id=1, source_target_pairs={{0,4},{4,0},{8,12},{12,8},{1,5},{5,1},{9,13},{13,9},{2,6},{6,2},{1... | collective-permute-start | bytes 3145736 | tf_op jit(solution)/shard_map/ppermute | solution.py:653
  60.1 45.8 %collective-permute-start.21 = (bf16[1024,512]{1,0:T(8,128)(2,1)S(1)}, bf16[1024,512]{1,0:T(8,128)(2,1)S(1)}, u32[]{:S(2)}, u32[]{:S(2)}) collective-permute-start(bf16[1024,512]{1,0:T(8,128)(2,1)S(1)} %constant_dynamic-slice_fusion.13), channel_id=1, source_target_pairs={{0,8},{8,0},{4,12},{12,4},{1,9},{9,1},{5,13},{13,5},{2,10},{10,2},... | collective-permute-start | bytes 3145736 | tf_op jit(solution)/shard_map/ppermute | solution.py:653
  60.6 73.9 %collective-permute-start.15 = (bf16[1024,512]{1,0:T(8,128)(2,1)S(1)}, bf16[1024,512]{1,0:T(8,128)(2,1)}, u32[]{:S(2)}, u32[]{:S(2)}) collective-permute-start(bf16[1024,512]{1,0:T(8,128)(2,1)S(1)} %pad_maximum_fusion.1), channel_id=1, source_target_pairs={{0,4},{4,0},{8,12},{12,8},{1,5},{5,1},{9,13},{13,9},{2,6},{6,2},{1... | collective-permute-start | bytes 3145736 | tf_op jit(solution)/shard_map/ppermute | solution.py:653
  61.9 75.6 %collective-permute-start.16 = (bf16[1024,512]{1,0:T(8,128)(2,1)S(1)}, bf16[1024,512]{1,0:T(8,128)(2,1)}, u32[]{:S(2)}, u32[]{:S(2)}) collective-permute-start(bf16[1024,512]{1,0:T(8,128)(2,1)S(1)} %pad_maximum_fusion.1), channel_id=1, source_target_pairs={{0,8},{8,0},{4,12},{12,4},{1,9},{9,1},{5,13},{13,5},{2,10},{10,2},... | collective-permute-start | bytes 3145736 | tf_op jit(solution)/shard_map/ppermute | solution.py:653
  106.9 46.6 %collective-permute-start.22 = (bf16[512,512]{1,0:T(8,128)(2,1)S(1)}, bf16[512,512]{1,0:T(8,128)(2,1)S(1)}, u32[]{:S(2)}, u32[]{:S(2)}) collective-permute-start(bf16[512,512]{1,0:T(8,128)(2,1)S(1)} %slice.73), channel_id=1, source_target_pairs={{0,8},{8,0},{4,12},{12,4},{1,9},{9,1},{5,13},{13,5},{2,10},{10,2},... | collective-permute-start | bytes 1572872 | tf_op jit(solution)/shard_map/ppermute | solution.py:661
  108.3 46.1 %collective-permute-start.23 = (bf16[512,512]{1,0:T(8,128)(2,1)S(1)}, bf16[512,512]{1,0:T(8,128)(2,1)S(1)}, u32[]{:S(2)}, u32[]{:S(2)}) collective-permute-start(bf16[512,512]{1,0:T(8,128)(2,1)S(1)} %slice.74), channel_id=1, source_target_pairs={{0,4},{4,0},{8,12},{12,8},{1,5},{5,1},{9,13},{13,9},{2,6},{6,2},{1... | collective-permute-start | bytes 1572872 | tf_op jit(solution)/shard_map/ppermute | solution.py:662
  155.2 90.5 %collective-permute-start.24 = (bf16[4,1024,512]{2,1,0:T(8,128)(2,1)}, bf16[4,1024,512]{2,1,0:T(8,128)(2,1)}, u32[]{:S(2)}, u32[]{:S(2)}) collective-permute-start(bf16[4,1024,512]{2,1,0:T(8,128)(2,1)} %bitcast_dynamic-update-slice_fusion.6.wd_own_ref), channel_id=1, source_target_pairs={{0,16},{16,0},{1,17},{17,1},{2,18},{18,2},{3,19},{19,3},{4,20},{20... | collective-permute-start | bytes 12582920 | tf_op jit(solution)/shard_map/ppermute | solution.py:678
  167.3 78.4 %collective-permute-start.19 = (bf16[4,1024,512]{2,1,0:T(8,128)(2,1)}, bf16[4,1024,512]{2,1,0:T(8,128)(2,1)}, u32[]{:S(2)}, u32[]{:S(2)}) collective-permute-start(bf16[4,1024,512]{2,1,0:T(8,128)(2,1)} %bitcast_dynamic-update-slice_fusion.8.wo_own_ref), channel_id=1, source_target_pairs={{0,16},{16,0},{1,17},{17,1},{2,18},{18,2},{3,19},{19,3},{4,20},{20... | collective-permute-start | bytes 12582920 | tf_op jit(solution)/shard_map/ppermute | solution.py:678
  330.6 30.5 %collective-permute-start.29 = (bf16[256,2048]{1,0:T(8,128)(2,1)}, bf16[256,2048]{1,0:T(8,128)(2,1)S(1)}, u32[]{:S(2)}, u32[]{:S(2)}) collective-permute-start(bf16[256,2048]{1,0:T(8,128)(2,1)} %get-tuple-element.434), channel_id=1, source_target_pairs={{0,1},{1,2},{2,3},{4,5},{5,6},{6,7},{8,9},{9,10},{10,11},{12,13},{... | collective-permute-start | bytes 3145736 | tf_op jit(solution)/shard_map/ppermute | solution.py:561
  364.2 31.0 %collective-permute-start.31 = (bf16[256,2048]{1,0:T(8,128)(2,1)S(1)}, bf16[256,2048]{1,0:T(8,128)(2,1)S(1)}, u32[]{:S(2)}, u32[]{:S(2)}) collective-permute-start(bf16[256,2048]{1,0:T(8,128)(2,1)S(1)} %add_convert_fusion.6.down_ref), channel_id=1, source_target_pairs={{0,1},{1,2},{2,3},{4,5},{5,6},{6,7},{8,9},{9,10},{10,11},{12,13},{... | collective-permute-start | bytes 3145736 | tf_op jit(solution)/shard_map/ppermute | solution.py:556
  396.0 28.4 %collective-permute-start.34 = (bf16[256,2048]{1,0:T(8,128)(2,1)S(1)}, bf16[256,2048]{1,0:T(8,128)(2,1)}, u32[]{:S(2)}, u32[]{:S(2)}) collective-permute-start(bf16[256,2048]{1,0:T(8,128)(2,1)S(1)} %collective-permute-done.32), channel_id=1, source_target_pairs={{1,0},{2,1},{5,4},{6,5},{9,8},{10,9},{13,12},{14,13},{17,16},{18,1... | collective-permute-start | bytes 3145736 | tf_op jit(solution)/shard_map/ppermute | solution.py:557
  424.4 29.7 %collective-permute-start.35 = (bf16[256,2048]{1,0:T(8,128)(2,1)S(1)}, bf16[256,2048]{1,0:T(8,128)(2,1)}, u32[]{:S(2)}, u32[]{:S(2)}) collective-permute-start(bf16[256,2048]{1,0:T(8,128)(2,1)S(1)} %collective-permute-done.33), channel_id=1, source_target_pairs={{2,3},{6,7},{10,11},{14,15},{18,19},{22,23},{26,27},{30,31}} | collective-permute-start | bytes 3145736 | tf_op jit(solution)/shard_map/ppermute | solution.py:556
  489.0 34.5 %collective-permute-start.40 = (bf16[2048,1024]{1,0:T(8,128)(2,1)S(1)}, bf16[2048,1024]{1,0:T(8,128)(2,1)S(1)}, u32[]{:S(2)}, u32[]{:S(2)}) collective-permute-start(bf16[2048,1024]{1,0:T(8,128)(2,1)S(1)} %convolution_convert_fusion.1), channel_id=1, source_target_pairs={{0,16},{16,0},{1,17},{17,1},{2,18},{18,2},{3,19},{19,3},{4,20},{20... | collective-permute-start | bytes 12582920 | tf_op jit(solution)/shard_map/ppermute | solution.py:641
  494.1 29.4 %collective-permute-start.39 = (bf16[2048,1024]{1,0:T(8,128)(2,1)S(1)}, bf16[2048,1024]{1,0:T(8,128)(2,1)S(1)}, u32[]{:S(2)}, u32[]{:S(2)}) collective-permute-start(bf16[2048,1024]{1,0:T(8,128)(2,1)S(1)} %convolution_convert_fusion.2), channel_id=1, source_target_pairs={{0,16},{16,0},{1,17},{17,1},{2,18},{18,2},{3,19},{19,3},{4,20},{20... | collective-permute-start | bytes 12582920 | tf_op jit(solution)/shard_map/ppermute | solution.py:641
  494.6 28.9 %collective-permute-start.37 = (bf16[256,2048]{1,0:T(8,128)(2,1)S(1)}, bf16[256,2048]{1,0:T(8,128)(2,1)S(1)}, u32[]{:S(2)}, u32[]{:S(2)}) collective-permute-start(bf16[256,2048]{1,0:T(8,128)(2,1)S(1)} %copy-done.21), channel_id=1, source_target_pairs={{0,1},{4,5},{8,9},{12,13},{16,17},{20,21},{24,25},{28,29}} | collective-permute-start | bytes 3145736 | tf_op jit(solution)/shard_map/ppermute | solution.py:561
  532.4 311.4 %reduce-scatter.8.cloned.1.call-start = ((), (), s32[]{:S(2)}) async-start(), calls=%async_computation.9 | async-start | bytes 5242880 | tf_op jit(solution)/shard_map/reduce_scatter | solution.py:645
  572.5 31.5 %collective-permute-start.44 = (bf16[256,2048]{1,0:T(8,128)(2,1)}, bf16[256,2048]{1,0:T(8,128)(2,1)S(1)}, u32[]{:S(2)}, u32[]{:S(2)}) collective-permute-start(bf16[256,2048]{1,0:T(8,128)(2,1)} %get-tuple-element.430), channel_id=1, source_target_pairs={{0,1},{1,2},{2,3},{4,5},{5,6},{6,7},{8,9},{9,10},{10,11},{12,13},{... | collective-permute-start | bytes 3145736 | tf_op jit(solution)/shard_map/ppermute | solution.py:561
  620.6 223.3 %reduce-scatter.12.cloned.1.call-start = ((), (), s32[]{:S(2)}) async-start(), calls=%async_computation.11 | async-start | bytes 1310720 | tf_op jit(solution)/shard_map/reduce_scatter | solution.py:645
  802.2 85.5 %reduce-scatter.10.cloned.1.call-start = ((), (), s32[]{:S(2)}) async-start(), calls=%async_computation.10 | async-start | bytes 5242880 | tf_op jit(solution)/shard_map/reduce_scatter | solution.py:645
  803.0 131.7 %reduce-scatter.14.cloned.1.call-start = ((), (), s32[]{:S(2)}) async-start(), calls=%async_computation.12 | async-start | bytes 3932160 | tf_op jit(solution)/shard_map/reduce_scatter | solution.py:645
  803.7 29.1 %collective-permute-start.66 = (bf16[256,2048]{1,0:T(8,128)(2,1)}, bf16[256,2048]{1,0:T(8,128)(2,1)S(1)}, u32[]{:S(2)}, u32[]{:S(2)}) collective-permute-start(bf16[256,2048]{1,0:T(8,128)(2,1)} %get-tuple-element.426), channel_id=1, source_target_pairs={{0,1},{1,2},{2,3},{4,5},{5,6},{6,7},{8,9},{9,10},{10,11},{12,13},{... | collective-permute-start | bytes 3145736 | tf_op jit(solution)/shard_map/ppermute | solution.py:561
  843.8 48.1 %collective-permute-start.76 = (bf16[512,1024]{1,0:T(8,128)(2,1)}, bf16[512,1024]{1,0:T(8,128)(2,1)S(1)}, u32[]{:S(2)}, u32[]{:S(2)}) collective-permute-start(bf16[512,1024]{1,0:T(8,128)(2,1)} %reduce-scatter.8.cloned.1.call-done), channel_id=1, source_target_pairs={{0,16},{16,0},{1,17},{17,1},{2,18},{18,2},{3,19},{19,3},{4,20},{20... | collective-permute-start | bytes 3145736 | tf_op jit(solution)/shard_map/ppermute | solution.py:635
  845.6 42.1 %collective-permute-start.77 = (bf16[256,1024]{1,0:T(8,128)(2,1)}, bf16[256,1024]{1,0:T(8,128)(2,1)}, u32[]{:S(2)}, u32[]{:S(2)}) collective-permute-start(bf16[256,1024]{1,0:T(8,128)(2,1)} %get-tuple-element.360), channel_id=1, source_target_pairs={{0,1},{1,2},{2,3},{4,5},{5,6},{6,7},{8,9},{9,10},{10,11},{12,13},{... | collective-permute-start | bytes 1572872 | tf_op jit(solution)/shard_map/ppermute | solution.py:556
  854.7 32.9 %collective-permute-start.78 = (bf16[256,1024]{1,0:T(8,128)(2,1)}, bf16[256,1024]{1,0:T(8,128)(2,1)}, u32[]{:S(2)}, u32[]{:S(2)}) collective-permute-start(bf16[256,1024]{1,0:T(8,128)(2,1)} %get-tuple-element.360), channel_id=1, source_target_pairs={{1,0},{2,1},{3,2},{5,4},{6,5},{7,6},{9,8},{10,9},{11,10},{13,12},{... | collective-permute-start | bytes 1572872 | tf_op jit(solution)/shard_map/ppermute | solution.py:557
  857.4 31.8 %collective-permute-start.71 = (bf16[256,1024]{1,0:T(8,128)(2,1)S(1)}, bf16[256,1024]{1,0:T(8,128)(2,1)}, u32[]{:S(2)}, u32[]{:S(2)}) collective-permute-start(bf16[256,1024]{1,0:T(8,128)(2,1)S(1)} %collective-permute-done.69), channel_id=1, source_target_pairs={{1,2},{2,3},{5,6},{6,7},{9,10},{10,11},{13,14},{14,15},{17,18},{18... | collective-permute-start | bytes 1572872 | tf_op jit(solution)/shard_map/ppermute | solution.py:556
  858.9 31.6 %collective-permute-start.72 = (bf16[256,1024]{1,0:T(8,128)(2,1)S(1)}, bf16[256,1024]{1,0:T(8,128)(2,1)}, u32[]{:S(2)}, u32[]{:S(2)}) collective-permute-start(bf16[256,1024]{1,0:T(8,128)(2,1)S(1)} %collective-permute-done.70), channel_id=1, source_target_pairs={{1,0},{2,1},{5,4},{6,5},{9,8},{10,9},{13,12},{14,13},{17,16},{18,1... | collective-permute-start | bytes 1572872 | tf_op jit(solution)/shard_map/ppermute | solution.py:557
  890.4 57.6 %collective-permute-start.73 = (bf16[256,1024]{1,0:T(8,128)(2,1)}, bf16[256,1024]{1,0:T(8,128)(2,1)}, u32[]{:S(2)}, u32[]{:S(2)}) collective-permute-start(bf16[256,1024]{1,0:T(8,128)(2,1)} %collective-permute-done.71), channel_id=1, source_target_pairs={{2,3},{6,7},{10,11},{14,15},{18,19},{22,23},{26,27},{30,31}} | collective-permute-start | bytes 1572872 | tf_op jit(solution)/shard_map/ppermute | solution.py:556
  892.9 55.1 %collective-permute-start.74 = (bf16[256,1024]{1,0:T(8,128)(2,1)}, bf16[256,1024]{1,0:T(8,128)(2,1)}, u32[]{:S(2)}, u32[]{:S(2)}) collective-permute-start(bf16[256,1024]{1,0:T(8,128)(2,1)} %collective-permute-done.72), channel_id=1, source_target_pairs={{1,0},{5,4},{9,8},{13,12},{17,16},{21,20},{25,24},{29,28}} | collective-permute-start | bytes 1572872 | tf_op jit(solution)/shard_map/ppermute | solution.py:557
  (115 other events, 1738.0 us)
Sparse Core Ops, SparseCore 0:
  10.5 48.1 all-gather.3
  61.1 88.1 all-gather.5
  151.7 54.9 all-gather.7
  532.5 53.8 reduce-scatter.5
  620.7 51.1 reduce-scatter.7
  802.3 29.6 reduce-scatter.11
  835.0 52.5 reduce-scatter.9
  890.6 43.9 reduce-scatter.13

commit v6 on v5

--- a/solution.py
+++ b/solution.py
@@ -208,14 +208,26 @@
 
 
 def forward_chunk_kernel(
-    idx_ref, att_ref, wo_own_ref, wo_oth_ref, x_ref, gain_ref, wg_ref, wu_ref, wd_own_ref, wd_oth_ref, *refs,
-    blocks, tiles,
+    idx_ref, *refs, blocks, tiles,
 ):
-    raw_ref, scale_ref, hb_ref, gate_ref, up_ref, mixed_ref, part_ref, acc_ref = refs[-8:]
+    own_ref, left1, left2, left3, right1, right2, right3 = refs[:7]
+    wo_own_ref, wo_oth_ref, x_ref, gain_ref, wg_ref, wu_ref, wd_own_ref, wd_oth_ref = refs[7:15]
+    raw_ref, scale_ref, hb_ref, gate_ref, up_ref, mixed_ref, part_ref, acc_ref, att_ref = refs[-9:]
     block = wo_own_ref.shape[2]
     depth = wo_own_ref.shape[1]
     step = pl.program_id(0)
     core = idx_ref[1]
+
+    @pl.when(step == 0)
+    def _():
+        quarter = own_ref.shape[1] // 2
+        pieces = (
+            own_ref[...], right1[...] + left3[...], right2[...] + left2[...], right3[...] + left1[...],
+        )
+        for half in range(2):
+            for number, piece in enumerate(pieces):
+                start = half * depth + number * quarter
+                att_ref[:, start : start + quarter] = piece[:, half * quarter : (half + 1) * quarter]
 
     @pl.when(step < blocks)
     def _():
@@ -257,7 +269,7 @@
         part_ref[...] = acc_ref[...].astype(BF16)
 
 
-TILE = 256
+TILE = 512
 
 
 def forward_chunk(index, attended, out_halves, block_input, gain, w_gate, w_up, down_halves, chunk, before):
@@ -286,7 +298,7 @@
             num_scalar_prefetch=1,
             grid=(blocks + tiles,),
             in_specs=[
-                pl.BlockSpec((chunk, attended.shape[1]), lambda j, idx: (idx[0], 0)),
+                *[pl.BlockSpec((chunk, attended[0].shape[1]), lambda j, idx: (idx[0], 0))] * 7,
                 out_half, out_half, rows, pl.BlockSpec((1, width), lambda j, idx: (0, 0)),
                 up_tile, up_tile, down_own, down_oth,
             ] + [pl.BlockSpec(memory_space=pl.ANY)] * len(before),
@@ -294,7 +306,7 @@
                 rows, pl.BlockSpec((chunk, 1), lambda j, idx: (idx[0], 0)), rows, act_tile, act_tile, act_tile,
                 pl.BlockSpec((chunk, width), lambda j, idx: (0, 0)),
             ],
-            scratch_shapes=[pltpu.VMEM((chunk, width), F32)],
+            scratch_shapes=[pltpu.VMEM((chunk, width), F32), pltpu.VMEM((chunk, 2 * depth), BF16)],
         ),
         out_shape=[
             jax.ShapeDtypeStruct((tokens, width), F32),
@@ -305,7 +317,7 @@
             jax.ShapeDtypeStruct((tokens, hidden), BF16),
             jax.ShapeDtypeStruct((chunk, width), BF16),
         ],
-        input_output_aliases={10 + i: i for i in range(len(before))},
+        input_output_aliases={16 + i: i for i in range(len(before))},
         compiler_params=pltpu.CompilerParams(vmem_limit_bytes=VMEM),
         cost_estimate=pl.CostEstimate(
             flops=2 * chunk * width * (width + 3 * hidden),
@@ -313,7 +325,7 @@
             transcendentals=0,
         ),
         name="forward_chunk",
-    )(index, attended, *out_halves, block_input, gain, w_gate, w_up, *down_halves, *before)
+    )(index, *attended, *out_halves, block_input, gain, w_gate, w_up, *down_halves, *before)
 
 
 def backward_chunk_kernel(
@@ -574,61 +586,39 @@
         return lax.dynamic_slice_in_dim(array, slot_chunk[slot] * chunk, chunk, 0)
 
     def gather_slots(own, work):
-        left1, right1 = line_step(own, own, 1)
-        left1, right1 = after((left1, right1), work(3, own))
-        left2, right2 = line_step(left1, right1, 2)
-        left2, right2 = after((left2, right2), work(2, jnp.where(col % 2 == 0, right1, left1)))
-        left3, right3 = line_step(left2, right2, 3)
-        left3, right3 = after((left3, right3), work(1, pick(right2, right1, left1, left2)))
-        return work(0, pick(right3, right2, left2, left3))
-
-    def gather_halves(own, work):
-        half = own.shape[1] // 2
-        left, right, token = {}, {}, ()
-        for part in range(2):
-            left[part, 0] = right[part, 0] = own[:, part * half : (part + 1) * half]
+        left, right, token = [own], [own], ()
         arrived = (
             lambda lefts, rights: lefts[0],
             lambda lefts, rights: jnp.where(col % 2 == 0, rights[1], lefts[1]),
             lambda lefts, rights: pick(rights[2], rights[1], lefts[1], lefts[2]),
             lambda lefts, rights: pick(rights[3], rights[2], lefts[2], lefts[3]),
         )
-
-        def slot_of(step, token):
-            halves = []
-            for part in range(2):
-                seen = tuple((left[part, k], right[part, k]) for k in range(step))
-                seen = after(seen, token)
-                halves.append(arrived[step - 1]([one[0] for one in seen], [one[1] for one in seen]))
-            return jnp.concatenate(halves, axis=1)
-
-        for step in range(1, cols):
-            for part in range(2):
-                sent = (left[part, step - 1], right[part, step - 1])
-                left[part, step], right[part, step] = line_step(*sent, step)
-            token = work(cols - step, slot_of(step, token))
-        return work(0, slot_of(cols, token))
+        for step in range(1, cols + 1):
+            seen = tuple(left), tuple(right)
+            if step < cols:
+                from_left, from_right = line_step(left[-1], right[-1], step)
+                left.append(from_left)
+                right.append(from_right)
+            token = work(cols - step, arrived[step - 1](*after(seen, token)))
 
     def sum_slots(make, window=lambda step, gate: ()):
         def at(step, gate):
-            return make(step, gate), window(step, gate)
+            window(step, gate)
+            return make(step, gate)
 
         first = make(0, ())
         up, down = sum_step(first, first, 1)
-        second, extra = at(1, first)
-        up, down = after((up, down), second, extra)
+        second = at(1, first)
         up = jnp.where(col == 0, second, first) + up
         down = jnp.where(col == 3, second, first) + down
         gate = (up, down)
         up, down = sum_step(up, down, 2)
-        third, extra = at(2, gate)
-        up, down = after((up, down), third, extra)
+        third = at(2, gate)
         up = jnp.where(col == 1, second, third) + up
         down = jnp.where(col == 2, second, third) + down
         gate = (up, down)
         up, down = sum_step(up, down, 3)
-        fourth, extra = at(3, gate)
-        up, down = after((up, down), fourth, extra)
+        fourth = at(3, gate)
         return fourth.astype(F32) + up.astype(F32) + down.astype(F32)
 
     def both_cores(half, axis):
@@ -708,27 +698,18 @@
         qkv, scales, gains, tables, seg_col, seg_row, heads
     )
 
-    steps_from = {}
-    for part in range(cores):
-        steps_from[part] = [(attended[:, part * half_width : (part + 1) * half_width],) * 2]
+    lefts, rights = [attended], [attended]
     for step in range(1, cols):
-        for part in range(cores):
-            sent = steps_from[part][-1]
-            steps_from[part].append(line_step(*sent, step))
+        from_left, from_right = line_step(lefts[-1], rights[-1], step)
+        lefts.append(from_left)
+        rights.append(from_right)
         if step == 1:
             down_pieces = row_second(after(down_pieces, attended))
             out_pieces = row_second(after(out_pieces, attended))
+            out_halves = row_blocks(out_pieces)
+        if step == 2:
             down_halves = row_blocks(down_pieces)
-        if step == 2:
-            out_halves = row_blocks(out_pieces)
-    attended_all = jnp.concatenate(
-        [
-            steps_from[part][0][0] if step == 0 else steps_from[part][step][1] + steps_from[part][cols - step][0]
-            for part in range(cores)
-            for step in range(cols)
-        ],
-        axis=1,
-    )
+    attended_all = (attended, *lefts[1:], *rights[1:])
 
     held = dict(forward=(), backward=(), attention=(), output=())
     gain_sums = dict(mlp=0.0, attn=0.0)
@@ -774,8 +755,7 @@
             got["up"] = sum_sent(hidden_left, other_half(up_right, 1))
             return blocks["down"][0], got["up"]
         blocks["gate"] = sum_kept(hidden_left, own_half(gate_right, 1), got["gate"])
-        blocks["up"] = sum_kept(hidden_left, own_half(up_right, 1), got["up"])
-        return blocks["gate"][0], blocks["up"][0]
+        return blocks["gate"][0]
 
     mlp_own = sum_slots(lambda slot, gate: mlp_parts[slot], mlp_window).astype(BF16)
 
@@ -786,9 +766,12 @@
         )
         held["attention"] = results[:2]
         gain_sums["attn"] = gain_sums["attn"] + results[2]
+        if slot == 3:
+            hidden_left, up_right = after((hidden_b, grad_up_in), mlp_rows)
+            blocks["up"] = sum_kept(hidden_left, own_half(up_right, 1), got["up"])
         return results[1]
 
-    gather_halves(mlp_own, attention_work)
+    gather_slots(mlp_own, attention_work)
     grad_attn_in, grad_att = held["attention"]
     own_grad_hidden = slot_rows(grad_output, 3).astype(F32) + mlp_own.astype(F32)
 
@@ -854,7 +837,7 @@
             return held["output"], results["out"], results["qkv"]
         return held["output"]
 
-    gather_halves((own_grad_hidden + input_own).astype(BF16), output_work)
+    gather_slots((own_grad_hidden + input_own).astype(BF16), output_work)
     ends = (local_width, 2 * local_width, 2 * local_width + width)
     gain_grads = jnp.split(gain_pack[0], ends)
     return (

time: 984 us -> 980 us (level)
  waiting for transfers between devices: 305 us -> 396 us
  starting transfers between devices: 145 us -> 104 us
  other arithmetic: 87.5 us -> 62.4 us
  Pallas kernels: 265 us -> 245 us
    ppermute x21 -> x12, waiting for transfers between devices: 20.3 us -> 52.9 us  [line_step(): lax.ppermute(from_left, 'col', [(i, i + 1) for i in range(step - 1, cols...]
    ppermute x2, waiting for transfers between devices: 25.4 us -> 0.01 us  [row_first(): lax.ppermute(half, 'row', by_x)]
    ppermute x2, waiting for transfers between devices: 2.91 us -> 27.2 us  [row_first(): lax.ppermute(half, 'row', by_y)]
    reduce_scatter x5, waiting for transfers between devices: 45.7 us -> 66.7 us  [sum_kept(): lax.psum_scatter(total, 'row', scatter_dimension=0, tiled=True)]
    ppermute x21 -> x12, starting transfers between devices: 44.2 us -> 24.9 us  [line_step(): lax.ppermute(from_left, 'col', [(i, i + 1) for i in range(step - 1, cols...]
    pallas_call x4, Pallas kernels: 97.1 us -> 80.8 us  [backward_chunk(): pl.pallas_call(functools.partial(backward_chunk_kernel, blocks=blocks, ti...]
    ppermute x21 -> x12, waiting for transfers between devices: 77.9 us -> 93.2 us  [line_step(): lax.ppermute(from_right, 'col', [(i + 1, i) for i in range(cols - step)])]
    ppermute x5, waiting for transfers between devices: 0.01 us -> 14.2 us  [sum_sent(): lax.ppermute(left_transposed(left_mat, right_other).astype(BF16), 'dp', s...]
  transfers between devices with their start and end apart: 96 -> 78, of which waited for: 37 -> 33; matrix products, arithmetic and copies ran while one was open for 19% -> 15% of each run, Pallas kernels for 22% -> 18%
where the time goes in v6:
time: 980 us; the launch traced here: 969 us
  waiting for transfers between devices  396 us (40%)
  Pallas kernels  245 us (25%)
  starting transfers between devices  104 us (11%)
  matrix products  81.6 us (8%)
  other arithmetic  62.4 us (6%)
  local copies, waits for them, and re-layouts  41.9 us (4%)
  blocking collectives  22.3 us (2%)
  between operations  15.9 us (2%)
    pallas_call x4, Pallas kernels, forward_chunk(): pl.pallas_call(functools.partial(forward_chunk_kernel, blocks=blocks, til...  94.1 us
    ppermute x12, waiting for transfers between devices, line_step(): lax.ppermute(from_right, 'col', [(i + 1, i) for i in range(cols - step)])  93.2 us
    pallas_call x4, Pallas kernels, backward_chunk(): pl.pallas_call(functools.partial(backward_chunk_kernel, blocks=blocks, ti...  80.8 us
    ppermute x9, waiting for transfers between devices, sum_step(): up = lax.ppermute(up, 'col', [(i, i + 1) for i in range(step)])  80.2 us
    reduce_scatter x5, waiting for transfers between devices, sum_kept(): lax.psum_scatter(total, 'row', scatter_dimension=0, tiled=True)  66.7 us
    dot_general x10, matrix products, left_transposed(): lax.dot_general(left_mat, right_mat, (((0,), (0,)), ((), ())), preferred_...  59.7 us
    ppermute x12, waiting for transfers between devices, line_step(): lax.ppermute(from_left, 'col', [(i, i + 1) for i in range(step - 1, cols...  52.9 us
    ppermute x9, starting transfers between devices, sum_step(): up = lax.ppermute(up, 'col', [(i, i + 1) for i in range(step)])  34.7 us
  transfers between devices with their start and end apart: 78, of which 33 were waited for; matrix products, arithmetic and copies ran while one was open for 15% of the time, Pallas kernels for 18%

profile of v6, /device:TPU:0, one launch (start us, length us, event | category | flops | bytes accessed | tf_op | source)
XLA Modules:
  0.0 968.8 jit_solution(8232288803959159582)
XLA Ops:
  25.0 15.6 %collective-permute-done.7 = bf16[256,512]{1,0:T(8,128)(2,1)S(1)} collective-permute-done((bf16[256,512]{1,0:T(8,128)(2,1)S(1)}, bf16[256,512]{1,0:T(8,128)(2,1)S(1)}, u32[]{:S(2)}, u32[]{:S(2)}) %collective-permute-start.7) | collective-permute-done | bytes 262176 | tf_op jit(solution)/shard_map/ppermute | solution.py:677
  40.7 17.9 %all-gather.4.cloned.1.call-done = bf16[2048,1536]{1,0:T(8,128)(2,1)} async-done(((bf16[256,1536]{1,0:T(8,128)(2,1)}), bf16[2048,1536]{1,0:T(8,128)(2,1)}) %all-gather.4.cloned.1.call-update) | async-done | bytes 6291472 | tf_op jit(solution)/shard_map/all_gather | solution.py:565
  62.7 10.0 %convolution_bitcast_fusion.q_ref.k_ref.v_ref = f32[1024,1536]{1,0:T(8,128)S(1)} fusion(bf16[1024,2048]{1,0:T(8,128)(2,1)} %x_ref.7, bf16[2048,1536]{1,0:T(8,128)(2,1)} %all-gather.4.cloned.1.call-done), kind=kOutput, calls=%fused_computation.4 | convolution fusion | flops 6442450944 | bytes 16777216 | tf_op jit(solution)/shard_map/dot_general | solution.py:25
  75.7 11.8 %all-reduce.1 = (f32[1024]{0:T(1024)S(1)}, f32[1024]{0:T(1024)S(1)}) all-reduce(f32[1024]{0:T(1024)S(1)} %get-tuple-element.390, f32[1024]{0:T(1024)S(1)} %get-tuple-element.389), channel_id=1, replica_groups=mesh['dp'=2,'row'=4,'col'=4] {'col'}, use_global_device_ids=true, to_apply=%region_1.2 | all-reduce | flops 2048 | bytes 16384 | tf_op jit(solution)/shard_map/psum | solution.py:688
  89.7 16.1 %attend_forward.1 = (bf16[1024,512]{1,0:T(8,128)(2,1)}, bf16[1024,512]{1,0:T(8,128)(2,1)}, bf16[1024,512]{1,0:T(8,128)(2,1)}, bf16[1024,512]{1,0:T(8,128)(2,1)}, f32[4,1024,1]{2,1,0:T(8,128)}) custom-call(f32[1024,1536]{1,0:T(8,128)} %copy-done.3, f32[1024,1536]{1,0:T(8,128)} %copy-done.3, f32[1024,1536]{1,0:T(8,128)} %copy-done.3, f32[1024,1]{1,0:T(8,128)} %copy.71.qs_ref, ...), custom_call_target="tpu_custom_call" | custom-call | flops 2147483648 | bytes 10485760 | tf_op jit(solution)/shard_map/attend_forward/pallas_call | solution.py:156
  110.2 27.2 %collective-permute-done.10 = bf16[1024,512]{1,0:T(8,128)(2,1)S(1)} collective-permute-done((bf16[1024,512]{1,0:T(8,128)(2,1)S(1)}, bf16[1024,512]{1,0:T(8,128)(2,1)S(1)}, u32[]{:S(2)}, u32[]{:S(2)}) %collective-permute-start.10) | collective-permute-done | bytes 1048608 | tf_op jit(solution)/shard_map/ppermute | solution.py:643
  155.2 10.5 %collective-permute-done.11 = bf16[512,512]{1,0:T(8,128)(2,1)S(1)} collective-permute-done((bf16[512,512]{1,0:T(8,128)(2,1)S(1)}, bf16[512,512]{1,0:T(8,128)(2,1)S(1)}, u32[]{:S(2)}, u32[]{:S(2)}) %collective-permute-start.11) | collective-permute-done | bytes 524320 | tf_op jit(solution)/shard_map/ppermute | solution.py:651
  172.1 21.7 %collective-permute-done.refs_1_ = bf16[1024,512]{1,0:T(8,128)(2,1)S(1)} collective-permute-done((bf16[1024,512]{1,0:T(8,128)(2,1)S(1)}, bf16[1024,512]{1,0:T(8,128)(2,1)S(1)}, u32[]{:S(2)}, u32[]{:S(2)}) %collective-permute-start) | collective-permute-done | bytes 1048608 | tf_op jit(solution)/shard_map/ppermute | solution.py:568
  201.1 24.2 %collective-permute-done.4.refs_5_ = bf16[1024,512]{1,0:T(8,128)(2,1)S(1)} collective-permute-done((bf16[1024,512]{1,0:T(8,128)(2,1)S(1)}, bf16[1024,512]{1,0:T(8,128)(2,1)S(1)}, u32[]{:S(2)}, u32[]{:S(2)}) %collective-permute-start.4) | collective-permute-done | bytes 1048608 | tf_op jit(solution)/shard_map/ppermute | solution.py:569
  227.2 24.0 %collective-permute-done.5.refs_6_ = bf16[1024,512]{1,0:T(8,128)(2,1)} collective-permute-done((bf16[1024,512]{1,0:T(8,128)(2,1)S(1)}, bf16[1024,512]{1,0:T(8,128)(2,1)}, u32[]{:S(2)}, u32[]{:S(2)}) %collective-permute-start.5) | collective-permute-done | bytes 1048608 | tf_op jit(solution)/shard_map/ppermute | solution.py:569
  251.3 23.5 %forward_chunk.4 = (f32[1024,2048]{1,0:T(8,128)}, f32[1024,1]{1,0:T(8,128)}, bf16[1024,2048]{1,0:T(8,128)(2,1)}, bf16[1024,2048]{1,0:T(8,128)(2,1)}, bf16[1024,2...) custom-call(s32[2]{0:T(128)} %get-tuple-element.448.idx_ref, ...), custom_call_target="tpu_custom_call" | custom-call | flops 8589934592 | bytes 33554432 | tf_op jit(solution)/shard_map/forward_chunk/pallas_call | solution.py:295
  277.0 23.6 %forward_chunk.5 = (f32[1024,2048]{1,0:T(8,128)}, f32[1024,1]{1,0:T(8,128)}, bf16[1024,2048]{1,0:T(8,128)(2,1)}, bf16[1024,2048]{1,0:T(8,128)(2,1)}, bf16[1024,2...) custom-call(s32[2]{0:T(128)} %get-tuple-element.449.idx_ref, ...), custom_call_target="tpu_custom_call", output_to_operand_aliasing={{0}: (16, {}), {1}: (17, {}), {2}: (18, {}), {3}: (19, {}),... | custom-call | flops 8589934592 | bytes 33554432 | tf_op jit(solution)/shard_map/forward_chunk/pallas_call | solution.py:295
  308.2 23.6 %forward_chunk.6 = (f32[1024,2048]{1,0:T(8,128)}, f32[1024,1]{1,0:T(8,128)}, bf16[1024,2048]{1,0:T(8,128)(2,1)}, bf16[1024,2048]{1,0:T(8,128)(2,1)}, bf16[1024,2...) custom-call(s32[2]{0:T(128)} %pad_add_fusion.3.idx_ref, ...), custom_call_target="tpu_custom_call", output_to_operand_aliasing={{0}: (16, {}), {1}: (17, {}), {2}: (18, {}), {3}: (19, {}),... | custom-call | flops 8589934592 | bytes 33554432 | tf_op jit(solution)/shard_map/forward_chunk/pallas_call | solution.py:295
  338.0 23.5 %forward_chunk.7 = (f32[1024,2048]{1,0:T(8,128)}, f32[1024,1]{1,0:T(8,128)}, bf16[1024,2048]{1,0:T(8,128)(2,1)}, bf16[1024,2048]{1,0:T(8,128)(2,1)}, bf16[1024,2...) custom-call(s32[2]{0:T(128)} %pad_add_fusion.1.idx_ref, ...), custom_call_target="tpu_custom_call", output_to_operand_aliasing={{0}: (16, {}), {1}: (17, {}), {2}: (18, {}), {3}: (19, {}),... | custom-call | flops 8589934592 | bytes 33554432 | tf_op jit(solution)/shard_map/forward_chunk/pallas_call | solution.py:295
  371.4 20.1 %backward_chunk.4 = (bf16[1024,2048]{1,0:T(8,128)(2,1)}, bf16[1024,2048]{1,0:T(8,128)(2,1)}, bf16[1024,2048]{1,0:T(8,128)(2,1)}, bf16[1024,2048]{1,0:T(8,128)(2,...) custom-call(s32[2]{0:T(128)} %pad_add_fusion.1.idx_ref, bf16[256,2048]{1,0:T(8,128)(2,1)} %copy-done.18, ...), custom_call_target="tpu_custom_call" | custom-call | flops 6442450944 | bytes 25165824 | tf_op jit(solution)/shard_map/backward_chunk/pallas_call | solution.py:397
  397.5 20.1 %backward_chunk.5 = (bf16[1024,2048]{1,0:T(8,128)(2,1)}, bf16[1024,2048]{1,0:T(8,128)(2,1)}, bf16[1024,2048]{1,0:T(8,128)(2,1)}, bf16[1024,2048]{1,0:T(8,128)(2,...) custom-call(s32[2]{0:T(128)} %pad_add_fusion.3.idx_ref, ...), custom_call_target="tpu_custom_call", output_to_operand_aliasing={{0}: (14, {}), {1}: (15, {}), {2}: (16, {}), {3}: (17, {})} | custom-call | flops 6442450944 | bytes 25165824 | tf_op jit(solution)/shard_map/backward_chunk/pallas_call | solution.py:397
  425.2 20.1 %backward_chunk.6 = (bf16[1024,2048]{1,0:T(8,128)(2,1)}, bf16[1024,2048]{1,0:T(8,128)(2,1)}, bf16[1024,2048]{1,0:T(8,128)(2,1)}, bf16[1024,2048]{1,0:T(8,128)(2,...) custom-call(s32[2]{0:T(128)} %get-tuple-element.449.idx_ref, ...), custom_call_target="tpu_custom_call", output_to_operand_aliasing={{0}: (14, {}), {1}: (15, {}), {2}: (16, {}), {3}: (17, {})} | custom-call | flops 6442450944 | bytes 25165824 | tf_op jit(solution)/shard_map/backward_chunk/pallas_call | solution.py:397
  448.1 20.5 %backward_chunk.7 = (bf16[1024,2048]{1,0:T(8,128)(2,1)}, bf16[1024,2048]{1,0:T(8,128)(2,1)}, bf16[1024,2048]{1,0:T(8,128)(2,1)}, bf16[1024,2048]{1,0:T(8,128)(2,...) custom-call(s32[2]{0:T(128)} %get-tuple-element.448.idx_ref, ...), custom_call_target="tpu_custom_call", output_to_operand_aliasing={{0}: (14, {}), {1}: (15, {}), {2}: (16, {}), {3}: (17, {})} | custom-call | flops 6442450944 | bytes 25165824 | tf_op jit(solution)/shard_map/backward_chunk/pallas_call | solution.py:397
  473.8 17.6 %collective-permute-done.31 = bf16[256,2048]{1,0:T(8,128)(2,1)S(1)} collective-permute-done((bf16[256,2048]{1,0:T(8,128)(2,1)}, bf16[256,2048]{1,0:T(8,128)(2,1)S(1)}, u32[]{:S(2)}, u32[]{:S(2)}) %collective-permute-start.31) | collective-permute-done | bytes 1048608 | tf_op jit(solution)/shard_map/ppermute | solution.py:573
  498.3 16.5 %collective-permute-done.32 = bf16[256,2048]{1,0:T(8,128)(2,1)S(1)} collective-permute-done((bf16[256,2048]{1,0:T(8,128)(2,1)S(1)}, bf16[256,2048]{1,0:T(8,128)(2,1)S(1)}, u32[]{:S(2)}, u32[]{:S(2)}) %collective-permute-start.32) | collective-permute-done | bytes 1048608 | tf_op jit(solution)/shard_map/ppermute | solution.py:573
  515.1 9.7 %collective-permute-start.33 = (bf16[256,2048]{1,0:T(8,128)(2,1)S(1)}, bf16[256,2048]{1,0:T(8,128)(2,1)S(1)}, u32[]{:S(2)}, u32[]{:S(2)}) collective-permute-start(bf16[256,2048]{1,0:T(8,128)(2,1)S(1)} %get-tuple-element.411), channel_id=1, source_target_pairs={{0,1},{1,2},{2,3},{4,5},{5,6},{6,7},{8,9},{9,10},{10,11},{12,13},{... | collective-permute-start | bytes 3145736 | tf_op jit(solution)/shard_map/ppermute | solution.py:573
  526.1 15.2 %collective-permute-done.33 = bf16[256,2048]{1,0:T(8,128)(2,1)S(1)} collective-permute-done((bf16[256,2048]{1,0:T(8,128)(2,1)S(1)}, bf16[256,2048]{1,0:T(8,128)(2,1)S(1)}, u32[]{:S(2)}, u32[]{:S(2)}) %collective-permute-start.33) | collective-permute-done | bytes 1048608 | tf_op jit(solution)/shard_map/ppermute | solution.py:573
  549.6 14.4 %collective-permute-done.37 = bf16[256,2048]{1,0:T(8,128)(2,1)S(1)} collective-permute-done((bf16[256,2048]{1,0:T(8,128)(2,1)S(1)}, bf16[256,2048]{1,0:T(8,128)(2,1)S(1)}, u32[]{:S(2)}, u32[]{:S(2)}) %collective-permute-start.37) | collective-permute-done | bytes 1048608 | tf_op jit(solution)/shard_map/ppermute | solution.py:568
  579.4 15.2 %collective-permute-done.41 = bf16[256,2048]{1,0:T(8,128)(2,1)} collective-permute-done((bf16[256,2048]{1,0:T(8,128)(2,1)S(1)}, bf16[256,2048]{1,0:T(8,128)(2,1)}, u32[]{:S(2)}, u32[]{:S(2)}) %collective-permute-start.41) | collective-permute-done | bytes 1048608 | tf_op jit(solution)/shard_map/ppermute | solution.py:569
  621.4 17.9 %attend_backward.1 = (f32[1024,512]{1,0:T(8,128)}, f32[1024,512]{1,0:T(8,128)}, bf16[1024,512]{1,0:T(8,128)(2,1)}, f32[1024,1]{1,0:T(8,128)}, f32[1024,1]{1,0:T(...) custom-call(f32[1024,1536]{1,0:T(8,128)} %copy-done.3, f32[1024,1536]{1,0:T(8,128)} %copy-done.3, f32[1024,1]{1,0:T(8,128)} %copy.71.qs_ref, ...), custom_call_target="tpu_custom_call" | custom-call | flops 5368709120 | bytes 20971520 | tf_op jit(solution)/shard_map/attend_backward/pallas_call | solution.py:180
  641.8 10.5 %all-reduce = (f32[1024]{0:T(1024)S(1)}, f32[1024]{0:T(1024)S(1)}) all-reduce(f32[1024]{0:T(1024)S(1)} %reduce.1, f32[1024]{0:T(1024)S(1)} %reduce), channel_id=1, replica_groups=mesh['dp'=2,'row'=4,'col'=4] {'col'}, use_global_device_ids=true, to_apply=%region_5.6 | all-reduce | flops 2048 | bytes 16384 | tf_op jit(solution)/shard_map/psum | solution.py:782
  701.6 10.6 %add_convert_fusion.2 = bf16[2048,1024]{1,0:T(8,128)(2,1)} fusion(bf16[2048,1024]{1,0:T(8,128)(2,1)} %collective-permute-done.55, bf16[1024,2048]{1,0:T(8,128)(2,1)} %get-tuple-element.315, bf16[1024,2048]{1,0:T(8,128)(2,1)} %get-tuple-element.316, s32[]{:T(128)S(6)} %select_n.310), kind=kOutput, calls=%fused_computation.2 | convolution fusion | flops 4301258752 | bytes 14680068 | tf_op jit(solution)/shard_map/dot_general | solution.py:35
  775.0 16.6 %collective-permute-done.47 = bf16[256,2048]{1,0:T(8,128)(2,1)S(1)} collective-permute-done((bf16[256,2048]{1,0:T(8,128)(2,1)}, bf16[256,2048]{1,0:T(8,128)(2,1)S(1)}, u32[]{:S(2)}, u32[]{:S(2)}) %collective-permute-start.47) | collective-permute-done | bytes 1048608 | tf_op jit(solution)/shard_map/ppermute | solution.py:573
  810.4 16.8 %collective-permute-done.49 = bf16[256,2048]{1,0:T(8,128)(2,1)S(1)} collective-permute-done((bf16[256,2048]{1,0:T(8,128)(2,1)}, bf16[256,2048]{1,0:T(8,128)(2,1)S(1)}, u32[]{:S(2)}, u32[]{:S(2)}) %collective-permute-start.49) | collective-permute-done | bytes 1048608 | tf_op jit(solution)/shard_map/ppermute | solution.py:568
  844.3 12.9 %collective-permute-done.53 = bf16[256,2048]{1,0:T(8,128)(2,1)} collective-permute-done((bf16[256,2048]{1,0:T(8,128)(2,1)S(1)}, bf16[256,2048]{1,0:T(8,128)(2,1)}, u32[]{:S(2)}, u32[]{:S(2)}) %collective-permute-start.53) | collective-permute-done | bytes 1048608 | tf_op jit(solution)/shard_map/ppermute | solution.py:569
  868.3 28.9 %reduce-scatter.10.cloned.1.call-done = bf16[512,1024]{1,0:T(8,128)(2,1)} async-done(((bf16[2048,1024]{1,0:T(8,128)(2,1)}), bf16[512,1024]{1,0:T(8,128)(2,1)}) %reduce-scatter.10.cloned.1.call-update) | async-done | bytes 1048592 | tf_op jit(solution)/shard_map/reduce_scatter | solution.py:635
  910.3 33.8 %reduce-scatter.14.cloned.1.call-done = bf16[512,768]{1,0:T(8,128)(2,1)} async-done(((bf16[2048,768]{1,0:T(8,128)(2,1)}), bf16[512,768]{1,0:T(8,128)(2,1)}) %reduce-scatter.14.cloned.1.call-update) | async-done | bytes 786448 | tf_op jit(solution)/shard_map/reduce_scatter | solution.py:635
  (364 shorter events, 362.3 us)
Async XLA Ops:
  7.2 51.4 %all-gather.4.cloned.1.call-start = ((), (), s32[]{:S(2)}) async-start(), calls=%async_computation.5 | async-start | bytes 7077888 | tf_op jit(solution)/shard_map/all_gather | solution.py:565
  9.5 241.8 %all-gather.6.cloned.1.call-start = ((), (), s32[]{:S(2)}) async-start(), calls=%async_computation.6 | async-start | bytes 9437184 | tf_op jit(solution)/shard_map/all_gather | solution.py:565
  10.7 240.6 %all-gather.8.cloned.1.call-start = ((), (), s32[]{:S(2)}) async-start(), calls=%async_computation.7 | async-start | bytes 9437184 | tf_op jit(solution)/shard_map/all_gather | solution.py:565
  13.0 797.3 %reduce-scatter.12.cloned.1.call-start = ((), (), s32[]{:S(2)}) async-start(), calls=%async_computation.11 | async-start | bytes 1310720 | tf_op jit(solution)/shard_map/reduce_scatter | solution.py:635
  58.6 47.2 %collective-permute-start.14 = (bf16[1024,512]{1,0:T(8,128)(2,1)S(1)}, bf16[1024,512]{1,0:T(8,128)(2,1)}, u32[]{:S(2)}, u32[]{:S(2)}) collective-permute-start(bf16[1024,512]{1,0:T(8,128)(2,1)S(1)} %constant_dynamic-slice_fusion.13), channel_id=1, source_target_pairs={{0,4},{4,0},{8,12},{12,8},{1,5},{5,1},{9,13},{13,9},{2,6},{6,2},{1... | collective-permute-start | bytes 3145736 | tf_op jit(solution)/shard_map/ppermute | solution.py:643
  60.1 45.8 %collective-permute-start.15 = (bf16[1024,512]{1,0:T(8,128)(2,1)S(1)}, bf16[1024,512]{1,0:T(8,128)(2,1)}, u32[]{:S(2)}, u32[]{:S(2)}) collective-permute-start(bf16[1024,512]{1,0:T(8,128)(2,1)S(1)} %constant_dynamic-slice_fusion.13), channel_id=1, source_target_pairs={{0,8},{8,0},{4,12},{12,4},{1,9},{9,1},{5,13},{13,5},{2,10},{10,2},... | collective-permute-start | bytes 3145736 | tf_op jit(solution)/shard_map/ppermute | solution.py:643
  60.6 76.7 %collective-permute-start.10 = (bf16[1024,512]{1,0:T(8,128)(2,1)S(1)}, bf16[1024,512]{1,0:T(8,128)(2,1)S(1)}, u32[]{:S(2)}, u32[]{:S(2)}) collective-permute-start(bf16[1024,512]{1,0:T(8,128)(2,1)S(1)} %pad_maximum_fusion.1), channel_id=1, source_target_pairs={{0,8},{8,0},{4,12},{12,4},{1,9},{9,1},{5,13},{13,5},{2,10},{10,2},... | collective-permute-start | bytes 3145736 | tf_op jit(solution)/shard_map/ppermute | solution.py:643
  62.1 75.2 %collective-permute-start.9 = (bf16[1024,512]{1,0:T(8,128)(2,1)S(1)}, bf16[1024,512]{1,0:T(8,128)(2,1)}, u32[]{:S(2)}, u32[]{:S(2)}) collective-permute-start(bf16[1024,512]{1,0:T(8,128)(2,1)S(1)} %pad_maximum_fusion.1), channel_id=1, source_target_pairs={{0,4},{4,0},{8,12},{12,8},{1,5},{5,1},{9,13},{13,9},{2,6},{6,2},{1... | collective-permute-start | bytes 3145736 | tf_op jit(solution)/shard_map/ppermute | solution.py:643
  106.9 46.6 %collective-permute-start.16 = (bf16[512,512]{1,0:T(8,128)(2,1)S(1)}, bf16[512,512]{1,0:T(8,128)(2,1)S(1)}, u32[]{:S(2)}, u32[]{:S(2)}) collective-permute-start(bf16[512,512]{1,0:T(8,128)(2,1)S(1)} %slice.53), channel_id=1, source_target_pairs={{0,8},{8,0},{4,12},{12,4},{1,9},{9,1},{5,13},{13,5},{2,10},{10,2},... | collective-permute-start | bytes 1572872 | tf_op jit(solution)/shard_map/ppermute | solution.py:651
  109.3 45.0 %collective-permute-start.17 = (bf16[512,512]{1,0:T(8,128)(2,1)S(1)}, bf16[512,512]{1,0:T(8,128)(2,1)S(1)}, u32[]{:S(2)}, u32[]{:S(2)}) collective-permute-start(bf16[512,512]{1,0:T(8,128)(2,1)S(1)} %slice.54), channel_id=1, source_target_pairs={{0,4},{4,0},{8,12},{12,8},{1,5},{5,1},{9,13},{13,9},{2,6},{6,2},{1... | collective-permute-start | bytes 1572872 | tf_op jit(solution)/shard_map/ppermute | solution.py:652
  138.4 27.2 %collective-permute-start.11 = (bf16[512,512]{1,0:T(8,128)(2,1)S(1)}, bf16[512,512]{1,0:T(8,128)(2,1)S(1)}, u32[]{:S(2)}, u32[]{:S(2)}) collective-permute-start(bf16[512,512]{1,0:T(8,128)(2,1)S(1)} %slice.51), channel_id=1, source_target_pairs={{0,8},{8,0},{4,12},{12,4},{1,9},{9,1},{5,13},{13,5},{2,10},{10,2},... | collective-permute-start | bytes 1572872 | tf_op jit(solution)/shard_map/ppermute | solution.py:651
  155.2 96.1 %collective-permute-start.18 = (bf16[4,1024,512]{2,1,0:T(8,128)(2,1)}, bf16[4,1024,512]{2,1,0:T(8,128)(2,1)}, u32[]{:S(2)}, u32[]{:S(2)}) collective-permute-start(bf16[4,1024,512]{2,1,0:T(8,128)(2,1)} %bitcast_dynamic-update-slice_fusion.6.refs_13_.wd_own_ref), channel_id=1, source_target_pairs={{0,16},{16,0},{1,17},{17,1},{2,18},{18,2},{3,19},{19,3},{4,20},{20... | collective-permute-start | bytes 12582920 | tf_op jit(solution)/shard_map/ppermute | solution.py:668
  167.3 84.0 %collective-permute-start.13 = (bf16[4,1024,512]{2,1,0:T(8,128)(2,1)}, bf16[4,1024,512]{2,1,0:T(8,128)(2,1)}, u32[]{:S(2)}, u32[]{:S(2)}) collective-permute-start(bf16[4,1024,512]{2,1,0:T(8,128)(2,1)} %bitcast_dynamic-update-slice_fusion.8.refs_7_.wo_own_ref), channel_id=1, source_target_pairs={{0,16},{16,0},{1,17},{17,1},{2,18},{18,2},{3,19},{19,3},{4,20},{20... | collective-permute-start | bytes 12582920 | tf_op jit(solution)/shard_map/ppermute | solution.py:668
  170.8 27.2 %collective-permute-start.3 = (bf16[1024,512]{1,0:T(8,128)(2,1)S(1)}, bf16[1024,512]{1,0:T(8,128)(2,1)S(1)}, u32[]{:S(2)}, u32[]{:S(2)}) collective-permute-start(bf16[1024,512]{1,0:T(8,128)(2,1)S(1)} %copy-done.11), channel_id=1, source_target_pairs={{1,0},{2,1},{3,2},{5,4},{6,5},{7,6},{9,8},{10,9},{11,10},{13,12},{... | collective-permute-start | bytes 3145736 | tf_op jit(solution)/shard_map/ppermute | solution.py:569
  197.9 27.4 %collective-permute-start.4 = (bf16[1024,512]{1,0:T(8,128)(2,1)S(1)}, bf16[1024,512]{1,0:T(8,128)(2,1)S(1)}, u32[]{:S(2)}, u32[]{:S(2)}) collective-permute-start(bf16[1024,512]{1,0:T(8,128)(2,1)S(1)} %collective-permute-done.3.refs_4_), channel_id=1, source_target_pairs={{1,0},{2,1},{5,4},{6,5},{9,8},{10,9},{13,12},{14,13},{17,16},{18,1... | collective-permute-start | bytes 3145736 | tf_op jit(solution)/shard_map/ppermute | solution.py:569
  199.2 28.0 %collective-permute-start.2 = (bf16[1024,512]{1,0:T(8,128)(2,1)}, bf16[1024,512]{1,0:T(8,128)(2,1)}, u32[]{:S(2)}, u32[]{:S(2)}) collective-permute-start(bf16[1024,512]{1,0:T(8,128)(2,1)} %collective-permute-done.1.refs_2_), channel_id=1, source_target_pairs={{2,3},{6,7},{10,11},{14,15},{18,19},{22,23},{26,27},{30,31}} | collective-permute-start | bytes 3145736 | tf_op jit(solution)/shard_map/ppermute | solution.py:568
  304.3 27.5 %collective-permute-start.21 = (bf16[256,2048]{1,0:T(8,128)(2,1)}, bf16[256,2048]{1,0:T(8,128)(2,1)S(1)}, u32[]{:S(2)}, u32[]{:S(2)}) collective-permute-start(bf16[256,2048]{1,0:T(8,128)(2,1)} %get-tuple-element.417), channel_id=1, source_target_pairs={{0,1},{1,2},{4,5},{5,6},{8,9},{9,10},{12,13},{13,14},{16,17},{17,1... | collective-permute-start | bytes 3145736 | tf_op jit(solution)/shard_map/ppermute | solution.py:573
  334.5 26.9 %collective-permute-start.23 = (bf16[256,2048]{1,0:T(8,128)(2,1)}, bf16[256,2048]{1,0:T(8,128)(2,1)S(1)}, u32[]{:S(2)}, u32[]{:S(2)}) collective-permute-start(bf16[256,2048]{1,0:T(8,128)(2,1)} %get-tuple-element.415), channel_id=1, source_target_pairs={{0,1},{1,2},{2,3},{4,5},{5,6},{6,7},{8,9},{9,10},{10,11},{12,13},{... | collective-permute-start | bytes 3145736 | tf_op jit(solution)/shard_map/ppermute | solution.py:573
  364.6 26.9 %collective-permute-start.25 = (bf16[256,2048]{1,0:T(8,128)(2,1)S(1)}, bf16[256,2048]{1,0:T(8,128)(2,1)S(1)}, u32[]{:S(2)}, u32[]{:S(2)}) collective-permute-start(bf16[256,2048]{1,0:T(8,128)(2,1)S(1)} %add_convert_fusion.6.down_ref), channel_id=1, source_target_pairs={{0,1},{1,2},{2,3},{4,5},{5,6},{6,7},{8,9},{9,10},{10,11},{12,13},{... | collective-permute-start | bytes 3145736 | tf_op jit(solution)/shard_map/ppermute | solution.py:568
  578.7 33.1 %collective-permute-start.39 = (bf16[256,2048]{1,0:T(8,128)(2,1)}, bf16[256,2048]{1,0:T(8,128)(2,1)S(1)}, u32[]{:S(2)}, u32[]{:S(2)}) collective-permute-start(bf16[256,2048]{1,0:T(8,128)(2,1)} %collective-permute-done.38), channel_id=1, source_target_pairs={{2,3},{6,7},{10,11},{14,15},{18,19},{22,23},{26,27},{30,31}} | collective-permute-start | bytes 3145736 | tf_op jit(solution)/shard_map/ppermute | solution.py:568
  669.7 31.9 %collective-permute-start.55 = (bf16[2048,1024]{1,0:T(8,128)(2,1)}, bf16[2048,1024]{1,0:T(8,128)(2,1)}, u32[]{:S(2)}, u32[]{:S(2)}) collective-permute-start(bf16[2048,1024]{1,0:T(8,128)(2,1)} %convolution_convert_fusion.2), channel_id=1, source_target_pairs={{0,16},{16,0},{1,17},{17,1},{2,18},{18,2},{3,19},{19,3},{4,20},{20... | collective-permute-start | bytes 12582920 | tf_op jit(solution)/shard_map/ppermute | solution.py:631
  701.3 131.3 %reduce-scatter.6.cloned.1.call-start = ((), (), s32[]{:S(2)}) async-start(), calls=%async_computation.8 | async-start | bytes 5242880 | tf_op jit(solution)/shard_map/reduce_scatter | solution.py:635
  712.3 128.8 %reduce-scatter.8.cloned.1.call-start = ((), (), s32[]{:S(2)}) async-start(), calls=%async_computation.9 | async-start | bytes 5242880 | tf_op jit(solution)/shard_map/reduce_scatter | solution.py:635
  733.7 163.5 %reduce-scatter.10.cloned.1.call-start = ((), (), s32[]{:S(2)}) async-start(), calls=%async_computation.10 | async-start | bytes 5242880 | tf_op jit(solution)/shard_map/reduce_scatter | solution.py:635
  755.4 188.7 %reduce-scatter.14.cloned.1.call-start = ((), (), s32[]{:S(2)}) async-start(), calls=%async_computation.12 | async-start | bytes 3932160 | tf_op jit(solution)/shard_map/reduce_scatter | solution.py:635
  763.1 28.5 %collective-permute-start.47 = (bf16[256,2048]{1,0:T(8,128)(2,1)}, bf16[256,2048]{1,0:T(8,128)(2,1)S(1)}, u32[]{:S(2)}, u32[]{:S(2)}) collective-permute-start(bf16[256,2048]{1,0:T(8,128)(2,1)} %get-tuple-element.408), channel_id=1, source_target_pairs={{0,1},{1,2},{2,3},{4,5},{5,6},{6,7},{8,9},{9,10},{10,11},{12,13},{... | collective-permute-start | bytes 3145736 | tf_op jit(solution)/shard_map/ppermute | solution.py:573
  768.4 27.4 %collective-permute-start.48 = (bf16[256,2048]{1,0:T(8,128)(2,1)}, bf16[256,2048]{1,0:T(8,128)(2,1)}, u32[]{:S(2)}, u32[]{:S(2)}) collective-permute-start(bf16[256,2048]{1,0:T(8,128)(2,1)} %get-tuple-element.407), channel_id=1, source_target_pairs={{3,2},{2,1},{1,0},{7,6},{6,5},{5,4},{11,10},{10,9},{9,8},{15,14},{... | collective-permute-start | bytes 3145736 | tf_op jit(solution)/shard_map/ppermute | solution.py:574
  804.6 26.7 %collective-permute-start.52 = (bf16[256,2048]{1,0:T(8,128)(2,1)}, bf16[256,2048]{1,0:T(8,128)(2,1)S(1)}, u32[]{:S(2)}, u32[]{:S(2)}) collective-permute-start(bf16[256,2048]{1,0:T(8,128)(2,1)} %add_convert_fusion.4.rows_ref), channel_id=1, source_target_pairs={{1,0},{2,1},{3,2},{5,4},{6,5},{7,6},{9,8},{10,9},{11,10},{13,12},{... | collective-permute-start | bytes 3145736 | tf_op jit(solution)/shard_map/ppermute | solution.py:569
  810.3 30.7 %collective-permute-start.64 = (bf16[512,256]{1,0:T(8,128)(2,1)}, bf16[512,256]{1,0:T(8,128)(2,1)S(1)}, u32[]{:S(2)}, u32[]{:S(2)}) collective-permute-start(bf16[512,256]{1,0:T(8,128)(2,1)} %reduce-scatter.12.cloned.1.call-done), channel_id=1, source_target_pairs={{0,16},{16,0},{1,17},{17,1},{2,18},{18,2},{3,19},{19,3},{4,20},{20... | collective-permute-start | bytes 786440 | tf_op jit(solution)/shard_map/ppermute | solution.py:625
  841.1 56.2 %collective-permute-start.58 = (bf16[512,1024]{1,0:T(8,128)(2,1)}, bf16[512,1024]{1,0:T(8,128)(2,1)}, u32[]{:S(2)}, u32[]{:S(2)}) collective-permute-start(bf16[512,1024]{1,0:T(8,128)(2,1)} %reduce-scatter.8.cloned.1.call-done), channel_id=1, source_target_pairs={{0,16},{16,0},{1,17},{17,1},{2,18},{18,2},{3,19},{19,3},{4,20},{20... | collective-permute-start | bytes 3145736 | tf_op jit(solution)/shard_map/ppermute | solution.py:625
  842.6 113.3 %collective-permute-start.51 = (bf16[256,2048]{1,0:T(8,128)(2,1)}, bf16[256,2048]{1,0:T(8,128)(2,1)}, u32[]{:S(2)}, u32[]{:S(2)}) collective-permute-start(bf16[256,2048]{1,0:T(8,128)(2,1)} %collective-permute-done.50), channel_id=1, source_target_pairs={{2,3},{6,7},{10,11},{14,15},{18,19},{22,23},{26,27},{30,31}} | collective-permute-start | bytes 3145736 | tf_op jit(solution)/shard_map/ppermute | solution.py:568
  857.2 98.7 %collective-permute-start.54 = (bf16[256,2048]{1,0:T(8,128)(2,1)}, bf16[256,2048]{1,0:T(8,128)(2,1)}, u32[]{:S(2)}, u32[]{:S(2)}) collective-permute-start(bf16[256,2048]{1,0:T(8,128)(2,1)} %collective-permute-done.53), channel_id=1, source_target_pairs={{1,0},{5,4},{9,8},{13,12},{17,16},{21,20},{25,24},{29,28}} | collective-permute-start | bytes 3145736 | tf_op jit(solution)/shard_map/ppermute | solution.py:569
  (98 other events, 1622.5 us)
Sparse Core Ops, SparseCore 0:
  10.5 48.1 all-gather.3
  61.1 88.1 all-gather.5
  151.7 54.9 all-gather.7
  701.4 27.1 reduce-scatter.11
  732.0 52.5 reduce-scatter.5
  788.0 53.0 reduce-scatter.7
  844.6 52.5 reduce-scatter.9
  900.2 43.8 reduce-scatter.13

commit v7 on v6

--- a/solution.py
+++ b/solution.py
@@ -200,6 +200,16 @@
         ),
         name="attend_backward",
     )(qkv, qkv, *scales, *gains, *tables, seg_col, seg_row, *saved, grad_att)
+
+
+def fetch_choice(idx_ref, refs, held_ref, sem):
+    for number, ref in enumerate(refs):
+
+        @pl.when(idx_ref[2] == number)
+        def _():
+            copy = pltpu.make_async_copy(ref, held_ref, sem)
+            copy.start()
+            copy.wait()
 
 
 def half_tile(step, core, tiles):
@@ -329,15 +339,16 @@
 
 
 def backward_chunk_kernel(
-    idx_ref, down_ref, raw_ref, scale_ref, x_ref, grad_ref, attn_gain_ref, mlp_gain_ref,
-    gate_ref, up_ref, wg_ref, wu_ref, wd_own_ref, wd_oth_ref, *refs, blocks, tiles,
+    idx_ref, raw_ref, scale_ref, x_ref, grad_ref, attn_gain_ref, mlp_gain_ref,
+    gate_ref, up_ref, wg_ref, wu_ref, wd_own_ref, wd_oth_ref, *refs, blocks, tiles, choices,
 ):
-    out_ref, gdi_ref, gg_ref, gu_ref, part_ref, gain_grad_ref, acc_ref = refs[-7:]
+    out_ref, gdi_ref, gg_ref, gu_ref, part_ref, gain_grad_ref, acc_ref, down_ref, sem = refs[-9:]
     block = wd_own_ref.shape[2]
     step = pl.program_id(0)
 
     @pl.when(step == 0)
     def _():
+        fetch_choice(idx_ref, refs[:choices], down_ref, sem)
         down_raw = down_ref[...].astype(F32)
         down_scale = lax.rsqrt(jnp.mean(down_raw * down_raw, axis=1, keepdims=True) + EPS)
         unit = down_raw * down_scale
@@ -395,18 +406,20 @@
     act_tile = pl.BlockSpec((chunk, TILE), lambda j, idx: (idx[0], tile_of(j, idx)))
     before = tuple(before)
     return pl.pallas_call(
-        functools.partial(backward_chunk_kernel, blocks=blocks, tiles=tiles),
+        functools.partial(backward_chunk_kernel, blocks=blocks, tiles=tiles, choices=len(down_rows)),
         grid_spec=pltpu.PrefetchScalarGridSpec(
             num_scalar_prefetch=1,
             grid=(tiles,),
             in_specs=[
-                fixed, rows, pl.BlockSpec((chunk, 1), lambda j, idx: (idx[0], 0)), rows, rows, gain_row, gain_row,
+                rows, pl.BlockSpec((chunk, 1), lambda j, idx: (idx[0], 0)), rows, rows, gain_row, gain_row,
                 act_tile, act_tile, up_tile, up_tile,
                 pl.BlockSpec((blocks, TILE, block), lambda j, idx: (0, jnp.minimum(j, tiles // 2 - 1), 0)),
                 pl.BlockSpec((blocks, TILE, block), lambda j, idx: (0, jnp.maximum(j - tiles // 2, 0), 0)),
-            ] + [pl.BlockSpec(memory_space=pl.ANY)] * len(before),
+            ] + [pl.BlockSpec(memory_space=pl.ANY)] * (len(down_rows) + len(before)),
             out_specs=[rows, rows, act_tile, act_tile, fixed, gain_row],
-            scratch_shapes=[pltpu.VMEM((chunk, width), F32)],
+            scratch_shapes=[
+                pltpu.VMEM((chunk, width), F32), pltpu.VMEM((chunk, width), BF16), pltpu.SemaphoreType.DMA(()),
+            ],
         ),
         out_shape=[
             jax.ShapeDtypeStruct((tokens, width), BF16),
@@ -416,22 +429,23 @@
             jax.ShapeDtypeStruct((chunk, width), BF16),
             jax.ShapeDtypeStruct((1, width), F32),
         ],
-        input_output_aliases={14 + i: i for i in range(len(before))},
+        input_output_aliases={13 + len(down_rows) + i: i for i in range(len(before))},
         compiler_params=pltpu.CompilerParams(vmem_limit_bytes=VMEM),
         cost_estimate=pl.CostEstimate(
             flops=6 * chunk * width * hidden, bytes_accessed=6 * width * hidden, transcendentals=0
         ),
         name="backward_chunk",
     )(
-        index, down_rows, raw, scale, block_input, grad_output, attn_gain, mlp_gain, gate, up, w_gate, w_up,
-        *down_halves, *before,
+        index, raw, scale, block_input, grad_output, attn_gain, mlp_gain, gate, up, w_gate, w_up,
+        *down_halves, *down_rows, *before,
     )
 
 
 def attention_chunk_kernel(
-    idx_ref, mlp_ref, grad_ref, raw_ref, scale_ref, gain_ref, wo_own_ref, wo_oth_ref, *refs, blocks,
+    idx_ref, grad_ref, raw_ref, scale_ref, gain_ref, wo_own_ref, wo_oth_ref, *refs, blocks, choices,
 ):
-    gai_ref, gatt_ref, gain_grad_ref = refs[-3:]
+    gai_ref, gatt_ref, gain_grad_ref, mlp_ref, sem = refs[-5:]
+    fetch_choice(idx_ref, refs[:choices], mlp_ref, sem)
     half, block = wo_own_ref.shape[1:]
     core = idx_ref[1]
     scale = scale_ref[...]
@@ -452,57 +466,65 @@
     tokens, width = grad_output.shape
     blocks, _, block = out_halves[0].shape
     rows = pl.BlockSpec((chunk, width), lambda j, idx: (idx[0], 0))
-    fixed = pl.BlockSpec((chunk, width), lambda j, idx: (0, 0))
     gain_row = pl.BlockSpec((1, width), lambda j, idx: (0, 0))
     own_heads = pl.BlockSpec((blocks, half, block), lambda j, idx: (0, 0, 0))
     before = tuple(before)
     return pl.pallas_call(
-        functools.partial(attention_chunk_kernel, blocks=blocks),
+        functools.partial(attention_chunk_kernel, blocks=blocks, choices=len(mlp_rows)),
         grid_spec=pltpu.PrefetchScalarGridSpec(
             num_scalar_prefetch=1,
             grid=(1,),
             in_specs=[
-                fixed, rows, rows, pl.BlockSpec((chunk, 1), lambda j, idx: (idx[0], 0)), gain_row,
+                rows, rows, pl.BlockSpec((chunk, 1), lambda j, idx: (idx[0], 0)), gain_row,
                 own_heads, own_heads,
-            ] + [pl.BlockSpec(memory_space=pl.ANY)] * len(before),
+            ] + [pl.BlockSpec(memory_space=pl.ANY)] * (len(mlp_rows) + len(before)),
             out_specs=[rows, pl.BlockSpec((chunk, 2 * half), lambda j, idx: (idx[0], 0)), gain_row],
+            scratch_shapes=[pltpu.VMEM((chunk, width), BF16), pltpu.SemaphoreType.DMA(())],
         ),
         out_shape=[
             jax.ShapeDtypeStruct((tokens, width), BF16),
             jax.ShapeDtypeStruct((tokens, 2 * half), BF16),
             jax.ShapeDtypeStruct((1, width), F32),
         ],
-        input_output_aliases={8 + i: i for i in range(len(before))},
+        input_output_aliases={7 + len(mlp_rows) + i: i for i in range(len(before))},
         compiler_params=pltpu.CompilerParams(vmem_limit_bytes=VMEM),
         cost_estimate=pl.CostEstimate(
             flops=4 * chunk * width * half, bytes_accessed=16 * chunk * width, transcendentals=0
         ),
         name="attention_chunk",
-    )(index, mlp_rows, grad_output, raw, scale, gain, *out_halves, *before)
-
-
-def place_rows_kernel(idx_ref, rows_ref, *refs):
-    refs[-1][...] = rows_ref[...].astype(refs[-1].dtype)
+    )(index, grad_output, raw, scale, gain, *out_halves, *mlp_rows, *before)
+
+
+def place_rows_kernel(idx_ref, *refs, choices):
+    out_ref, held_ref, sem = refs[-3:]
+    step = pl.program_id(0)
+
+    @pl.when(step == 0)
+    def _():
+        fetch_choice(idx_ref, refs[:choices], held_ref, sem)
+
+    size = out_ref.shape[0]
+    out_ref[...] = held_ref[pl.ds(pl.multiple_of(step * size, size), size), :].astype(out_ref.dtype)
 
 
 def place_rows(index, rows_in, tokens, dtype, before):
-    chunk, width = rows_in.shape
+    chunk, width = rows_in[0].shape
     before = tuple(before)
     return pl.pallas_call(
-        place_rows_kernel,
+        functools.partial(place_rows_kernel, choices=len(rows_in)),
         grid_spec=pltpu.PrefetchScalarGridSpec(
             num_scalar_prefetch=1,
-            grid=(2,),
-            in_specs=[pl.BlockSpec((chunk // 2, width), lambda j, idx: (j, 0))]
-            + [pl.BlockSpec(memory_space=pl.ANY)] * len(before),
-            out_specs=pl.BlockSpec((chunk // 2, width), lambda j, idx: (2 * idx[0] + j, 0)),
+            grid=(4,),
+            in_specs=[pl.BlockSpec(memory_space=pl.ANY)] * (len(rows_in) + len(before)),
+            out_specs=pl.BlockSpec((chunk // 4, width), lambda j, idx: (4 * idx[0] + j, 0)),
+            scratch_shapes=[pltpu.VMEM((chunk, width), BF16), pltpu.SemaphoreType.DMA(())],
         ),
         out_shape=jax.ShapeDtypeStruct((tokens, width), dtype),
-        input_output_aliases={2: 0} if before else {},
+        input_output_aliases={1 + len(rows_in): 0} if before else {},
         compiler_params=pltpu.CompilerParams(vmem_limit_bytes=VMEM),
         cost_estimate=pl.CostEstimate(flops=0, bytes_accessed=6 * chunk * width, transcendentals=0),
         name="place_rows",
-    )(index, rows_in, *before)
+    )(index, *rows_in, *before)
 
 
 def after(value, *tokens):
@@ -580,7 +602,10 @@
         return jnp.where(col < 2, low, high)
 
     slot_chunk = [pick(3, 3, 0, 0), pick(2, 2, 1, 1), pick(1, 0, 3, 2), col]
-    slot_index = [jnp.stack([one, core]).astype(jnp.int32) for one in slot_chunk]
+    slot_index = [
+        jnp.stack([one, core, choice]).astype(jnp.int32)
+        for one, choice in zip(slot_chunk, (col, col, col % 2, 0 * col))
+    ]
 
     def slot_rows(array, slot):
         return lax.dynamic_slice_in_dim(array, slot_chunk[slot] * chunk, chunk, 0)
@@ -588,10 +613,10 @@
     def gather_slots(own, work):
         left, right, token = [own], [own], ()
         arrived = (
-            lambda lefts, rights: lefts[0],
-            lambda lefts, rights: jnp.where(col % 2 == 0, rights[1], lefts[1]),
-            lambda lefts, rights: pick(rights[2], rights[1], lefts[1], lefts[2]),
-            lambda lefts, rights: pick(rights[3], rights[2], lefts[2], lefts[3]),
+            lambda lefts, rights: (lefts[0],),
+            lambda lefts, rights: (rights[1], lefts[1]),
+            lambda lefts, rights: (rights[2], rights[1], lefts[1], lefts[2]),
+            lambda lefts, rights: (rights[3], rights[2], lefts[2], lefts[3]),
         )
         for step in range(1, cols + 1):
             seen = tuple(left), tuple(right)
@@ -618,7 +643,7 @@
         down = jnp.where(col == 2, second, third) + down
         gate = (up, down)
         up, down = sum_step(up, down, 3)
-        fourth = at(3, gate)
+        fourth = lax.optimization_barrier(at(3, gate))
         return fourth.astype(F32) + up.astype(F32) + down.astype(F32)
 
     def both_cores(half, axis):
@@ -703,11 +728,11 @@
         from_left, from_right = line_step(lefts[-1], rights[-1], step)
         lefts.append(from_left)
         rights.append(from_right)
-        if step == 1:
-            down_pieces = row_second(after(down_pieces, attended))
-            out_pieces = row_second(after(out_pieces, attended))
+        if step == 2:
+            down_pieces = row_second(after(down_pieces, lefts[1], rights[1]))
+            out_pieces = row_second(after(out_pieces, lefts[1], rights[1]))
+        if step == 3:
             out_halves = row_blocks(out_pieces)
-        if step == 2:
             down_halves = row_blocks(down_pieces)
     attended_all = (attended, *lefts[1:], *rights[1:])
 
@@ -767,7 +792,7 @@
         held["attention"] = results[:2]
         gain_sums["attn"] = gain_sums["attn"] + results[2]
         if slot == 3:
-            hidden_left, up_right = after((hidden_b, grad_up_in), mlp_rows)
+            hidden_left, up_right = after((hidden_b, grad_up_in), mlp_rows[0])
             blocks["up"] = sum_kept(hidden_left, own_half(up_right, 1), got["up"])
         return results[1]
 

time: 980 us -> 1060 us (1.082)
  waiting for transfers between devices: 396 us -> 473 us
  Pallas kernels: 245 us -> 260 us
  other arithmetic: 62.4 us -> 50.2 us
    ppermute x12, waiting for transfers between devices: 93.2 us -> 130 us  [line_step(): lax.ppermute(from_right, 'col', [(i + 1, i) for i in range(cols - step)])]
    all_gather x3, waiting for transfers between devices: 17.9 us -> 41.2 us  [gather(): lax.all_gather(own_half(weight, axis), ('row', 'dp'), axis=axis, tiled=True)]
    ppermute x2, waiting for transfers between devices: 0.01 us -> 19.6 us  [row_first(): lax.ppermute(half, 'row', by_x)]
    select_n x9 -> x0, other arithmetic: 18.9 us -> none  [the longest x6 15.7 us: pick(): return jnp.where(col < 2, low, high)]
    ppermute x3, waiting for transfers between devices: 15.6 us -> 32.8 us  [shards(): lax.ppermute(out_half, 'col', [(i, (i - step) % cols) for i in range(cols)])]
    ppermute x2, waiting for transfers between devices: 13.9 us -> 0.6 us  [row_second(): lax.ppermute(pieces[1][:middle], 'row', by_y)]
  transfers between devices with their start and end apart: 78 -> 78, of which waited for: 33 -> 36; matrix products, arithmetic and copies ran while one was open for 15% -> 14% of each run, Pallas kernels for 18% -> 18%
where the time goes in v7:
time: 1060 us; the launch traced here: 1050 us
  waiting for transfers between devices  473 us (45%)
  Pallas kernels  260 us (25%)
  starting transfers between devices  96.9 us (9%)
  matrix products  80.5 us (8%)
  other arithmetic  50.2 us (5%)
  local copies, waits for them, and re-layouts  48.1 us (5%)
  blocking collectives  24.1 us (2%)
  between operations  16.1 us (2%)
    ppermute x12, waiting for transfers between devices, line_step(): lax.ppermute(from_right, 'col', [(i + 1, i) for i in range(cols - step)])  130 us
    pallas_call x4, Pallas kernels, forward_chunk(): pl.pallas_call(functools.partial(forward_chunk_kernel, blocks=blocks, til...  94.1 us
    pallas_call x4, Pallas kernels, backward_chunk(): pl.pallas_call(functools.partial(backward_chunk_kernel, blocks=blocks, ti...  89.4 us
    ppermute x9, waiting for transfers between devices, sum_step(): up = lax.ppermute(up, 'col', [(i, i + 1) for i in range(step)])  81.9 us
    reduce_scatter x5, waiting for transfers between devices, sum_kept(): lax.psum_scatter(total, 'row', scatter_dimension=0, tiled=True)  60.8 us
    dot_general x10, matrix products, left_transposed(): lax.dot_general(left_mat, right_mat, (((0,), (0,)), ((), ())), preferred_...  59.9 us
    ppermute x12, waiting for transfers between devices, line_step(): lax.ppermute(from_left, 'col', [(i, i + 1) for i in range(step - 1, cols...  48.6 us
    all_gather x3, waiting for transfers between devices, gather(): lax.all_gather(own_half(weight, axis), ('row', 'dp'), axis=axis, tiled=True)  41.2 us
  transfers between devices with their start and end apart: 78, of which 36 were waited for; matrix products, arithmetic and copies ran while one was open for 14% of the time, Pallas kernels for 18%

profile of v7, /device:TPU:0, one launch (start us, length us, event | category | flops | bytes accessed | tf_op | source)
XLA Modules:
  0.0 1048.5 jit_solution(8294563779740742677)
XLA Ops:
  17.4 41.2 %all-gather.4.cloned.1.call-done = bf16[2048,1536]{1,0:T(8,128)(2,1)} async-done(((bf16[256,1536]{1,0:T(8,128)(2,1)}), bf16[2048,1536]{1,0:T(8,128)(2,1)}) %all-gather.4.cloned.1.call-update) | async-done | bytes 6291472 | tf_op jit(solution)/shard_map/all_gather | solution.py:587
  58.6 10.0 convolution_bitcast_fusion.q_ref.k_ref.v_ref
  71.7 11.9 %all-reduce.1 = (f32[1024]{0:T(1024)S(1)}, f32[1024]{0:T(1024)S(1)}) all-reduce(f32[1024]{0:T(1024)S(1)} %get-tuple-element.390, f32[1024]{0:T(1024)S(1)} %get-tuple-element.389), channel_id=1, replica_groups=mesh['dp'=2,'row'=4,'col'=4] {'col'}, use_global_device_ids=true, to_apply=%region_1.2 | all-reduce | flops 2048 | bytes 16384 | tf_op jit(solution)/shard_map/psum | solution.py:713
  85.7 16.2 %attend_forward.1 = (bf16[1024,512]{1,0:T(8,128)(2,1)}, bf16[1024,512]{1,0:T(8,128)(2,1)}, bf16[1024,512]{1,0:T(8,128)(2,1)}, bf16[1024,512]{1,0:T(8,128)(2,1)}, f32[4,1024,1]{2,1,0:T(8,128)}) custom-call(f32[1024,1536]{1,0:T(8,128)} %copy-done.3, f32[1024,1536]{1,0:T(8,128)} %copy-done.3, f32[1024,1536]{1,0:T(8,128)} %copy-done.3, f32[1024,1]{1,0:T(8,128)} %copy.71.qs_ref, ...), custom_call_target="tpu_custom_call" | custom-call | flops 2147483648 | bytes 10485760 | tf_op jit(solution)/shard_map/attend_forward/pallas_call | solution.py:156
  108.6 24.1 %collective-permute-done.6 = bf16[256,512]{1,0:T(8,128)(2,1)S(1)} collective-permute-done((bf16[256,512]{1,0:T(8,128)(2,1)S(1)}, bf16[256,512]{1,0:T(8,128)(2,1)S(1)}, u32[]{:S(2)}, u32[]{:S(2)}) %collective-permute-start.6) | collective-permute-done | bytes 262176 | tf_op jit(solution)/shard_map/ppermute | solution.py:702
  147.9 24.8 %collective-permute-done.3.refs_4_ = bf16[1024,512]{1,0:T(8,128)(2,1)S(1)} collective-permute-done((bf16[1024,512]{1,0:T(8,128)(2,1)S(1)}, bf16[1024,512]{1,0:T(8,128)(2,1)S(1)}, u32[]{:S(2)}, u32[]{:S(2)}) %collective-permute-start.3) | collective-permute-done | bytes 1048608 | tf_op jit(solution)/shard_map/ppermute | solution.py:591
  172.7 19.6 %collective-permute-done.14 = bf16[1024,512]{1,0:T(8,128)(2,1)} collective-permute-done((bf16[1024,512]{1,0:T(8,128)(2,1)}, bf16[1024,512]{1,0:T(8,128)(2,1)}, u32[]{:S(2)}, u32[]{:S(2)}) %collective-permute-start.14) | collective-permute-done | bytes 1048608 | tf_op jit(solution)/shard_map/ppermute | solution.py:668
  197.1 18.2 %collective-permute-done.10 = bf16[1024,512]{1,0:T(8,128)(2,1)} collective-permute-done((bf16[1024,512]{1,0:T(8,128)(2,1)}, bf16[1024,512]{1,0:T(8,128)(2,1)}, u32[]{:S(2)}, u32[]{:S(2)}) %collective-permute-start.10) | collective-permute-done | bytes 1048608 | tf_op jit(solution)/shard_map/ppermute | solution.py:668
  245.1 31.0 %collective-permute-done.4.refs_5_ = bf16[1024,512]{1,0:T(8,128)(2,1)} collective-permute-done((bf16[1024,512]{1,0:T(8,128)(2,1)S(1)}, bf16[1024,512]{1,0:T(8,128)(2,1)}, u32[]{:S(2)}, u32[]{:S(2)}) %collective-permute-start.4) | collective-permute-done | bytes 1048608 | tf_op jit(solution)/shard_map/ppermute | solution.py:591
  278.1 24.8 %collective-permute-done.5.refs_6_ = bf16[1024,512]{1,0:T(8,128)(2,1)S(1)} collective-permute-done((bf16[1024,512]{1,0:T(8,128)(2,1)}, bf16[1024,512]{1,0:T(8,128)(2,1)S(1)}, u32[]{:S(2)}, u32[]{:S(2)}) %collective-permute-start.5) | collective-permute-done | bytes 1048608 | tf_op jit(solution)/shard_map/ppermute | solution.py:591
  303.8 23.5 %forward_chunk.4 = (f32[1024,2048]{1,0:T(8,128)}, f32[1024,1]{1,0:T(8,128)}, bf16[1024,2048]{1,0:T(8,128)(2,1)}, bf16[1024,2048]{1,0:T(8,128)(2,1)}, bf16[1024,2...) custom-call(s32[3]{0:T(128)} %get-tuple-element.448.idx_ref, ...), custom_call_target="tpu_custom_call" | custom-call | flops 8589934592 | bytes 33554432 | tf_op jit(solution)/shard_map/forward_chunk/pallas_call | solution.py:305
  329.7 23.6 %forward_chunk.5 = (f32[1024,2048]{1,0:T(8,128)}, f32[1024,1]{1,0:T(8,128)}, bf16[1024,2048]{1,0:T(8,128)(2,1)}, bf16[1024,2048]{1,0:T(8,128)(2,1)}, bf16[1024,2...) custom-call(s32[3]{0:T(128)} %get-tuple-element.449.idx_ref, ...), custom_call_target="tpu_custom_call", output_to_operand_aliasing={{0}: (16, {}), {1}: (17, {}), {2}: (18, {}), {3}: (19, {}),... | custom-call | flops 8589934592 | bytes 33554432 | tf_op jit(solution)/shard_map/forward_chunk/pallas_call | solution.py:305
  361.1 23.5 %forward_chunk.6 = (f32[1024,2048]{1,0:T(8,128)}, f32[1024,1]{1,0:T(8,128)}, bf16[1024,2048]{1,0:T(8,128)(2,1)}, bf16[1024,2048]{1,0:T(8,128)(2,1)}, bf16[1024,2...) custom-call(s32[3]{0:T(128)} %pad_add_fusion.1.idx_ref, ...), custom_call_target="tpu_custom_call", output_to_operand_aliasing={{0}: (16, {}), {1}: (17, {}), {2}: (18, {}), {3}: (19, {}),... | custom-call | flops 8589934592 | bytes 33554432 | tf_op jit(solution)/shard_map/forward_chunk/pallas_call | solution.py:305
  391.0 23.5 %forward_chunk.7 = (f32[1024,2048]{1,0:T(8,128)}, f32[1024,1]{1,0:T(8,128)}, bf16[1024,2048]{1,0:T(8,128)(2,1)}, bf16[1024,2048]{1,0:T(8,128)(2,1)}, bf16[1024,2...) custom-call(s32[3]{0:T(128)} %pad_add_fusion.idx_ref, ...), custom_call_target="tpu_custom_call", output_to_operand_aliasing={{0}: (16, {}), {1}: (17, {}), {2}: (18, {}), {3}: (19, {}),... | custom-call | flops 8589934592 | bytes 33554432 | tf_op jit(solution)/shard_map/forward_chunk/pallas_call | solution.py:305
  423.1 19.0 %collective-permute-done.25.refs_1_.refs_2_ = bf16[256,2048]{1,0:T(8,128)(2,1)S(1)} collective-permute-done((bf16[256,2048]{1,0:T(8,128)(2,1)S(1)}, bf16[256,2048]{1,0:T(8,128)(2,1)S(1)}, u32[]{:S(2)}, u32[]{:S(2)}) %collective-permute-start.25) | collective-permute-done | bytes 1048608 | tf_op jit(solution)/shard_map/ppermute | solution.py:590
  448.0 22.2 %backward_chunk.4 = (bf16[1024,2048]{1,0:T(8,128)(2,1)}, bf16[1024,2048]{1,0:T(8,128)(2,1)}, bf16[1024,2048]{1,0:T(8,128)(2,1)}, bf16[1024,2048]{1,0:T(8,128)(2,...) custom-call(s32[3]{0:T(128)} %pad_add_fusion.idx_ref, f32[1024,2048]{1,0:T(8,128)} %get-tuple-element.246.raw_ref, ...), custom_call_target="tpu_custom_call" | custom-call | flops 6442450944 | bytes 25165824 | tf_op jit(solution)/shard_map/backward_chunk/pallas_call | solution.py:408
  472.7 22.3 %backward_chunk.5 = (bf16[1024,2048]{1,0:T(8,128)(2,1)}, bf16[1024,2048]{1,0:T(8,128)(2,1)}, bf16[1024,2048]{1,0:T(8,128)(2,1)}, bf16[1024,2048]{1,0:T(8,128)(2,...) custom-call(s32[3]{0:T(128)} %pad_add_fusion.1.idx_ref, ...), custom_call_target="tpu_custom_call", output_to_operand_aliasing={{0}: (15, {}), {1}: (16, {}), {2}: (17, {}), {3}: (18, {})} | custom-call | flops 6442450944 | bytes 25165824 | tf_op jit(solution)/shard_map/backward_chunk/pallas_call | solution.py:408
  495.0 22.4 %backward_chunk.6 = (bf16[1024,2048]{1,0:T(8,128)(2,1)}, bf16[1024,2048]{1,0:T(8,128)(2,1)}, bf16[1024,2048]{1,0:T(8,128)(2,1)}, bf16[1024,2048]{1,0:T(8,128)(2,...) custom-call(s32[3]{0:T(128)} %get-tuple-element.449.idx_ref, ...), custom_call_target="tpu_custom_call", output_to_operand_aliasing={{0}: (17, {}), {1}: (18, {}), {2}: (19, {}), {3}: (20, {})} | custom-call | flops 6442450944 | bytes 25165824 | tf_op jit(solution)/shard_map/backward_chunk/pallas_call | solution.py:408
  518.5 22.5 %backward_chunk.7 = (bf16[1024,2048]{1,0:T(8,128)(2,1)}, bf16[1024,2048]{1,0:T(8,128)(2,1)}, bf16[1024,2048]{1,0:T(8,128)(2,1)}, bf16[1024,2048]{1,0:T(8,128)(2,...) custom-call(s32[3]{0:T(128)} %get-tuple-element.448.idx_ref, ...), custom_call_target="tpu_custom_call", output_to_operand_aliasing={{0}: (17, {}), {1}: (18, {}), {2}: (19, {}), {3}: (20, {})} | custom-call | flops 6442450944 | bytes 25165824 | tf_op jit(solution)/shard_map/backward_chunk/pallas_call | solution.py:408
  547.5 18.5 %collective-permute-done.31 = bf16[256,2048]{1,0:T(8,128)(2,1)S(1)} collective-permute-done((bf16[256,2048]{1,0:T(8,128)(2,1)}, bf16[256,2048]{1,0:T(8,128)(2,1)S(1)}, u32[]{:S(2)}, u32[]{:S(2)}) %collective-permute-start.31) | collective-permute-done | bytes 1048608 | tf_op jit(solution)/shard_map/ppermute | solution.py:595
  572.8 17.3 %collective-permute-done.32 = bf16[256,2048]{1,0:T(8,128)(2,1)S(1)} collective-permute-done((bf16[256,2048]{1,0:T(8,128)(2,1)S(1)}, bf16[256,2048]{1,0:T(8,128)(2,1)S(1)}, u32[]{:S(2)}, u32[]{:S(2)}) %collective-permute-start.32) | collective-permute-done | bytes 1048608 | tf_op jit(solution)/shard_map/ppermute | solution.py:595
  600.2 15.4 %collective-permute-done.33 = bf16[256,2048]{1,0:T(8,128)(2,1)S(1)} collective-permute-done((bf16[256,2048]{1,0:T(8,128)(2,1)S(1)}, bf16[256,2048]{1,0:T(8,128)(2,1)S(1)}, u32[]{:S(2)}, u32[]{:S(2)}) %collective-permute-start.33) | collective-permute-done | bytes 1048608 | tf_op jit(solution)/shard_map/ppermute | solution.py:595
  623.9 14.6 %collective-permute-done.37.refs_1_.refs_2_ = bf16[256,2048]{1,0:T(8,128)(2,1)S(1)} collective-permute-done((bf16[256,2048]{1,0:T(8,128)(2,1)S(1)}, bf16[256,2048]{1,0:T(8,128)(2,1)S(1)}, u32[]{:S(2)}, u32[]{:S(2)}) %collective-permute-start.37) | collective-permute-done | bytes 1048608 | tf_op jit(solution)/shard_map/ppermute | solution.py:590
  648.8 20.4 %collective-permute-done.41.refs_0_.refs_1_ = bf16[256,2048]{1,0:T(8,128)(2,1)S(1)} collective-permute-done((bf16[256,2048]{1,0:T(8,128)(2,1)S(1)}, bf16[256,2048]{1,0:T(8,128)(2,1)S(1)}, u32[]{:S(2)}, u32[]{:S(2)}) %collective-permute-start.41) | collective-permute-done | bytes 1048608 | tf_op jit(solution)/shard_map/ppermute | solution.py:591
  697.9 17.9 %attend_backward.1 = (f32[1024,512]{1,0:T(8,128)}, f32[1024,512]{1,0:T(8,128)}, bf16[1024,512]{1,0:T(8,128)(2,1)}, f32[1024,1]{1,0:T(8,128)}, f32[1024,1]{1,0:T(...) custom-call(f32[1024,1536]{1,0:T(8,128)} %copy-done.3, f32[1024,1536]{1,0:T(8,128)} %copy-done.3, f32[1024,1]{1,0:T(8,128)} %copy.71.qs_ref, ...), custom_call_target="tpu_custom_call" | custom-call | flops 5368709120 | bytes 20971520 | tf_op jit(solution)/shard_map/attend_backward/pallas_call | solution.py:180
  718.4 12.2 %all-reduce = (f32[1024]{0:T(1024)S(1)}, f32[1024]{0:T(1024)S(1)}) all-reduce(f32[1024]{0:T(1024)S(1)} %reduce.1, f32[1024]{0:T(1024)S(1)} %reduce), channel_id=1, replica_groups=mesh['dp'=2,'row'=4,'col'=4] {'col'}, use_global_device_ids=true, to_apply=%region_5.6 | all-reduce | flops 2048 | bytes 16384 | tf_op jit(solution)/shard_map/psum | solution.py:807
  779.3 10.6 %add_convert_fusion.2 = bf16[2048,1024]{1,0:T(8,128)(2,1)} fusion(bf16[2048,1024]{1,0:T(8,128)(2,1)} %collective-permute-done.55, bf16[1024,2048]{1,0:T(8,128)(2,1)} %get-tuple-element.315, bf16[1024,2048]{1,0:T(8,128)(2,1)} %get-tuple-element.316, s32[]{:T(128)S(6)} %select_n.216), kind=kOutput, calls=%fused_computation.2 | convolution fusion | flops 4301258752 | bytes 14680068 | tf_op jit(solution)/shard_map/dot_general | solution.py:35
  863.2 16.3 %collective-permute-done.47 = bf16[256,2048]{1,0:T(8,128)(2,1)S(1)} collective-permute-done((bf16[256,2048]{1,0:T(8,128)(2,1)S(1)}, bf16[256,2048]{1,0:T(8,128)(2,1)S(1)}, u32[]{:S(2)}, u32[]{:S(2)}) %collective-permute-start.47) | collective-permute-done | bytes 1048608 | tf_op jit(solution)/shard_map/ppermute | solution.py:595
  895.0 15.0 %collective-permute-done.49.refs_1_.refs_2_ = bf16[256,2048]{1,0:T(8,128)(2,1)} collective-permute-done((bf16[256,2048]{1,0:T(8,128)(2,1)S(1)}, bf16[256,2048]{1,0:T(8,128)(2,1)}, u32[]{:S(2)}, u32[]{:S(2)}) %collective-permute-start.49) | collective-permute-done | bytes 1048608 | tf_op jit(solution)/shard_map/ppermute | solution.py:590
  926.4 14.1 %collective-permute-done.53.refs_0_.refs_1_ = bf16[256,2048]{1,0:T(8,128)(2,1)S(1)} collective-permute-done((bf16[256,2048]{1,0:T(8,128)(2,1)}, bf16[256,2048]{1,0:T(8,128)(2,1)S(1)}, u32[]{:S(2)}, u32[]{:S(2)}) %collective-permute-start.53) | collective-permute-done | bytes 1048608 | tf_op jit(solution)/shard_map/ppermute | solution.py:591
  941.9 34.1 %reduce-scatter.10.cloned.1.call-done = bf16[512,1024]{1,0:T(8,128)(2,1)} async-done(((bf16[2048,1024]{1,0:T(8,128)(2,1)}), bf16[512,1024]{1,0:T(8,128)(2,1)}) %reduce-scatter.10.cloned.1.call-update) | async-done | bytes 1048592 | tf_op jit(solution)/shard_map/reduce_scatter | solution.py:660
  996.3 26.6 %reduce-scatter.14.cloned.1.call-done = bf16[512,768]{1,0:T(8,128)(2,1)} async-done(((bf16[2048,768]{1,0:T(8,128)(2,1)}), bf16[512,768]{1,0:T(8,128)(2,1)}) %reduce-scatter.14.cloned.1.call-update) | async-done | bytes 786448 | tf_op jit(solution)/shard_map/reduce_scatter | solution.py:660
  (378 shorter events, 374.9 us)
Async XLA Ops:
  7.2 51.4 %all-gather.4.cloned.1.call-start = ((), (), s32[]{:S(2)}) async-start(), calls=%async_computation.5 | async-start | bytes 7077888 | tf_op jit(solution)/shard_map/all_gather | solution.py:587
  9.5 293.4 %all-gather.6.cloned.1.call-start = ((), (), s32[]{:S(2)}) async-start(), calls=%async_computation.6 | async-start | bytes 9437184 | tf_op jit(solution)/shard_map/all_gather | solution.py:587
  10.6 292.2 %all-gather.8.cloned.1.call-start = ((), (), s32[]{:S(2)}) async-start(), calls=%async_computation.7 | async-start | bytes 9437184 | tf_op jit(solution)/shard_map/all_gather | solution.py:587
  13.1 881.9 %reduce-scatter.12.cloned.1.call-start = ((), (), s32[]{:S(2)}) async-start(), calls=%async_computation.11 | async-start | bytes 1310720 | tf_op jit(solution)/shard_map/reduce_scatter | solution.py:660
  101.9 45.5 %collective-permute-start = (bf16[1024,512]{1,0:T(8,128)(2,1)}, bf16[1024,512]{1,0:T(8,128)(2,1)S(1)}, u32[]{:S(2)}, u32[]{:S(2)}) collective-permute-start(bf16[1024,512]{1,0:T(8,128)(2,1)} %get-tuple-element.347.refs_0_.att_ref), channel_id=1, source_target_pairs={{0,1},{1,2},{2,3},{4,5},{5,6},{6,7},{8,9},{9,10},{10,11},{12,13},{... | collective-permute-start | bytes 3145736 | tf_op jit(solution)/shard_map/ppermute | solution.py:590
  103.4 29.3 %collective-permute-start.6 = (bf16[256,512]{1,0:T(8,128)(2,1)S(1)}, bf16[256,512]{1,0:T(8,128)(2,1)S(1)}, u32[]{:S(2)}, u32[]{:S(2)}) collective-permute-start(bf16[256,512]{1,0:T(8,128)(2,1)S(1)} %constant_dynamic-slice_fusion.12), channel_id=1, source_target_pairs={{0,3},{1,0},{2,1},{3,2},{4,7},{5,4},{6,5},{7,6},{8,11},{9,8},{10,9... | collective-permute-start | bytes 786440 | tf_op jit(solution)/shard_map/ppermute | solution.py:702
  103.5 34.8 %collective-permute-start.7 = (bf16[256,512]{1,0:T(8,128)(2,1)S(1)}, bf16[256,512]{1,0:T(8,128)(2,1)S(1)}, u32[]{:S(2)}, u32[]{:S(2)}) collective-permute-start(bf16[256,512]{1,0:T(8,128)(2,1)S(1)} %constant_dynamic-slice_fusion.12), channel_id=1, source_target_pairs={{0,2},{1,3},{2,0},{3,1},{4,6},{5,7},{6,4},{7,5},{8,10},{9,11},{10,... | collective-permute-start | bytes 786440 | tf_op jit(solution)/shard_map/ppermute | solution.py:702
  105.6 35.9 %collective-permute-start.8 = (bf16[256,512]{1,0:T(8,128)(2,1)S(1)}, bf16[256,512]{1,0:T(8,128)(2,1)S(1)}, u32[]{:S(2)}, u32[]{:S(2)}) collective-permute-start(bf16[256,512]{1,0:T(8,128)(2,1)S(1)} %constant_dynamic-slice_fusion.12), channel_id=1, source_target_pairs={{0,1},{1,2},{2,3},{3,0},{4,5},{5,6},{6,7},{7,4},{8,9},{9,10},{10,1... | collective-permute-start | bytes 786440 | tf_op jit(solution)/shard_map/ppermute | solution.py:702
  142.5 30.2 %collective-permute-start.3 = (bf16[1024,512]{1,0:T(8,128)(2,1)S(1)}, bf16[1024,512]{1,0:T(8,128)(2,1)S(1)}, u32[]{:S(2)}, u32[]{:S(2)}) collective-permute-start(bf16[1024,512]{1,0:T(8,128)(2,1)S(1)} %copy-done.11), channel_id=1, source_target_pairs={{1,0},{2,1},{3,2},{5,4},{6,5},{7,6},{9,8},{10,9},{11,10},{13,12},{... | collective-permute-start | bytes 3145736 | tf_op jit(solution)/shard_map/ppermute | solution.py:591
  143.8 48.5 %collective-permute-start.14 = (bf16[1024,512]{1,0:T(8,128)(2,1)}, bf16[1024,512]{1,0:T(8,128)(2,1)}, u32[]{:S(2)}, u32[]{:S(2)}) collective-permute-start(bf16[1024,512]{1,0:T(8,128)(2,1)} %constant_dynamic-slice_fusion.13), channel_id=1, source_target_pairs={{0,4},{4,0},{8,12},{12,8},{1,5},{5,1},{9,13},{13,9},{2,6},{6,2},{1... | collective-permute-start | bytes 3145736 | tf_op jit(solution)/shard_map/ppermute | solution.py:668
  145.3 47.5 %collective-permute-start.15 = (bf16[1024,512]{1,0:T(8,128)(2,1)}, bf16[1024,512]{1,0:T(8,128)(2,1)}, u32[]{:S(2)}, u32[]{:S(2)}) collective-permute-start(bf16[1024,512]{1,0:T(8,128)(2,1)} %constant_dynamic-slice_fusion.13), channel_id=1, source_target_pairs={{0,8},{8,0},{4,12},{12,4},{1,9},{9,1},{5,13},{13,5},{2,10},{10,2},... | collective-permute-start | bytes 3145736 | tf_op jit(solution)/shard_map/ppermute | solution.py:668
  146.1 69.3 %collective-permute-start.10 = (bf16[1024,512]{1,0:T(8,128)(2,1)}, bf16[1024,512]{1,0:T(8,128)(2,1)}, u32[]{:S(2)}, u32[]{:S(2)}) collective-permute-start(bf16[1024,512]{1,0:T(8,128)(2,1)} %pad_maximum_fusion.1), channel_id=1, source_target_pairs={{0,8},{8,0},{4,12},{12,4},{1,9},{9,1},{5,13},{13,5},{2,10},{10,2},... | collective-permute-start | bytes 3145736 | tf_op jit(solution)/shard_map/ppermute | solution.py:668
  147.4 68.0 %collective-permute-start.9 = (bf16[1024,512]{1,0:T(8,128)(2,1)}, bf16[1024,512]{1,0:T(8,128)(2,1)}, u32[]{:S(2)}, u32[]{:S(2)}) collective-permute-start(bf16[1024,512]{1,0:T(8,128)(2,1)} %pad_maximum_fusion.1), channel_id=1, source_target_pairs={{0,4},{4,0},{8,12},{12,8},{1,5},{5,1},{9,13},{13,9},{2,6},{6,2},{1... | collective-permute-start | bytes 3145736 | tf_op jit(solution)/shard_map/ppermute | solution.py:668
  193.9 39.2 %collective-permute-start.16 = (bf16[512,512]{1,0:T(8,128)(2,1)S(1)}, bf16[512,512]{1,0:T(8,128)(2,1)S(1)}, u32[]{:S(2)}, u32[]{:S(2)}) collective-permute-start(bf16[512,512]{1,0:T(8,128)(2,1)S(1)} %slice.53), channel_id=1, source_target_pairs={{0,8},{8,0},{4,12},{12,4},{1,9},{9,1},{5,13},{13,5},{2,10},{10,2},... | collective-permute-start | bytes 1572872 | tf_op jit(solution)/shard_map/ppermute | solution.py:676
  195.9 38.1 %collective-permute-start.17 = (bf16[512,512]{1,0:T(8,128)(2,1)S(1)}, bf16[512,512]{1,0:T(8,128)(2,1)S(1)}, u32[]{:S(2)}, u32[]{:S(2)}) collective-permute-start(bf16[512,512]{1,0:T(8,128)(2,1)S(1)} %slice.54), channel_id=1, source_target_pairs={{0,4},{4,0},{8,12},{12,8},{1,5},{5,1},{9,13},{13,9},{2,6},{6,2},{1... | collective-permute-start | bytes 1572872 | tf_op jit(solution)/shard_map/ppermute | solution.py:677
  234.8 68.1 %collective-permute-start.18 = (bf16[4,1024,512]{2,1,0:T(8,128)(2,1)}, bf16[4,1024,512]{2,1,0:T(8,128)(2,1)}, u32[]{:S(2)}, u32[]{:S(2)}) collective-permute-start(bf16[4,1024,512]{2,1,0:T(8,128)(2,1)} %bitcast_dynamic-update-slice_fusion.6.refs_13_.wd_own_ref), channel_id=1, source_target_pairs={{0,16},{16,0},{1,17},{17,1},{2,18},{18,2},{3,19},{19,3},{4,20},{20... | collective-permute-start | bytes 12582920 | tf_op jit(solution)/shard_map/ppermute | solution.py:693
  242.1 60.8 %collective-permute-start.13 = (bf16[4,1024,512]{2,1,0:T(8,128)(2,1)}, bf16[4,1024,512]{2,1,0:T(8,128)(2,1)}, u32[]{:S(2)}, u32[]{:S(2)}) collective-permute-start(bf16[4,1024,512]{2,1,0:T(8,128)(2,1)} %bitcast_dynamic-update-slice_fusion.8.refs_7_.wo_own_ref), channel_id=1, source_target_pairs={{0,16},{16,0},{1,17},{17,1},{2,18},{18,2},{3,19},{19,3},{4,20},{20... | collective-permute-start | bytes 12582920 | tf_op jit(solution)/shard_map/ppermute | solution.py:693
  242.9 33.2 %collective-permute-start.4 = (bf16[1024,512]{1,0:T(8,128)(2,1)S(1)}, bf16[1024,512]{1,0:T(8,128)(2,1)}, u32[]{:S(2)}, u32[]{:S(2)}) collective-permute-start(bf16[1024,512]{1,0:T(8,128)(2,1)S(1)} %collective-permute-done.3.refs_4_), channel_id=1, source_target_pairs={{1,0},{2,1},{5,4},{6,5},{9,8},{10,9},{13,12},{14,13},{17,16},{18,1... | collective-permute-start | bytes 3145736 | tf_op jit(solution)/shard_map/ppermute | solution.py:591
  244.2 33.8 %collective-permute-start.2 = (bf16[1024,512]{1,0:T(8,128)(2,1)S(1)}, bf16[1024,512]{1,0:T(8,128)(2,1)S(1)}, u32[]{:S(2)}, u32[]{:S(2)}) collective-permute-start(bf16[1024,512]{1,0:T(8,128)(2,1)S(1)} %collective-permute-done.1.refs_2_), channel_id=1, source_target_pairs={{2,3},{6,7},{10,11},{14,15},{18,19},{22,23},{26,27},{30,31}} | collective-permute-start | bytes 3145736 | tf_op jit(solution)/shard_map/ppermute | solution.py:590
  470.2 47.2 %collective-permute-start.27 = (bf16[256,2048]{1,0:T(8,128)(2,1)S(1)}, bf16[256,2048]{1,0:T(8,128)(2,1)S(1)}, u32[]{:S(2)}, u32[]{:S(2)}) collective-permute-start(bf16[256,2048]{1,0:T(8,128)(2,1)S(1)} %collective-permute-done.26.refs_3_.refs_2_), channel_id=1, source_target_pairs={{2,3},{6,7},{10,11},{14,15},{18,19},{22,23},{26,27},{30,31}} | collective-permute-start | bytes 3145736 | tf_op jit(solution)/shard_map/ppermute | solution.py:590
  471.0 46.5 %collective-permute-start.30 = (bf16[256,2048]{1,0:T(8,128)(2,1)S(1)}, bf16[256,2048]{1,0:T(8,128)(2,1)}, u32[]{:S(2)}, u32[]{:S(2)}) collective-permute-start(bf16[256,2048]{1,0:T(8,128)(2,1)S(1)} %collective-permute-done.29.refs_0_.refs_1_), channel_id=1, source_target_pairs={{1,0},{5,4},{9,8},{13,12},{17,16},{21,20},{25,24},{29,28}} | collective-permute-start | bytes 3145736 | tf_op jit(solution)/shard_map/ppermute | solution.py:591
  647.2 44.0 %collective-permute-start.39 = (bf16[256,2048]{1,0:T(8,128)(2,1)S(1)}, bf16[256,2048]{1,0:T(8,128)(2,1)}, u32[]{:S(2)}, u32[]{:S(2)}) collective-permute-start(bf16[256,2048]{1,0:T(8,128)(2,1)S(1)} %collective-permute-done.38.refs_3_.refs_2_), channel_id=1, source_target_pairs={{2,3},{6,7},{10,11},{14,15},{18,19},{22,23},{26,27},{30,31}} | collective-permute-start | bytes 3145736 | tf_op jit(solution)/shard_map/ppermute | solution.py:590
  747.4 31.9 %collective-permute-start.55 = (bf16[2048,1024]{1,0:T(8,128)(2,1)}, bf16[2048,1024]{1,0:T(8,128)(2,1)}, u32[]{:S(2)}, u32[]{:S(2)}) collective-permute-start(bf16[2048,1024]{1,0:T(8,128)(2,1)} %convolution_convert_fusion.2), channel_id=1, source_target_pairs={{0,16},{16,0},{1,17},{17,1},{2,18},{18,2},{3,19},{19,3},{4,20},{20... | collective-permute-start | bytes 12582920 | tf_op jit(solution)/shard_map/ppermute | solution.py:656
  779.0 137.5 %reduce-scatter.6.cloned.1.call-start = ((), (), s32[]{:S(2)}) async-start(), calls=%async_computation.8 | async-start | bytes 5242880 | tf_op jit(solution)/shard_map/reduce_scatter | solution.py:660
  790.0 131.7 %reduce-scatter.8.cloned.1.call-start = ((), (), s32[]{:S(2)}) async-start(), calls=%async_computation.9 | async-start | bytes 5242880 | tf_op jit(solution)/shard_map/reduce_scatter | solution.py:660
  811.5 164.5 %reduce-scatter.10.cloned.1.call-start = ((), (), s32[]{:S(2)}) async-start(), calls=%async_computation.10 | async-start | bytes 5242880 | tf_op jit(solution)/shard_map/reduce_scatter | solution.py:660
  833.3 189.7 %reduce-scatter.14.cloned.1.call-start = ((), (), s32[]{:S(2)}) async-start(), calls=%async_computation.12 | async-start | bytes 3932160 | tf_op jit(solution)/shard_map/reduce_scatter | solution.py:660
  851.4 28.1 %collective-permute-start.47 = (bf16[256,2048]{1,0:T(8,128)(2,1)S(1)}, bf16[256,2048]{1,0:T(8,128)(2,1)S(1)}, u32[]{:S(2)}, u32[]{:S(2)}) collective-permute-start(bf16[256,2048]{1,0:T(8,128)(2,1)S(1)} %copy-done.38), channel_id=1, source_target_pairs={{0,1},{1,2},{2,3},{4,5},{5,6},{6,7},{8,9},{9,10},{10,11},{12,13},{... | collective-permute-start | bytes 3145736 | tf_op jit(solution)/shard_map/ppermute | solution.py:595
  916.5 59.5 %collective-permute-start.56 = (bf16[512,1024]{1,0:T(8,128)(2,1)}, bf16[512,1024]{1,0:T(8,128)(2,1)}, u32[]{:S(2)}, u32[]{:S(2)}) collective-permute-start(bf16[512,1024]{1,0:T(8,128)(2,1)} %reduce-scatter.6.cloned.1.call-done), channel_id=1, source_target_pairs={{0,16},{16,0},{1,17},{17,1},{2,18},{18,2},{3,19},{19,3},{4,20},{20... | collective-permute-start | bytes 3145736 | tf_op jit(solution)/shard_map/ppermute | solution.py:650
  921.7 63.9 %collective-permute-start.58 = (bf16[512,1024]{1,0:T(8,128)(2,1)}, bf16[512,1024]{1,0:T(8,128)(2,1)}, u32[]{:S(2)}, u32[]{:S(2)}) collective-permute-start(bf16[512,1024]{1,0:T(8,128)(2,1)} %reduce-scatter.8.cloned.1.call-done), channel_id=1, source_target_pairs={{0,16},{16,0},{1,17},{17,1},{2,18},{18,2},{3,19},{19,3},{4,20},{20... | collective-permute-start | bytes 3145736 | tf_op jit(solution)/shard_map/ppermute | solution.py:650
  924.7 112.8 %collective-permute-start.51 = (bf16[256,2048]{1,0:T(8,128)(2,1)S(1)}, bf16[256,2048]{1,0:T(8,128)(2,1)}, u32[]{:S(2)}, u32[]{:S(2)}) collective-permute-start(bf16[256,2048]{1,0:T(8,128)(2,1)S(1)} %collective-permute-done.50.refs_3_.refs_2_), channel_id=1, source_target_pairs={{2,3},{6,7},{10,11},{14,15},{18,19},{22,23},{26,27},{30,31}} | collective-permute-start | bytes 3145736 | tf_op jit(solution)/shard_map/ppermute | solution.py:590
  940.4 97.1 %collective-permute-start.54 = (bf16[256,2048]{1,0:T(8,128)(2,1)S(1)}, bf16[256,2048]{1,0:T(8,128)(2,1)}, u32[]{:S(2)}, u32[]{:S(2)}) collective-permute-start(bf16[256,2048]{1,0:T(8,128)(2,1)S(1)} %collective-permute-done.53.refs_0_.refs_1_), channel_id=1, source_target_pairs={{1,0},{5,4},{9,8},{13,12},{17,16},{21,20},{25,24},{29,28}} | collective-permute-start | bytes 3145736 | tf_op jit(solution)/shard_map/ppermute | solution.py:591
  (109 other events, 2082.3 us)
Sparse Core Ops, SparseCore 0:
  10.5 48.1 all-gather.3
  61.1 54.2 all-gather.5
  117.3 76.5 all-gather.7
  779.2 28.1 reduce-scatter.11
  810.7 52.5 reduce-scatter.5
  866.8 53.0 reduce-scatter.7
  923.4 52.5 reduce-scatter.9
  979.0 43.8 reduce-scatter.13

commit v8 on v7

--- a/solution.py
+++ b/solution.py
@@ -218,13 +218,13 @@
 
 
 def forward_chunk_kernel(
-    idx_ref, *refs, blocks, tiles,
+    idx_ref, *refs, out_steps, tiles,
 ):
     own_ref, left1, left2, left3, right1, right2, right3 = refs[:7]
     wo_own_ref, wo_oth_ref, x_ref, gain_ref, wg_ref, wu_ref, wd_own_ref, wd_oth_ref = refs[7:15]
     raw_ref, scale_ref, hb_ref, gate_ref, up_ref, mixed_ref, part_ref, acc_ref, att_ref = refs[-9:]
-    block = wo_own_ref.shape[2]
-    depth = wo_own_ref.shape[1]
+    depth, out_tile = wo_own_ref.shape
+    blocks, _, block = wd_own_ref.shape
     step = pl.program_id(0)
     core = idx_ref[1]
 
@@ -239,18 +239,19 @@
                 start = half * depth + number * quarter
                 att_ref[:, start : start + quarter] = piece[:, half * quarter : (half + 1) * quarter]
 
-    @pl.when(step < blocks)
+    @pl.when(step < out_steps)
     def _():
         own = att_ref[:, pl.ds(pl.multiple_of(core * depth, depth), depth)]
         other = att_ref[:, pl.ds(pl.multiple_of((1 - core) * depth, depth), depth)]
-        raw_ref[:, pl.ds(pl.multiple_of(step * block, block), block)] = plain_dot(
-            own, wo_own_ref[0]
-        ) + plain_dot(other, wo_oth_ref[0])
-
-    @pl.when(step == blocks - 1)
-    def _():
-        raw = raw_ref[...]
+        acc_ref[:, pl.ds(pl.multiple_of(step * out_tile, out_tile), out_tile)] = plain_dot(
+            own, wo_own_ref[...]
+        ) + plain_dot(other, wo_oth_ref[...])
+
+    @pl.when(step == out_steps - 1)
+    def _():
+        raw = acc_ref[...]
         scale = lax.rsqrt(jnp.mean(raw * raw, axis=1, keepdims=True) + EPS)
+        raw_ref[...] = raw.astype(BF16)
         scale_ref[...] = scale
         hb_ref[...] = (x_ref[...].astype(F32) + raw * scale * gain_ref[...]).astype(BF16)
         acc_ref[...] = jnp.zeros_like(acc_ref)
@@ -266,15 +267,15 @@
         for j in range(blocks):
             acc_ref[:, j * block : (j + 1) * block] += plain_dot(mixed, wd_ref[j])
 
-    @pl.when((step >= blocks) & (step < blocks + tiles // 2))
+    @pl.when((step >= out_steps) & (step < out_steps + tiles // 2))
     def _():
         tile_work(wd_own_ref)
 
-    @pl.when(step >= blocks + tiles // 2)
+    @pl.when(step >= out_steps + tiles // 2)
     def _():
         tile_work(wd_oth_ref)
 
-    @pl.when(step == blocks + tiles - 1)
+    @pl.when(step == out_steps + tiles - 1)
     def _():
         part_ref[...] = acc_ref[...].astype(BF16)
 
@@ -285,28 +286,30 @@
 def forward_chunk(index, attended, out_halves, block_input, gain, w_gate, w_up, down_halves, chunk, before):
     tokens, width = block_input.shape
     hidden = w_gate.shape[1]
-    blocks, depth, block = out_halves[0].shape
+    depth = out_halves[0].shape[0]
+    blocks, _, block = down_halves[0].shape
     tiles = hidden // TILE
+    out_steps = width // TILE
 
     def tile_of(j, idx):
-        return half_tile(jnp.maximum(j - blocks, 0), idx[1], tiles)
+        return half_tile(jnp.maximum(j - out_steps, 0), idx[1], tiles)
 
     rows = pl.BlockSpec((chunk, width), lambda j, idx: (idx[0], 0))
-    out_half = pl.BlockSpec((1, depth, block), lambda j, idx: (jnp.minimum(j, blocks - 1), 0, 0))
+    out_half = pl.BlockSpec((depth, TILE), lambda j, idx: (0, jnp.minimum(j, out_steps - 1)))
     up_tile = pl.BlockSpec((width, TILE), lambda j, idx: (0, tile_of(j, idx)))
     down_own = pl.BlockSpec(
-        (blocks, TILE, block), lambda j, idx: (0, jnp.clip(j - blocks, 0, tiles // 2 - 1), 0)
+        (blocks, TILE, block), lambda j, idx: (0, jnp.clip(j - out_steps, 0, tiles // 2 - 1), 0)
     )
     down_oth = pl.BlockSpec(
-        (blocks, TILE, block), lambda j, idx: (0, jnp.maximum(j - blocks - tiles // 2, 0), 0)
+        (blocks, TILE, block), lambda j, idx: (0, jnp.maximum(j - out_steps - tiles // 2, 0), 0)
     )
     act_tile = pl.BlockSpec((chunk, TILE), lambda j, idx: (idx[0], tile_of(j, idx)))
     before = tuple(before)
     return pl.pallas_call(
-        functools.partial(forward_chunk_kernel, blocks=blocks, tiles=tiles),
+        functools.partial(forward_chunk_kernel, out_steps=out_steps, tiles=tiles),
         grid_spec=pltpu.PrefetchScalarGridSpec(
             num_scalar_prefetch=1,
-            grid=(blocks + tiles,),
+            grid=(out_steps + tiles,),
             in_specs=[
                 *[pl.BlockSpec((chunk, attended[0].shape[1]), lambda j, idx: (idx[0], 0))] * 7,
                 out_half, out_half, rows, pl.BlockSpec((1, width), lambda j, idx: (0, 0)),
@@ -319,7 +322,7 @@
             scratch_shapes=[pltpu.VMEM((chunk, width), F32), pltpu.VMEM((chunk, 2 * depth), BF16)],
         ),
         out_shape=[
-            jax.ShapeDtypeStruct((tokens, width), F32),
+            jax.ShapeDtypeStruct((tokens, width), BF16),
             jax.ShapeDtypeStruct((tokens, 1), F32),
             jax.ShapeDtypeStruct((tokens, width), BF16),
             jax.ShapeDtypeStruct((tokens, hidden), BF16),
@@ -339,11 +342,10 @@
 
 
 def backward_chunk_kernel(
-    idx_ref, raw_ref, scale_ref, x_ref, grad_ref, attn_gain_ref, mlp_gain_ref,
-    gate_ref, up_ref, wg_ref, wu_ref, wd_own_ref, wd_oth_ref, *refs, blocks, tiles, choices,
+    idx_ref, grad_ref, mlp_gain_ref, gate_ref, up_ref, wg_ref, wu_ref, wd_own_ref, wd_oth_ref, *refs, tiles, choices,
 ):
-    out_ref, gdi_ref, gg_ref, gu_ref, part_ref, gain_grad_ref, acc_ref, down_ref, sem = refs[-9:]
-    block = wd_own_ref.shape[2]
+    gdi_ref, gg_ref, gu_ref, part_ref, gain_grad_ref, acc_ref, down_ref, sem = refs[-8:]
+    blocks, _, block = wd_own_ref.shape
     step = pl.program_id(0)
 
     @pl.when(step == 0)
@@ -352,12 +354,9 @@
         down_raw = down_ref[...].astype(F32)
         down_scale = lax.rsqrt(jnp.mean(down_raw * down_raw, axis=1, keepdims=True) + EPS)
         unit = down_raw * down_scale
-        mlp_gain = mlp_gain_ref[...]
-        hidden = x_ref[...].astype(F32) + raw_ref[...] * scale_ref[...] * attn_gain_ref[...]
-        out_ref[...] = (hidden + unit * mlp_gain).astype(BF16)
         grad_y = grad_ref[...].astype(F32)
         gain_grad_ref[...] = jnp.sum(grad_y * unit, axis=0, keepdims=True)
-        grad_unit = grad_y * mlp_gain
+        grad_unit = grad_y * mlp_gain_ref[...]
         mean = jnp.mean(grad_unit * unit, axis=1, keepdims=True)
         gdi_ref[...] = (down_scale * (grad_unit - unit * mean)).astype(BF16)
         acc_ref[...] = jnp.zeros_like(acc_ref)
@@ -388,10 +387,9 @@
 
 
 def backward_chunk(
-    index, down_rows, raw, scale, block_input, grad_output, attn_gain, mlp_gain, gate, up, w_gate, w_up,
-    down_halves, chunk, before,
+    index, down_rows, grad_output, mlp_gain, gate, up, w_gate, w_up, down_halves, chunk, before,
 ):
-    tokens, width = block_input.shape
+    tokens, width = grad_output.shape
     hidden = w_gate.shape[1]
     blocks, _, block = down_halves[0].shape
     tiles = hidden // TILE
@@ -400,99 +398,118 @@
         return half_tile(j, idx[1], tiles)
 
     rows = pl.BlockSpec((chunk, width), lambda j, idx: (idx[0], 0))
-    fixed = pl.BlockSpec((chunk, width), lambda j, idx: (0, 0))
     gain_row = pl.BlockSpec((1, width), lambda j, idx: (0, 0))
     up_tile = pl.BlockSpec((width, TILE), lambda j, idx: (0, tile_of(j, idx)))
     act_tile = pl.BlockSpec((chunk, TILE), lambda j, idx: (idx[0], tile_of(j, idx)))
     before = tuple(before)
     return pl.pallas_call(
-        functools.partial(backward_chunk_kernel, blocks=blocks, tiles=tiles, choices=len(down_rows)),
+        functools.partial(backward_chunk_kernel, tiles=tiles, choices=len(down_rows)),
         grid_spec=pltpu.PrefetchScalarGridSpec(
             num_scalar_prefetch=1,
             grid=(tiles,),
             in_specs=[
-                rows, pl.BlockSpec((chunk, 1), lambda j, idx: (idx[0], 0)), rows, rows, gain_row, gain_row,
-                act_tile, act_tile, up_tile, up_tile,
+                rows, gain_row, act_tile, act_tile, up_tile, up_tile,
                 pl.BlockSpec((blocks, TILE, block), lambda j, idx: (0, jnp.minimum(j, tiles // 2 - 1), 0)),
                 pl.BlockSpec((blocks, TILE, block), lambda j, idx: (0, jnp.maximum(j - tiles // 2, 0), 0)),
             ] + [pl.BlockSpec(memory_space=pl.ANY)] * (len(down_rows) + len(before)),
-            out_specs=[rows, rows, act_tile, act_tile, fixed, gain_row],
+            out_specs=[rows, act_tile, act_tile, pl.BlockSpec((chunk, width), lambda j, idx: (0, 0)), gain_row],
             scratch_shapes=[
                 pltpu.VMEM((chunk, width), F32), pltpu.VMEM((chunk, width), BF16), pltpu.SemaphoreType.DMA(()),
             ],
         ),
         out_shape=[
             jax.ShapeDtypeStruct((tokens, width), BF16),
-            jax.ShapeDtypeStruct((tokens, width), BF16),
             jax.ShapeDtypeStruct((tokens, hidden), BF16),
             jax.ShapeDtypeStruct((tokens, hidden), BF16),
             jax.ShapeDtypeStruct((chunk, width), BF16),
             jax.ShapeDtypeStruct((1, width), F32),
         ],
-        input_output_aliases={13 + len(down_rows) + i: i for i in range(len(before))},
+        input_output_aliases={9 + len(down_rows) + i: i for i in range(len(before))},
         compiler_params=pltpu.CompilerParams(vmem_limit_bytes=VMEM),
         cost_estimate=pl.CostEstimate(
             flops=6 * chunk * width * hidden, bytes_accessed=6 * width * hidden, transcendentals=0
         ),
         name="backward_chunk",
-    )(
-        index, raw, scale, block_input, grad_output, attn_gain, mlp_gain, gate, up, w_gate, w_up,
-        *down_halves, *down_rows, *before,
-    )
+    )(index, grad_output, mlp_gain, gate, up, w_gate, w_up, *down_halves, *down_rows, *before)
+
+
+PARTS = 4
 
 
 def attention_chunk_kernel(
-    idx_ref, grad_ref, raw_ref, scale_ref, gain_ref, wo_own_ref, wo_oth_ref, *refs, blocks, choices,
+    idx_ref, grad_ref, raw_ref, scale_ref, x_ref, attn_gain_ref, mlp_gain_ref, wo_own_ref, wo_oth_ref, *refs, choices,
 ):
-    gai_ref, gatt_ref, gain_grad_ref, mlp_ref, sem = refs[-5:]
-    fetch_choice(idx_ref, refs[:choices], mlp_ref, sem)
-    half, block = wo_own_ref.shape[1:]
+    gai_ref, gatt_ref, out_ref, gain_grad_ref, mlp_held_ref, down_held_ref, sem = refs[-7:]
+    half = wo_own_ref.shape[0]
     core = idx_ref[1]
+    step = pl.program_id(0)
+
+    @pl.when(step == 0)
+    def _():
+        fetch_choice(idx_ref, refs[:choices], mlp_held_ref, sem)
+        fetch_choice(idx_ref, refs[choices : 2 * choices], down_held_ref, sem)
+        gain_grad_ref[...] = jnp.zeros_like(gain_grad_ref)
+
+    size = grad_ref.shape[0]
+    here = pl.ds(pl.multiple_of(step * size, size), size)
     scale = scale_ref[...]
-    unit = raw_ref[...] * scale
-    grad_hidden = grad_ref[...].astype(F32) + mlp_ref[...].astype(F32)
-    gain_grad_ref[...] = jnp.sum(grad_hidden * unit, axis=0, keepdims=True)
-    grad_unit = grad_hidden * gain_ref[...]
+    unit = raw_ref[...].astype(F32) * scale
+    grad_hidden = grad_ref[...].astype(F32) + mlp_held_ref[here, :].astype(F32)
+    gain_grad_ref[...] += jnp.sum(grad_hidden * unit, axis=0, keepdims=True)
+    grad_unit = grad_hidden * attn_gain_ref[...]
     mean = jnp.mean(grad_unit * unit, axis=1, keepdims=True)
-    gai_ref[...] = (scale * (grad_unit - unit * mean)).astype(BF16)
+    grad_attn_in = (scale * (grad_unit - unit * mean)).astype(BF16)
+    gai_ref[...] = grad_attn_in
     for place, w_ref in ((core, wo_own_ref), (1 - core, wo_oth_ref)):
-        total = times_transposed(gai_ref[:, :block], w_ref[0])
-        for j in range(1, blocks):
-            total += times_transposed(gai_ref[:, j * block : (j + 1) * block], w_ref[j])
-        gatt_ref[:, pl.ds(pl.multiple_of(place * half, half), half)] = total.astype(BF16)
-
-
-def attention_chunk(index, mlp_rows, grad_output, raw, scale, gain, out_halves, half, chunk, before):
+        gatt_ref[:, pl.ds(pl.multiple_of(place * half, half), half)] = times_transposed(
+            grad_attn_in, w_ref[...]
+        ).astype(BF16)
+    down_raw = down_held_ref[here, :].astype(F32)
+    down_scale = lax.rsqrt(jnp.mean(down_raw * down_raw, axis=1, keepdims=True) + EPS)
+    hidden = x_ref[...].astype(F32) + unit * attn_gain_ref[...]
+    out_ref[...] = (hidden + down_raw * down_scale * mlp_gain_ref[...]).astype(BF16)
+
+
+def attention_chunk(
+    index, mlp_rows, down_rows, grad_output, raw, scale, block_input, attn_gain, mlp_gain, out_halves, half, chunk,
+    before,
+):
     tokens, width = grad_output.shape
-    blocks, _, block = out_halves[0].shape
-    rows = pl.BlockSpec((chunk, width), lambda j, idx: (idx[0], 0))
+    size = chunk // PARTS
+    rows = pl.BlockSpec((size, width), lambda j, idx: (PARTS * idx[0] + j, 0))
     gain_row = pl.BlockSpec((1, width), lambda j, idx: (0, 0))
-    own_heads = pl.BlockSpec((blocks, half, block), lambda j, idx: (0, 0, 0))
+    own_heads = pl.BlockSpec((half, width), lambda j, idx: (0, 0))
     before = tuple(before)
+    chosen = (*mlp_rows, *down_rows)
     return pl.pallas_call(
-        functools.partial(attention_chunk_kernel, blocks=blocks, choices=len(mlp_rows)),
+        functools.partial(attention_chunk_kernel, choices=len(mlp_rows)),
         grid_spec=pltpu.PrefetchScalarGridSpec(
             num_scalar_prefetch=1,
-            grid=(1,),
+            grid=(PARTS,),
             in_specs=[
-                rows, rows, pl.BlockSpec((chunk, 1), lambda j, idx: (idx[0], 0)), gain_row,
+                rows, rows, pl.BlockSpec((size, 1), lambda j, idx: (PARTS * idx[0] + j, 0)), rows, gain_row, gain_row,
                 own_heads, own_heads,
-            ] + [pl.BlockSpec(memory_space=pl.ANY)] * (len(mlp_rows) + len(before)),
-            out_specs=[rows, pl.BlockSpec((chunk, 2 * half), lambda j, idx: (idx[0], 0)), gain_row],
-            scratch_shapes=[pltpu.VMEM((chunk, width), BF16), pltpu.SemaphoreType.DMA(())],
+            ] + [pl.BlockSpec(memory_space=pl.ANY)] * (len(chosen) + len(before)),
+            out_specs=[
+                rows, pl.BlockSpec((size, 2 * half), lambda j, idx: (PARTS * idx[0] + j, 0)), rows, gain_row,
+            ],
+            scratch_shapes=[
+                pltpu.VMEM((chunk, width), BF16), pltpu.VMEM((chunk, width), BF16), pltpu.SemaphoreType.DMA(()),
+            ],
         ),
         out_shape=[
             jax.ShapeDtypeStruct((tokens, width), BF16),
             jax.ShapeDtypeStruct((tokens, 2 * half), BF16),
+            jax.ShapeDtypeStruct((tokens, width), BF16),
             jax.ShapeDtypeStruct((1, width), F32),
         ],
-        input_output_aliases={7 + len(mlp_rows) + i: i for i in range(len(before))},
+        input_output_aliases={9 + len(chosen) + i: i for i in range(len(before))},
         compiler_params=pltpu.CompilerParams(vmem_limit_bytes=VMEM),
         cost_estimate=pl.CostEstimate(
             flops=4 * chunk * width * half, bytes_accessed=16 * chunk * width, transcendentals=0
         ),
         name="attention_chunk",
-    )(index, grad_output, raw, scale, gain, *out_halves, *mlp_rows, *before)
+    )(index, grad_output, raw, scale, block_input, attn_gain, mlp_gain, *out_halves, *chosen, *before)
 
 
 def place_rows_kernel(idx_ref, *refs, choices):
@@ -692,21 +709,31 @@
             held = lax.dynamic_update_slice(held, piece[None], (block, start, 0))
         return held, lax.ppermute(held, "dp", swap)
 
+    def row_columns(pieces):
+        if rows != 4:
+            return lax.all_gather(pieces[0], "row", axis=1, tiled=True)
+        own, by_one, by_two, corner_top, corner_low = pieces
+        height, block = own.shape
+        held = unset((height, rows * block), own.dtype)
+        for piece, number, start in (
+            (own, row, 0), (by_one, row ^ 1, 0), (by_two, row ^ 2, 0),
+            (corner_top, row ^ 3, 0), (corner_low, row ^ 3, height // 2),
+        ):
+            held = lax.dynamic_update_slice(held, piece, (start, number * block))
+        return held
+
     full_qkv = gather(jnp.concatenate([w_query, w_key, w_value], axis=1), 0)
     full_gate = gather(w_gate, 0)
     full_up = gather(w_up, 0)
-    out_half = own_half(w_out, 0)
-    out_stack = jnp.concatenate(
-        [out_half]
-        + [
-            lax.ppermute(out_half, "col", [(i, (i - step) % cols) for i in range(cols)])
-            for step in range(1, cols)
-        ],
-        axis=0,
-    )
-    down_start, out_start = after((own_half(w_down, 0), out_stack), full_qkv)
-    down_pieces = row_first(down_start)
-    out_pieces = row_first(out_start)
+    out_pieces = row_first(own_half(w_out, 0))
+    out_pieces = row_second(out_pieces)
+    out_own = row_columns(out_pieces)
+    out_left, out_right = [out_own], [out_own]
+    for step in range(1, cols):
+        one, two = line_step(out_left[-1], out_right[-1], step)
+        out_left.append(one)
+        out_right.append(two)
+    down_pieces = row_first(after(own_half(w_down, 0), full_qkv))
 
     qkv = plain_dot(block_input, full_qkv)
     query_raw, key_raw = qkv[:, :local_width], qkv[:, local_width : 2 * local_width]
@@ -728,11 +755,14 @@
         from_left, from_right = line_step(lefts[-1], rights[-1], step)
         lefts.append(from_left)
         rights.append(from_right)
+        if step == 1:
+            out_halves = jnp.concatenate(
+                [out_own] + [out_right[k] + out_left[cols - k] for k in range(1, cols)], axis=0
+            )
+            out_halves = (out_halves, lax.ppermute(out_halves, "dp", swap))
         if step == 2:
             down_pieces = row_second(after(down_pieces, lefts[1], rights[1]))
-            out_pieces = row_second(after(out_pieces, lefts[1], rights[1]))
         if step == 3:
-            out_halves = row_blocks(out_pieces)
             down_halves = row_blocks(down_pieces)
     attended_all = (attended, *lefts[1:], *rights[1:])
 
@@ -750,19 +780,21 @@
     down_own = sum_slots(forward_work).astype(BF16)
     attn_raw, attn_scale, hidden_b, gate_proj, up_proj, mixed_act = held["forward"]
     mlp_parts = [None] * cols
+    down_slots = [None] * cols
 
     def backward_work(slot, down_rows):
+        down_slots[slot] = down_rows
         results = backward_chunk(
-            slot_index[slot], down_rows, attn_raw, attn_scale, block_input, grad_output, attn_row, mlp_row,
-            gate_proj, up_proj, full_gate, full_up, down_halves, chunk, held["backward"],
+            slot_index[slot], down_rows, grad_output, mlp_row, gate_proj, up_proj, full_gate, full_up,
+            down_halves, chunk, held["backward"],
         )
-        held["backward"] = results[:4]
-        mlp_parts[slot] = results[4]
-        gain_sums["mlp"] = gain_sums["mlp"] + results[5]
-        return results[4]
+        held["backward"] = results[:3]
+        mlp_parts[slot] = results[3]
+        gain_sums["mlp"] = gain_sums["mlp"] + results[4]
+        return results[3]
 
     gather_slots(down_own, backward_work)
-    block_output, grad_down_in, grad_gate_in, grad_up_in = held["backward"]
+    grad_down_in, grad_gate_in, grad_up_in = held["backward"]
 
     blocks = {}
     got = {}
@@ -786,18 +818,18 @@
 
     def attention_work(slot, mlp_rows):
         results = attention_chunk(
-            slot_index[slot], mlp_rows, grad_output, attn_raw, attn_scale, attn_row, out_halves, half_width,
-            chunk, held["attention"],
+            slot_index[slot], mlp_rows, down_slots[slot], grad_output, attn_raw, attn_scale, block_input, attn_row,
+            mlp_row, out_halves, half_width, chunk, held["attention"],
         )
-        held["attention"] = results[:2]
-        gain_sums["attn"] = gain_sums["attn"] + results[2]
+        held["attention"] = results[:3]
+        gain_sums["attn"] = gain_sums["attn"] + results[3]
         if slot == 3:
             hidden_left, up_right = after((hidden_b, grad_up_in), mlp_rows[0])
             blocks["up"] = sum_kept(hidden_left, own_half(up_right, 1), got["up"])
         return results[1]
 
     gather_slots(mlp_own, attention_work)
-    grad_attn_in, grad_att = held["attention"]
+    grad_attn_in, grad_att, block_output = held["attention"]
     own_grad_hidden = slot_rows(grad_output, 3).astype(F32) + mlp_own.astype(F32)
 
     query_dz, key_dz, grad_value_in, query_dot, key_dot, grad_query_gain, grad_key_gain = attend_backward(

time: 1060 us -> 1020 us (0.962)
  waiting for transfers between devices: 473 us -> 415 us
  starting transfers between devices: 96.9 us -> 111 us
    all_gather x3, waiting for transfers between devices: 41.2 us -> 0.04 us  [gather(): lax.all_gather(own_half(weight, axis), ('row', 'dp'), axis=axis, tiled=True)]
    ppermute x3 -> x1, waiting for transfers between devices: 32.8 us -> 0.01 us  [shards(): out_halves = (out_halves, lax.ppermute(out_halves, 'dp', swap))]
    ppermute x12 -> x15, waiting for transfers between devices: 48.6 us -> 69.1 us  [line_step(): lax.ppermute(from_left, 'col', [(i, i + 1) for i in range(step - 1, cols...]
    ppermute x2, waiting for transfers between devices: 0.6 us -> 15.7 us  [row_second(): lax.ppermute(pieces[1][:middle], 'row', by_y)]
    ppermute x2, waiting for transfers between devices: 18.8 us -> 7.11 us  [row_first(): lax.ppermute(half, 'row', by_y)]
    ppermute x12 -> x15, starting transfers between devices: 19.6 us -> 26.7 us  [line_step(): lax.ppermute(from_left, 'col', [(i, i + 1) for i in range(step - 1, cols...]
    ppermute x12 -> x15, waiting for transfers between devices: 130 us -> 125 us  [line_step(): lax.ppermute(from_right, 'col', [(i + 1, i) for i in range(cols - step)])]
  transfers between devices with their start and end apart: 78 -> 81, of which waited for: 36 -> 40; matrix products, arithmetic and copies ran while one was open for 14% -> 15% of each run, Pallas kernels for 18% -> 19%
where the time goes in v8:
time: 1020 us; the launch traced here: 1010 us
  waiting for transfers between devices  415 us (41%)
  Pallas kernels  265 us (26%)
  starting transfers between devices  111 us (11%)
  matrix products  80.5 us (8%)
  other arithmetic  57.3 us (6%)
  local copies, waits for them, and re-layouts  38.9 us (4%)
  blocking collectives  24.3 us (2%)
  between operations  16.1 us (2%)
    ppermute x15, waiting for transfers between devices, line_step(): lax.ppermute(from_right, 'col', [(i + 1, i) for i in range(cols - step)])  125 us
    pallas_call x4, Pallas kernels, forward_chunk(): pl.pallas_call(functools.partial(forward_chunk_kernel, out_steps=out_step...  93.2 us
    ppermute x9, waiting for transfers between devices, sum_step(): up = lax.ppermute(up, 'col', [(i, i + 1) for i in range(step)])  80.9 us
    pallas_call x4, Pallas kernels, backward_chunk(): pl.pallas_call(functools.partial(backward_chunk_kernel, tiles=tiles, choi...  80.3 us
    ppermute x15, waiting for transfers between devices, line_step(): lax.ppermute(from_left, 'col', [(i, i + 1) for i in range(step - 1, cols...  69.1 us
    reduce_scatter x5, waiting for transfers between devices, sum_kept(): lax.psum_scatter(total, 'row', scatter_dimension=0, tiled=True)  63.1 us
    dot_general x10, matrix products, left_transposed(): lax.dot_general(left_mat, right_mat, (((0,), (0,)), ((), ())), preferred_...  59.9 us
    pallas_call x4, Pallas kernels, attention_chunk(): pl.pallas_call(functools.partial(attention_chunk_kernel, choices=len(mlp_...  41.7 us
  transfers between devices with their start and end apart: 81, of which 40 were waited for; matrix products, arithmetic and copies ran while one was open for 15% of the time, Pallas kernels for 19%

profile of v8, /device:TPU:0, one launch (start us, length us, event | category | flops | bytes accessed | tf_op | source)
XLA Modules:
  0.0 1008.8 jit_solution(8620250158098807285)
XLA Ops:
  41.0 16.9 %collective-permute-done.11 = bf16[256,2048]{1,0:T(8,128)(2,1)} collective-permute-done((bf16[256,2048]{1,0:T(8,128)(2,1)}, bf16[256,2048]{1,0:T(8,128)(2,1)}, u32[]{:S(2)}, u32[]{:S(2)}) %collective-permute-start.11) | collective-permute-done | bytes 1048608 | tf_op jit(solution)/shard_map/ppermute | solution.py:607
  71.6 14.8 %collective-permute-done.14 = bf16[256,2048]{1,0:T(8,128)(2,1)} collective-permute-done((bf16[256,2048]{1,0:T(8,128)(2,1)}, bf16[256,2048]{1,0:T(8,128)(2,1)}, u32[]{:S(2)}, u32[]{:S(2)}) %collective-permute-start.14) | collective-permute-done | bytes 1048608 | tf_op jit(solution)/shard_map/ppermute | solution.py:608
  100.8 12.1 %all-reduce.1 = (f32[1024]{0:T(1024)S(1)}, f32[1024]{0:T(1024)S(1)}) all-reduce(f32[1024]{0:T(1024)S(1)} %get-tuple-element.382, f32[1024]{0:T(1024)S(1)} %get-tuple-element.381), channel_id=1, replica_groups=mesh['dp'=2,'row'=4,'col'=4] {'col'}, use_global_device_ids=true, to_apply=%region_1.2 | all-reduce | flops 2048 | bytes 16384 | tf_op jit(solution)/shard_map/psum | solution.py:740
  115.0 16.2 %attend_forward.1 = (bf16[1024,512]{1,0:T(8,128)(2,1)}, bf16[1024,512]{1,0:T(8,128)(2,1)}, bf16[1024,512]{1,0:T(8,128)(2,1)}, bf16[1024,512]{1,0:T(8,128)(2,1)}, f32[4,1024,1]{2,1,0:T(8,128)}) custom-call(f32[1024,1536]{1,0:T(8,128)} %copy-done.3, f32[1024,1536]{1,0:T(8,128)} %copy-done.3, f32[1024,1536]{1,0:T(8,128)} %copy-done.3, f32[1024,1]{1,0:T(8,128)} %copy.71.qs_ref, ...), custom_call_target="tpu_custom_call" | custom-call | flops 2147483648 | bytes 10485760 | tf_op jit(solution)/shard_map/attend_forward/pallas_call | solution.py:156
  152.7 16.0 %collective-permute-done.17 = bf16[1024,512]{1,0:T(8,128)(2,1)} collective-permute-done((bf16[1024,512]{1,0:T(8,128)(2,1)S(1)}, bf16[1024,512]{1,0:T(8,128)(2,1)}, u32[]{:S(2)}, u32[]{:S(2)}) %collective-permute-start.17) | collective-permute-done | bytes 1048608 | tf_op jit(solution)/shard_map/ppermute | solution.py:685
  185.5 12.6 %collective-permute-done.19 = bf16[512,512]{1,0:T(8,128)(2,1)S(1)} collective-permute-done((bf16[512,512]{1,0:T(8,128)(2,1)S(1)}, bf16[512,512]{1,0:T(8,128)(2,1)S(1)}, u32[]{:S(2)}, u32[]{:S(2)}) %collective-permute-start.19) | collective-permute-done | bytes 524320 | tf_op jit(solution)/shard_map/ppermute | solution.py:693
  202.5 27.3 %collective-permute-done.4.refs_5_ = bf16[1024,512]{1,0:T(8,128)(2,1)} collective-permute-done((bf16[1024,512]{1,0:T(8,128)(2,1)S(1)}, bf16[1024,512]{1,0:T(8,128)(2,1)}, u32[]{:S(2)}, u32[]{:S(2)}) %collective-permute-start.4) | collective-permute-done | bytes 1048608 | tf_op jit(solution)/shard_map/ppermute | solution.py:608
  231.7 24.9 %collective-permute-done.5.refs_6_ = bf16[1024,512]{1,0:T(8,128)(2,1)S(1)} collective-permute-done((bf16[1024,512]{1,0:T(8,128)(2,1)}, bf16[1024,512]{1,0:T(8,128)(2,1)S(1)}, u32[]{:S(2)}, u32[]{:S(2)}) %collective-permute-start.5) | collective-permute-done | bytes 1048608 | tf_op jit(solution)/shard_map/ppermute | solution.py:608
  257.6 23.3 %forward_chunk.4 = (bf16[1024,2048]{1,0:T(8,128)(2,1)}, f32[1024,1]{1,0:T(8,128)}, bf16[1024,2048]{1,0:T(8,128)(2,1)}, bf16[1024,2048]{1,0:T(8,128)(2,1)}, bf16[...) custom-call(s32[3]{0:T(128)} %get-tuple-element.442.idx_ref, ...), custom_call_target="tpu_custom_call" | custom-call | flops 8589934592 | bytes 33554432 | tf_op jit(solution)/shard_map/forward_chunk/pallas_call | solution.py:308
  283.5 23.4 %forward_chunk.5 = (bf16[1024,2048]{1,0:T(8,128)(2,1)}, f32[1024,1]{1,0:T(8,128)}, bf16[1024,2048]{1,0:T(8,128)(2,1)}, bf16[1024,2048]{1,0:T(8,128)(2,1)}, bf16[...) custom-call(s32[3]{0:T(128)} %get-tuple-element.443.idx_ref, ...), custom_call_target="tpu_custom_call", output_to_operand_aliasing={{0}: (16, {}), {1}: (17, {}), {2}: (18, {}), {3}: (19, {}),... | custom-call | flops 8589934592 | bytes 33554432 | tf_op jit(solution)/shard_map/forward_chunk/pallas_call | solution.py:308
  314.5 23.4 %forward_chunk.6 = (bf16[1024,2048]{1,0:T(8,128)(2,1)}, f32[1024,1]{1,0:T(8,128)}, bf16[1024,2048]{1,0:T(8,128)(2,1)}, bf16[1024,2048]{1,0:T(8,128)(2,1)}, bf16[...) custom-call(s32[3]{0:T(128)} %pad_add_fusion.1.idx_ref, ...), custom_call_target="tpu_custom_call", output_to_operand_aliasing={{0}: (16, {}), {1}: (17, {}), {2}: (18, {}), {3}: (19, {}),... | custom-call | flops 8589934592 | bytes 33554432 | tf_op jit(solution)/shard_map/forward_chunk/pallas_call | solution.py:308
  344.7 23.2 %forward_chunk.7 = (bf16[1024,2048]{1,0:T(8,128)(2,1)}, f32[1024,1]{1,0:T(8,128)}, bf16[1024,2048]{1,0:T(8,128)(2,1)}, bf16[1024,2048]{1,0:T(8,128)(2,1)}, bf16[...) custom-call(s32[3]{0:T(128)} %pad_add_fusion.idx_ref, ...), custom_call_target="tpu_custom_call", output_to_operand_aliasing={{0}: (16, {}), {1}: (17, {}), {2}: (18, {}), {3}: (19, {}),... | custom-call | flops 8589934592 | bytes 33554432 | tf_op jit(solution)/shard_map/forward_chunk/pallas_call | solution.py:308
  376.3 19.1 %collective-permute-done.28.refs_1_.refs_2_.refs_3_.refs_6_ = bf16[256,2048]{1,0:T(8,128)(2,1)S(1)} collective-permute-done((bf16[256,2048]{1,0:T(8,128)(2,1)S(1)}, bf16[256,2048]{1,0:T(8,128)(2,1)S(1)}, u32[]{:S(2)}, u32[]{:S(2)}) %collective-permute-start.28) | collective-permute-done | bytes 1048608 | tf_op jit(solution)/shard_map/ppermute | solution.py:607
  401.0 20.0 %backward_chunk.4 = (bf16[1024,2048]{1,0:T(8,128)(2,1)}, bf16[1024,2048]{1,0:T(8,128)(2,1)}, bf16[1024,2048]{1,0:T(8,128)(2,1)}, bf16[256,2048]{1,0:T(8,128)(2,1)}, f32[1,2048]{1,0:T(1,128)}) custom-call(s32[3]{0:T(128)} %pad_add_fusion.idx_ref, bf16[1024,2048]{1,0:T(8,128)(2,1)} %grad_ref.15, f32[1,2048]{1,0:T(1,128)} %bitcast.84, ...), custom_call_target="tpu_custom_call" | custom-call | flops 6442450944 | bytes 25165824 | tf_op jit(solution)/shard_map/backward_chunk/pallas_call | solution.py:405
  425.2 20.0 %backward_chunk.5 = (bf16[1024,2048]{1,0:T(8,128)(2,1)}, bf16[1024,2048]{1,0:T(8,128)(2,1)}, bf16[1024,2048]{1,0:T(8,128)(2,1)}, bf16[256,2048]{1,0:T(8,128)(2,1)}, f32[1,2048]{1,0:T(1,128)}) custom-call(s32[3]{0:T(128)} %pad_add_fusion.1.idx_ref, bf16[1024,2048]{1,0:T(8,128)(2,1)} %grad_ref.15, ...), custom_call_target="tpu_custom_call", output_to_operand_aliasing={{0}: (11, {}), {1}: (12, {}), {2}: (13, {})} | custom-call | flops 6442450944 | bytes 25165824 | tf_op jit(solution)/shard_map/backward_chunk/pallas_call | solution.py:405
  445.3 20.0 %backward_chunk.6 = (bf16[1024,2048]{1,0:T(8,128)(2,1)}, bf16[1024,2048]{1,0:T(8,128)(2,1)}, bf16[1024,2048]{1,0:T(8,128)(2,1)}, bf16[256,2048]{1,0:T(8,128)(2,1)}, f32[1,2048]{1,0:T(1,128)}) custom-call(s32[3]{0:T(128)} %get-tuple-element.443.idx_ref, bf16[1024,2048]{1,0:T(8,128)(2,1)} %grad_ref.15, ...), custom_call_target="tpu_custom_call", output_to_operand_aliasing={{0}: (13, {}), {1}: (14, {}), {2}: (15, {})} | custom-call | flops 6442450944 | bytes 25165824 | tf_op jit(solution)/shard_map/backward_chunk/pallas_call | solution.py:405
  466.3 20.4 %backward_chunk.7 = (bf16[1024,2048]{1,0:T(8,128)(2,1)}, bf16[1024,2048]{1,0:T(8,128)(2,1)}, bf16[1024,2048]{1,0:T(8,128)(2,1)}, bf16[256,2048]{1,0:T(8,128)(2,1)}, f32[1,2048]{1,0:T(1,128)}) custom-call(s32[3]{0:T(128)} %get-tuple-element.442.idx_ref, bf16[1024,2048]{1,0:T(8,128)(2,1)} %grad_ref.15, ...), custom_call_target="tpu_custom_call", output_to_operand_aliasing={{0}: (13, {}), {1}: (14, {}), {2}: (15, {})} | custom-call | flops 6442450944 | bytes 25165824 | tf_op jit(solution)/shard_map/backward_chunk/pallas_call | solution.py:405
  493.0 17.9 %collective-permute-done.34 = bf16[256,2048]{1,0:T(8,128)(2,1)S(1)} collective-permute-done((bf16[256,2048]{1,0:T(8,128)(2,1)}, bf16[256,2048]{1,0:T(8,128)(2,1)S(1)}, u32[]{:S(2)}, u32[]{:S(2)}) %collective-permute-start.34) | collective-permute-done | bytes 1048608 | tf_op jit(solution)/shard_map/ppermute | solution.py:612
  517.7 16.7 %collective-permute-done.35 = bf16[256,2048]{1,0:T(8,128)(2,1)S(1)} collective-permute-done((bf16[256,2048]{1,0:T(8,128)(2,1)S(1)}, bf16[256,2048]{1,0:T(8,128)(2,1)S(1)}, u32[]{:S(2)}, u32[]{:S(2)}) %collective-permute-start.35) | collective-permute-done | bytes 1048608 | tf_op jit(solution)/shard_map/ppermute | solution.py:612
  544.1 15.6 %collective-permute-done.36 = bf16[256,2048]{1,0:T(8,128)(2,1)S(1)} collective-permute-done((bf16[256,2048]{1,0:T(8,128)(2,1)S(1)}, bf16[256,2048]{1,0:T(8,128)(2,1)S(1)}, u32[]{:S(2)}, u32[]{:S(2)}) %collective-permute-start.36) | collective-permute-done | bytes 1048608 | tf_op jit(solution)/shard_map/ppermute | solution.py:612
  567.9 14.7 %collective-permute-done.40.refs_1_.refs_2_ = bf16[256,2048]{1,0:T(8,128)(2,1)S(1)} collective-permute-done((bf16[256,2048]{1,0:T(8,128)(2,1)S(1)}, bf16[256,2048]{1,0:T(8,128)(2,1)S(1)}, u32[]{:S(2)}, u32[]{:S(2)}) %collective-permute-start.40) | collective-permute-done | bytes 1048608 | tf_op jit(solution)/shard_map/ppermute | solution.py:607
  592.9 20.3 %collective-permute-done.44.refs_0_.refs_1_ = bf16[256,2048]{1,0:T(8,128)(2,1)S(1)} collective-permute-done((bf16[256,2048]{1,0:T(8,128)(2,1)S(1)}, bf16[256,2048]{1,0:T(8,128)(2,1)S(1)}, u32[]{:S(2)}, u32[]{:S(2)}) %collective-permute-start.44) | collective-permute-done | bytes 1048608 | tf_op jit(solution)/shard_map/ppermute | solution.py:608
  614.5 10.7 %attention_chunk.4 = (bf16[1024,2048]{1,0:T(8,128)(2,1)}, bf16[1024,512]{1,0:T(8,128)(2,1)}, bf16[1024,2048]{1,0:T(8,128)(2,1)}, f32[1,2048]{1,0:T(1,128)}) custom-call(s32[3]{0:T(128)} %pad_add_fusion.idx_ref, bf16[1024,2048]{1,0:T(8,128)(2,1)} %grad_ref.15, bf16[1024,2048]{1,0:T(8,128)(2,1)} %get-tuple-element.238.raw_ref, ...), custom_call_target="tpu_custom_call" | custom-call | flops 536870912 | bytes 8388608 | tf_op jit(solution)/shard_map/attention_chunk/pallas_call | solution.py:484
  635.6 10.3 %attention_chunk.6 = (bf16[1024,2048]{1,0:T(8,128)(2,1)}, bf16[1024,512]{1,0:T(8,128)(2,1)}, bf16[1024,2048]{1,0:T(8,128)(2,1)}, f32[1,2048]{1,0:T(1,128)}) custom-call(s32[3]{0:T(128)} %get-tuple-element.443.idx_ref, bf16[1024,2048]{1,0:T(8,128)(2,1)} %grad_ref.15, ...), custom_call_target="tpu_custom_call", output_to_operand_aliasing={{0}: (17, {}), {1}: (18, {}), {2}: (19, {})} | custom-call | flops 536870912 | bytes 8388608 | tf_op jit(solution)/shard_map/attention_chunk/pallas_call | solution.py:484
  656.3 18.0 %attend_backward.1 = (f32[1024,512]{1,0:T(8,128)}, f32[1024,512]{1,0:T(8,128)}, bf16[1024,512]{1,0:T(8,128)(2,1)}, f32[1024,1]{1,0:T(8,128)}, f32[1024,1]{1,0:T(...) custom-call(f32[1024,1536]{1,0:T(8,128)} %copy-done.3, f32[1024,1536]{1,0:T(8,128)} %copy-done.3, f32[1024,1]{1,0:T(8,128)} %copy.71.qs_ref, ...), custom_call_target="tpu_custom_call" | custom-call | flops 5368709120 | bytes 20971520 | tf_op jit(solution)/shard_map/attend_backward/pallas_call | solution.py:180
  676.8 12.2 %all-reduce = (f32[1024]{0:T(1024)S(1)}, f32[1024]{0:T(1024)S(1)}) all-reduce(f32[1024]{0:T(1024)S(1)} %reduce.1, f32[1024]{0:T(1024)S(1)} %reduce), channel_id=1, replica_groups=mesh['dp'=2,'row'=4,'col'=4] {'col'}, use_global_device_ids=true, to_apply=%region_5.6 | all-reduce | flops 2048 | bytes 16384 | tf_op jit(solution)/shard_map/psum | solution.py:839
  737.7 10.7 %add_convert_fusion.2 = bf16[2048,1024]{1,0:T(8,128)(2,1)} fusion(bf16[2048,1024]{1,0:T(8,128)(2,1)} %collective-permute-done.58, bf16[1024,2048]{1,0:T(8,128)(2,1)} %get-tuple-element.307, bf16[1024,2048]{1,0:T(8,128)(2,1)} %get-tuple-element.308, s32[]{:T(128)S(6)} %select_n.228), kind=kOutput, calls=%fused_computation.2 | convolution fusion | flops 4301258752 | bytes 14680068 | tf_op jit(solution)/shard_map/dot_general | solution.py:35
  821.7 16.3 %collective-permute-done.50 = bf16[256,2048]{1,0:T(8,128)(2,1)S(1)} collective-permute-done((bf16[256,2048]{1,0:T(8,128)(2,1)S(1)}, bf16[256,2048]{1,0:T(8,128)(2,1)S(1)}, u32[]{:S(2)}, u32[]{:S(2)}) %collective-permute-start.50) | collective-permute-done | bytes 1048608 | tf_op jit(solution)/shard_map/ppermute | solution.py:612
  853.4 14.8 %collective-permute-done.52.refs_1_.refs_2_ = bf16[256,2048]{1,0:T(8,128)(2,1)} collective-permute-done((bf16[256,2048]{1,0:T(8,128)(2,1)S(1)}, bf16[256,2048]{1,0:T(8,128)(2,1)}, u32[]{:S(2)}, u32[]{:S(2)}) %collective-permute-start.52) | collective-permute-done | bytes 1048608 | tf_op jit(solution)/shard_map/ppermute | solution.py:607
  884.6 14.0 %collective-permute-done.56.refs_0_.refs_1_ = bf16[256,2048]{1,0:T(8,128)(2,1)S(1)} collective-permute-done((bf16[256,2048]{1,0:T(8,128)(2,1)}, bf16[256,2048]{1,0:T(8,128)(2,1)S(1)}, u32[]{:S(2)}, u32[]{:S(2)}) %collective-permute-start.56) | collective-permute-done | bytes 1048608 | tf_op jit(solution)/shard_map/ppermute | solution.py:608
  900.1 36.2 %reduce-scatter.10.cloned.1.call-done = bf16[512,1024]{1,0:T(8,128)(2,1)} async-done(((bf16[2048,1024]{1,0:T(8,128)(2,1)}), bf16[512,1024]{1,0:T(8,128)(2,1)}) %reduce-scatter.10.cloned.1.call-update) | async-done | bytes 1048592 | tf_op jit(solution)/shard_map/reduce_scatter | solution.py:677
  956.6 26.6 %reduce-scatter.14.cloned.1.call-done = bf16[512,768]{1,0:T(8,128)(2,1)} async-done(((bf16[2048,768]{1,0:T(8,128)(2,1)}), bf16[512,768]{1,0:T(8,128)(2,1)}) %reduce-scatter.14.cloned.1.call-update) | async-done | bytes 786448 | tf_op jit(solution)/shard_map/reduce_scatter | solution.py:677
  (386 shorter events, 404.0 us)
Async XLA Ops:
  7.2 80.5 %all-gather.4.cloned.1.call-start = ((), (), s32[]{:S(2)}) async-start(), calls=%async_computation.5 | async-start | bytes 7077888 | tf_op jit(solution)/shard_map/all_gather | solution.py:604
  9.5 247.2 %all-gather.6.cloned.1.call-start = ((), (), s32[]{:S(2)}) async-start(), calls=%async_computation.6 | async-start | bytes 9437184 | tf_op jit(solution)/shard_map/all_gather | solution.py:604
  10.6 246.0 %all-gather.8.cloned.1.call-start = ((), (), s32[]{:S(2)}) async-start(), calls=%async_computation.7 | async-start | bytes 9437184 | tf_op jit(solution)/shard_map/all_gather | solution.py:604
  13.0 840.3 %reduce-scatter.12.cloned.1.call-start = ((), (), s32[]{:S(2)}) async-start(), calls=%async_computation.11 | async-start | bytes 1310720 | tf_op jit(solution)/shard_map/reduce_scatter | solution.py:677
  69.9 65.7 %collective-permute-start.13 = (bf16[256,2048]{1,0:T(8,128)(2,1)}, bf16[256,2048]{1,0:T(8,128)(2,1)}, u32[]{:S(2)}, u32[]{:S(2)}) collective-permute-start(bf16[256,2048]{1,0:T(8,128)(2,1)} %collective-permute-done.12), channel_id=1, source_target_pairs={{2,3},{6,7},{10,11},{14,15},{18,19},{22,23},{26,27},{30,31}} | collective-permute-start | bytes 3145736 | tf_op jit(solution)/shard_map/ppermute | solution.py:607
  86.4 54.5 %collective-permute-start.15 = (bf16[256,2048]{1,0:T(8,128)(2,1)}, bf16[256,2048]{1,0:T(8,128)(2,1)}, u32[]{:S(2)}, u32[]{:S(2)}) collective-permute-start(bf16[256,2048]{1,0:T(8,128)(2,1)} %collective-permute-done.14), channel_id=1, source_target_pairs={{1,0},{5,4},{9,8},{13,12},{17,16},{21,20},{25,24},{29,28}} | collective-permute-start | bytes 3145736 | tf_op jit(solution)/shard_map/ppermute | solution.py:608
  134.1 34.6 %collective-permute-start.17 = (bf16[1024,512]{1,0:T(8,128)(2,1)S(1)}, bf16[1024,512]{1,0:T(8,128)(2,1)}, u32[]{:S(2)}, u32[]{:S(2)}) collective-permute-start(bf16[1024,512]{1,0:T(8,128)(2,1)S(1)} %constant_dynamic-slice_fusion.10), channel_id=1, source_target_pairs={{0,4},{4,0},{8,12},{12,8},{1,5},{5,1},{9,13},{13,9},{2,6},{6,2},{1... | collective-permute-start | bytes 3145736 | tf_op jit(solution)/shard_map/ppermute | solution.py:685
  135.7 37.9 %collective-permute-start.18 = (bf16[1024,512]{1,0:T(8,128)(2,1)S(1)}, bf16[1024,512]{1,0:T(8,128)(2,1)}, u32[]{:S(2)}, u32[]{:S(2)}) collective-permute-start(bf16[1024,512]{1,0:T(8,128)(2,1)S(1)} %constant_dynamic-slice_fusion.10), channel_id=1, source_target_pairs={{0,8},{8,0},{4,12},{12,4},{1,9},{9,1},{5,13},{13,5},{2,10},{10,2},... | collective-permute-start | bytes 3145736 | tf_op jit(solution)/shard_map/ppermute | solution.py:685
  145.1 111.5 %collective-permute-start.16 = (bf16[1024,2048]{1,0:T(8,128)(2,1)}, bf16[1024,2048]{1,0:T(8,128)(2,1)}, u32[]{:S(2)}, u32[]{:S(2)}) collective-permute-start(bf16[1024,2048]{1,0:T(8,128)(2,1)} %pad_maximum_fusion.refs_7_.wo_own_ref), channel_id=1, source_target_pairs={{0,16},{16,0},{1,17},{17,1},{2,18},{18,2},{3,19},{19,3},{4,20},{20... | collective-permute-start | bytes 12582920 | tf_op jit(solution)/shard_map/ppermute | solution.py:762
  199.7 56.9 %collective-permute-start.21 = (bf16[4,1024,512]{2,1,0:T(8,128)(2,1)}, bf16[4,1024,512]{2,1,0:T(8,128)(2,1)}, u32[]{:S(2)}, u32[]{:S(2)}) collective-permute-start(bf16[4,1024,512]{2,1,0:T(8,128)(2,1)} %bitcast_dynamic-update-slice_fusion.3.refs_13_.wd_own_ref), channel_id=1, source_target_pairs={{0,16},{16,0},{1,17},{17,1},{2,18},{18,2},{3,19},{19,3},{4,20},{20... | collective-permute-start | bytes 12582920 | tf_op jit(solution)/shard_map/ppermute | solution.py:710
  200.5 29.3 %collective-permute-start.4 = (bf16[1024,512]{1,0:T(8,128)(2,1)S(1)}, bf16[1024,512]{1,0:T(8,128)(2,1)}, u32[]{:S(2)}, u32[]{:S(2)}) collective-permute-start(bf16[1024,512]{1,0:T(8,128)(2,1)S(1)} %collective-permute-done.3.refs_4_), channel_id=1, source_target_pairs={{1,0},{2,1},{5,4},{6,5},{9,8},{10,9},{13,12},{14,13},{17,16},{18,1... | collective-permute-start | bytes 3145736 | tf_op jit(solution)/shard_map/ppermute | solution.py:608
  201.8 29.9 %collective-permute-start.2 = (bf16[1024,512]{1,0:T(8,128)(2,1)S(1)}, bf16[1024,512]{1,0:T(8,128)(2,1)S(1)}, u32[]{:S(2)}, u32[]{:S(2)}) collective-permute-start(bf16[1024,512]{1,0:T(8,128)(2,1)S(1)} %collective-permute-done.1.refs_2_), channel_id=1, source_target_pairs={{2,3},{6,7},{10,11},{14,15},{18,19},{22,23},{26,27},{30,31}} | collective-permute-start | bytes 3145736 | tf_op jit(solution)/shard_map/ppermute | solution.py:607
  229.8 26.8 %collective-permute-start.5 = (bf16[1024,512]{1,0:T(8,128)(2,1)}, bf16[1024,512]{1,0:T(8,128)(2,1)S(1)}, u32[]{:S(2)}, u32[]{:S(2)}) collective-permute-start(bf16[1024,512]{1,0:T(8,128)(2,1)} %collective-permute-done.4.refs_5_), channel_id=1, source_target_pairs={{1,0},{5,4},{9,8},{13,12},{17,16},{21,20},{25,24},{29,28}} | collective-permute-start | bytes 3145736 | tf_op jit(solution)/shard_map/ppermute | solution.py:608
  280.9 26.0 %collective-permute-start.22 = (bf16[256,2048]{1,0:T(8,128)(2,1)}, bf16[256,2048]{1,0:T(8,128)(2,1)S(1)}, u32[]{:S(2)}, u32[]{:S(2)}) collective-permute-start(bf16[256,2048]{1,0:T(8,128)(2,1)} %get-tuple-element.196), channel_id=1, source_target_pairs={{0,1},{4,5},{8,9},{12,13},{16,17},{20,21},{24,25},{28,29}} | collective-permute-start | bytes 3145736 | tf_op jit(solution)/shard_map/ppermute | solution.py:612
  310.6 27.3 %collective-permute-start.24 = (bf16[256,2048]{1,0:T(8,128)(2,1)}, bf16[256,2048]{1,0:T(8,128)(2,1)S(1)}, u32[]{:S(2)}, u32[]{:S(2)}) collective-permute-start(bf16[256,2048]{1,0:T(8,128)(2,1)} %get-tuple-element.412), channel_id=1, source_target_pairs={{0,1},{1,2},{4,5},{5,6},{8,9},{9,10},{12,13},{13,14},{16,17},{17,1... | collective-permute-start | bytes 3145736 | tf_op jit(solution)/shard_map/ppermute | solution.py:612
  340.6 27.3 %collective-permute-start.26 = (bf16[256,2048]{1,0:T(8,128)(2,1)}, bf16[256,2048]{1,0:T(8,128)(2,1)S(1)}, u32[]{:S(2)}, u32[]{:S(2)}) collective-permute-start(bf16[256,2048]{1,0:T(8,128)(2,1)} %get-tuple-element.410), channel_id=1, source_target_pairs={{0,1},{1,2},{2,3},{4,5},{5,6},{6,7},{8,9},{9,10},{10,11},{12,13},{... | collective-permute-start | bytes 3145736 | tf_op jit(solution)/shard_map/ppermute | solution.py:612
  421.0 44.2 %collective-permute-start.32 = (bf16[256,2048]{1,0:T(8,128)(2,1)S(1)}, bf16[256,2048]{1,0:T(8,128)(2,1)S(1)}, u32[]{:S(2)}, u32[]{:S(2)}) collective-permute-start(bf16[256,2048]{1,0:T(8,128)(2,1)S(1)} %collective-permute-done.29.refs_3_.refs_2_.refs_7_.refs_6_), channel_id=1, source_target_pairs={{2,3},{6,7},{10,11},{14,15},{18,19},{22,23},{26,27},{30,31}} | collective-permute-start | bytes 3145736 | tf_op jit(solution)/shard_map/ppermute | solution.py:607
  423.8 41.5 %collective-permute-start.33 = (bf16[256,2048]{1,0:T(8,128)(2,1)S(1)}, bf16[256,2048]{1,0:T(8,128)(2,1)}, u32[]{:S(2)}, u32[]{:S(2)}) collective-permute-start(bf16[256,2048]{1,0:T(8,128)(2,1)S(1)} %collective-permute-done.31.refs_0_.refs_1_.refs_4_.refs_5_), channel_id=1, source_target_pairs={{1,0},{5,4},{9,8},{13,12},{17,16},{21,20},{25,24},{29,28}} | collective-permute-start | bytes 3145736 | tf_op jit(solution)/shard_map/ppermute | solution.py:608
  591.2 54.7 %collective-permute-start.42 = (bf16[256,2048]{1,0:T(8,128)(2,1)S(1)}, bf16[256,2048]{1,0:T(8,128)(2,1)}, u32[]{:S(2)}, u32[]{:S(2)}) collective-permute-start(bf16[256,2048]{1,0:T(8,128)(2,1)S(1)} %collective-permute-done.41.refs_3_.refs_2_), channel_id=1, source_target_pairs={{2,3},{6,7},{10,11},{14,15},{18,19},{22,23},{26,27},{30,31}} | collective-permute-start | bytes 3145736 | tf_op jit(solution)/shard_map/ppermute | solution.py:607
  613.2 32.7 %collective-permute-start.45 = (bf16[256,2048]{1,0:T(8,128)(2,1)S(1)}, bf16[256,2048]{1,0:T(8,128)(2,1)}, u32[]{:S(2)}, u32[]{:S(2)}) collective-permute-start(bf16[256,2048]{1,0:T(8,128)(2,1)S(1)} %collective-permute-done.44.refs_0_.refs_1_), channel_id=1, source_target_pairs={{1,0},{5,4},{9,8},{13,12},{17,16},{21,20},{25,24},{29,28}} | collective-permute-start | bytes 3145736 | tf_op jit(solution)/shard_map/ppermute | solution.py:608
  705.9 31.9 %collective-permute-start.58 = (bf16[2048,1024]{1,0:T(8,128)(2,1)}, bf16[2048,1024]{1,0:T(8,128)(2,1)}, u32[]{:S(2)}, u32[]{:S(2)}) collective-permute-start(bf16[2048,1024]{1,0:T(8,128)(2,1)} %convolution_convert_fusion.2), channel_id=1, source_target_pairs={{0,16},{16,0},{1,17},{17,1},{2,18},{18,2},{3,19},{19,3},{4,20},{20... | collective-permute-start | bytes 12582920 | tf_op jit(solution)/shard_map/ppermute | solution.py:673
  737.5 137.3 %reduce-scatter.6.cloned.1.call-start = ((), (), s32[]{:S(2)}) async-start(), calls=%async_computation.8 | async-start | bytes 5242880 | tf_op jit(solution)/shard_map/reduce_scatter | solution.py:677
  748.4 131.7 %reduce-scatter.8.cloned.1.call-start = ((), (), s32[]{:S(2)}) async-start(), calls=%async_computation.9 | async-start | bytes 5242880 | tf_op jit(solution)/shard_map/reduce_scatter | solution.py:677
  769.8 166.5 %reduce-scatter.10.cloned.1.call-start = ((), (), s32[]{:S(2)}) async-start(), calls=%async_computation.10 | async-start | bytes 5242880 | tf_op jit(solution)/shard_map/reduce_scatter | solution.py:677
  791.6 191.7 %reduce-scatter.14.cloned.1.call-start = ((), (), s32[]{:S(2)}) async-start(), calls=%async_computation.12 | async-start | bytes 3932160 | tf_op jit(solution)/shard_map/reduce_scatter | solution.py:677
  809.7 28.4 %collective-permute-start.50 = (bf16[256,2048]{1,0:T(8,128)(2,1)S(1)}, bf16[256,2048]{1,0:T(8,128)(2,1)S(1)}, u32[]{:S(2)}, u32[]{:S(2)}) collective-permute-start(bf16[256,2048]{1,0:T(8,128)(2,1)S(1)} %copy-done.38), channel_id=1, source_target_pairs={{0,1},{1,2},{2,3},{4,5},{5,6},{6,7},{8,9},{9,10},{10,11},{12,13},{... | collective-permute-start | bytes 3145736 | tf_op jit(solution)/shard_map/ppermute | solution.py:612
  815.4 26.9 %collective-permute-start.51 = (bf16[256,2048]{1,0:T(8,128)(2,1)S(1)}, bf16[256,2048]{1,0:T(8,128)(2,1)S(1)}, u32[]{:S(2)}, u32[]{:S(2)}) collective-permute-start(bf16[256,2048]{1,0:T(8,128)(2,1)S(1)} %copy-done.37), channel_id=1, source_target_pairs={{3,2},{2,1},{1,0},{7,6},{6,5},{5,4},{11,10},{10,9},{9,8},{15,14},{... | collective-permute-start | bytes 3145736 | tf_op jit(solution)/shard_map/ppermute | solution.py:613
  853.3 27.2 %collective-permute-start.67 = (bf16[512,256]{1,0:T(8,128)(2,1)}, bf16[512,256]{1,0:T(8,128)(2,1)}, u32[]{:S(2)}, u32[]{:S(2)}) collective-permute-start(bf16[512,256]{1,0:T(8,128)(2,1)} %reduce-scatter.12.cloned.1.call-done), channel_id=1, source_target_pairs={{0,16},{16,0},{1,17},{17,1},{2,18},{18,2},{3,19},{19,3},{4,20},{20... | collective-permute-start | bytes 786440 | tf_op jit(solution)/shard_map/ppermute | solution.py:667
  874.8 61.5 %collective-permute-start.59 = (bf16[512,1024]{1,0:T(8,128)(2,1)}, bf16[512,1024]{1,0:T(8,128)(2,1)}, u32[]{:S(2)}, u32[]{:S(2)}) collective-permute-start(bf16[512,1024]{1,0:T(8,128)(2,1)} %reduce-scatter.6.cloned.1.call-done), channel_id=1, source_target_pairs={{0,16},{16,0},{1,17},{17,1},{2,18},{18,2},{3,19},{19,3},{4,20},{20... | collective-permute-start | bytes 3145736 | tf_op jit(solution)/shard_map/ppermute | solution.py:667
  880.1 65.8 %collective-permute-start.61 = (bf16[512,1024]{1,0:T(8,128)(2,1)}, bf16[512,1024]{1,0:T(8,128)(2,1)}, u32[]{:S(2)}, u32[]{:S(2)}) collective-permute-start(bf16[512,1024]{1,0:T(8,128)(2,1)} %reduce-scatter.8.cloned.1.call-done), channel_id=1, source_target_pairs={{0,16},{16,0},{1,17},{17,1},{2,18},{18,2},{3,19},{19,3},{4,20},{20... | collective-permute-start | bytes 3145736 | tf_op jit(solution)/shard_map/ppermute | solution.py:667
  882.9 114.8 %collective-permute-start.54 = (bf16[256,2048]{1,0:T(8,128)(2,1)S(1)}, bf16[256,2048]{1,0:T(8,128)(2,1)}, u32[]{:S(2)}, u32[]{:S(2)}) collective-permute-start(bf16[256,2048]{1,0:T(8,128)(2,1)S(1)} %collective-permute-done.53.refs_3_.refs_2_), channel_id=1, source_target_pairs={{2,3},{6,7},{10,11},{14,15},{18,19},{22,23},{26,27},{30,31}} | collective-permute-start | bytes 3145736 | tf_op jit(solution)/shard_map/ppermute | solution.py:607
  898.6 99.2 %collective-permute-start.57 = (bf16[256,2048]{1,0:T(8,128)(2,1)S(1)}, bf16[256,2048]{1,0:T(8,128)(2,1)}, u32[]{:S(2)}, u32[]{:S(2)}) collective-permute-start(bf16[256,2048]{1,0:T(8,128)(2,1)S(1)} %collective-permute-done.56.refs_0_.refs_1_), channel_id=1, source_target_pairs={{1,0},{5,4},{9,8},{13,12},{17,16},{21,20},{25,24},{29,28}} | collective-permute-start | bytes 3145736 | tf_op jit(solution)/shard_map/ppermute | solution.py:608
  (112 other events, 2072.3 us)
Sparse Core Ops, SparseCore 0:
  10.5 51.8 all-gather.3
  64.9 54.2 all-gather.5
  121.6 78.8 all-gather.7
  737.6 30.0 reduce-scatter.11
  771.0 52.5 reduce-scatter.5
  827.1 53.0 reduce-scatter.7
  883.7 52.5 reduce-scatter.9
  939.3 43.8 reduce-scatter.13

commit v9 on v8

--- a/solution.py
+++ b/solution.py
@@ -283,9 +283,9 @@
 TILE = 512
 
 
-def forward_chunk(index, attended, out_halves, block_input, gain, w_gate, w_up, down_halves, chunk, before):
+def forward_chunk(index, attended, out_halves, block_input, gain, w_gate_up, down_halves, chunk, before):
     tokens, width = block_input.shape
-    hidden = w_gate.shape[1]
+    hidden = w_gate_up.shape[1] // 2
     depth = out_halves[0].shape[0]
     blocks, _, block = down_halves[0].shape
     tiles = hidden // TILE
@@ -296,7 +296,8 @@
 
     rows = pl.BlockSpec((chunk, width), lambda j, idx: (idx[0], 0))
     out_half = pl.BlockSpec((depth, TILE), lambda j, idx: (0, jnp.minimum(j, out_steps - 1)))
-    up_tile = pl.BlockSpec((width, TILE), lambda j, idx: (0, tile_of(j, idx)))
+    gate_tile = pl.BlockSpec((width, TILE), lambda j, idx: (0, tile_of(j, idx)))
+    up_tile = pl.BlockSpec((width, TILE), lambda j, idx: (0, tiles + tile_of(j, idx)))
     down_own = pl.BlockSpec(
         (blocks, TILE, block), lambda j, idx: (0, jnp.clip(j - out_steps, 0, tiles // 2 - 1), 0)
     )
@@ -313,7 +314,7 @@
             in_specs=[
                 *[pl.BlockSpec((chunk, attended[0].shape[1]), lambda j, idx: (idx[0], 0))] * 7,
                 out_half, out_half, rows, pl.BlockSpec((1, width), lambda j, idx: (0, 0)),
-                up_tile, up_tile, down_own, down_oth,
+                gate_tile, up_tile, down_own, down_oth,
             ] + [pl.BlockSpec(memory_space=pl.ANY)] * len(before),
             out_specs=[
                 rows, pl.BlockSpec((chunk, 1), lambda j, idx: (idx[0], 0)), rows, act_tile, act_tile, act_tile,
@@ -338,7 +339,7 @@
             transcendentals=0,
         ),
         name="forward_chunk",
-    )(index, *attended, *out_halves, block_input, gain, w_gate, w_up, *down_halves, *before)
+    )(index, *attended, *out_halves, block_input, gain, w_gate_up, w_gate_up, *down_halves, *before)
 
 
 def backward_chunk_kernel(
@@ -387,10 +388,10 @@
 
 
 def backward_chunk(
-    index, down_rows, grad_output, mlp_gain, gate, up, w_gate, w_up, down_halves, chunk, before,
+    index, down_rows, grad_output, mlp_gain, gate, up, w_gate_up, down_halves, chunk, before,
 ):
     tokens, width = grad_output.shape
-    hidden = w_gate.shape[1]
+    hidden = w_gate_up.shape[1] // 2
     blocks, _, block = down_halves[0].shape
     tiles = hidden // TILE
 
@@ -399,7 +400,8 @@
 
     rows = pl.BlockSpec((chunk, width), lambda j, idx: (idx[0], 0))
     gain_row = pl.BlockSpec((1, width), lambda j, idx: (0, 0))
-    up_tile = pl.BlockSpec((width, TILE), lambda j, idx: (0, tile_of(j, idx)))
+    gate_tile = pl.BlockSpec((width, TILE), lambda j, idx: (0, tile_of(j, idx)))
+    up_tile = pl.BlockSpec((width, TILE), lambda j, idx: (0, tiles + tile_of(j, idx)))
     act_tile = pl.BlockSpec((chunk, TILE), lambda j, idx: (idx[0], tile_of(j, idx)))
     before = tuple(before)
     return pl.pallas_call(
@@ -408,7 +410,7 @@
             num_scalar_prefetch=1,
             grid=(tiles,),
             in_specs=[
-                rows, gain_row, act_tile, act_tile, up_tile, up_tile,
+                rows, gain_row, act_tile, act_tile, gate_tile, up_tile,
                 pl.BlockSpec((blocks, TILE, block), lambda j, idx: (0, jnp.minimum(j, tiles // 2 - 1), 0)),
                 pl.BlockSpec((blocks, TILE, block), lambda j, idx: (0, jnp.maximum(j - tiles // 2, 0), 0)),
             ] + [pl.BlockSpec(memory_space=pl.ANY)] * (len(down_rows) + len(before)),
@@ -430,33 +432,32 @@
             flops=6 * chunk * width * hidden, bytes_accessed=6 * width * hidden, transcendentals=0
         ),
         name="backward_chunk",
-    )(index, grad_output, mlp_gain, gate, up, w_gate, w_up, *down_halves, *down_rows, *before)
+    )(index, grad_output, mlp_gain, gate, up, w_gate_up, w_gate_up, *down_halves, *down_rows, *before)
 
 
 PARTS = 4
 
 
 def attention_chunk_kernel(
-    idx_ref, grad_ref, raw_ref, scale_ref, x_ref, attn_gain_ref, mlp_gain_ref, wo_own_ref, wo_oth_ref, *refs, choices,
+    idx_ref, grad_ref, raw_ref, scale_ref, gain_ref, wo_own_ref, wo_oth_ref, *refs, choices,
 ):
-    gai_ref, gatt_ref, out_ref, gain_grad_ref, mlp_held_ref, down_held_ref, sem = refs[-7:]
+    gai_ref, gatt_ref, gain_grad_ref, held_ref, sem = refs[-5:]
     half = wo_own_ref.shape[0]
     core = idx_ref[1]
     step = pl.program_id(0)
 
     @pl.when(step == 0)
     def _():
-        fetch_choice(idx_ref, refs[:choices], mlp_held_ref, sem)
-        fetch_choice(idx_ref, refs[choices : 2 * choices], down_held_ref, sem)
+        fetch_choice(idx_ref, refs[:choices], held_ref, sem)
         gain_grad_ref[...] = jnp.zeros_like(gain_grad_ref)
 
     size = grad_ref.shape[0]
-    here = pl.ds(pl.multiple_of(step * size, size), size)
     scale = scale_ref[...]
     unit = raw_ref[...].astype(F32) * scale
-    grad_hidden = grad_ref[...].astype(F32) + mlp_held_ref[here, :].astype(F32)
+    mlp = held_ref[pl.ds(pl.multiple_of(step * size, size), size), :]
+    grad_hidden = grad_ref[...].astype(F32) + mlp.astype(F32)
     gain_grad_ref[...] += jnp.sum(grad_hidden * unit, axis=0, keepdims=True)
-    grad_unit = grad_hidden * attn_gain_ref[...]
+    grad_unit = grad_hidden * gain_ref[...]
     mean = jnp.mean(grad_unit * unit, axis=1, keepdims=True)
     grad_attn_in = (scale * (grad_unit - unit * mean)).astype(BF16)
     gai_ref[...] = grad_attn_in
@@ -464,52 +465,79 @@
         gatt_ref[:, pl.ds(pl.multiple_of(place * half, half), half)] = times_transposed(
             grad_attn_in, w_ref[...]
         ).astype(BF16)
-    down_raw = down_held_ref[here, :].astype(F32)
-    down_scale = lax.rsqrt(jnp.mean(down_raw * down_raw, axis=1, keepdims=True) + EPS)
-    hidden = x_ref[...].astype(F32) + unit * attn_gain_ref[...]
-    out_ref[...] = (hidden + down_raw * down_scale * mlp_gain_ref[...]).astype(BF16)
-
-
-def attention_chunk(
-    index, mlp_rows, down_rows, grad_output, raw, scale, block_input, attn_gain, mlp_gain, out_halves, half, chunk,
-    before,
-):
+
+
+def attention_chunk(index, mlp_rows, grad_output, raw, scale, gain, out_halves, half, chunk, before):
     tokens, width = grad_output.shape
     size = chunk // PARTS
     rows = pl.BlockSpec((size, width), lambda j, idx: (PARTS * idx[0] + j, 0))
     gain_row = pl.BlockSpec((1, width), lambda j, idx: (0, 0))
     own_heads = pl.BlockSpec((half, width), lambda j, idx: (0, 0))
     before = tuple(before)
-    chosen = (*mlp_rows, *down_rows)
     return pl.pallas_call(
         functools.partial(attention_chunk_kernel, choices=len(mlp_rows)),
         grid_spec=pltpu.PrefetchScalarGridSpec(
             num_scalar_prefetch=1,
             grid=(PARTS,),
             in_specs=[
-                rows, rows, pl.BlockSpec((size, 1), lambda j, idx: (PARTS * idx[0] + j, 0)), rows, gain_row, gain_row,
+                rows, rows, pl.BlockSpec((size, 1), lambda j, idx: (PARTS * idx[0] + j, 0)), gain_row,
                 own_heads, own_heads,
-            ] + [pl.BlockSpec(memory_space=pl.ANY)] * (len(chosen) + len(before)),
-            out_specs=[
-                rows, pl.BlockSpec((size, 2 * half), lambda j, idx: (PARTS * idx[0] + j, 0)), rows, gain_row,
-            ],
-            scratch_shapes=[
-                pltpu.VMEM((chunk, width), BF16), pltpu.VMEM((chunk, width), BF16), pltpu.SemaphoreType.DMA(()),
-            ],
+            ] + [pl.BlockSpec(memory_space=pl.ANY)] * (len(mlp_rows) + len(before)),
+            out_specs=[rows, pl.BlockSpec((size, 2 * half), lambda j, idx: (PARTS * idx[0] + j, 0)), gain_row],
+            scratch_shapes=[pltpu.VMEM((chunk, width), BF16), pltpu.SemaphoreType.DMA(())],
         ),
         out_shape=[
             jax.ShapeDtypeStruct((tokens, width), BF16),
             jax.ShapeDtypeStruct((tokens, 2 * half), BF16),
-            jax.ShapeDtypeStruct((tokens, width), BF16),
             jax.ShapeDtypeStruct((1, width), F32),
         ],
-        input_output_aliases={9 + len(chosen) + i: i for i in range(len(before))},
+        input_output_aliases={7 + len(mlp_rows) + i: i for i in range(len(before))},
         compiler_params=pltpu.CompilerParams(vmem_limit_bytes=VMEM),
         cost_estimate=pl.CostEstimate(
             flops=4 * chunk * width * half, bytes_accessed=16 * chunk * width, transcendentals=0
         ),
         name="attention_chunk",
-    )(index, grad_output, raw, scale, block_input, attn_gain, mlp_gain, *out_halves, *chosen, *before)
+    )(index, grad_output, raw, scale, gain, *out_halves, *mlp_rows, *before)
+
+
+def output_chunk_kernel(idx_ref, raw_ref, scale_ref, x_ref, attn_gain_ref, mlp_gain_ref, *refs, choices):
+    out_ref, held_ref, sem = refs[-3:]
+    step = pl.program_id(0)
+
+    @pl.when(step == 0)
+    def _():
+        fetch_choice(idx_ref, refs[:choices], held_ref, sem)
+
+    size = out_ref.shape[0]
+    down_raw = held_ref[pl.ds(pl.multiple_of(step * size, size), size), :].astype(F32)
+    down_scale = lax.rsqrt(jnp.mean(down_raw * down_raw, axis=1, keepdims=True) + EPS)
+    hidden = x_ref[...].astype(F32) + raw_ref[...].astype(F32) * scale_ref[...] * attn_gain_ref[...]
+    out_ref[...] = (hidden + down_raw * down_scale * mlp_gain_ref[...]).astype(BF16)
+
+
+def output_chunk(index, down_rows, raw, scale, block_input, attn_gain, mlp_gain, chunk, before):
+    tokens, width = block_input.shape
+    size = chunk // PARTS
+    rows = pl.BlockSpec((size, width), lambda j, idx: (PARTS * idx[0] + j, 0))
+    gain_row = pl.BlockSpec((1, width), lambda j, idx: (0, 0))
+    before = tuple(before)
+    return pl.pallas_call(
+        functools.partial(output_chunk_kernel, choices=len(down_rows)),
+        grid_spec=pltpu.PrefetchScalarGridSpec(
+            num_scalar_prefetch=1,
+            grid=(PARTS,),
+            in_specs=[
+                rows, pl.BlockSpec((size, 1), lambda j, idx: (PARTS * idx[0] + j, 0)), rows, gain_row, gain_row,
+            ] + [pl.BlockSpec(memory_space=pl.ANY)] * (len(down_rows) + len(before)),
+            out_specs=rows,
+            scratch_shapes=[pltpu.VMEM((chunk, width), BF16), pltpu.SemaphoreType.DMA(())],
+        ),
+        out_shape=jax.ShapeDtypeStruct((tokens, width), BF16),
+        input_output_aliases={6 + len(down_rows): 0} if before else {},
+        compiler_params=pltpu.CompilerParams(vmem_limit_bytes=VMEM),
+        cost_estimate=pl.CostEstimate(flops=0, bytes_accessed=8 * chunk * width, transcendentals=0),
+        name="output_chunk",
+    )(index, raw, scale, block_input, attn_gain, mlp_gain, *down_rows, *before)
 
 
 def place_rows_kernel(idx_ref, *refs, choices):
@@ -672,8 +700,8 @@
     def sum_sent(left_mat, right_other):
         return lax.ppermute(left_transposed(left_mat, right_other).astype(BF16), "dp", swap)
 
-    def sum_kept(left_mat, right_own, got):
-        total = (left_transposed(left_mat, right_own) + got.astype(F32)).astype(BF16)
+    def sum_kept(left_mat, right_own, sent):
+        total = (left_transposed(left_mat, right_own) + sent.astype(F32)).astype(BF16)
         return total, lax.psum_scatter(total, "row", scatter_dimension=0, tiled=True)
 
     by_x = [(0, 1), (1, 0), (2, 3), (3, 2)]
@@ -723,8 +751,7 @@
         return held
 
     full_qkv = gather(jnp.concatenate([w_query, w_key, w_value], axis=1), 0)
-    full_gate = gather(w_gate, 0)
-    full_up = gather(w_up, 0)
+    full_gate_up = gather(jnp.concatenate([w_gate, w_up], axis=1), 0)
     out_pieces = row_first(own_half(w_out, 0))
     out_pieces = row_second(out_pieces)
     out_own = row_columns(out_pieces)
@@ -766,12 +793,12 @@
             down_halves = row_blocks(down_pieces)
     attended_all = (attended, *lefts[1:], *rights[1:])
 
-    held = dict(forward=(), backward=(), attention=(), output=())
+    held = dict(forward=(), backward=(), attention=(), output=(), block_output=())
     gain_sums = dict(mlp=0.0, attn=0.0)
 
     def forward_work(slot, gate):
         results = forward_chunk(
-            slot_index[slot], after(attended_all, gate), out_halves, block_input, attn_row, full_gate, full_up,
+            slot_index[slot], after(attended_all, gate), out_halves, block_input, attn_row, full_gate_up,
             down_halves, chunk, held["forward"],
         )
         held["forward"] = results[:6]
@@ -785,7 +812,7 @@
     def backward_work(slot, down_rows):
         down_slots[slot] = down_rows
         results = backward_chunk(
-            slot_index[slot], down_rows, grad_output, mlp_row, gate_proj, up_proj, full_gate, full_up,
+            slot_index[slot], down_rows, grad_output, mlp_row, gate_proj, up_proj, full_gate_up,
             down_halves, chunk, held["backward"],
         )
         held["backward"] = results[:3]
@@ -818,18 +845,25 @@
 
     def attention_work(slot, mlp_rows):
         results = attention_chunk(
-            slot_index[slot], mlp_rows, down_slots[slot], grad_output, attn_raw, attn_scale, block_input, attn_row,
-            mlp_row, out_halves, half_width, chunk, held["attention"],
+            slot_index[slot], mlp_rows, grad_output, attn_raw, attn_scale, attn_row, out_halves, half_width,
+            chunk, held["attention"],
         )
-        held["attention"] = results[:3]
-        gain_sums["attn"] = gain_sums["attn"] + results[3]
+        held["attention"] = results[:2]
+        gain_sums["attn"] = gain_sums["attn"] + results[2]
         if slot == 3:
             hidden_left, up_right = after((hidden_b, grad_up_in), mlp_rows[0])
             blocks["up"] = sum_kept(hidden_left, own_half(up_right, 1), got["up"])
+        for other in {2: (3, 2), 1: (1, 0)}.get(slot, ()):
+            output = output_chunk(
+                slot_index[other], down_slots[other], after(attn_raw, mlp_rows), attn_scale, block_input, attn_row,
+                mlp_row, chunk, held["block_output"],
+            )
+            held["block_output"] = (output,)
         return results[1]
 
     gather_slots(mlp_own, attention_work)
-    grad_attn_in, grad_att, block_output = held["attention"]
+    grad_attn_in, grad_att = held["attention"]
+    (block_output,) = held["block_output"]
     own_grad_hidden = slot_rows(grad_output, 3).astype(F32) + mlp_own.astype(F32)
 
     query_dz, key_dz, grad_value_in, query_dot, key_dot, grad_query_gain, grad_key_gain = attend_backward(
@@ -860,13 +894,13 @@
             gain_pack = pack + lax.ppermute(pack, "dp", swap)
             return got["qkv"], got["out"], gain_pack
         if step == 2:
-            blocks["qkv"] = sum_kept(tokens_in, interleaved(own_half, pieces_in), got["qkv"])
+            blocks["out"] = sum_kept(left_out, own_half(right_out, 1), got["out"])
+            blocks["qkv"] = sum_kept(after(tokens_in, blocks["out"][0]), interleaved(own_half, pieces_in), got["qkv"]
+            )
             if rows == 4:
                 gain_pack = pack + lax.ppermute(pack, "row", by_x)
-            return blocks["qkv"][0], gain_pack
-        blocks["out"] = sum_kept(left_out, own_half(right_out, 1), got["out"])
+            return
         gain_pack = pack + lax.ppermute(pack, "row", by_y) if rows == 4 else lax.psum(pack, "row")
-        return blocks["out"][0], gain_pack
 
     input_own = sum_slots(
         lambda slot, gate: times_transposed(after(slot_rows(grad_qkv, slot), gate), full_qkv).astype(BF16), input_window

time: 1020 us -> 996 us (0.976)
  waiting for transfers between devices: 415 us -> 370 us
  Pallas kernels: 265 us -> 281 us
    reduce_scatter x5, waiting for transfers between devices: 63.1 us -> 31.2 us  [sum_kept(): lax.psum_scatter(total, 'row', scatter_dimension=0, tiled=True)]
    pallas_call x0 -> x4, Pallas kernels: none -> 24.5 us  [output_chunk(): pl.pallas_call(functools.partial(output_chunk_kernel, choices=len(down_ro...]
    ppermute x15, waiting for transfers between devices: 69.1 us -> 53.5 us  [line_step(): lax.ppermute(from_left, 'col', [(i, i + 1) for i in range(step - 1, cols...]
  transfers between devices with their start and end apart: 81 -> 80, of which waited for: 40 -> 35; matrix products, arithmetic and copies ran while one was open for 15% -> 17% of each run, Pallas kernels for 19% -> 24%
where the time goes in v9:
time: 996 us; the launch traced here: 985 us
  waiting for transfers between devices  370 us (37%)
  Pallas kernels  281 us (28%)
  starting transfers between devices  111 us (11%)
  matrix products  88.1 us (9%)
  other arithmetic  59.7 us (6%)
  local copies, waits for them, and re-layouts  34.7 us (3%)
  blocking collectives  24.4 us (2%)
  between operations  16.2 us (2%)
    ppermute x15, waiting for transfers between devices, line_step(): lax.ppermute(from_right, 'col', [(i + 1, i) for i in range(cols - step)])  127 us
    pallas_call x4, Pallas kernels, forward_chunk(): pl.pallas_call(functools.partial(forward_chunk_kernel, out_steps=out_step...  93.1 us
    ppermute x9, waiting for transfers between devices, sum_step(): up = lax.ppermute(up, 'col', [(i, i + 1) for i in range(step)])  90.4 us
    pallas_call x4, Pallas kernels, backward_chunk(): pl.pallas_call(functools.partial(backward_chunk_kernel, tiles=tiles, choi...  80.2 us
    dot_general x10, matrix products, left_transposed(): lax.dot_general(left_mat, right_mat, (((0,), (0,)), ((), ())), preferred_...  63.1 us
    ppermute x15, waiting for transfers between devices, line_step(): lax.ppermute(from_left, 'col', [(i, i + 1) for i in range(step - 1, cols...  53.5 us
    ppermute x9, starting transfers between devices, sum_step(): up = lax.ppermute(up, 'col', [(i, i + 1) for i in range(step)])  38.2 us
    pallas_call x4, Pallas kernels, attention_chunk(): pl.pallas_call(functools.partial(attention_chunk_kernel, choices=len(mlp_...  33.6 us
  transfers between devices with their start and end apart: 80, of which 35 were waited for; matrix products, arithmetic and copies ran while one was open for 17% of the time, Pallas kernels for 24%

profile of v9, /device:TPU:0, one launch (start us, length us, event | category | flops | bytes accessed | tf_op | source)
XLA Modules:
  0.0 985.2 jit_solution(9992253317239262881)
XLA Ops:
  40.8 16.8 %collective-permute-done.11 = bf16[256,2048]{1,0:T(8,128)(2,1)} collective-permute-done((bf16[256,2048]{1,0:T(8,128)(2,1)}, bf16[256,2048]{1,0:T(8,128)(2,1)}, u32[]{:S(2)}, u32[]{:S(2)}) %collective-permute-start.11) | collective-permute-done | bytes 1048608 | tf_op jit(solution)/shard_map/ppermute | solution.py:635
  70.2 16.0 %collective-permute-done.14 = bf16[256,2048]{1,0:T(8,128)(2,1)} collective-permute-done((bf16[256,2048]{1,0:T(8,128)(2,1)}, bf16[256,2048]{1,0:T(8,128)(2,1)}, u32[]{:S(2)}, u32[]{:S(2)}) %collective-permute-start.14) | collective-permute-done | bytes 1048608 | tf_op jit(solution)/shard_map/ppermute | solution.py:636
  87.5 10.2 %convolution_bitcast_fusion.q_ref.k_ref.v_ref = f32[1024,1536]{1,0:T(8,128)S(1)} fusion(bf16[1024,2048]{1,0:T(8,128)(2,1)} %x_ref.7, bf16[2048,1536]{1,0:T(8,128)(2,1)} %all-gather.3.cloned.1.call-done), kind=kOutput, calls=%fused_computation.4 | convolution fusion | flops 6442450944 | bytes 16777216 | tf_op jit(solution)/shard_map/dot_general | solution.py:25
  100.7 12.1 %all-reduce.1 = (f32[1024]{0:T(1024)S(1)}, f32[1024]{0:T(1024)S(1)}) all-reduce(f32[1024]{0:T(1024)S(1)} %get-tuple-element.380, f32[1024]{0:T(1024)S(1)} %get-tuple-element.379), channel_id=1, replica_groups=mesh['dp'=2,'row'=4,'col'=4] {'col'}, use_global_device_ids=true, to_apply=%region_1.2 | all-reduce | flops 2048 | bytes 16384 | tf_op jit(solution)/shard_map/psum | solution.py:767
  115.0 16.1 %attend_forward.1 = (bf16[1024,512]{1,0:T(8,128)(2,1)}, bf16[1024,512]{1,0:T(8,128)(2,1)}, bf16[1024,512]{1,0:T(8,128)(2,1)}, bf16[1024,512]{1,0:T(8,128)(2,1)}, f32[4,1024,1]{2,1,0:T(8,128)}) custom-call(f32[1024,1536]{1,0:T(8,128)} %copy-done.3, f32[1024,1536]{1,0:T(8,128)} %copy-done.3, f32[1024,1536]{1,0:T(8,128)} %copy-done.3, f32[1024,1]{1,0:T(8,128)} %copy.71.qs_ref, ...), custom_call_target="tpu_custom_call" | custom-call | flops 2147483648 | bytes 10485760 | tf_op jit(solution)/shard_map/attend_forward/pallas_call | solution.py:156
  152.7 21.6 %collective-permute-done.17 = bf16[1024,512]{1,0:T(8,128)(2,1)} collective-permute-done((bf16[1024,512]{1,0:T(8,128)(2,1)S(1)}, bf16[1024,512]{1,0:T(8,128)(2,1)}, u32[]{:S(2)}, u32[]{:S(2)}) %collective-permute-start.17) | collective-permute-done | bytes 1048608 | tf_op jit(solution)/shard_map/ppermute | solution.py:713
  193.0 27.5 %collective-permute-done.4.refs_5_ = bf16[1024,512]{1,0:T(8,128)(2,1)} collective-permute-done((bf16[1024,512]{1,0:T(8,128)(2,1)S(1)}, bf16[1024,512]{1,0:T(8,128)(2,1)}, u32[]{:S(2)}, u32[]{:S(2)}) %collective-permute-start.4) | collective-permute-done | bytes 1048608 | tf_op jit(solution)/shard_map/ppermute | solution.py:636
  222.5 24.8 %collective-permute-done.5.refs_6_ = bf16[1024,512]{1,0:T(8,128)(2,1)S(1)} collective-permute-done((bf16[1024,512]{1,0:T(8,128)(2,1)}, bf16[1024,512]{1,0:T(8,128)(2,1)S(1)}, u32[]{:S(2)}, u32[]{:S(2)}) %collective-permute-start.5) | collective-permute-done | bytes 1048608 | tf_op jit(solution)/shard_map/ppermute | solution.py:636
  248.3 23.2 %forward_chunk.4 = (bf16[1024,2048]{1,0:T(8,128)(2,1)}, f32[1024,1]{1,0:T(8,128)}, bf16[1024,2048]{1,0:T(8,128)(2,1)}, bf16[1024,2048]{1,0:T(8,128)(2,1)}, bf16[...) custom-call(s32[3]{0:T(128)} %get-tuple-element.440.idx_ref, ...), custom_call_target="tpu_custom_call" | custom-call | flops 8589934592 | bytes 33554432 | tf_op jit(solution)/shard_map/forward_chunk/pallas_call | solution.py:309
  274.1 23.3 %forward_chunk.5 = (bf16[1024,2048]{1,0:T(8,128)(2,1)}, f32[1024,1]{1,0:T(8,128)}, bf16[1024,2048]{1,0:T(8,128)(2,1)}, bf16[1024,2048]{1,0:T(8,128)(2,1)}, bf16[...) custom-call(s32[3]{0:T(128)} %get-tuple-element.441.idx_ref, ...), custom_call_target="tpu_custom_call", output_to_operand_aliasing={{0}: (16, {}), {1}: (17, {}), {2}: (18, {}), {3}: (19, {}),... | custom-call | flops 8589934592 | bytes 33554432 | tf_op jit(solution)/shard_map/forward_chunk/pallas_call | solution.py:309
  305.2 23.4 %forward_chunk.6 = (bf16[1024,2048]{1,0:T(8,128)(2,1)}, f32[1024,1]{1,0:T(8,128)}, bf16[1024,2048]{1,0:T(8,128)(2,1)}, bf16[1024,2048]{1,0:T(8,128)(2,1)}, bf16[...) custom-call(s32[3]{0:T(128)} %pad_add_fusion.1.idx_ref, ...), custom_call_target="tpu_custom_call", output_to_operand_aliasing={{0}: (16, {}), {1}: (17, {}), {2}: (18, {}), {3}: (19, {}),... | custom-call | flops 8589934592 | bytes 33554432 | tf_op jit(solution)/shard_map/forward_chunk/pallas_call | solution.py:309
  335.5 23.2 %forward_chunk.7 = (bf16[1024,2048]{1,0:T(8,128)(2,1)}, f32[1024,1]{1,0:T(8,128)}, bf16[1024,2048]{1,0:T(8,128)(2,1)}, bf16[1024,2048]{1,0:T(8,128)(2,1)}, bf16[...) custom-call(s32[3]{0:T(128)} %pad_add_fusion.idx_ref, ...), custom_call_target="tpu_custom_call", output_to_operand_aliasing={{0}: (16, {}), {1}: (17, {}), {2}: (18, {}), {3}: (19, {}),... | custom-call | flops 8589934592 | bytes 33554432 | tf_op jit(solution)/shard_map/forward_chunk/pallas_call | solution.py:309
  367.0 18.8 %collective-permute-done.28.refs_1_.refs_2_ = bf16[256,2048]{1,0:T(8,128)(2,1)S(1)} collective-permute-done((bf16[256,2048]{1,0:T(8,128)(2,1)S(1)}, bf16[256,2048]{1,0:T(8,128)(2,1)S(1)}, u32[]{:S(2)}, u32[]{:S(2)}) %collective-permute-start.28) | collective-permute-done | bytes 1048608 | tf_op jit(solution)/shard_map/ppermute | solution.py:635
  391.3 19.9 %backward_chunk.4 = (bf16[1024,2048]{1,0:T(8,128)(2,1)}, bf16[1024,2048]{1,0:T(8,128)(2,1)}, bf16[1024,2048]{1,0:T(8,128)(2,1)}, bf16[256,2048]{1,0:T(8,128)(2,1)}, f32[1,2048]{1,0:T(1,128)}) custom-call(s32[3]{0:T(128)} %pad_add_fusion.idx_ref, bf16[1024,2048]{1,0:T(8,128)(2,1)} %grad_ref.15, f32[1,2048]{1,0:T(1,128)} %bitcast.96, ...), custom_call_target="tpu_custom_call" | custom-call | flops 6442450944 | bytes 25165824 | tf_op jit(solution)/shard_map/backward_chunk/pallas_call | solution.py:407
  415.0 20.0 %backward_chunk.5 = (bf16[1024,2048]{1,0:T(8,128)(2,1)}, bf16[1024,2048]{1,0:T(8,128)(2,1)}, bf16[1024,2048]{1,0:T(8,128)(2,1)}, bf16[256,2048]{1,0:T(8,128)(2,1)}, f32[1,2048]{1,0:T(1,128)}) custom-call(s32[3]{0:T(128)} %pad_add_fusion.1.idx_ref, bf16[1024,2048]{1,0:T(8,128)(2,1)} %grad_ref.15, ...), custom_call_target="tpu_custom_call", output_to_operand_aliasing={{0}: (11, {}), {1}: (12, {}), {2}: (13, {})} | custom-call | flops 6442450944 | bytes 25165824 | tf_op jit(solution)/shard_map/backward_chunk/pallas_call | solution.py:407
  435.0 20.0 %backward_chunk.6 = (bf16[1024,2048]{1,0:T(8,128)(2,1)}, bf16[1024,2048]{1,0:T(8,128)(2,1)}, bf16[1024,2048]{1,0:T(8,128)(2,1)}, bf16[256,2048]{1,0:T(8,128)(2,1)}, f32[1,2048]{1,0:T(1,128)}) custom-call(s32[3]{0:T(128)} %get-tuple-element.441.idx_ref, bf16[1024,2048]{1,0:T(8,128)(2,1)} %grad_ref.15, ...), custom_call_target="tpu_custom_call", output_to_operand_aliasing={{0}: (13, {}), {1}: (14, {}), {2}: (15, {})} | custom-call | flops 6442450944 | bytes 25165824 | tf_op jit(solution)/shard_map/backward_chunk/pallas_call | solution.py:407
  456.3 20.4 %backward_chunk.7 = (bf16[1024,2048]{1,0:T(8,128)(2,1)}, bf16[1024,2048]{1,0:T(8,128)(2,1)}, bf16[1024,2048]{1,0:T(8,128)(2,1)}, bf16[256,2048]{1,0:T(8,128)(2,1)}, f32[1,2048]{1,0:T(1,128)}) custom-call(s32[3]{0:T(128)} %get-tuple-element.440.idx_ref, bf16[1024,2048]{1,0:T(8,128)(2,1)} %grad_ref.15, ...), custom_call_target="tpu_custom_call", output_to_operand_aliasing={{0}: (13, {}), {1}: (14, {}), {2}: (15, {})} | custom-call | flops 6442450944 | bytes 25165824 | tf_op jit(solution)/shard_map/backward_chunk/pallas_call | solution.py:407
  482.2 17.4 %collective-permute-done.34 = bf16[256,2048]{1,0:T(8,128)(2,1)S(1)} collective-permute-done((bf16[256,2048]{1,0:T(8,128)(2,1)}, bf16[256,2048]{1,0:T(8,128)(2,1)S(1)}, u32[]{:S(2)}, u32[]{:S(2)}) %collective-permute-start.34) | collective-permute-done | bytes 1048608 | tf_op jit(solution)/shard_map/ppermute | solution.py:640
  506.5 16.3 %collective-permute-done.35 = bf16[256,2048]{1,0:T(8,128)(2,1)S(1)} collective-permute-done((bf16[256,2048]{1,0:T(8,128)(2,1)S(1)}, bf16[256,2048]{1,0:T(8,128)(2,1)S(1)}, u32[]{:S(2)}, u32[]{:S(2)}) %collective-permute-start.35) | collective-permute-done | bytes 1048608 | tf_op jit(solution)/shard_map/ppermute | solution.py:640
  523.1 9.3 collective-permute-start.36
  533.7 15.1 %collective-permute-done.36 = bf16[256,2048]{1,0:T(8,128)(2,1)S(1)} collective-permute-done((bf16[256,2048]{1,0:T(8,128)(2,1)S(1)}, bf16[256,2048]{1,0:T(8,128)(2,1)S(1)}, u32[]{:S(2)}, u32[]{:S(2)}) %collective-permute-start.36) | collective-permute-done | bytes 1048608 | tf_op jit(solution)/shard_map/ppermute | solution.py:640
  557.1 14.2 %collective-permute-done.40.refs_1_.refs_2_ = bf16[256,2048]{1,0:T(8,128)(2,1)S(1)} collective-permute-done((bf16[256,2048]{1,0:T(8,128)(2,1)S(1)}, bf16[256,2048]{1,0:T(8,128)(2,1)S(1)}, u32[]{:S(2)}, u32[]{:S(2)}) %collective-permute-start.40) | collective-permute-done | bytes 1048608 | tf_op jit(solution)/shard_map/ppermute | solution.py:635
  581.9 20.3 %collective-permute-done.43.refs_0_.refs_1_ = bf16[256,2048]{1,0:T(8,128)(2,1)} collective-permute-done((bf16[256,2048]{1,0:T(8,128)(2,1)}, bf16[256,2048]{1,0:T(8,128)(2,1)}, u32[]{:S(2)}, u32[]{:S(2)}) %collective-permute-start.43) | collective-permute-done | bytes 1048608 | tf_op jit(solution)/shard_map/ppermute | solution.py:636
  603.9 9.5 convolution_convert_fusion.2
  647.3 17.9 %attend_backward.1 = (f32[1024,512]{1,0:T(8,128)}, f32[1024,512]{1,0:T(8,128)}, bf16[1024,512]{1,0:T(8,128)(2,1)}, f32[1024,1]{1,0:T(8,128)}, f32[1024,1]{1,0:T(...) custom-call(f32[1024,1536]{1,0:T(8,128)} %copy-done.3, f32[1024,1536]{1,0:T(8,128)} %copy-done.3, f32[1024,1]{1,0:T(8,128)} %copy.71.qs_ref, ...), custom_call_target="tpu_custom_call" | custom-call | flops 5368709120 | bytes 20971520 | tf_op jit(solution)/shard_map/attend_backward/pallas_call | solution.py:180
  667.7 12.3 %all-reduce = (f32[1024]{0:T(1024)S(1)}, f32[1024]{0:T(1024)S(1)}) all-reduce(f32[1024]{0:T(1024)S(1)} %reduce.1, f32[1024]{0:T(1024)S(1)} %reduce), channel_id=1, replica_groups=mesh['dp'=2,'row'=4,'col'=4] {'col'}, use_global_device_ids=true, to_apply=%region_5.6 | all-reduce | flops 2048 | bytes 16384 | tf_op jit(solution)/shard_map/psum | solution.py:873
  694.6 16.2 %collective-permute-done.46 = bf16[256,2048]{1,0:T(8,128)(2,1)S(1)} collective-permute-done((bf16[256,2048]{1,0:T(8,128)(2,1)S(1)}, bf16[256,2048]{1,0:T(8,128)(2,1)S(1)}, u32[]{:S(2)}, u32[]{:S(2)}) %collective-permute-start.46) | collective-permute-done | bytes 1048608 | tf_op jit(solution)/shard_map/ppermute | solution.py:640
  716.7 10.6 %add_convert_fusion.2 = bf16[2048,1024]{1,0:T(8,128)(2,1)} fusion(bf16[2048,1024]{1,0:T(8,128)(2,1)} %collective-permute-done.58, bf16[1024,2048]{1,0:T(8,128)(2,1)} %get-tuple-element.304, bf16[1024,2048]{1,0:T(8,128)(2,1)} %get-tuple-element.305, s32[]{:T(128)S(6)} %select_n.227), kind=kOutput, calls=%fused_computation.2 | convolution fusion | flops 4301258752 | bytes 14680068 | tf_op jit(solution)/shard_map/dot_general | solution.py:35
  795.6 10.3 %collective-permute-done.48 = bf16[256,2048]{1,0:T(8,128)(2,1)} collective-permute-done((bf16[256,2048]{1,0:T(8,128)(2,1)}, bf16[256,2048]{1,0:T(8,128)(2,1)}, u32[]{:S(2)}, u32[]{:S(2)}) %collective-permute-start.48) | collective-permute-done | bytes 1048608 | tf_op jit(solution)/shard_map/ppermute | solution.py:640
  821.6 15.1 %collective-permute-done.50 = bf16[256,2048]{1,0:T(8,128)(2,1)S(1)} collective-permute-done((bf16[256,2048]{1,0:T(8,128)(2,1)S(1)}, bf16[256,2048]{1,0:T(8,128)(2,1)S(1)}, u32[]{:S(2)}, u32[]{:S(2)}) %collective-permute-start.50) | collective-permute-done | bytes 1048608 | tf_op jit(solution)/shard_map/ppermute | solution.py:640
  888.0 18.7 %collective-permute-done.56.refs_0_.refs_1_ = bf16[256,2048]{1,0:T(8,128)(2,1)S(1)} collective-permute-done((bf16[256,2048]{1,0:T(8,128)(2,1)}, bf16[256,2048]{1,0:T(8,128)(2,1)S(1)}, u32[]{:S(2)}, u32[]{:S(2)}) %collective-permute-start.56) | collective-permute-done | bytes 1048608 | tf_op jit(solution)/shard_map/ppermute | solution.py:636
  933.1 26.6 %reduce-scatter.14.cloned.1.call-done = bf16[512,768]{1,0:T(8,128)(2,1)} async-done(((bf16[2048,768]{1,0:T(8,128)(2,1)}), bf16[512,768]{1,0:T(8,128)(2,1)}) %reduce-scatter.14.cloned.1.call-update) | async-done | bytes 786448 | tf_op jit(solution)/shard_map/reduce_scatter | solution.py:705
  (382 shorter events, 401.6 us)
Async XLA Ops:
  7.2 80.3 %all-gather.3.cloned.1.call-start = ((), (), s32[]{:S(2)}) async-start(), calls=%async_computation.5 | async-start | bytes 7077888 | tf_op jit(solution)/shard_map/all_gather | solution.py:632
  9.5 237.9 %all-gather.5.cloned.1.call-start = ((), (), s32[]{:S(2)}) async-start(), calls=%async_computation.6 | async-start | bytes 18874368 | tf_op jit(solution)/shard_map/all_gather | solution.py:632
  12.7 864.2 %reduce-scatter.12.cloned.1.call-start = ((), (), s32[]{:S(2)}) async-start(), calls=%async_computation.10 | async-start | bytes 1310720 | tf_op jit(solution)/shard_map/reduce_scatter | solution.py:705
  68.5 67.5 %collective-permute-start.13 = (bf16[256,2048]{1,0:T(8,128)(2,1)}, bf16[256,2048]{1,0:T(8,128)(2,1)}, u32[]{:S(2)}, u32[]{:S(2)}) collective-permute-start(bf16[256,2048]{1,0:T(8,128)(2,1)} %collective-permute-done.12), channel_id=1, source_target_pairs={{2,3},{6,7},{10,11},{14,15},{18,19},{22,23},{26,27},{30,31}} | collective-permute-start | bytes 3145736 | tf_op jit(solution)/shard_map/ppermute | solution.py:635
  86.2 54.6 %collective-permute-start.15 = (bf16[256,2048]{1,0:T(8,128)(2,1)}, bf16[256,2048]{1,0:T(8,128)(2,1)}, u32[]{:S(2)}, u32[]{:S(2)}) collective-permute-start(bf16[256,2048]{1,0:T(8,128)(2,1)} %collective-permute-done.14), channel_id=1, source_target_pairs={{1,0},{5,4},{9,8},{13,12},{17,16},{21,20},{25,24},{29,28}} | collective-permute-start | bytes 3145736 | tf_op jit(solution)/shard_map/ppermute | solution.py:636
  134.0 40.4 %collective-permute-start.17 = (bf16[1024,512]{1,0:T(8,128)(2,1)S(1)}, bf16[1024,512]{1,0:T(8,128)(2,1)}, u32[]{:S(2)}, u32[]{:S(2)}) collective-permute-start(bf16[1024,512]{1,0:T(8,128)(2,1)S(1)} %constant_dynamic-slice_fusion.10), channel_id=1, source_target_pairs={{0,4},{4,0},{8,12},{12,8},{1,5},{5,1},{9,13},{13,9},{2,6},{6,2},{1... | collective-permute-start | bytes 3145736 | tf_op jit(solution)/shard_map/ppermute | solution.py:713
  136.0 38.3 %collective-permute-start.18 = (bf16[1024,512]{1,0:T(8,128)(2,1)S(1)}, bf16[1024,512]{1,0:T(8,128)(2,1)}, u32[]{:S(2)}, u32[]{:S(2)}) collective-permute-start(bf16[1024,512]{1,0:T(8,128)(2,1)S(1)} %constant_dynamic-slice_fusion.10), channel_id=1, source_target_pairs={{0,8},{8,0},{4,12},{12,4},{1,9},{9,1},{5,13},{13,5},{2,10},{10,2},... | collective-permute-start | bytes 3145736 | tf_op jit(solution)/shard_map/ppermute | solution.py:713
  145.0 102.3 %collective-permute-start.16 = (bf16[1024,2048]{1,0:T(8,128)(2,1)}, bf16[1024,2048]{1,0:T(8,128)(2,1)}, u32[]{:S(2)}, u32[]{:S(2)}) collective-permute-start(bf16[1024,2048]{1,0:T(8,128)(2,1)} %pad_maximum_fusion.refs_7_.wo_own_ref), channel_id=1, source_target_pairs={{0,16},{16,0},{1,17},{17,1},{2,18},{18,2},{3,19},{19,3},{4,20},{20... | collective-permute-start | bytes 12582920 | tf_op jit(solution)/shard_map/ppermute | solution.py:789
  190.2 57.1 %collective-permute-start.21 = (bf16[4,1024,512]{2,1,0:T(8,128)(2,1)}, bf16[4,1024,512]{2,1,0:T(8,128)(2,1)}, u32[]{:S(2)}, u32[]{:S(2)}) collective-permute-start(bf16[4,1024,512]{2,1,0:T(8,128)(2,1)} %bitcast_dynamic-update-slice_fusion.3.refs_13_.wd_own_ref), channel_id=1, source_target_pairs={{0,16},{16,0},{1,17},{17,1},{2,18},{18,2},{3,19},{19,3},{4,20},{20... | collective-permute-start | bytes 12582920 | tf_op jit(solution)/shard_map/ppermute | solution.py:738
  191.0 29.6 %collective-permute-start.4 = (bf16[1024,512]{1,0:T(8,128)(2,1)S(1)}, bf16[1024,512]{1,0:T(8,128)(2,1)}, u32[]{:S(2)}, u32[]{:S(2)}) collective-permute-start(bf16[1024,512]{1,0:T(8,128)(2,1)S(1)} %collective-permute-done.3.refs_4_), channel_id=1, source_target_pairs={{1,0},{2,1},{5,4},{6,5},{9,8},{10,9},{13,12},{14,13},{17,16},{18,1... | collective-permute-start | bytes 3145736 | tf_op jit(solution)/shard_map/ppermute | solution.py:636
  192.3 30.2 %collective-permute-start.2 = (bf16[1024,512]{1,0:T(8,128)(2,1)S(1)}, bf16[1024,512]{1,0:T(8,128)(2,1)S(1)}, u32[]{:S(2)}, u32[]{:S(2)}) collective-permute-start(bf16[1024,512]{1,0:T(8,128)(2,1)S(1)} %collective-permute-done.1.refs_2_), channel_id=1, source_target_pairs={{2,3},{6,7},{10,11},{14,15},{18,19},{22,23},{26,27},{30,31}} | collective-permute-start | bytes 3145736 | tf_op jit(solution)/shard_map/ppermute | solution.py:635
  220.5 26.8 %collective-permute-start.5 = (bf16[1024,512]{1,0:T(8,128)(2,1)}, bf16[1024,512]{1,0:T(8,128)(2,1)S(1)}, u32[]{:S(2)}, u32[]{:S(2)}) collective-permute-start(bf16[1024,512]{1,0:T(8,128)(2,1)} %collective-permute-done.4.refs_5_), channel_id=1, source_target_pairs={{1,0},{5,4},{9,8},{13,12},{17,16},{21,20},{25,24},{29,28}} | collective-permute-start | bytes 3145736 | tf_op jit(solution)/shard_map/ppermute | solution.py:636
  301.2 27.3 %collective-permute-start.24 = (bf16[256,2048]{1,0:T(8,128)(2,1)}, bf16[256,2048]{1,0:T(8,128)(2,1)S(1)}, u32[]{:S(2)}, u32[]{:S(2)}) collective-permute-start(bf16[256,2048]{1,0:T(8,128)(2,1)} %get-tuple-element.410), channel_id=1, source_target_pairs={{0,1},{1,2},{4,5},{5,6},{8,9},{9,10},{12,13},{13,14},{16,17},{17,1... | collective-permute-start | bytes 3145736 | tf_op jit(solution)/shard_map/ppermute | solution.py:640
  331.3 27.4 %collective-permute-start.26 = (bf16[256,2048]{1,0:T(8,128)(2,1)}, bf16[256,2048]{1,0:T(8,128)(2,1)S(1)}, u32[]{:S(2)}, u32[]{:S(2)}) collective-permute-start(bf16[256,2048]{1,0:T(8,128)(2,1)} %get-tuple-element.408), channel_id=1, source_target_pairs={{0,1},{1,2},{2,3},{4,5},{5,6},{6,7},{8,9},{9,10},{10,11},{12,13},{... | collective-permute-start | bytes 3145736 | tf_op jit(solution)/shard_map/ppermute | solution.py:640
  411.3 43.7 %collective-permute-start.32 = (bf16[256,2048]{1,0:T(8,128)(2,1)S(1)}, bf16[256,2048]{1,0:T(8,128)(2,1)S(1)}, u32[]{:S(2)}, u32[]{:S(2)}) collective-permute-start(bf16[256,2048]{1,0:T(8,128)(2,1)S(1)} %collective-permute-done.29.refs_3_.refs_2_), channel_id=1, source_target_pairs={{2,3},{6,7},{10,11},{14,15},{18,19},{22,23},{26,27},{30,31}} | collective-permute-start | bytes 3145736 | tf_op jit(solution)/shard_map/ppermute | solution.py:635
  413.5 41.4 %collective-permute-start.33 = (bf16[256,2048]{1,0:T(8,128)(2,1)}, bf16[256,2048]{1,0:T(8,128)(2,1)S(1)}, u32[]{:S(2)}, u32[]{:S(2)}) collective-permute-start(bf16[256,2048]{1,0:T(8,128)(2,1)} %collective-permute-done.31.refs_0_.refs_1_), channel_id=1, source_target_pairs={{1,0},{5,4},{9,8},{13,12},{17,16},{21,20},{25,24},{29,28}} | collective-permute-start | bytes 3145736 | tf_op jit(solution)/shard_map/ppermute | solution.py:636
  580.2 58.6 %collective-permute-start.44 = (bf16[256,2048]{1,0:T(8,128)(2,1)S(1)}, bf16[256,2048]{1,0:T(8,128)(2,1)}, u32[]{:S(2)}, u32[]{:S(2)}) collective-permute-start(bf16[256,2048]{1,0:T(8,128)(2,1)S(1)} %collective-permute-done.41.refs_3_.refs_2_), channel_id=1, source_target_pairs={{2,3},{6,7},{10,11},{14,15},{18,19},{22,23},{26,27},{30,31}} | collective-permute-start | bytes 3145736 | tf_op jit(solution)/shard_map/ppermute | solution.py:635
  602.2 36.6 %collective-permute-start.45 = (bf16[256,2048]{1,0:T(8,128)(2,1)}, bf16[256,2048]{1,0:T(8,128)(2,1)}, u32[]{:S(2)}, u32[]{:S(2)}) collective-permute-start(bf16[256,2048]{1,0:T(8,128)(2,1)} %collective-permute-done.43.refs_0_.refs_1_), channel_id=1, source_target_pairs={{1,0},{5,4},{9,8},{13,12},{17,16},{21,20},{25,24},{29,28}} | collective-permute-start | bytes 3145736 | tf_op jit(solution)/shard_map/ppermute | solution.py:636
  613.4 103.3 %collective-permute-start.58 = (bf16[2048,1024]{1,0:T(8,128)(2,1)}, bf16[2048,1024]{1,0:T(8,128)(2,1)}, u32[]{:S(2)}, u32[]{:S(2)}) collective-permute-start(bf16[2048,1024]{1,0:T(8,128)(2,1)} %convolution_convert_fusion.2), channel_id=1, source_target_pairs={{0,16},{16,0},{1,17},{17,1},{2,18},{18,2},{3,19},{19,3},{4,20},{20... | collective-permute-start | bytes 12582920 | tf_op jit(solution)/shard_map/ppermute | solution.py:701
  716.7 162.3 %reduce-scatter.6.cloned.1.call-start = ((), (), s32[]{:S(2)}) async-start(), calls=%async_computation.7 | async-start | bytes 5242880 | tf_op jit(solution)/shard_map/reduce_scatter | solution.py:705
  727.4 157.3 %reduce-scatter.8.cloned.1.call-start = ((), (), s32[]{:S(2)}) async-start(), calls=%async_computation.8 | async-start | bytes 5242880 | tf_op jit(solution)/shard_map/reduce_scatter | solution.py:705
  749.1 163.7 %reduce-scatter.10.cloned.1.call-start = ((), (), s32[]{:S(2)}) async-start(), calls=%async_computation.9 | async-start | bytes 5242880 | tf_op jit(solution)/shard_map/reduce_scatter | solution.py:705
  770.9 188.8 %reduce-scatter.14.cloned.1.call-start = ((), (), s32[]{:S(2)}) async-start(), calls=%async_computation.11 | async-start | bytes 3932160 | tf_op jit(solution)/shard_map/reduce_scatter | solution.py:705
  778.4 27.5 %collective-permute-start.48 = (bf16[256,2048]{1,0:T(8,128)(2,1)}, bf16[256,2048]{1,0:T(8,128)(2,1)}, u32[]{:S(2)}, u32[]{:S(2)}) collective-permute-start(bf16[256,2048]{1,0:T(8,128)(2,1)} %get-tuple-element.401), channel_id=1, source_target_pairs={{0,1},{1,2},{4,5},{5,6},{8,9},{9,10},{12,13},{13,14},{16,17},{17,1... | collective-permute-start | bytes 3145736 | tf_op jit(solution)/shard_map/ppermute | solution.py:640
  807.7 29.0 %collective-permute-start.50 = (bf16[256,2048]{1,0:T(8,128)(2,1)S(1)}, bf16[256,2048]{1,0:T(8,128)(2,1)S(1)}, u32[]{:S(2)}, u32[]{:S(2)}) collective-permute-start(bf16[256,2048]{1,0:T(8,128)(2,1)S(1)} %get-tuple-element.399), channel_id=1, source_target_pairs={{0,1},{1,2},{2,3},{4,5},{5,6},{6,7},{8,9},{9,10},{10,11},{12,13},{... | collective-permute-start | bytes 3145736 | tf_op jit(solution)/shard_map/ppermute | solution.py:640
  843.3 33.7 %collective-permute-start.52 = (bf16[256,2048]{1,0:T(8,128)(2,1)S(1)}, bf16[256,2048]{1,0:T(8,128)(2,1)}, u32[]{:S(2)}, u32[]{:S(2)}) collective-permute-start(bf16[256,2048]{1,0:T(8,128)(2,1)S(1)} %add_convert_fusion.4.refs_0_), channel_id=1, source_target_pairs={{0,1},{1,2},{2,3},{4,5},{5,6},{6,7},{8,9},{9,10},{10,11},{12,13},{... | collective-permute-start | bytes 3145736 | tf_op jit(solution)/shard_map/ppermute | solution.py:635
  846.1 31.6 %collective-permute-start.55 = (bf16[256,2048]{1,0:T(8,128)(2,1)S(1)}, bf16[256,2048]{1,0:T(8,128)(2,1)}, u32[]{:S(2)}, u32[]{:S(2)}) collective-permute-start(bf16[256,2048]{1,0:T(8,128)(2,1)S(1)} %add_convert_fusion.4.refs_0_), channel_id=1, source_target_pairs={{1,0},{2,1},{3,2},{5,4},{6,5},{7,6},{9,8},{10,9},{11,10},{13,12},{... | collective-permute-start | bytes 3145736 | tf_op jit(solution)/shard_map/ppermute | solution.py:636
  877.7 29.0 %collective-permute-start.56 = (bf16[256,2048]{1,0:T(8,128)(2,1)}, bf16[256,2048]{1,0:T(8,128)(2,1)S(1)}, u32[]{:S(2)}, u32[]{:S(2)}) collective-permute-start(bf16[256,2048]{1,0:T(8,128)(2,1)} %collective-permute-done.55.refs_0_.refs_1_), channel_id=1, source_target_pairs={{1,0},{2,1},{5,4},{6,5},{9,8},{10,9},{13,12},{14,13},{17,16},{18,1... | collective-permute-start | bytes 3145736 | tf_op jit(solution)/shard_map/ppermute | solution.py:636
  879.0 33.8 %collective-permute-start.59 = (bf16[512,1024]{1,0:T(8,128)(2,1)}, bf16[512,1024]{1,0:T(8,128)(2,1)}, u32[]{:S(2)}, u32[]{:S(2)}) collective-permute-start(bf16[512,1024]{1,0:T(8,128)(2,1)} %reduce-scatter.6.cloned.1.call-done), channel_id=1, source_target_pairs={{0,16},{16,0},{1,17},{17,1},{2,18},{18,2},{3,19},{19,3},{4,20},{20... | collective-permute-start | bytes 3145736 | tf_op jit(solution)/shard_map/ppermute | solution.py:695
  884.7 37.6 %collective-permute-start.61 = (bf16[512,1024]{1,0:T(8,128)(2,1)}, bf16[512,1024]{1,0:T(8,128)(2,1)}, u32[]{:S(2)}, u32[]{:S(2)}) collective-permute-start(bf16[512,1024]{1,0:T(8,128)(2,1)} %reduce-scatter.8.cloned.1.call-done), channel_id=1, source_target_pairs={{0,16},{16,0},{1,17},{17,1},{2,18},{18,2},{3,19},{19,3},{4,20},{20... | collective-permute-start | bytes 3145736 | tf_op jit(solution)/shard_map/ppermute | solution.py:695
  886.3 87.9 %collective-permute-start.54 = (bf16[256,2048]{1,0:T(8,128)(2,1)S(1)}, bf16[256,2048]{1,0:T(8,128)(2,1)}, u32[]{:S(2)}, u32[]{:S(2)}) collective-permute-start(bf16[256,2048]{1,0:T(8,128)(2,1)S(1)} %collective-permute-done.53.refs_3_.refs_2_), channel_id=1, source_target_pairs={{2,3},{6,7},{10,11},{14,15},{18,19},{22,23},{26,27},{30,31}} | collective-permute-start | bytes 3145736 | tf_op jit(solution)/shard_map/ppermute | solution.py:635
  906.7 67.6 %collective-permute-start.57 = (bf16[256,2048]{1,0:T(8,128)(2,1)S(1)}, bf16[256,2048]{1,0:T(8,128)(2,1)}, u32[]{:S(2)}, u32[]{:S(2)}) collective-permute-start(bf16[256,2048]{1,0:T(8,128)(2,1)S(1)} %collective-permute-done.56.refs_0_.refs_1_), channel_id=1, source_target_pairs={{1,0},{5,4},{9,8},{13,12},{17,16},{21,20},{25,24},{29,28}} | collective-permute-start | bytes 3145736 | tf_op jit(solution)/shard_map/ppermute | solution.py:636
  (109 other events, 2054.6 us)
Sparse Core Ops, SparseCore 0:
  10.5 51.5 all-gather.2
  64.5 107.9 all-gather.4
  716.8 27.4 reduce-scatter.11
  747.7 52.5 reduce-scatter.5
  803.7 52.9 reduce-scatter.7
  860.1 52.5 reduce-scatter.9
  915.8 43.8 reduce-scatter.13

commit v10 on v9

--- a/solution.py
+++ b/solution.py
@@ -212,6 +212,42 @@
             copy.wait()
 
 
+def qkv_kernel(idx_ref, x_ref, own_ref, oth_ref, out_ref):
+    step = pl.program_id(0)
+
+    @pl.when(step < 3)
+    def _():
+        out_ref[...] = plain_dot(x_ref[...], own_ref[...])
+
+    @pl.when(step >= 3)
+    def _():
+        out_ref[...] = plain_dot(x_ref[...], oth_ref[...])
+
+
+def qkv_product(index, block_input, halves):
+    tokens, width = block_input.shape
+    part = halves[0].shape[1] // 3
+    return pl.pallas_call(
+        qkv_kernel,
+        grid_spec=pltpu.PrefetchScalarGridSpec(
+            num_scalar_prefetch=1,
+            grid=(6,),
+            in_specs=[
+                pl.BlockSpec((tokens, width), lambda j, idx: (0, 0)),
+                pl.BlockSpec((width, part), lambda j, idx: (0, jnp.minimum(j, 2))),
+                pl.BlockSpec((width, part), lambda j, idx: (0, jnp.maximum(j - 3, 0))),
+            ],
+            out_specs=pl.BlockSpec((tokens, part), lambda j, idx: (0, 2 * (j % 3) + (idx[1] + j // 3) % 2)),
+        ),
+        out_shape=jax.ShapeDtypeStruct((tokens, 6 * part), F32),
+        compiler_params=pltpu.CompilerParams(vmem_limit_bytes=VMEM),
+        cost_estimate=pl.CostEstimate(
+            flops=12 * tokens * width * part, bytes_accessed=20 * tokens * width, transcendentals=0
+        ),
+        name="qkv",
+    )(index, block_input, *halves)
+
+
 def half_tile(step, core, tiles):
     per_half = tiles // 2
     return ((core + step // per_half) % 2) * per_half + step % per_half
@@ -469,8 +505,8 @@
 
 def attention_chunk(index, mlp_rows, grad_output, raw, scale, gain, out_halves, half, chunk, before):
     tokens, width = grad_output.shape
-    size = chunk // PARTS
-    rows = pl.BlockSpec((size, width), lambda j, idx: (PARTS * idx[0] + j, 0))
+    size = chunk
+    rows = pl.BlockSpec((size, width), lambda j, idx: (idx[0], 0))
     gain_row = pl.BlockSpec((1, width), lambda j, idx: (0, 0))
     own_heads = pl.BlockSpec((half, width), lambda j, idx: (0, 0))
     before = tuple(before)
@@ -478,12 +514,12 @@
         functools.partial(attention_chunk_kernel, choices=len(mlp_rows)),
         grid_spec=pltpu.PrefetchScalarGridSpec(
             num_scalar_prefetch=1,
-            grid=(PARTS,),
+            grid=(1,),
             in_specs=[
-                rows, rows, pl.BlockSpec((size, 1), lambda j, idx: (PARTS * idx[0] + j, 0)), gain_row,
+                rows, rows, pl.BlockSpec((size, 1), lambda j, idx: (idx[0], 0)), gain_row,
                 own_heads, own_heads,
             ] + [pl.BlockSpec(memory_space=pl.ANY)] * (len(mlp_rows) + len(before)),
-            out_specs=[rows, pl.BlockSpec((size, 2 * half), lambda j, idx: (PARTS * idx[0] + j, 0)), gain_row],
+            out_specs=[rows, pl.BlockSpec((size, 2 * half), lambda j, idx: (idx[0], 0)), gain_row],
             scratch_shapes=[pltpu.VMEM((chunk, width), BF16), pltpu.SemaphoreType.DMA(())],
         ),
         out_shape=[
@@ -628,9 +664,6 @@
         half = array.shape[axis] // 2
         return lax.dynamic_slice_in_dim(array, (1 - core) * half, half, axis)
 
-    def gather(weight, axis):
-        return lax.all_gather(own_half(weight, axis), ("row", "dp"), axis=axis, tiled=True)
-
     def line_step(from_left, from_right, step):
         from_left = lax.ppermute(from_left, "col", [(i, i + 1) for i in range(step - 1, cols - 1)])
         from_right = lax.ppermute(from_right, "col", [(i + 1, i) for i in range(cols - step)])
@@ -750,8 +783,11 @@
             held = lax.dynamic_update_slice(held, piece, (start, number * block))
         return held
 
-    full_qkv = gather(jnp.concatenate([w_query, w_key, w_value], axis=1), 0)
-    full_gate_up = gather(jnp.concatenate([w_gate, w_up], axis=1), 0)
+    qkv_start = jnp.concatenate([own_half(one, 1) for one in (w_query, w_key, w_value)], axis=1)
+    qkv_pieces = row_first(qkv_start)
+    tables = rope_tables(positions)
+    seg_col, seg_row = segment_ids[:, None], segment_ids[None, :]
+    qkv_pieces = row_second(after(qkv_pieces, tables, seg_col))
     out_pieces = row_first(own_half(w_out, 0))
     out_pieces = row_second(out_pieces)
     out_own = row_columns(out_pieces)
@@ -760,9 +796,14 @@
         one, two = line_step(out_left[-1], out_right[-1], step)
         out_left.append(one)
         out_right.append(two)
-    down_pieces = row_first(after(own_half(w_down, 0), full_qkv))
-
-    qkv = plain_dot(block_input, full_qkv)
+    gate_up_half, down_half = after(
+        (own_half(jnp.concatenate([w_gate, w_up], axis=1), 0), own_half(w_down, 0)), qkv_pieces
+    )
+    full_gate_up = lax.all_gather(gate_up_half, ("row", "dp"), axis=0, tiled=True)
+    down_pieces = row_first(down_half)
+    qkv_halves = [one.reshape(width, 3 * half_width) for one in row_blocks(qkv_pieces)]
+
+    qkv = qkv_product(slot_index[3], block_input, qkv_halves)
     query_raw, key_raw = qkv[:, :local_width], qkv[:, local_width : 2 * local_width]
     query_sq, key_sq = lax.psum(
         (jnp.sum(query_raw * query_raw, axis=1), jnp.sum(key_raw * key_raw, axis=1)), "col"
@@ -771,8 +812,6 @@
     key_scale = lax.rsqrt(key_sq / width + EPS)[:, None]
     scales = (query_scale, key_scale)
     gains = (query_gain[None, :], key_gain[None, :])
-    tables = rope_tables(positions)
-    seg_col, seg_row = segment_ids[:, None], segment_ids[None, :]
     query_rot, key_rot, value_heads, attended, log_total = attend_forward(
         qkv, scales, gains, tables, seg_col, seg_row, heads
     )
@@ -793,19 +832,19 @@
             down_halves = row_blocks(down_pieces)
     attended_all = (attended, *lefts[1:], *rights[1:])
 
-    held = dict(forward=(), backward=(), attention=(), output=(), block_output=())
+    held = dict(f=(), b=(), a=(), o=(), m=())
     gain_sums = dict(mlp=0.0, attn=0.0)
 
     def forward_work(slot, gate):
         results = forward_chunk(
             slot_index[slot], after(attended_all, gate), out_halves, block_input, attn_row, full_gate_up,
-            down_halves, chunk, held["forward"],
+            down_halves, chunk, held["f"],
         )
-        held["forward"] = results[:6]
+        held["f"] = results[:6]
         return results[6]
 
     down_own = sum_slots(forward_work).astype(BF16)
-    attn_raw, attn_scale, hidden_b, gate_proj, up_proj, mixed_act = held["forward"]
+    attn_raw, attn_scale, hidden_b, gate_proj, up_proj, mixed_act = held["f"]
     mlp_parts = [None] * cols
     down_slots = [None] * cols
 
@@ -813,15 +852,15 @@
         down_slots[slot] = down_rows
         results = backward_chunk(
             slot_index[slot], down_rows, grad_output, mlp_row, gate_proj, up_proj, full_gate_up,
-            down_halves, chunk, held["backward"],
+            down_halves, chunk, held["b"],
         )
-        held["backward"] = results[:3]
+        held["b"] = results[:3]
         mlp_parts[slot] = results[3]
         gain_sums["mlp"] = gain_sums["mlp"] + results[4]
         return results[3]
 
     gather_slots(down_own, backward_work)
-    grad_down_in, grad_gate_in, grad_up_in = held["backward"]
+    grad_down_in, grad_gate_in, grad_up_in = held["b"]
 
     blocks = {}
     got = {}
@@ -846,9 +885,9 @@
     def attention_work(slot, mlp_rows):
         results = attention_chunk(
             slot_index[slot], mlp_rows, grad_output, attn_raw, attn_scale, attn_row, out_halves, half_width,
-            chunk, held["attention"],
+            chunk, held["a"],
         )
-        held["attention"] = results[:2]
+        held["a"] = results[:2]
         gain_sums["attn"] = gain_sums["attn"] + results[2]
         if slot == 3:
             hidden_left, up_right = after((hidden_b, grad_up_in), mlp_rows[0])
@@ -856,14 +895,14 @@
         for other in {2: (3, 2), 1: (1, 0)}.get(slot, ()):
             output = output_chunk(
                 slot_index[other], down_slots[other], after(attn_raw, mlp_rows), attn_scale, block_input, attn_row,
-                mlp_row, chunk, held["block_output"],
+                mlp_row, chunk, held["m"],
             )
-            held["block_output"] = (output,)
+            held["m"] = (output,)
         return results[1]
 
     gather_slots(mlp_own, attention_work)
-    grad_attn_in, grad_att = held["attention"]
-    (block_output,) = held["block_output"]
+    grad_attn_in, grad_att = held["a"]
+    (block_output,) = held["m"]
     own_grad_hidden = slot_rows(grad_output, 3).astype(F32) + mlp_own.astype(F32)
 
     query_dz, key_dz, grad_value_in, query_dot, key_dot, grad_query_gain, grad_key_gain = attend_backward(
@@ -877,34 +916,36 @@
     grad_key_in = (
         key_scale * (key_dz - key_raw * key_scale * (key_dot / width)[:, None])
     ).astype(BF16)
-    grad_qkv = jnp.concatenate([grad_query_in, grad_key_in, grad_value_in], axis=1)
     gain_pack = jnp.concatenate([grad_query_gain, grad_key_gain, gain_sums["attn"], gain_sums["mlp"]], axis=1)
 
-    def interleaved(picker, pieces_in):
-        return jnp.concatenate([picker(one, 1) for one in pieces_in], axis=1)
+    grad_halves = [
+        jnp.concatenate([picker(one, 1) for one in (grad_query_in, grad_key_in, grad_value_in)], axis=1)
+        for picker in (own_half, other_half)
+    ]
+
+    def input_work(slot, gate):
+        own, other = after([slot_rows(one, slot) for one in grad_halves], gate)
+        return (times_transposed(own, qkv_halves[0]) + times_transposed(other, qkv_halves[1])).astype(BF16)
 
     def input_window(step, gate):
         nonlocal gain_pack
-        pack, *pieces_in, tokens_in, left_out, right_out = after(
-            (gain_pack, grad_query_in, grad_key_in, grad_value_in, block_input, grad_attn_in, attended), gate
+        pack, own, other, tokens_in, left_out, right_out = after(
+            (gain_pack, *grad_halves, block_input, grad_attn_in, attended), gate
         )
         if step == 1:
-            got["qkv"] = sum_sent(tokens_in, interleaved(other_half, pieces_in))
+            got["qkv"] = sum_sent(tokens_in, other)
             got["out"] = sum_sent(left_out, other_half(right_out, 1))
             gain_pack = pack + lax.ppermute(pack, "dp", swap)
             return got["qkv"], got["out"], gain_pack
         if step == 2:
             blocks["out"] = sum_kept(left_out, own_half(right_out, 1), got["out"])
-            blocks["qkv"] = sum_kept(after(tokens_in, blocks["out"][0]), interleaved(own_half, pieces_in), got["qkv"]
-            )
+            blocks["qkv"] = sum_kept(after(tokens_in, blocks["out"][0]), own, got["qkv"])
             if rows == 4:
                 gain_pack = pack + lax.ppermute(pack, "row", by_x)
             return
         gain_pack = pack + lax.ppermute(pack, "row", by_y) if rows == 4 else lax.psum(pack, "row")
 
-    input_own = sum_slots(
-        lambda slot, gate: times_transposed(after(slot_rows(grad_qkv, slot), gate), full_qkv).astype(BF16), input_window
-    )
+    input_own = sum_slots(input_work, input_window)
 
     results = {}
     quarter = local_width // 2
@@ -914,26 +955,26 @@
         return jnp.concatenate([pair[0], pair[1]], axis=1)
 
     def output_work(slot, rows_in):
-        held["output"] = (place_rows(slot_index[slot], rows_in, tokens_here, F32, held["output"]),)
+        held["o"] = (place_rows(slot_index[slot], rows_in, tokens_here, F32, held["o"]),)
         if slot == 3:
             results["down"] = jnp.transpose(both_cores(blocks["down"][1], 1))
             results["gate"] = both_cores(blocks["gate"][1], 1)
-            return held["output"], results["down"], results["gate"]
+            return held["o"], results["down"], results["gate"]
         if slot == 2:
             results["up"] = both_cores(blocks["up"][1], 1)
-            return held["output"], results["up"]
+            return held["o"], results["up"]
         if slot == 1:
             results["out"] = jnp.transpose(both_cores(blocks["out"][1], 1))
             results["qkv"] = [projection(index) for index in range(3)]
-            return held["output"], results["out"], results["qkv"]
-        return held["output"]
+            return held["o"], results["out"], results["qkv"]
+        return held["o"]
 
     gather_slots((own_grad_hidden + input_own).astype(BF16), output_work)
     ends = (local_width, 2 * local_width, 2 * local_width + width)
     gain_grads = jnp.split(gain_pack[0], ends)
     return (
         block_output,
-        held["output"][0],
+        held["o"][0],
         *results["qkv"],
         results["out"],
         results["gate"],

time: 996 us -> 1020 us (1.024)
    pallas_call x0 -> x1, Pallas kernels: none -> 13 us  [qkv_product(): pl.pallas_call(qkv_kernel, grid_spec=pltpu.PrefetchScalarGridSpec(num_sca...]
    dot_general x4 -> x8, matrix products: 14.8 us -> 20.7 us  [times_transposed(): lax.dot_general(left_mat, right_mat, (((1,), (1,)), ((), ())), preferred_...]
    ppermute x2 -> x3, waiting for transfers between devices: 27 us -> 25.6 us  [row_first(): lax.ppermute(half, 'row', by_x)]
  transfers between devices with their start and end apart: 80 -> 84, of which waited for: 35 -> 36; matrix products, arithmetic and copies ran while one was open for 17% -> 17% of each run, Pallas kernels for 24% -> 24%
where the time goes in v10:
time: 1020 us; the launch traced here: 1010 us
  waiting for transfers between devices  372 us (36%)
  Pallas kernels  286 us (28%)
  starting transfers between devices  119 us (12%)
  matrix products  84.3 us (8%)
  other arithmetic  60.5 us (6%)
  local copies, waits for them, and re-layouts  44.6 us (4%)
  blocking collectives  24.3 us (2%)
  between operations  16.3 us (2%)
    ppermute x15, waiting for transfers between devices, line_step(): lax.ppermute(from_right, 'col', [(i + 1, i) for i in range(cols - step)])  126 us
    pallas_call x4, Pallas kernels, forward_chunk(): pl.pallas_call(functools.partial(forward_chunk_kernel, out_steps=out_step...  93.2 us
    ppermute x9, waiting for transfers between devices, sum_step(): up = lax.ppermute(up, 'col', [(i, i + 1) for i in range(step)])  85 us
    pallas_call x4, Pallas kernels, backward_chunk(): pl.pallas_call(functools.partial(backward_chunk_kernel, tiles=tiles, choi...  80.2 us
    dot_general x10, matrix products, left_transposed(): lax.dot_general(left_mat, right_mat, (((0,), (0,)), ((), ())), preferred_...  63.6 us
    ppermute x15, waiting for transfers between devices, line_step(): lax.ppermute(from_left, 'col', [(i, i + 1) for i in range(step - 1, cols...  62.1 us
    ppermute x9, starting transfers between devices, sum_step(): up = lax.ppermute(up, 'col', [(i, i + 1) for i in range(step)])  42 us
    reduce_scatter x5, waiting for transfers between devices, sum_kept(): lax.psum_scatter(total, 'row', scatter_dimension=0, tiled=True)  30.6 us
  transfers between devices with their start and end apart: 84, of which 36 were waited for; matrix products, arithmetic and copies ran while one was open for 17% of the time, Pallas kernels for 24%

profile of v10, /device:TPU:0, one launch (start us, length us, event | category | flops | bytes accessed | tf_op | source)
XLA Modules:
  0.0 1007.5 jit_solution(10087033869291301948)
XLA Ops:
  18.9 12.3 %collective-permute-done = bf16[512,768]{1,0:T(8,128)(2,1)} collective-permute-done((bf16[512,768]{1,0:T(8,128)(2,1)}, bf16[512,768]{1,0:T(8,128)(2,1)}, u32[]{:S(2)}, u32[]{:S(2)}) %collective-permute-start) | collective-permute-done | bytes 786464 | tf_op jit(solution)/shard_map/ppermute | solution.py:746
  55.7 13.3 %collective-permute-done.11 = bf16[256,512]{1,0:T(8,128)(2,1)S(1)} collective-permute-done((bf16[256,512]{1,0:T(8,128)(2,1)S(1)}, bf16[256,512]{1,0:T(8,128)(2,1)S(1)}, u32[]{:S(2)}, u32[]{:S(2)}) %collective-permute-start.11) | collective-permute-done | bytes 262176 | tf_op jit(solution)/shard_map/ppermute | solution.py:746
  84.0 20.6 %collective-permute-done.16 = bf16[256,2048]{1,0:T(8,128)(2,1)S(1)} collective-permute-done((bf16[256,2048]{1,0:T(8,128)(2,1)}, bf16[256,2048]{1,0:T(8,128)(2,1)S(1)}, u32[]{:S(2)}, u32[]{:S(2)}) %collective-permute-start.16) | collective-permute-done | bytes 1048608 | tf_op jit(solution)/shard_map/ppermute | solution.py:668
  114.9 19.9 %collective-permute-done.19 = bf16[256,2048]{1,0:T(8,128)(2,1)} collective-permute-done((bf16[256,2048]{1,0:T(8,128)(2,1)S(1)}, bf16[256,2048]{1,0:T(8,128)(2,1)}, u32[]{:S(2)}, u32[]{:S(2)}) %collective-permute-start.19) | collective-permute-done | bytes 1048608 | tf_op jit(solution)/shard_map/ppermute | solution.py:669
  136.1 13.0 %qkv.1.q_ref.k_ref.v_ref = f32[1024,1536]{1,0:T(8,128)} custom-call(s32[3]{0:T(128)} %pad_add_fusion.idx_ref, bf16[1024,2048]{1,0:T(8,128)(2,1)} %x_ref.9, bf16[2048,768]{1,0:T(8,128)(2,1)} %bitcast.102, bf16[2048,768]{1,0:T(8,128)(2,1)} %bitcast.10.oth_ref), custom_call_target="tpu_custom_call" | custom-call | flops 6442450944 | bytes 41943040 | tf_op jit(solution)/shard_map/qkv/pallas_call | solution.py:230
  151.7 12.1 %all-reduce.1 = (f32[1024]{0:T(1024)S(1)}, f32[1024]{0:T(1024)S(1)}) all-reduce(f32[1024]{0:T(1024)S(1)} %get-tuple-element.390, f32[1024]{0:T(1024)S(1)} %get-tuple-element.389), channel_id=1, replica_groups=mesh['dp'=2,'row'=4,'col'=4] {'col'}, use_global_device_ids=true, to_apply=%region_1.2 | all-reduce | flops 2048 | bytes 16384 | tf_op jit(solution)/shard_map/psum | solution.py:808
  166.0 16.1 %attend_forward.1 = (bf16[1024,512]{1,0:T(8,128)(2,1)}, bf16[1024,512]{1,0:T(8,128)(2,1)}, bf16[1024,512]{1,0:T(8,128)(2,1)}, bf16[1024,512]{1,0:T(8,128)(2,1)}, f32[4,1024,1]{2,1,0:T(8,128)}) custom-call(f32[1024,1536]{1,0:T(8,128)} %qkv.1.q_ref.k_ref.v_ref, f32[1024,1536]{1,0:T(8,128)} %qkv.1.q_ref.k_ref.v_ref, f32[1024,1536]{1,0:T(8,128)} %qkv.1.q_ref.k_ref.v_ref, ...), custom_call_target="tpu_custom_call" | custom-call | flops 2147483648 | bytes 10485760 | tf_op jit(solution)/shard_map/attend_forward/pallas_call | solution.py:156
  222.6 24.5 %collective-permute-done.9.refs_5_ = bf16[1024,512]{1,0:T(8,128)(2,1)S(1)} collective-permute-done((bf16[1024,512]{1,0:T(8,128)(2,1)S(1)}, bf16[1024,512]{1,0:T(8,128)(2,1)S(1)}, u32[]{:S(2)}, u32[]{:S(2)}) %collective-permute-start.9) | collective-permute-done | bytes 1048608 | tf_op jit(solution)/shard_map/ppermute | solution.py:669
  249.8 23.9 %collective-permute-done.10.refs_6_ = bf16[1024,512]{1,0:T(8,128)(2,1)S(1)} collective-permute-done((bf16[1024,512]{1,0:T(8,128)(2,1)S(1)}, bf16[1024,512]{1,0:T(8,128)(2,1)S(1)}, u32[]{:S(2)}, u32[]{:S(2)}) %collective-permute-start.10) | collective-permute-done | bytes 1048608 | tf_op jit(solution)/shard_map/ppermute | solution.py:669
  275.0 23.2 %forward_chunk.4 = (bf16[1024,2048]{1,0:T(8,128)(2,1)}, f32[1024,1]{1,0:T(8,128)}, bf16[1024,2048]{1,0:T(8,128)(2,1)}, bf16[1024,2048]{1,0:T(8,128)(2,1)}, bf16[...) custom-call(s32[3]{0:T(128)} %get-tuple-element.459.idx_ref, ...), custom_call_target="tpu_custom_call" | custom-call | flops 8589934592 | bytes 33554432 | tf_op jit(solution)/shard_map/forward_chunk/pallas_call | solution.py:345
  300.7 23.4 %forward_chunk.5 = (bf16[1024,2048]{1,0:T(8,128)(2,1)}, f32[1024,1]{1,0:T(8,128)}, bf16[1024,2048]{1,0:T(8,128)(2,1)}, bf16[1024,2048]{1,0:T(8,128)(2,1)}, bf16[...) custom-call(s32[3]{0:T(128)} %get-tuple-element.460.idx_ref, ...), custom_call_target="tpu_custom_call", output_to_operand_aliasing={{0}: (16, {}), {1}: (17, {}), {2}: (18, {}), {3}: (19, {}),... | custom-call | flops 8589934592 | bytes 33554432 | tf_op jit(solution)/shard_map/forward_chunk/pallas_call | solution.py:345
  331.9 23.4 %forward_chunk.6 = (bf16[1024,2048]{1,0:T(8,128)(2,1)}, f32[1024,1]{1,0:T(8,128)}, bf16[1024,2048]{1,0:T(8,128)(2,1)}, bf16[1024,2048]{1,0:T(8,128)(2,1)}, bf16[...) custom-call(s32[3]{0:T(128)} %pad_add_fusion.1.idx_ref, ...), custom_call_target="tpu_custom_call", output_to_operand_aliasing={{0}: (16, {}), {1}: (17, {}), {2}: (18, {}), {3}: (19, {}),... | custom-call | flops 8589934592 | bytes 33554432 | tf_op jit(solution)/shard_map/forward_chunk/pallas_call | solution.py:345
  364.5 23.2 %forward_chunk.7 = (bf16[1024,2048]{1,0:T(8,128)(2,1)}, f32[1024,1]{1,0:T(8,128)}, bf16[1024,2048]{1,0:T(8,128)(2,1)}, bf16[1024,2048]{1,0:T(8,128)(2,1)}, bf16[...) custom-call(s32[3]{0:T(128)} %pad_add_fusion.idx_ref, ...), custom_call_target="tpu_custom_call", output_to_operand_aliasing={{0}: (16, {}), {1}: (17, {}), {2}: (18, {}), {3}: (19, {}),... | custom-call | flops 8589934592 | bytes 33554432 | tf_op jit(solution)/shard_map/forward_chunk/pallas_call | solution.py:345
  396.0 18.3 %collective-permute-done.33.refs_1_.refs_2_ = bf16[256,2048]{1,0:T(8,128)(2,1)S(1)} collective-permute-done((bf16[256,2048]{1,0:T(8,128)(2,1)S(1)}, bf16[256,2048]{1,0:T(8,128)(2,1)S(1)}, u32[]{:S(2)}, u32[]{:S(2)}) %collective-permute-start.33) | collective-permute-done | bytes 1048608 | tf_op jit(solution)/shard_map/ppermute | solution.py:668
  419.8 20.0 %backward_chunk.4 = (bf16[1024,2048]{1,0:T(8,128)(2,1)}, bf16[1024,2048]{1,0:T(8,128)(2,1)}, bf16[1024,2048]{1,0:T(8,128)(2,1)}, bf16[256,2048]{1,0:T(8,128)(2,1)}, f32[1,2048]{1,0:T(1,128)}) custom-call(s32[3]{0:T(128)} %pad_add_fusion.idx_ref, bf16[1024,2048]{1,0:T(8,128)(2,1)} %grad_ref.15, f32[1,2048]{1,0:T(1,128)} %bitcast.119, ...), custom_call_target="tpu_custom_call" | custom-call | flops 6442450944 | bytes 25165824 | tf_op jit(solution)/shard_map/backward_chunk/pallas_call | solution.py:443
  443.1 20.0 %backward_chunk.5 = (bf16[1024,2048]{1,0:T(8,128)(2,1)}, bf16[1024,2048]{1,0:T(8,128)(2,1)}, bf16[1024,2048]{1,0:T(8,128)(2,1)}, bf16[256,2048]{1,0:T(8,128)(2,1)}, f32[1,2048]{1,0:T(1,128)}) custom-call(s32[3]{0:T(128)} %pad_add_fusion.1.idx_ref, bf16[1024,2048]{1,0:T(8,128)(2,1)} %grad_ref.15, ...), custom_call_target="tpu_custom_call", output_to_operand_aliasing={{0}: (11, {}), {1}: (12, {}), {2}: (13, {})} | custom-call | flops 6442450944 | bytes 25165824 | tf_op jit(solution)/shard_map/backward_chunk/pallas_call | solution.py:443
  463.2 19.9 %backward_chunk.6 = (bf16[1024,2048]{1,0:T(8,128)(2,1)}, bf16[1024,2048]{1,0:T(8,128)(2,1)}, bf16[1024,2048]{1,0:T(8,128)(2,1)}, bf16[256,2048]{1,0:T(8,128)(2,1)}, f32[1,2048]{1,0:T(1,128)}) custom-call(s32[3]{0:T(128)} %get-tuple-element.460.idx_ref, bf16[1024,2048]{1,0:T(8,128)(2,1)} %grad_ref.15, ...), custom_call_target="tpu_custom_call", output_to_operand_aliasing={{0}: (13, {}), {1}: (14, {}), {2}: (15, {})} | custom-call | flops 6442450944 | bytes 25165824 | tf_op jit(solution)/shard_map/backward_chunk/pallas_call | solution.py:443
  484.5 20.3 %backward_chunk.7 = (bf16[1024,2048]{1,0:T(8,128)(2,1)}, bf16[1024,2048]{1,0:T(8,128)(2,1)}, bf16[1024,2048]{1,0:T(8,128)(2,1)}, bf16[256,2048]{1,0:T(8,128)(2,1)}, f32[1,2048]{1,0:T(1,128)}) custom-call(s32[3]{0:T(128)} %get-tuple-element.459.idx_ref, bf16[1024,2048]{1,0:T(8,128)(2,1)} %grad_ref.15, ...), custom_call_target="tpu_custom_call", output_to_operand_aliasing={{0}: (13, {}), {1}: (14, {}), {2}: (15, {})} | custom-call | flops 6442450944 | bytes 25165824 | tf_op jit(solution)/shard_map/backward_chunk/pallas_call | solution.py:443
  510.3 16.8 %collective-permute-done.39 = bf16[256,2048]{1,0:T(8,128)(2,1)S(1)} collective-permute-done((bf16[256,2048]{1,0:T(8,128)(2,1)}, bf16[256,2048]{1,0:T(8,128)(2,1)S(1)}, u32[]{:S(2)}, u32[]{:S(2)}) %collective-permute-start.39) | collective-permute-done | bytes 1048608 | tf_op jit(solution)/shard_map/ppermute | solution.py:673
  533.9 15.6 %collective-permute-done.40 = bf16[256,2048]{1,0:T(8,128)(2,1)S(1)} collective-permute-done((bf16[256,2048]{1,0:T(8,128)(2,1)S(1)}, bf16[256,2048]{1,0:T(8,128)(2,1)S(1)}, u32[]{:S(2)}, u32[]{:S(2)}) %collective-permute-start.40) | collective-permute-done | bytes 1048608 | tf_op jit(solution)/shard_map/ppermute | solution.py:673
  549.9 10.3 %collective-permute-start.41 = (bf16[256,2048]{1,0:T(8,128)(2,1)S(1)}, bf16[256,2048]{1,0:T(8,128)(2,1)S(1)}, u32[]{:S(2)}, u32[]{:S(2)}) collective-permute-start(bf16[256,2048]{1,0:T(8,128)(2,1)S(1)} %get-tuple-element.409), channel_id=1, source_target_pairs={{0,1},{1,2},{2,3},{4,5},{5,6},{6,7},{8,9},{9,10},{10,11},{12,13},{... | collective-permute-start | bytes 3145736 | tf_op jit(solution)/shard_map/ppermute | solution.py:673
  561.5 15.1 %collective-permute-done.41 = bf16[256,2048]{1,0:T(8,128)(2,1)S(1)} collective-permute-done((bf16[256,2048]{1,0:T(8,128)(2,1)S(1)}, bf16[256,2048]{1,0:T(8,128)(2,1)S(1)}, u32[]{:S(2)}, u32[]{:S(2)}) %collective-permute-start.41) | collective-permute-done | bytes 1048608 | tf_op jit(solution)/shard_map/ppermute | solution.py:673
  584.8 13.8 %collective-permute-done.45.refs_1_.refs_2_ = bf16[256,2048]{1,0:T(8,128)(2,1)S(1)} collective-permute-done((bf16[256,2048]{1,0:T(8,128)(2,1)S(1)}, bf16[256,2048]{1,0:T(8,128)(2,1)S(1)}, u32[]{:S(2)}, u32[]{:S(2)}) %collective-permute-start.45) | collective-permute-done | bytes 1048608 | tf_op jit(solution)/shard_map/ppermute | solution.py:668
  609.7 20.3 %collective-permute-done.48.refs_0_.refs_1_ = bf16[256,2048]{1,0:T(8,128)(2,1)} collective-permute-done((bf16[256,2048]{1,0:T(8,128)(2,1)}, bf16[256,2048]{1,0:T(8,128)(2,1)}, u32[]{:S(2)}, u32[]{:S(2)}) %collective-permute-start.48) | collective-permute-done | bytes 1048608 | tf_op jit(solution)/shard_map/ppermute | solution.py:669
  631.6 9.5 convolution_convert_fusion.2
  667.3 18.1 %attend_backward.1 = (f32[1024,512]{1,0:T(8,128)}, f32[1024,512]{1,0:T(8,128)}, bf16[1024,512]{1,0:T(8,128)(2,1)}, f32[1024,1]{1,0:T(8,128)}, f32[1024,1]{1,0:T(...) custom-call(f32[1024,1536]{1,0:T(8,128)} %qkv.1.q_ref.k_ref.v_ref, f32[1024,1536]{1,0:T(8,128)} %qkv.1.q_ref.k_ref.v_ref, ...), custom_call_target="tpu_custom_call" | custom-call | flops 5368709120 | bytes 20971520 | tf_op jit(solution)/shard_map/attend_backward/pallas_call | solution.py:180
  687.9 12.2 %all-reduce = (f32[1024]{0:T(1024)S(1)}, f32[1024]{0:T(1024)S(1)}) all-reduce(f32[1024]{0:T(1024)S(1)} %reduce.1, f32[1024]{0:T(1024)S(1)} %reduce), channel_id=1, replica_groups=mesh['dp'=2,'row'=4,'col'=4] {'col'}, use_global_device_ids=true, to_apply=%region_5.6 | all-reduce | flops 2048 | bytes 16384 | tf_op jit(solution)/shard_map/psum | solution.py:912
  720.0 14.3 %collective-permute-done.51 = bf16[256,2048]{1,0:T(8,128)(2,1)S(1)} collective-permute-done((bf16[256,2048]{1,0:T(8,128)(2,1)S(1)}, bf16[256,2048]{1,0:T(8,128)(2,1)S(1)}, u32[]{:S(2)}, u32[]{:S(2)}) %collective-permute-start.51) | collective-permute-done | bytes 1048608 | tf_op jit(solution)/shard_map/ppermute | solution.py:673
  738.7 10.6 %add_convert_fusion.2 = bf16[2048,1024]{1,0:T(8,128)(2,1)} fusion(bf16[2048,1024]{1,0:T(8,128)(2,1)} %collective-permute-done.63, bf16[1024,2048]{1,0:T(8,128)(2,1)} %get-tuple-element.318, bf16[1024,2048]{1,0:T(8,128)(2,1)} %get-tuple-element.319, s32[]{:T(128)S(6)} %select_n.242), kind=kOutput, calls=%fused_computation.2 | convolution fusion | flops 4301258752 | bytes 14680068 | tf_op jit(solution)/shard_map/dot_general | solution.py:35
  841.7 16.3 %collective-permute-done.55 = bf16[256,2048]{1,0:T(8,128)(2,1)S(1)} collective-permute-done((bf16[256,2048]{1,0:T(8,128)(2,1)S(1)}, bf16[256,2048]{1,0:T(8,128)(2,1)S(1)}, u32[]{:S(2)}, u32[]{:S(2)}) %collective-permute-start.55) | collective-permute-done | bytes 1048608 | tf_op jit(solution)/shard_map/ppermute | solution.py:673
  910.6 18.9 %collective-permute-done.61.refs_0_.refs_1_ = bf16[256,2048]{1,0:T(8,128)(2,1)S(1)} collective-permute-done((bf16[256,2048]{1,0:T(8,128)(2,1)}, bf16[256,2048]{1,0:T(8,128)(2,1)S(1)}, u32[]{:S(2)}, u32[]{:S(2)}) %collective-permute-start.61) | collective-permute-done | bytes 1048608 | tf_op jit(solution)/shard_map/ppermute | solution.py:669
  955.4 26.5 %reduce-scatter.14.cloned.1.call-done = bf16[512,768]{1,0:T(8,128)(2,1)} async-done(((bf16[2048,768]{1,0:T(8,128)(2,1)}), bf16[512,768]{1,0:T(8,128)(2,1)}) %reduce-scatter.14.cloned.1.call-update) | async-done | bytes 786448 | tf_op jit(solution)/shard_map/reduce_scatter | solution.py:738
  (409 shorter events, 425.3 us)
Async XLA Ops:
  7.2 266.6 %all-gather.2.cloned.1.call-start = ((), (), s32[]{:S(2)}) async-start(), calls=%async_computation.5 | async-start | bytes 18874368 | tf_op jit(solution)/shard_map/all_gather | solution.py:802
  45.8 853.7 %reduce-scatter.12.cloned.1.call-start = ((), (), s32[]{:S(2)}) async-start(), calls=%async_computation.9 | async-start | bytes 1310720 | tf_op jit(solution)/shard_map/reduce_scatter | solution.py:738
  53.8 82.3 %collective-permute-start.4 = (bf16[4,512,768]{2,1,0:T(8,128)(2,1)}, bf16[4,512,768]{2,1,0:T(8,128)(2,1)}, u32[]{:S(2)}, u32[]{:S(2)}) collective-permute-start(bf16[4,512,768]{2,1,0:T(8,128)(2,1)} %bitcast_dynamic-update-slice_fusion.8), channel_id=1, source_target_pairs={{0,16},{16,0},{1,17},{17,1},{2,18},{18,2},{3,19},{19,3},{4,20},{20... | collective-permute-start | bytes 9437192 | tf_op jit(solution)/shard_map/ppermute | solution.py:771
  111.6 81.7 %collective-permute-start.22 = (bf16[1024,512]{1,0:T(8,128)(2,1)S(1)}, bf16[1024,512]{1,0:T(8,128)(2,1)}, u32[]{:S(2)}, u32[]{:S(2)}) collective-permute-start(bf16[1024,512]{1,0:T(8,128)(2,1)S(1)} %constant_dynamic-slice_fusion.14), channel_id=1, source_target_pairs={{0,4},{4,0},{8,12},{12,8},{1,5},{5,1},{9,13},{13,9},{2,6},{6,2},{1... | collective-permute-start | bytes 3145736 | tf_op jit(solution)/shard_map/ppermute | solution.py:746
  112.6 80.7 %collective-permute-start.23 = (bf16[1024,512]{1,0:T(8,128)(2,1)S(1)}, bf16[1024,512]{1,0:T(8,128)(2,1)}, u32[]{:S(2)}, u32[]{:S(2)}) collective-permute-start(bf16[1024,512]{1,0:T(8,128)(2,1)S(1)} %constant_dynamic-slice_fusion.14), channel_id=1, source_target_pairs={{0,8},{8,0},{4,12},{12,4},{1,9},{9,1},{5,13},{13,5},{2,10},{10,2},... | collective-permute-start | bytes 3145736 | tf_op jit(solution)/shard_map/ppermute | solution.py:746
  113.2 70.6 %collective-permute-start.18 = (bf16[256,2048]{1,0:T(8,128)(2,1)}, bf16[256,2048]{1,0:T(8,128)(2,1)}, u32[]{:S(2)}, u32[]{:S(2)}) collective-permute-start(bf16[256,2048]{1,0:T(8,128)(2,1)} %collective-permute-done.17), channel_id=1, source_target_pairs={{2,3},{6,7},{10,11},{14,15},{18,19},{22,23},{26,27},{30,31}} | collective-permute-start | bytes 3145736 | tf_op jit(solution)/shard_map/ppermute | solution.py:668
  134.8 54.6 %collective-permute-start.20 = (bf16[256,2048]{1,0:T(8,128)(2,1)}, bf16[256,2048]{1,0:T(8,128)(2,1)}, u32[]{:S(2)}, u32[]{:S(2)}) collective-permute-start(bf16[256,2048]{1,0:T(8,128)(2,1)} %collective-permute-done.19), channel_id=1, source_target_pairs={{1,0},{5,4},{9,8},{13,12},{17,16},{21,20},{25,24},{29,28}} | collective-permute-start | bytes 3145736 | tf_op jit(solution)/shard_map/ppermute | solution.py:669
  193.3 80.4 %collective-permute-start.21 = (bf16[1024,2048]{1,0:T(8,128)(2,1)}, bf16[1024,2048]{1,0:T(8,128)(2,1)}, u32[]{:S(2)}, u32[]{:S(2)}) collective-permute-start(bf16[1024,2048]{1,0:T(8,128)(2,1)} %pad_maximum_fusion.refs_7_.wo_own_ref), channel_id=1, source_target_pairs={{0,16},{16,0},{1,17},{17,1},{2,18},{18,2},{3,19},{19,3},{4,20},{20... | collective-permute-start | bytes 12582920 | tf_op jit(solution)/shard_map/ppermute | solution.py:828
  219.7 54.1 %collective-permute-start.26 = (bf16[4,1024,512]{2,1,0:T(8,128)(2,1)}, bf16[4,1024,512]{2,1,0:T(8,128)(2,1)}, u32[]{:S(2)}, u32[]{:S(2)}) collective-permute-start(bf16[4,1024,512]{2,1,0:T(8,128)(2,1)} %bitcast_dynamic-update-slice_fusion.6.refs_13_.wd_own_ref), channel_id=1, source_target_pairs={{0,16},{16,0},{1,17},{17,1},{2,18},{18,2},{3,19},{19,3},{4,20},{20... | collective-permute-start | bytes 12582920 | tf_op jit(solution)/shard_map/ppermute | solution.py:771
  219.7 27.5 %collective-permute-start.9 = (bf16[1024,512]{1,0:T(8,128)(2,1)S(1)}, bf16[1024,512]{1,0:T(8,128)(2,1)S(1)}, u32[]{:S(2)}, u32[]{:S(2)}) collective-permute-start(bf16[1024,512]{1,0:T(8,128)(2,1)S(1)} %collective-permute-done.8.refs_4_), channel_id=1, source_target_pairs={{1,0},{2,1},{5,4},{6,5},{9,8},{10,9},{13,12},{14,13},{17,16},{18,1... | collective-permute-start | bytes 3145736 | tf_op jit(solution)/shard_map/ppermute | solution.py:669
  221.0 27.4 %collective-permute-start.6 = (bf16[1024,512]{1,0:T(8,128)(2,1)S(1)}, bf16[1024,512]{1,0:T(8,128)(2,1)}, u32[]{:S(2)}, u32[]{:S(2)}) collective-permute-start(bf16[1024,512]{1,0:T(8,128)(2,1)S(1)} %collective-permute-done.5.refs_1_), channel_id=1, source_target_pairs={{1,2},{2,3},{5,6},{6,7},{9,10},{10,11},{13,14},{14,15},{17,18},{18... | collective-permute-start | bytes 3145736 | tf_op jit(solution)/shard_map/ppermute | solution.py:668
  327.9 27.3 %collective-permute-start.29 = (bf16[256,2048]{1,0:T(8,128)(2,1)}, bf16[256,2048]{1,0:T(8,128)(2,1)S(1)}, u32[]{:S(2)}, u32[]{:S(2)}) collective-permute-start(bf16[256,2048]{1,0:T(8,128)(2,1)} %get-tuple-element.416), channel_id=1, source_target_pairs={{0,1},{1,2},{4,5},{5,6},{8,9},{9,10},{12,13},{13,14},{16,17},{17,1... | collective-permute-start | bytes 3145736 | tf_op jit(solution)/shard_map/ppermute | solution.py:673
  358.0 29.7 %collective-permute-start.31 = (bf16[256,2048]{1,0:T(8,128)(2,1)}, bf16[256,2048]{1,0:T(8,128)(2,1)S(1)}, u32[]{:S(2)}, u32[]{:S(2)}) collective-permute-start(bf16[256,2048]{1,0:T(8,128)(2,1)} %get-tuple-element.414), channel_id=1, source_target_pairs={{0,1},{1,2},{2,3},{4,5},{5,6},{6,7},{8,9},{9,10},{10,11},{12,13},{... | collective-permute-start | bytes 3145736 | tf_op jit(solution)/shard_map/ppermute | solution.py:673
  439.9 43.3 %collective-permute-start.37 = (bf16[256,2048]{1,0:T(8,128)(2,1)S(1)}, bf16[256,2048]{1,0:T(8,128)(2,1)S(1)}, u32[]{:S(2)}, u32[]{:S(2)}) collective-permute-start(bf16[256,2048]{1,0:T(8,128)(2,1)S(1)} %collective-permute-done.34.refs_3_.refs_2_), channel_id=1, source_target_pairs={{2,3},{6,7},{10,11},{14,15},{18,19},{22,23},{26,27},{30,31}} | collective-permute-start | bytes 3145736 | tf_op jit(solution)/shard_map/ppermute | solution.py:668
  441.7 41.4 %collective-permute-start.38 = (bf16[256,2048]{1,0:T(8,128)(2,1)}, bf16[256,2048]{1,0:T(8,128)(2,1)S(1)}, u32[]{:S(2)}, u32[]{:S(2)}) collective-permute-start(bf16[256,2048]{1,0:T(8,128)(2,1)} %collective-permute-done.36.refs_0_.refs_1_), channel_id=1, source_target_pairs={{1,0},{5,4},{9,8},{13,12},{17,16},{21,20},{25,24},{29,28}} | collective-permute-start | bytes 3145736 | tf_op jit(solution)/shard_map/ppermute | solution.py:669
  549.9 26.7 %collective-permute-start.41 = (bf16[256,2048]{1,0:T(8,128)(2,1)S(1)}, bf16[256,2048]{1,0:T(8,128)(2,1)S(1)}, u32[]{:S(2)}, u32[]{:S(2)}) collective-permute-start(bf16[256,2048]{1,0:T(8,128)(2,1)S(1)} %get-tuple-element.409), channel_id=1, source_target_pairs={{0,1},{1,2},{2,3},{4,5},{5,6},{6,7},{8,9},{9,10},{10,11},{12,13},{... | collective-permute-start | bytes 3145736 | tf_op jit(solution)/shard_map/ppermute | solution.py:673
  608.0 52.8 %collective-permute-start.49 = (bf16[256,2048]{1,0:T(8,128)(2,1)S(1)}, bf16[256,2048]{1,0:T(8,128)(2,1)}, u32[]{:S(2)}, u32[]{:S(2)}) collective-permute-start(bf16[256,2048]{1,0:T(8,128)(2,1)S(1)} %collective-permute-done.46.refs_3_.refs_2_), channel_id=1, source_target_pairs={{2,3},{6,7},{10,11},{14,15},{18,19},{22,23},{26,27},{30,31}} | collective-permute-start | bytes 3145736 | tf_op jit(solution)/shard_map/ppermute | solution.py:668
  629.9 30.8 %collective-permute-start.50 = (bf16[256,2048]{1,0:T(8,128)(2,1)}, bf16[256,2048]{1,0:T(8,128)(2,1)}, u32[]{:S(2)}, u32[]{:S(2)}) collective-permute-start(bf16[256,2048]{1,0:T(8,128)(2,1)} %collective-permute-done.48.refs_0_.refs_1_), channel_id=1, source_target_pairs={{1,0},{5,4},{9,8},{13,12},{17,16},{21,20},{25,24},{29,28}} | collective-permute-start | bytes 3145736 | tf_op jit(solution)/shard_map/ppermute | solution.py:669
  641.2 97.6 %collective-permute-start.63 = (bf16[2048,1024]{1,0:T(8,128)(2,1)}, bf16[2048,1024]{1,0:T(8,128)(2,1)}, u32[]{:S(2)}, u32[]{:S(2)}) collective-permute-start(bf16[2048,1024]{1,0:T(8,128)(2,1)} %convolution_convert_fusion.2), channel_id=1, source_target_pairs={{0,16},{16,0},{1,17},{17,1},{2,18},{18,2},{3,19},{19,3},{4,20},{20... | collective-permute-start | bytes 12582920 | tf_op jit(solution)/shard_map/ppermute | solution.py:734
  738.4 163.2 %reduce-scatter.6.cloned.1.call-start = ((), (), s32[]{:S(2)}) async-start(), calls=%async_computation.6 | async-start | bytes 5242880 | tf_op jit(solution)/shard_map/reduce_scatter | solution.py:738
  749.4 157.9 %reduce-scatter.8.cloned.1.call-start = ((), (), s32[]{:S(2)}) async-start(), calls=%async_computation.7 | async-start | bytes 5242880 | tf_op jit(solution)/shard_map/reduce_scatter | solution.py:738
  770.9 164.2 %reduce-scatter.10.cloned.1.call-start = ((), (), s32[]{:S(2)}) async-start(), calls=%async_computation.8 | async-start | bytes 5242880 | tf_op jit(solution)/shard_map/reduce_scatter | solution.py:738
  792.7 189.3 %reduce-scatter.14.cloned.1.call-start = ((), (), s32[]{:S(2)}) async-start(), calls=%async_computation.10 | async-start | bytes 3932160 | tf_op jit(solution)/shard_map/reduce_scatter | solution.py:738
  799.4 27.8 %collective-permute-start.53 = (bf16[256,2048]{1,0:T(8,128)(2,1)}, bf16[256,2048]{1,0:T(8,128)(2,1)}, u32[]{:S(2)}, u32[]{:S(2)}) collective-permute-start(bf16[256,2048]{1,0:T(8,128)(2,1)} %get-tuple-element.407), channel_id=1, source_target_pairs={{0,1},{1,2},{4,5},{5,6},{8,9},{9,10},{12,13},{13,14},{16,17},{17,1... | collective-permute-start | bytes 3145736 | tf_op jit(solution)/shard_map/ppermute | solution.py:673
  828.9 29.2 %collective-permute-start.55 = (bf16[256,2048]{1,0:T(8,128)(2,1)S(1)}, bf16[256,2048]{1,0:T(8,128)(2,1)S(1)}, u32[]{:S(2)}, u32[]{:S(2)}) collective-permute-start(bf16[256,2048]{1,0:T(8,128)(2,1)S(1)} %get-tuple-element.405), channel_id=1, source_target_pairs={{0,1},{1,2},{2,3},{4,5},{5,6},{6,7},{8,9},{9,10},{10,11},{12,13},{... | collective-permute-start | bytes 3145736 | tf_op jit(solution)/shard_map/ppermute | solution.py:673
  864.4 35.3 %collective-permute-start.57 = (bf16[256,2048]{1,0:T(8,128)(2,1)S(1)}, bf16[256,2048]{1,0:T(8,128)(2,1)}, u32[]{:S(2)}, u32[]{:S(2)}) collective-permute-start(bf16[256,2048]{1,0:T(8,128)(2,1)S(1)} %add_convert_fusion.4.refs_0_), channel_id=1, source_target_pairs={{0,1},{1,2},{2,3},{4,5},{5,6},{6,7},{8,9},{9,10},{10,11},{12,13},{... | collective-permute-start | bytes 3145736 | tf_op jit(solution)/shard_map/ppermute | solution.py:668
  867.6 32.8 %collective-permute-start.60 = (bf16[256,2048]{1,0:T(8,128)(2,1)S(1)}, bf16[256,2048]{1,0:T(8,128)(2,1)}, u32[]{:S(2)}, u32[]{:S(2)}) collective-permute-start(bf16[256,2048]{1,0:T(8,128)(2,1)S(1)} %add_convert_fusion.4.refs_0_), channel_id=1, source_target_pairs={{1,0},{2,1},{3,2},{5,4},{6,5},{7,6},{9,8},{10,9},{11,10},{13,12},{... | collective-permute-start | bytes 3145736 | tf_op jit(solution)/shard_map/ppermute | solution.py:669
  900.4 29.2 %collective-permute-start.61 = (bf16[256,2048]{1,0:T(8,128)(2,1)}, bf16[256,2048]{1,0:T(8,128)(2,1)S(1)}, u32[]{:S(2)}, u32[]{:S(2)}) collective-permute-start(bf16[256,2048]{1,0:T(8,128)(2,1)} %collective-permute-done.60.refs_0_.refs_1_), channel_id=1, source_target_pairs={{1,0},{2,1},{5,4},{6,5},{9,8},{10,9},{13,12},{14,13},{17,16},{18,1... | collective-permute-start | bytes 3145736 | tf_op jit(solution)/shard_map/ppermute | solution.py:669
  901.7 33.4 %collective-permute-start.64 = (bf16[512,1024]{1,0:T(8,128)(2,1)}, bf16[512,1024]{1,0:T(8,128)(2,1)}, u32[]{:S(2)}, u32[]{:S(2)}) collective-permute-start(bf16[512,1024]{1,0:T(8,128)(2,1)} %reduce-scatter.6.cloned.1.call-done), channel_id=1, source_target_pairs={{0,16},{16,0},{1,17},{17,1},{2,18},{18,2},{3,19},{19,3},{4,20},{20... | collective-permute-start | bytes 3145736 | tf_op jit(solution)/shard_map/ppermute | solution.py:728
  907.3 37.4 %collective-permute-start.66 = (bf16[512,1024]{1,0:T(8,128)(2,1)}, bf16[512,1024]{1,0:T(8,128)(2,1)}, u32[]{:S(2)}, u32[]{:S(2)}) collective-permute-start(bf16[512,1024]{1,0:T(8,128)(2,1)} %reduce-scatter.8.cloned.1.call-done), channel_id=1, source_target_pairs={{0,16},{16,0},{1,17},{17,1},{2,18},{18,2},{3,19},{19,3},{4,20},{20... | collective-permute-start | bytes 3145736 | tf_op jit(solution)/shard_map/ppermute | solution.py:728
  908.9 87.6 %collective-permute-start.59 = (bf16[256,2048]{1,0:T(8,128)(2,1)S(1)}, bf16[256,2048]{1,0:T(8,128)(2,1)}, u32[]{:S(2)}, u32[]{:S(2)}) collective-permute-start(bf16[256,2048]{1,0:T(8,128)(2,1)S(1)} %collective-permute-done.58.refs_3_.refs_2_), channel_id=1, source_target_pairs={{2,3},{6,7},{10,11},{14,15},{18,19},{22,23},{26,27},{30,31}} | collective-permute-start | bytes 3145736 | tf_op jit(solution)/shard_map/ppermute | solution.py:668
  929.5 66.9 %collective-permute-start.62 = (bf16[256,2048]{1,0:T(8,128)(2,1)S(1)}, bf16[256,2048]{1,0:T(8,128)(2,1)}, u32[]{:S(2)}, u32[]{:S(2)}) collective-permute-start(bf16[256,2048]{1,0:T(8,128)(2,1)S(1)} %collective-permute-done.61.refs_0_.refs_1_), channel_id=1, source_target_pairs={{1,0},{5,4},{9,8},{13,12},{17,16},{21,20},{25,24},{29,28}} | collective-permute-start | bytes 3145736 | tf_op jit(solution)/shard_map/ppermute | solution.py:669
  (116 other events, 2087.9 us)
Sparse Core Ops, SparseCore 0:
  45.9 119.9 all-gather.1
  738.6 27.8 reduce-scatter.11
  770.0 52.5 reduce-scatter.5
  826.0 53.0 reduce-scatter.7
  882.5 52.5 reduce-scatter.9
  938.0 43.9 reduce-scatter.13

commit v11 on v9

--- a/solution.py
+++ b/solution.py
@@ -469,8 +469,8 @@
 
 def attention_chunk(index, mlp_rows, grad_output, raw, scale, gain, out_halves, half, chunk, before):
     tokens, width = grad_output.shape
-    size = chunk // PARTS
-    rows = pl.BlockSpec((size, width), lambda j, idx: (PARTS * idx[0] + j, 0))
+    size = chunk
+    rows = pl.BlockSpec((size, width), lambda j, idx: (idx[0], 0))
     gain_row = pl.BlockSpec((1, width), lambda j, idx: (0, 0))
     own_heads = pl.BlockSpec((half, width), lambda j, idx: (0, 0))
     before = tuple(before)
@@ -478,12 +478,12 @@
         functools.partial(attention_chunk_kernel, choices=len(mlp_rows)),
         grid_spec=pltpu.PrefetchScalarGridSpec(
             num_scalar_prefetch=1,
-            grid=(PARTS,),
+            grid=(1,),
             in_specs=[
-                rows, rows, pl.BlockSpec((size, 1), lambda j, idx: (PARTS * idx[0] + j, 0)), gain_row,
+                rows, rows, pl.BlockSpec((size, 1), lambda j, idx: (idx[0], 0)), gain_row,
                 own_heads, own_heads,
             ] + [pl.BlockSpec(memory_space=pl.ANY)] * (len(mlp_rows) + len(before)),
-            out_specs=[rows, pl.BlockSpec((size, 2 * half), lambda j, idx: (PARTS * idx[0] + j, 0)), gain_row],
+            out_specs=[rows, pl.BlockSpec((size, 2 * half), lambda j, idx: (idx[0], 0)), gain_row],
             scratch_shapes=[pltpu.VMEM((chunk, width), BF16), pltpu.SemaphoreType.DMA(())],
         ),
         out_shape=[
@@ -793,19 +793,19 @@
             down_halves = row_blocks(down_pieces)
     attended_all = (attended, *lefts[1:], *rights[1:])
 
-    held = dict(forward=(), backward=(), attention=(), output=(), block_output=())
+    held = dict(f=(), b=(), a=(), o=(), m=())
     gain_sums = dict(mlp=0.0, attn=0.0)
 
     def forward_work(slot, gate):
         results = forward_chunk(
             slot_index[slot], after(attended_all, gate), out_halves, block_input, attn_row, full_gate_up,
-            down_halves, chunk, held["forward"],
+            down_halves, chunk, held["f"],
         )
-        held["forward"] = results[:6]
+        held["f"] = results[:6]
         return results[6]
 
     down_own = sum_slots(forward_work).astype(BF16)
-    attn_raw, attn_scale, hidden_b, gate_proj, up_proj, mixed_act = held["forward"]
+    attn_raw, attn_scale, hidden_b, gate_proj, up_proj, mixed_act = held["f"]
     mlp_parts = [None] * cols
     down_slots = [None] * cols
 
@@ -813,15 +813,15 @@
         down_slots[slot] = down_rows
         results = backward_chunk(
             slot_index[slot], down_rows, grad_output, mlp_row, gate_proj, up_proj, full_gate_up,
-            down_halves, chunk, held["backward"],
+            down_halves, chunk, held["b"],
         )
-        held["backward"] = results[:3]
+        held["b"] = results[:3]
         mlp_parts[slot] = results[3]
         gain_sums["mlp"] = gain_sums["mlp"] + results[4]
         return results[3]
 
     gather_slots(down_own, backward_work)
-    grad_down_in, grad_gate_in, grad_up_in = held["backward"]
+    grad_down_in, grad_gate_in, grad_up_in = held["b"]
 
     blocks = {}
     got = {}
@@ -846,9 +846,9 @@
     def attention_work(slot, mlp_rows):
         results = attention_chunk(
             slot_index[slot], mlp_rows, grad_output, attn_raw, attn_scale, attn_row, out_halves, half_width,
-            chunk, held["attention"],
+            chunk, held["a"],
         )
-        held["attention"] = results[:2]
+        held["a"] = results[:2]
         gain_sums["attn"] = gain_sums["attn"] + results[2]
         if slot == 3:
             hidden_left, up_right = after((hidden_b, grad_up_in), mlp_rows[0])
@@ -856,14 +856,14 @@
         for other in {2: (3, 2), 1: (1, 0)}.get(slot, ()):
             output = output_chunk(
                 slot_index[other], down_slots[other], after(attn_raw, mlp_rows), attn_scale, block_input, attn_row,
-                mlp_row, chunk, held["block_output"],
+                mlp_row, chunk, held["m"],
             )
-            held["block_output"] = (output,)
+            held["m"] = (output,)
         return results[1]
 
     gather_slots(mlp_own, attention_work)
-    grad_attn_in, grad_att = held["attention"]
-    (block_output,) = held["block_output"]
+    grad_attn_in, grad_att = held["a"]
+    (block_output,) = held["m"]
     own_grad_hidden = slot_rows(grad_output, 3).astype(F32) + mlp_own.astype(F32)
 
     query_dz, key_dz, grad_value_in, query_dot, key_dot, grad_query_gain, grad_key_gain = attend_backward(
@@ -871,12 +871,20 @@
         (query_rot, key_rot, value_heads, attended, log_total), grad_att, heads,
     )
     query_dot, key_dot = lax.psum((query_dot[:, 0], key_dot[:, 0]), "col")
-    grad_query_in = (
-        query_scale * (query_dz - query_raw * query_scale * (query_dot / width)[:, None])
-    ).astype(BF16)
-    grad_key_in = (
-        key_scale * (key_dz - key_raw * key_scale * (key_dot / width)[:, None])
-    ).astype(BF16)
+
+    def qkv_grads(pick_rows):
+        pieces = []
+        for grad, raw, scale, dot in (
+            (query_dz, query_raw, query_scale, query_dot), (key_dz, key_raw, key_scale, key_dot),
+        ):
+            grad, raw, scale, dot = (pick_rows(one) for one in (grad, raw, scale, (dot / width)[:, None]))
+            pieces.append((scale * (grad - raw * scale * dot)).astype(BF16))
+        return (*pieces, pick_rows(grad_value_in))
+
+    first_rows = jnp.concatenate(qkv_grads(lambda one: slot_rows(one, 0)), axis=1)
+    first_part = times_transposed(first_rows, full_qkv).astype(BF16)
+    query_dz, key_dz = after((query_dz, key_dz), first_part)
+    grad_query_in, grad_key_in, grad_value_in = qkv_grads(lambda one: one)
     grad_qkv = jnp.concatenate([grad_query_in, grad_key_in, grad_value_in], axis=1)
     gain_pack = jnp.concatenate([grad_query_gain, grad_key_gain, gain_sums["attn"], gain_sums["mlp"]], axis=1)
 
@@ -902,9 +910,12 @@
             return
         gain_pack = pack + lax.ppermute(pack, "row", by_y) if rows == 4 else lax.psum(pack, "row")
 
-    input_own = sum_slots(
-        lambda slot, gate: times_transposed(after(slot_rows(grad_qkv, slot), gate), full_qkv).astype(BF16), input_window
-    )
+    def input_work(slot, gate):
+        if slot == 0:
+            return first_part
+        return times_transposed(after(slot_rows(grad_qkv, slot), gate), full_qkv).astype(BF16)
+
+    input_own = sum_slots(input_work, input_window)
 
     results = {}
     quarter = local_width // 2
@@ -914,26 +925,26 @@
         return jnp.concatenate([pair[0], pair[1]], axis=1)
 
     def output_work(slot, rows_in):
-        held["output"] = (place_rows(slot_index[slot], rows_in, tokens_here, F32, held["output"]),)
+        held["o"] = (place_rows(slot_index[slot], rows_in, tokens_here, F32, held["o"]),)
         if slot == 3:
             results["down"] = jnp.transpose(both_cores(blocks["down"][1], 1))
             results["gate"] = both_cores(blocks["gate"][1], 1)
-            return held["output"], results["down"], results["gate"]
+            return held["o"], results["down"], results["gate"]
         if slot == 2:
             results["up"] = both_cores(blocks["up"][1], 1)
-            return held["output"], results["up"]
+            return held["o"], results["up"]
         if slot == 1:
             results["out"] = jnp.transpose(both_cores(blocks["out"][1], 1))
             results["qkv"] = [projection(index) for index in range(3)]
-            return held["output"], results["out"], results["qkv"]
-        return held["output"]
+            return held["o"], results["out"], results["qkv"]
+        return held["o"]
 
     gather_slots((own_grad_hidden + input_own).astype(BF16), output_work)
     ends = (local_width, 2 * local_width, 2 * local_width + width)
     gain_grads = jnp.split(gain_pack[0], ends)
     return (
         block_output,
-        held["output"][0],
+        held["o"][0],
         *results["qkv"],
         results["out"],
         results["gate"],

time: 996 us -> 989 us (level)
  transfers between devices with their start and end apart: 80 -> 80, of which waited for: 35 -> 35; matrix products, arithmetic and copies ran while one was open for 17% -> 17% of each run, Pallas kernels for 24% -> 23%
where the time goes in v11:
time: 989 us; the launch traced here: 978 us
  waiting for transfers between devices  363 us (37%)
  Pallas kernels  273 us (28%)
  starting transfers between devices  112 us (11%)
  matrix products  90.9 us (9%)
  other arithmetic  63.2 us (6%)
  local copies, waits for them, and re-layouts  35.1 us (4%)
  blocking collectives  24.1 us (2%)
  between operations  16.2 us (2%)
    ppermute x15, waiting for transfers between devices, line_step(): lax.ppermute(from_right, 'col', [(i + 1, i) for i in range(cols - step)])  127 us
    pallas_call x4, Pallas kernels, forward_chunk(): pl.pallas_call(functools.partial(forward_chunk_kernel, out_steps=out_step...  93.1 us
    ppermute x9, waiting for transfers between devices, sum_step(): up = lax.ppermute(up, 'col', [(i, i + 1) for i in range(step)])  86.4 us
    pallas_call x4, Pallas kernels, backward_chunk(): pl.pallas_call(functools.partial(backward_chunk_kernel, tiles=tiles, choi...  80.2 us
    dot_general x10, matrix products, left_transposed(): lax.dot_general(left_mat, right_mat, (((0,), (0,)), ((), ())), preferred_...  63.1 us
    ppermute x15, waiting for transfers between devices, line_step(): lax.ppermute(from_left, 'col', [(i, i + 1) for i in range(step - 1, cols...  52.5 us
    ppermute x9, starting transfers between devices, sum_step(): up = lax.ppermute(up, 'col', [(i, i + 1) for i in range(step)])  38.4 us
    reduce_scatter x5, waiting for transfers between devices, sum_kept(): lax.psum_scatter(total, 'row', scatter_dimension=0, tiled=True)  31.3 us
  transfers between devices with their start and end apart: 80, of which 35 were waited for; matrix products, arithmetic and copies ran while one was open for 17% of the time, Pallas kernels for 23%

profile of v11, /device:TPU:0, one launch (start us, length us, event | category | flops | bytes accessed | tf_op | source)
XLA Modules:
  0.0 978.1 jit_solution(2292786477880380860)
XLA Ops:
  40.8 16.8 %collective-permute-done.11 = bf16[256,2048]{1,0:T(8,128)(2,1)} collective-permute-done((bf16[256,2048]{1,0:T(8,128)(2,1)}, bf16[256,2048]{1,0:T(8,128)(2,1)}, u32[]{:S(2)}, u32[]{:S(2)}) %collective-permute-start.11) | collective-permute-done | bytes 1048608 | tf_op jit(solution)/shard_map/ppermute | solution.py:635
  70.2 16.0 %collective-permute-done.14 = bf16[256,2048]{1,0:T(8,128)(2,1)} collective-permute-done((bf16[256,2048]{1,0:T(8,128)(2,1)}, bf16[256,2048]{1,0:T(8,128)(2,1)}, u32[]{:S(2)}, u32[]{:S(2)}) %collective-permute-start.14) | collective-permute-done | bytes 1048608 | tf_op jit(solution)/shard_map/ppermute | solution.py:636
  87.5 10.0 %convolution_bitcast_fusion.q_ref.k_ref.v_ref = f32[1024,1536]{1,0:T(8,128)S(1)} fusion(bf16[1024,2048]{1,0:T(8,128)(2,1)} %x_ref.7, bf16[2048,1536]{1,0:T(8,128)(2,1)} %all-gather.3.cloned.1.call-done), kind=kOutput, calls=%fused_computation.4 | convolution fusion | flops 6442450944 | bytes 16777216 | tf_op jit(solution)/shard_map/dot_general | solution.py:25
  101.5 12.0 %all-reduce.1 = (f32[1024]{0:T(1024)S(1)}, f32[1024]{0:T(1024)S(1)}) all-reduce(f32[1024]{0:T(1024)S(1)} %get-tuple-element.384, f32[1024]{0:T(1024)S(1)} %get-tuple-element.383), channel_id=1, replica_groups=mesh['dp'=2,'row'=4,'col'=4] {'col'}, use_global_device_ids=true, to_apply=%region_1.2 | all-reduce | flops 2048 | bytes 16384 | tf_op jit(solution)/shard_map/psum | solution.py:767
  115.6 16.2 %attend_forward.1 = (bf16[1024,512]{1,0:T(8,128)(2,1)}, bf16[1024,512]{1,0:T(8,128)(2,1)}, bf16[1024,512]{1,0:T(8,128)(2,1)}, bf16[1024,512]{1,0:T(8,128)(2,1)}, f32[4,1024,1]{2,1,0:T(8,128)}) custom-call(f32[1024,1536]{1,0:T(8,128)} %copy-done.3, f32[1024,1536]{1,0:T(8,128)} %copy-done.3, f32[1024,1536]{1,0:T(8,128)} %copy-done.3, f32[1024,1]{1,0:T(8,128)} %copy.71.qs_ref, ...), custom_call_target="tpu_custom_call" | custom-call | flops 2147483648 | bytes 10485760 | tf_op jit(solution)/shard_map/attend_forward/pallas_call | solution.py:156
  152.6 21.7 %collective-permute-done.17 = bf16[1024,512]{1,0:T(8,128)(2,1)} collective-permute-done((bf16[1024,512]{1,0:T(8,128)(2,1)S(1)}, bf16[1024,512]{1,0:T(8,128)(2,1)}, u32[]{:S(2)}, u32[]{:S(2)}) %collective-permute-start.17) | collective-permute-done | bytes 1048608 | tf_op jit(solution)/shard_map/ppermute | solution.py:713
  192.8 27.7 %collective-permute-done.4.refs_5_ = bf16[1024,512]{1,0:T(8,128)(2,1)} collective-permute-done((bf16[1024,512]{1,0:T(8,128)(2,1)S(1)}, bf16[1024,512]{1,0:T(8,128)(2,1)}, u32[]{:S(2)}, u32[]{:S(2)}) %collective-permute-start.4) | collective-permute-done | bytes 1048608 | tf_op jit(solution)/shard_map/ppermute | solution.py:636
  222.5 24.8 %collective-permute-done.5.refs_6_ = bf16[1024,512]{1,0:T(8,128)(2,1)S(1)} collective-permute-done((bf16[1024,512]{1,0:T(8,128)(2,1)}, bf16[1024,512]{1,0:T(8,128)(2,1)S(1)}, u32[]{:S(2)}, u32[]{:S(2)}) %collective-permute-start.5) | collective-permute-done | bytes 1048608 | tf_op jit(solution)/shard_map/ppermute | solution.py:636
  248.3 23.2 %forward_chunk.4 = (bf16[1024,2048]{1,0:T(8,128)(2,1)}, f32[1024,1]{1,0:T(8,128)}, bf16[1024,2048]{1,0:T(8,128)(2,1)}, bf16[1024,2048]{1,0:T(8,128)(2,1)}, bf16[...) custom-call(s32[3]{0:T(128)} %get-tuple-element.445.idx_ref, ...), custom_call_target="tpu_custom_call" | custom-call | flops 8589934592 | bytes 33554432 | tf_op jit(solution)/shard_map/forward_chunk/pallas_call | solution.py:309
  274.1 23.3 %forward_chunk.5 = (bf16[1024,2048]{1,0:T(8,128)(2,1)}, f32[1024,1]{1,0:T(8,128)}, bf16[1024,2048]{1,0:T(8,128)(2,1)}, bf16[1024,2048]{1,0:T(8,128)(2,1)}, bf16[...) custom-call(s32[3]{0:T(128)} %get-tuple-element.446.idx_ref, ...), custom_call_target="tpu_custom_call", output_to_operand_aliasing={{0}: (16, {}), {1}: (17, {}), {2}: (18, {}), {3}: (19, {}),... | custom-call | flops 8589934592 | bytes 33554432 | tf_op jit(solution)/shard_map/forward_chunk/pallas_call | solution.py:309
  305.1 23.4 %forward_chunk.6 = (bf16[1024,2048]{1,0:T(8,128)(2,1)}, f32[1024,1]{1,0:T(8,128)}, bf16[1024,2048]{1,0:T(8,128)(2,1)}, bf16[1024,2048]{1,0:T(8,128)(2,1)}, bf16[...) custom-call(s32[3]{0:T(128)} %pad_add_fusion.1.idx_ref, ...), custom_call_target="tpu_custom_call", output_to_operand_aliasing={{0}: (16, {}), {1}: (17, {}), {2}: (18, {}), {3}: (19, {}),... | custom-call | flops 8589934592 | bytes 33554432 | tf_op jit(solution)/shard_map/forward_chunk/pallas_call | solution.py:309
  335.6 23.2 %forward_chunk.7 = (bf16[1024,2048]{1,0:T(8,128)(2,1)}, f32[1024,1]{1,0:T(8,128)}, bf16[1024,2048]{1,0:T(8,128)(2,1)}, bf16[1024,2048]{1,0:T(8,128)(2,1)}, bf16[...) custom-call(s32[3]{0:T(128)} %pad_add_fusion.idx_ref, ...), custom_call_target="tpu_custom_call", output_to_operand_aliasing={{0}: (16, {}), {1}: (17, {}), {2}: (18, {}), {3}: (19, {}),... | custom-call | flops 8589934592 | bytes 33554432 | tf_op jit(solution)/shard_map/forward_chunk/pallas_call | solution.py:309
  367.1 18.7 %collective-permute-done.28.refs_1_.refs_2_ = bf16[256,2048]{1,0:T(8,128)(2,1)S(1)} collective-permute-done((bf16[256,2048]{1,0:T(8,128)(2,1)S(1)}, bf16[256,2048]{1,0:T(8,128)(2,1)S(1)}, u32[]{:S(2)}, u32[]{:S(2)}) %collective-permute-start.28) | collective-permute-done | bytes 1048608 | tf_op jit(solution)/shard_map/ppermute | solution.py:635
  391.3 20.0 %backward_chunk.4 = (bf16[1024,2048]{1,0:T(8,128)(2,1)}, bf16[1024,2048]{1,0:T(8,128)(2,1)}, bf16[1024,2048]{1,0:T(8,128)(2,1)}, bf16[256,2048]{1,0:T(8,128)(2,1)}, f32[1,2048]{1,0:T(1,128)}) custom-call(s32[3]{0:T(128)} %pad_add_fusion.idx_ref, bf16[1024,2048]{1,0:T(8,128)(2,1)} %grad_ref.15, f32[1,2048]{1,0:T(1,128)} %bitcast.95, ...), custom_call_target="tpu_custom_call" | custom-call | flops 6442450944 | bytes 25165824 | tf_op jit(solution)/shard_map/backward_chunk/pallas_call | solution.py:407
  414.9 19.9 %backward_chunk.5 = (bf16[1024,2048]{1,0:T(8,128)(2,1)}, bf16[1024,2048]{1,0:T(8,128)(2,1)}, bf16[1024,2048]{1,0:T(8,128)(2,1)}, bf16[256,2048]{1,0:T(8,128)(2,1)}, f32[1,2048]{1,0:T(1,128)}) custom-call(s32[3]{0:T(128)} %pad_add_fusion.1.idx_ref, bf16[1024,2048]{1,0:T(8,128)(2,1)} %grad_ref.15, ...), custom_call_target="tpu_custom_call", output_to_operand_aliasing={{0}: (11, {}), {1}: (12, {}), {2}: (13, {})} | custom-call | flops 6442450944 | bytes 25165824 | tf_op jit(solution)/shard_map/backward_chunk/pallas_call | solution.py:407
  434.8 20.0 %backward_chunk.6 = (bf16[1024,2048]{1,0:T(8,128)(2,1)}, bf16[1024,2048]{1,0:T(8,128)(2,1)}, bf16[1024,2048]{1,0:T(8,128)(2,1)}, bf16[256,2048]{1,0:T(8,128)(2,1)}, f32[1,2048]{1,0:T(1,128)}) custom-call(s32[3]{0:T(128)} %get-tuple-element.446.idx_ref, bf16[1024,2048]{1,0:T(8,128)(2,1)} %grad_ref.15, ...), custom_call_target="tpu_custom_call", output_to_operand_aliasing={{0}: (13, {}), {1}: (14, {}), {2}: (15, {})} | custom-call | flops 6442450944 | bytes 25165824 | tf_op jit(solution)/shard_map/backward_chunk/pallas_call | solution.py:407
  456.2 20.3 %backward_chunk.7 = (bf16[1024,2048]{1,0:T(8,128)(2,1)}, bf16[1024,2048]{1,0:T(8,128)(2,1)}, bf16[1024,2048]{1,0:T(8,128)(2,1)}, bf16[256,2048]{1,0:T(8,128)(2,1)}, f32[1,2048]{1,0:T(1,128)}) custom-call(s32[3]{0:T(128)} %get-tuple-element.445.idx_ref, bf16[1024,2048]{1,0:T(8,128)(2,1)} %grad_ref.15, ...), custom_call_target="tpu_custom_call", output_to_operand_aliasing={{0}: (13, {}), {1}: (14, {}), {2}: (15, {})} | custom-call | flops 6442450944 | bytes 25165824 | tf_op jit(solution)/shard_map/backward_chunk/pallas_call | solution.py:407
  482.1 17.3 %collective-permute-done.34 = bf16[256,2048]{1,0:T(8,128)(2,1)S(1)} collective-permute-done((bf16[256,2048]{1,0:T(8,128)(2,1)}, bf16[256,2048]{1,0:T(8,128)(2,1)S(1)}, u32[]{:S(2)}, u32[]{:S(2)}) %collective-permute-start.34) | collective-permute-done | bytes 1048608 | tf_op jit(solution)/shard_map/ppermute | solution.py:640
  506.2 16.1 %collective-permute-done.35 = bf16[256,2048]{1,0:T(8,128)(2,1)S(1)} collective-permute-done((bf16[256,2048]{1,0:T(8,128)(2,1)S(1)}, bf16[256,2048]{1,0:T(8,128)(2,1)S(1)}, u32[]{:S(2)}, u32[]{:S(2)}) %collective-permute-start.35) | collective-permute-done | bytes 1048608 | tf_op jit(solution)/shard_map/ppermute | solution.py:640
  522.7 9.6 collective-permute-start.36
  533.6 15.1 %collective-permute-done.36 = bf16[256,2048]{1,0:T(8,128)(2,1)S(1)} collective-permute-done((bf16[256,2048]{1,0:T(8,128)(2,1)S(1)}, bf16[256,2048]{1,0:T(8,128)(2,1)S(1)}, u32[]{:S(2)}, u32[]{:S(2)}) %collective-permute-start.36) | collective-permute-done | bytes 1048608 | tf_op jit(solution)/shard_map/ppermute | solution.py:640
  556.9 14.1 %collective-permute-done.40.refs_1_.refs_2_ = bf16[256,2048]{1,0:T(8,128)(2,1)S(1)} collective-permute-done((bf16[256,2048]{1,0:T(8,128)(2,1)S(1)}, bf16[256,2048]{1,0:T(8,128)(2,1)S(1)}, u32[]{:S(2)}, u32[]{:S(2)}) %collective-permute-start.40) | collective-permute-done | bytes 1048608 | tf_op jit(solution)/shard_map/ppermute | solution.py:635
  582.0 20.1 %collective-permute-done.43.refs_0_.refs_1_ = bf16[256,2048]{1,0:T(8,128)(2,1)} collective-permute-done((bf16[256,2048]{1,0:T(8,128)(2,1)}, bf16[256,2048]{1,0:T(8,128)(2,1)}, u32[]{:S(2)}, u32[]{:S(2)}) %collective-permute-start.43) | collective-permute-done | bytes 1048608 | tf_op jit(solution)/shard_map/ppermute | solution.py:636
  603.7 9.5 convolution_convert_fusion.2
  639.3 18.1 %attend_backward.1 = (f32[1024,512]{1,0:T(8,128)}, f32[1024,512]{1,0:T(8,128)}, bf16[1024,512]{1,0:T(8,128)(2,1)}, f32[1024,1]{1,0:T(8,128)}, f32[1024,1]{1,0:T(...) custom-call(f32[1024,1536]{1,0:T(8,128)} %copy-done.3, f32[1024,1536]{1,0:T(8,128)} %copy-done.3, f32[1024,1]{1,0:T(8,128)} %copy.71.qs_ref, ...), custom_call_target="tpu_custom_call" | custom-call | flops 5368709120 | bytes 20971520 | tf_op jit(solution)/shard_map/attend_backward/pallas_call | solution.py:180
  659.9 12.1 %all-reduce = (f32[1024]{0:T(1024)S(1)}, f32[1024]{0:T(1024)S(1)}) all-reduce(f32[1024]{0:T(1024)S(1)} %reduce.1, f32[1024]{0:T(1024)S(1)} %reduce), channel_id=1, replica_groups=mesh['dp'=2,'row'=4,'col'=4] {'col'}, use_global_device_ids=true, to_apply=%region_5.6 | all-reduce | flops 2048 | bytes 16384 | tf_op jit(solution)/shard_map/psum | solution.py:873
  690.9 12.4 %collective-permute-done.46 = bf16[256,2048]{1,0:T(8,128)(2,1)S(1)} collective-permute-done((bf16[256,2048]{1,0:T(8,128)(2,1)S(1)}, bf16[256,2048]{1,0:T(8,128)(2,1)S(1)}, u32[]{:S(2)}, u32[]{:S(2)}) %collective-permute-start.46) | collective-permute-done | bytes 1048608 | tf_op jit(solution)/shard_map/ppermute | solution.py:640
  709.5 10.6 %add_convert_fusion.2 = bf16[2048,1024]{1,0:T(8,128)(2,1)} fusion(bf16[2048,1024]{1,0:T(8,128)(2,1)} %collective-permute-done.58, bf16[1024,2048]{1,0:T(8,128)(2,1)} %get-tuple-element.308, bf16[1024,2048]{1,0:T(8,128)(2,1)} %get-tuple-element.309, s32[]{:T(128)S(6)} %select_n.235), kind=kOutput, calls=%fused_computation.2 | convolution fusion | flops 4301258752 | bytes 14680068 | tf_op jit(solution)/shard_map/dot_general | solution.py:35
  788.1 10.3 %collective-permute-done.48 = bf16[256,2048]{1,0:T(8,128)(2,1)} collective-permute-done((bf16[256,2048]{1,0:T(8,128)(2,1)}, bf16[256,2048]{1,0:T(8,128)(2,1)}, u32[]{:S(2)}, u32[]{:S(2)}) %collective-permute-start.48) | collective-permute-done | bytes 1048608 | tf_op jit(solution)/shard_map/ppermute | solution.py:640
  814.1 15.1 %collective-permute-done.50 = bf16[256,2048]{1,0:T(8,128)(2,1)S(1)} collective-permute-done((bf16[256,2048]{1,0:T(8,128)(2,1)S(1)}, bf16[256,2048]{1,0:T(8,128)(2,1)S(1)}, u32[]{:S(2)}, u32[]{:S(2)}) %collective-permute-start.50) | collective-permute-done | bytes 1048608 | tf_op jit(solution)/shard_map/ppermute | solution.py:640
  880.8 18.8 %collective-permute-done.56.refs_0_.refs_1_ = bf16[256,2048]{1,0:T(8,128)(2,1)S(1)} collective-permute-done((bf16[256,2048]{1,0:T(8,128)(2,1)}, bf16[256,2048]{1,0:T(8,128)(2,1)S(1)}, u32[]{:S(2)}, u32[]{:S(2)}) %collective-permute-start.56) | collective-permute-done | bytes 1048608 | tf_op jit(solution)/shard_map/ppermute | solution.py:636
  926.0 26.6 %reduce-scatter.14.cloned.1.call-done = bf16[512,768]{1,0:T(8,128)(2,1)} async-done(((bf16[2048,768]{1,0:T(8,128)(2,1)}), bf16[512,768]{1,0:T(8,128)(2,1)}) %reduce-scatter.14.cloned.1.call-update) | async-done | bytes 786448 | tf_op jit(solution)/shard_map/reduce_scatter | solution.py:705
  (393 shorter events, 398.7 us)
Async XLA Ops:
  7.2 80.3 %all-gather.3.cloned.1.call-start = ((), (), s32[]{:S(2)}) async-start(), calls=%async_computation.5 | async-start | bytes 7077888 | tf_op jit(solution)/shard_map/all_gather | solution.py:632
  9.5 237.9 %all-gather.5.cloned.1.call-start = ((), (), s32[]{:S(2)}) async-start(), calls=%async_computation.6 | async-start | bytes 18874368 | tf_op jit(solution)/shard_map/all_gather | solution.py:632
  12.7 857.0 %reduce-scatter.12.cloned.1.call-start = ((), (), s32[]{:S(2)}) async-start(), calls=%async_computation.10 | async-start | bytes 1310720 | tf_op jit(solution)/shard_map/reduce_scatter | solution.py:705
  68.6 67.8 %collective-permute-start.13 = (bf16[256,2048]{1,0:T(8,128)(2,1)}, bf16[256,2048]{1,0:T(8,128)(2,1)}, u32[]{:S(2)}, u32[]{:S(2)}) collective-permute-start(bf16[256,2048]{1,0:T(8,128)(2,1)} %collective-permute-done.12), channel_id=1, source_target_pairs={{2,3},{6,7},{10,11},{14,15},{18,19},{22,23},{26,27},{30,31}} | collective-permute-start | bytes 3145736 | tf_op jit(solution)/shard_map/ppermute | solution.py:635
  86.2 55.2 %collective-permute-start.15 = (bf16[256,2048]{1,0:T(8,128)(2,1)}, bf16[256,2048]{1,0:T(8,128)(2,1)}, u32[]{:S(2)}, u32[]{:S(2)}) collective-permute-start(bf16[256,2048]{1,0:T(8,128)(2,1)} %collective-permute-done.14), channel_id=1, source_target_pairs={{1,0},{5,4},{9,8},{13,12},{17,16},{21,20},{25,24},{29,28}} | collective-permute-start | bytes 3145736 | tf_op jit(solution)/shard_map/ppermute | solution.py:636
  134.7 39.7 %collective-permute-start.17 = (bf16[1024,512]{1,0:T(8,128)(2,1)S(1)}, bf16[1024,512]{1,0:T(8,128)(2,1)}, u32[]{:S(2)}, u32[]{:S(2)}) collective-permute-start(bf16[1024,512]{1,0:T(8,128)(2,1)S(1)} %constant_dynamic-slice_fusion.10), channel_id=1, source_target_pairs={{0,4},{4,0},{8,12},{12,8},{1,5},{5,1},{9,13},{13,9},{2,6},{6,2},{1... | collective-permute-start | bytes 3145736 | tf_op jit(solution)/shard_map/ppermute | solution.py:713
  136.4 37.9 %collective-permute-start.18 = (bf16[1024,512]{1,0:T(8,128)(2,1)S(1)}, bf16[1024,512]{1,0:T(8,128)(2,1)}, u32[]{:S(2)}, u32[]{:S(2)}) collective-permute-start(bf16[1024,512]{1,0:T(8,128)(2,1)S(1)} %constant_dynamic-slice_fusion.10), channel_id=1, source_target_pairs={{0,8},{8,0},{4,12},{12,4},{1,9},{9,1},{5,13},{13,5},{2,10},{10,2},... | collective-permute-start | bytes 3145736 | tf_op jit(solution)/shard_map/ppermute | solution.py:713
  145.6 101.7 %collective-permute-start.16 = (bf16[1024,2048]{1,0:T(8,128)(2,1)}, bf16[1024,2048]{1,0:T(8,128)(2,1)}, u32[]{:S(2)}, u32[]{:S(2)}) collective-permute-start(bf16[1024,2048]{1,0:T(8,128)(2,1)} %pad_maximum_fusion.refs_7_.wo_own_ref), channel_id=1, source_target_pairs={{0,16},{16,0},{1,17},{17,1},{2,18},{18,2},{3,19},{19,3},{4,20},{20... | collective-permute-start | bytes 12582920 | tf_op jit(solution)/shard_map/ppermute | solution.py:789
  190.0 57.3 %collective-permute-start.21 = (bf16[4,1024,512]{2,1,0:T(8,128)(2,1)}, bf16[4,1024,512]{2,1,0:T(8,128)(2,1)}, u32[]{:S(2)}, u32[]{:S(2)}) collective-permute-start(bf16[4,1024,512]{2,1,0:T(8,128)(2,1)} %bitcast_dynamic-update-slice_fusion.3.refs_13_.wd_own_ref), channel_id=1, source_target_pairs={{0,16},{16,0},{1,17},{17,1},{2,18},{18,2},{3,19},{19,3},{4,20},{20... | collective-permute-start | bytes 12582920 | tf_op jit(solution)/shard_map/ppermute | solution.py:738
  190.7 29.8 %collective-permute-start.4 = (bf16[1024,512]{1,0:T(8,128)(2,1)S(1)}, bf16[1024,512]{1,0:T(8,128)(2,1)}, u32[]{:S(2)}, u32[]{:S(2)}) collective-permute-start(bf16[1024,512]{1,0:T(8,128)(2,1)S(1)} %collective-permute-done.3.refs_4_), channel_id=1, source_target_pairs={{1,0},{2,1},{5,4},{6,5},{9,8},{10,9},{13,12},{14,13},{17,16},{18,1... | collective-permute-start | bytes 3145736 | tf_op jit(solution)/shard_map/ppermute | solution.py:636
  192.1 30.4 %collective-permute-start.2 = (bf16[1024,512]{1,0:T(8,128)(2,1)S(1)}, bf16[1024,512]{1,0:T(8,128)(2,1)S(1)}, u32[]{:S(2)}, u32[]{:S(2)}) collective-permute-start(bf16[1024,512]{1,0:T(8,128)(2,1)S(1)} %collective-permute-done.1.refs_2_), channel_id=1, source_target_pairs={{2,3},{6,7},{10,11},{14,15},{18,19},{22,23},{26,27},{30,31}} | collective-permute-start | bytes 3145736 | tf_op jit(solution)/shard_map/ppermute | solution.py:635
  220.5 26.8 %collective-permute-start.5 = (bf16[1024,512]{1,0:T(8,128)(2,1)}, bf16[1024,512]{1,0:T(8,128)(2,1)S(1)}, u32[]{:S(2)}, u32[]{:S(2)}) collective-permute-start(bf16[1024,512]{1,0:T(8,128)(2,1)} %collective-permute-done.4.refs_5_), channel_id=1, source_target_pairs={{1,0},{5,4},{9,8},{13,12},{17,16},{21,20},{25,24},{29,28}} | collective-permute-start | bytes 3145736 | tf_op jit(solution)/shard_map/ppermute | solution.py:636
  301.2 27.3 %collective-permute-start.24 = (bf16[256,2048]{1,0:T(8,128)(2,1)}, bf16[256,2048]{1,0:T(8,128)(2,1)S(1)}, u32[]{:S(2)}, u32[]{:S(2)}) collective-permute-start(bf16[256,2048]{1,0:T(8,128)(2,1)} %get-tuple-element.415), channel_id=1, source_target_pairs={{0,1},{1,2},{4,5},{5,6},{8,9},{9,10},{12,13},{13,14},{16,17},{17,1... | collective-permute-start | bytes 3145736 | tf_op jit(solution)/shard_map/ppermute | solution.py:640
  331.2 27.6 %collective-permute-start.26 = (bf16[256,2048]{1,0:T(8,128)(2,1)}, bf16[256,2048]{1,0:T(8,128)(2,1)S(1)}, u32[]{:S(2)}, u32[]{:S(2)}) collective-permute-start(bf16[256,2048]{1,0:T(8,128)(2,1)} %get-tuple-element.413), channel_id=1, source_target_pairs={{0,1},{1,2},{2,3},{4,5},{5,6},{6,7},{8,9},{9,10},{10,11},{12,13},{... | collective-permute-start | bytes 3145736 | tf_op jit(solution)/shard_map/ppermute | solution.py:640
  411.3 43.6 %collective-permute-start.32 = (bf16[256,2048]{1,0:T(8,128)(2,1)S(1)}, bf16[256,2048]{1,0:T(8,128)(2,1)S(1)}, u32[]{:S(2)}, u32[]{:S(2)}) collective-permute-start(bf16[256,2048]{1,0:T(8,128)(2,1)S(1)} %collective-permute-done.29.refs_3_.refs_2_), channel_id=1, source_target_pairs={{2,3},{6,7},{10,11},{14,15},{18,19},{22,23},{26,27},{30,31}} | collective-permute-start | bytes 3145736 | tf_op jit(solution)/shard_map/ppermute | solution.py:635
  413.4 41.4 %collective-permute-start.33 = (bf16[256,2048]{1,0:T(8,128)(2,1)}, bf16[256,2048]{1,0:T(8,128)(2,1)S(1)}, u32[]{:S(2)}, u32[]{:S(2)}) collective-permute-start(bf16[256,2048]{1,0:T(8,128)(2,1)} %collective-permute-done.31.refs_0_.refs_1_), channel_id=1, source_target_pairs={{1,0},{5,4},{9,8},{13,12},{17,16},{21,20},{25,24},{29,28}} | collective-permute-start | bytes 3145736 | tf_op jit(solution)/shard_map/ppermute | solution.py:636
  580.2 52.6 %collective-permute-start.44 = (bf16[256,2048]{1,0:T(8,128)(2,1)S(1)}, bf16[256,2048]{1,0:T(8,128)(2,1)}, u32[]{:S(2)}, u32[]{:S(2)}) collective-permute-start(bf16[256,2048]{1,0:T(8,128)(2,1)S(1)} %collective-permute-done.41.refs_3_.refs_2_), channel_id=1, source_target_pairs={{2,3},{6,7},{10,11},{14,15},{18,19},{22,23},{26,27},{30,31}} | collective-permute-start | bytes 3145736 | tf_op jit(solution)/shard_map/ppermute | solution.py:635
  602.1 30.8 %collective-permute-start.45 = (bf16[256,2048]{1,0:T(8,128)(2,1)}, bf16[256,2048]{1,0:T(8,128)(2,1)}, u32[]{:S(2)}, u32[]{:S(2)}) collective-permute-start(bf16[256,2048]{1,0:T(8,128)(2,1)} %collective-permute-done.43.refs_0_.refs_1_), channel_id=1, source_target_pairs={{1,0},{5,4},{9,8},{13,12},{17,16},{21,20},{25,24},{29,28}} | collective-permute-start | bytes 3145736 | tf_op jit(solution)/shard_map/ppermute | solution.py:636
  613.3 96.2 %collective-permute-start.58 = (bf16[2048,1024]{1,0:T(8,128)(2,1)}, bf16[2048,1024]{1,0:T(8,128)(2,1)}, u32[]{:S(2)}, u32[]{:S(2)}) collective-permute-start(bf16[2048,1024]{1,0:T(8,128)(2,1)} %convolution_convert_fusion.2), channel_id=1, source_target_pairs={{0,16},{16,0},{1,17},{17,1},{2,18},{18,2},{3,19},{19,3},{4,20},{20... | collective-permute-start | bytes 12582920 | tf_op jit(solution)/shard_map/ppermute | solution.py:701
  709.3 162.6 %reduce-scatter.6.cloned.1.call-start = ((), (), s32[]{:S(2)}) async-start(), calls=%async_computation.7 | async-start | bytes 5242880 | tf_op jit(solution)/shard_map/reduce_scatter | solution.py:705
  720.2 157.4 %reduce-scatter.8.cloned.1.call-start = ((), (), s32[]{:S(2)}) async-start(), calls=%async_computation.8 | async-start | bytes 5242880 | tf_op jit(solution)/shard_map/reduce_scatter | solution.py:705
  741.7 164.0 %reduce-scatter.10.cloned.1.call-start = ((), (), s32[]{:S(2)}) async-start(), calls=%async_computation.9 | async-start | bytes 5242880 | tf_op jit(solution)/shard_map/reduce_scatter | solution.py:705
  763.4 189.1 %reduce-scatter.14.cloned.1.call-start = ((), (), s32[]{:S(2)}) async-start(), calls=%async_computation.11 | async-start | bytes 3932160 | tf_op jit(solution)/shard_map/reduce_scatter | solution.py:705
  771.0 27.5 %collective-permute-start.48 = (bf16[256,2048]{1,0:T(8,128)(2,1)}, bf16[256,2048]{1,0:T(8,128)(2,1)}, u32[]{:S(2)}, u32[]{:S(2)}) collective-permute-start(bf16[256,2048]{1,0:T(8,128)(2,1)} %get-tuple-element.406), channel_id=1, source_target_pairs={{0,1},{1,2},{4,5},{5,6},{8,9},{9,10},{12,13},{13,14},{16,17},{17,1... | collective-permute-start | bytes 3145736 | tf_op jit(solution)/shard_map/ppermute | solution.py:640
  800.2 29.0 %collective-permute-start.50 = (bf16[256,2048]{1,0:T(8,128)(2,1)S(1)}, bf16[256,2048]{1,0:T(8,128)(2,1)S(1)}, u32[]{:S(2)}, u32[]{:S(2)}) collective-permute-start(bf16[256,2048]{1,0:T(8,128)(2,1)S(1)} %get-tuple-element.404), channel_id=1, source_target_pairs={{0,1},{1,2},{2,3},{4,5},{5,6},{6,7},{8,9},{9,10},{10,11},{12,13},{... | collective-permute-start | bytes 3145736 | tf_op jit(solution)/shard_map/ppermute | solution.py:640
  835.8 34.0 %collective-permute-start.52 = (bf16[256,2048]{1,0:T(8,128)(2,1)S(1)}, bf16[256,2048]{1,0:T(8,128)(2,1)}, u32[]{:S(2)}, u32[]{:S(2)}) collective-permute-start(bf16[256,2048]{1,0:T(8,128)(2,1)S(1)} %add_convert_fusion.4.refs_0_), channel_id=1, source_target_pairs={{0,1},{1,2},{2,3},{4,5},{5,6},{6,7},{8,9},{9,10},{10,11},{12,13},{... | collective-permute-start | bytes 3145736 | tf_op jit(solution)/shard_map/ppermute | solution.py:635
  838.7 31.8 %collective-permute-start.55 = (bf16[256,2048]{1,0:T(8,128)(2,1)S(1)}, bf16[256,2048]{1,0:T(8,128)(2,1)}, u32[]{:S(2)}, u32[]{:S(2)}) collective-permute-start(bf16[256,2048]{1,0:T(8,128)(2,1)S(1)} %add_convert_fusion.4.refs_0_), channel_id=1, source_target_pairs={{1,0},{2,1},{3,2},{5,4},{6,5},{7,6},{9,8},{10,9},{11,10},{13,12},{... | collective-permute-start | bytes 3145736 | tf_op jit(solution)/shard_map/ppermute | solution.py:636
  870.6 29.0 %collective-permute-start.56 = (bf16[256,2048]{1,0:T(8,128)(2,1)}, bf16[256,2048]{1,0:T(8,128)(2,1)S(1)}, u32[]{:S(2)}, u32[]{:S(2)}) collective-permute-start(bf16[256,2048]{1,0:T(8,128)(2,1)} %collective-permute-done.55.refs_0_.refs_1_), channel_id=1, source_target_pairs={{1,0},{2,1},{5,4},{6,5},{9,8},{10,9},{13,12},{14,13},{17,16},{18,1... | collective-permute-start | bytes 3145736 | tf_op jit(solution)/shard_map/ppermute | solution.py:636
  871.9 33.8 %collective-permute-start.59 = (bf16[512,1024]{1,0:T(8,128)(2,1)}, bf16[512,1024]{1,0:T(8,128)(2,1)}, u32[]{:S(2)}, u32[]{:S(2)}) collective-permute-start(bf16[512,1024]{1,0:T(8,128)(2,1)} %reduce-scatter.6.cloned.1.call-done), channel_id=1, source_target_pairs={{0,16},{16,0},{1,17},{17,1},{2,18},{18,2},{3,19},{19,3},{4,20},{20... | collective-permute-start | bytes 3145736 | tf_op jit(solution)/shard_map/ppermute | solution.py:695
  877.6 37.7 %collective-permute-start.61 = (bf16[512,1024]{1,0:T(8,128)(2,1)}, bf16[512,1024]{1,0:T(8,128)(2,1)}, u32[]{:S(2)}, u32[]{:S(2)}) collective-permute-start(bf16[512,1024]{1,0:T(8,128)(2,1)} %reduce-scatter.8.cloned.1.call-done), channel_id=1, source_target_pairs={{0,16},{16,0},{1,17},{17,1},{2,18},{18,2},{3,19},{19,3},{4,20},{20... | collective-permute-start | bytes 3145736 | tf_op jit(solution)/shard_map/ppermute | solution.py:695
  879.2 88.0 %collective-permute-start.54 = (bf16[256,2048]{1,0:T(8,128)(2,1)S(1)}, bf16[256,2048]{1,0:T(8,128)(2,1)}, u32[]{:S(2)}, u32[]{:S(2)}) collective-permute-start(bf16[256,2048]{1,0:T(8,128)(2,1)S(1)} %collective-permute-done.53.refs_3_.refs_2_), channel_id=1, source_target_pairs={{2,3},{6,7},{10,11},{14,15},{18,19},{22,23},{26,27},{30,31}} | collective-permute-start | bytes 3145736 | tf_op jit(solution)/shard_map/ppermute | solution.py:635
  899.6 67.6 %collective-permute-start.57 = (bf16[256,2048]{1,0:T(8,128)(2,1)S(1)}, bf16[256,2048]{1,0:T(8,128)(2,1)}, u32[]{:S(2)}, u32[]{:S(2)}) collective-permute-start(bf16[256,2048]{1,0:T(8,128)(2,1)S(1)} %collective-permute-done.56.refs_0_.refs_1_), channel_id=1, source_target_pairs={{1,0},{5,4},{9,8},{13,12},{17,16},{21,20},{25,24},{29,28}} | collective-permute-start | bytes 3145736 | tf_op jit(solution)/shard_map/ppermute | solution.py:636
  (111 other events, 2175.7 us)
Sparse Core Ops, SparseCore 0:
  10.5 51.5 all-gather.2
  64.5 107.7 all-gather.4
  709.4 27.6 reduce-scatter.11
  740.5 52.5 reduce-scatter.5
  796.5 53.0 reduce-scatter.7
  853.0 52.6 reduce-scatter.9
  908.6 43.8 reduce-scatter.13

commit v12 on v11

--- a/solution.py
+++ b/solution.py
@@ -871,20 +871,12 @@
         (query_rot, key_rot, value_heads, attended, log_total), grad_att, heads,
     )
     query_dot, key_dot = lax.psum((query_dot[:, 0], key_dot[:, 0]), "col")
-
-    def qkv_grads(pick_rows):
-        pieces = []
-        for grad, raw, scale, dot in (
-            (query_dz, query_raw, query_scale, query_dot), (key_dz, key_raw, key_scale, key_dot),
-        ):
-            grad, raw, scale, dot = (pick_rows(one) for one in (grad, raw, scale, (dot / width)[:, None]))
-            pieces.append((scale * (grad - raw * scale * dot)).astype(BF16))
-        return (*pieces, pick_rows(grad_value_in))
-
-    first_rows = jnp.concatenate(qkv_grads(lambda one: slot_rows(one, 0)), axis=1)
-    first_part = times_transposed(first_rows, full_qkv).astype(BF16)
-    query_dz, key_dz = after((query_dz, key_dz), first_part)
-    grad_query_in, grad_key_in, grad_value_in = qkv_grads(lambda one: one)
+    grad_query_in = (
+        query_scale * (query_dz - query_raw * query_scale * (query_dot / width)[:, None])
+    ).astype(BF16)
+    grad_key_in = (
+        key_scale * (key_dz - key_raw * key_scale * (key_dot / width)[:, None])
+    ).astype(BF16)
     grad_qkv = jnp.concatenate([grad_query_in, grad_key_in, grad_value_in], axis=1)
     gain_pack = jnp.concatenate([grad_query_gain, grad_key_gain, gain_sums["attn"], gain_sums["mlp"]], axis=1)
 
@@ -910,10 +902,15 @@
             return
         gain_pack = pack + lax.ppermute(pack, "row", by_y) if rows == 4 else lax.psum(pack, "row")
 
+    rest = {}
+
     def input_work(slot, gate):
         if slot == 0:
-            return first_part
-        return times_transposed(after(slot_rows(grad_qkv, slot), gate), full_qkv).astype(BF16)
+            return times_transposed(slot_rows(grad_qkv, 0), full_qkv).astype(BF16)
+        if slot == 1:
+            others = jnp.concatenate([slot_rows(grad_qkv, one) for one in (1, 2, 3)], axis=0)
+            rest[0] = times_transposed(after(others, gate), full_qkv).astype(BF16)
+        return rest[0][(slot - 1) * chunk : slot * chunk]
 
     input_own = sum_slots(input_work, input_window)
 

time: 989 us -> 986 us (level)
  matrix products: 90.9 us -> 80.2 us
  waiting for transfers between devices: 363 us -> 373 us
    dot_general x4 -> x2, matrix products: 17.8 us -> 7.12 us  [times_transposed(): lax.dot_general(left_mat, right_mat, (((1,), (1,)), ((), ())), preferred_...]
  transfers between devices with their start and end apart: 80 -> 80, of which waited for: 35 -> 34; matrix products, arithmetic and copies ran while one was open for 17% -> 16% of each run, Pallas kernels for 23% -> 23%
where the time goes in v12:
time: 986 us; the launch traced here: 975 us
  waiting for transfers between devices  373 us (38%)
  Pallas kernels  273 us (28%)
  starting transfers between devices  110 us (11%)
  matrix products  80.2 us (8%)
  other arithmetic  62.1 us (6%)
  local copies, waits for them, and re-layouts  36.4 us (4%)
  blocking collectives  24.3 us (2%)
  between operations  16.1 us (2%)
    ppermute x15, waiting for transfers between devices, line_step(): lax.ppermute(from_right, 'col', [(i + 1, i) for i in range(cols - step)])  127 us
    ppermute x9, waiting for transfers between devices, sum_step(): up = lax.ppermute(up, 'col', [(i, i + 1) for i in range(step)])  95.9 us
    pallas_call x4, Pallas kernels, forward_chunk(): pl.pallas_call(functools.partial(forward_chunk_kernel, out_steps=out_step...  93.1 us
    pallas_call x4, Pallas kernels, backward_chunk(): pl.pallas_call(functools.partial(backward_chunk_kernel, tiles=tiles, choi...  80.2 us
    dot_general x10, matrix products, left_transposed(): lax.dot_general(left_mat, right_mat, (((0,), (0,)), ((), ())), preferred_...  63.1 us
    ppermute x15, waiting for transfers between devices, line_step(): lax.ppermute(from_left, 'col', [(i, i + 1) for i in range(step - 1, cols...  53.8 us
    ppermute x9, starting transfers between devices, sum_step(): up = lax.ppermute(up, 'col', [(i, i + 1) for i in range(step)])  38.1 us
    reduce_scatter x5, waiting for transfers between devices, sum_kept(): lax.psum_scatter(total, 'row', scatter_dimension=0, tiled=True)  29.9 us
  transfers between devices with their start and end apart: 80, of which 34 were waited for; matrix products, arithmetic and copies ran while one was open for 16% of the time, Pallas kernels for 23%

profile of v12, /device:TPU:0, one launch (start us, length us, event | category | flops | bytes accessed | tf_op | source)
XLA Modules:
  0.0 975.3 jit_solution(17187298759201815771)
XLA Ops:
  40.9 16.7 %collective-permute-done.11 = bf16[256,2048]{1,0:T(8,128)(2,1)} collective-permute-done((bf16[256,2048]{1,0:T(8,128)(2,1)}, bf16[256,2048]{1,0:T(8,128)(2,1)}, u32[]{:S(2)}, u32[]{:S(2)}) %collective-permute-start.11) | collective-permute-done | bytes 1048608 | tf_op jit(solution)/shard_map/ppermute | solution.py:635
  70.2 16.0 %collective-permute-done.14 = bf16[256,2048]{1,0:T(8,128)(2,1)} collective-permute-done((bf16[256,2048]{1,0:T(8,128)(2,1)}, bf16[256,2048]{1,0:T(8,128)(2,1)}, u32[]{:S(2)}, u32[]{:S(2)}) %collective-permute-start.14) | collective-permute-done | bytes 1048608 | tf_op jit(solution)/shard_map/ppermute | solution.py:636
  87.5 10.0 %convolution_bitcast_fusion.q_ref.k_ref.v_ref = f32[1024,1536]{1,0:T(8,128)S(1)} fusion(bf16[1024,2048]{1,0:T(8,128)(2,1)} %x_ref.7, bf16[2048,1536]{1,0:T(8,128)(2,1)} %all-gather.3.cloned.1.call-done), kind=kOutput, calls=%fused_computation.4 | convolution fusion | flops 6442450944 | bytes 16777216 | tf_op jit(solution)/shard_map/dot_general | solution.py:25
  100.6 12.1 %all-reduce.1 = (f32[1024]{0:T(1024)S(1)}, f32[1024]{0:T(1024)S(1)}) all-reduce(f32[1024]{0:T(1024)S(1)} %get-tuple-element.376, f32[1024]{0:T(1024)S(1)} %get-tuple-element.375), channel_id=1, replica_groups=mesh['dp'=2,'row'=4,'col'=4] {'col'}, use_global_device_ids=true, to_apply=%region_1.2 | all-reduce | flops 2048 | bytes 16384 | tf_op jit(solution)/shard_map/psum | solution.py:767
  114.9 16.1 %attend_forward.1 = (bf16[1024,512]{1,0:T(8,128)(2,1)}, bf16[1024,512]{1,0:T(8,128)(2,1)}, bf16[1024,512]{1,0:T(8,128)(2,1)}, bf16[1024,512]{1,0:T(8,128)(2,1)}, f32[4,1024,1]{2,1,0:T(8,128)}) custom-call(f32[1024,1536]{1,0:T(8,128)} %copy-done.3, f32[1024,1536]{1,0:T(8,128)} %copy-done.3, f32[1024,1536]{1,0:T(8,128)} %copy-done.3, f32[1024,1]{1,0:T(8,128)} %copy.71.qs_ref, ...), custom_call_target="tpu_custom_call" | custom-call | flops 2147483648 | bytes 10485760 | tf_op jit(solution)/shard_map/attend_forward/pallas_call | solution.py:156
  152.7 21.6 %collective-permute-done.17 = bf16[1024,512]{1,0:T(8,128)(2,1)} collective-permute-done((bf16[1024,512]{1,0:T(8,128)(2,1)S(1)}, bf16[1024,512]{1,0:T(8,128)(2,1)}, u32[]{:S(2)}, u32[]{:S(2)}) %collective-permute-start.17) | collective-permute-done | bytes 1048608 | tf_op jit(solution)/shard_map/ppermute | solution.py:713
  193.1 27.5 %collective-permute-done.4.refs_5_ = bf16[1024,512]{1,0:T(8,128)(2,1)} collective-permute-done((bf16[1024,512]{1,0:T(8,128)(2,1)S(1)}, bf16[1024,512]{1,0:T(8,128)(2,1)}, u32[]{:S(2)}, u32[]{:S(2)}) %collective-permute-start.4) | collective-permute-done | bytes 1048608 | tf_op jit(solution)/shard_map/ppermute | solution.py:636
  222.5 24.8 %collective-permute-done.5.refs_6_ = bf16[1024,512]{1,0:T(8,128)(2,1)S(1)} collective-permute-done((bf16[1024,512]{1,0:T(8,128)(2,1)}, bf16[1024,512]{1,0:T(8,128)(2,1)S(1)}, u32[]{:S(2)}, u32[]{:S(2)}) %collective-permute-start.5) | collective-permute-done | bytes 1048608 | tf_op jit(solution)/shard_map/ppermute | solution.py:636
  248.4 23.2 %forward_chunk.4 = (bf16[1024,2048]{1,0:T(8,128)(2,1)}, f32[1024,1]{1,0:T(8,128)}, bf16[1024,2048]{1,0:T(8,128)(2,1)}, bf16[1024,2048]{1,0:T(8,128)(2,1)}, bf16[...) custom-call(s32[3]{0:T(128)} %get-tuple-element.435.idx_ref, ...), custom_call_target="tpu_custom_call" | custom-call | flops 8589934592 | bytes 33554432 | tf_op jit(solution)/shard_map/forward_chunk/pallas_call | solution.py:309
  274.2 23.3 %forward_chunk.5 = (bf16[1024,2048]{1,0:T(8,128)(2,1)}, f32[1024,1]{1,0:T(8,128)}, bf16[1024,2048]{1,0:T(8,128)(2,1)}, bf16[1024,2048]{1,0:T(8,128)(2,1)}, bf16[...) custom-call(s32[3]{0:T(128)} %get-tuple-element.436.idx_ref, ...), custom_call_target="tpu_custom_call", output_to_operand_aliasing={{0}: (16, {}), {1}: (17, {}), {2}: (18, {}), {3}: (19, {}),... | custom-call | flops 8589934592 | bytes 33554432 | tf_op jit(solution)/shard_map/forward_chunk/pallas_call | solution.py:309
  305.2 23.4 %forward_chunk.6 = (bf16[1024,2048]{1,0:T(8,128)(2,1)}, f32[1024,1]{1,0:T(8,128)}, bf16[1024,2048]{1,0:T(8,128)(2,1)}, bf16[1024,2048]{1,0:T(8,128)(2,1)}, bf16[...) custom-call(s32[3]{0:T(128)} %pad_add_fusion.1.idx_ref, ...), custom_call_target="tpu_custom_call", output_to_operand_aliasing={{0}: (16, {}), {1}: (17, {}), {2}: (18, {}), {3}: (19, {}),... | custom-call | flops 8589934592 | bytes 33554432 | tf_op jit(solution)/shard_map/forward_chunk/pallas_call | solution.py:309
  335.4 23.2 %forward_chunk.7 = (bf16[1024,2048]{1,0:T(8,128)(2,1)}, f32[1024,1]{1,0:T(8,128)}, bf16[1024,2048]{1,0:T(8,128)(2,1)}, bf16[1024,2048]{1,0:T(8,128)(2,1)}, bf16[...) custom-call(s32[3]{0:T(128)} %pad_add_fusion.idx_ref, ...), custom_call_target="tpu_custom_call", output_to_operand_aliasing={{0}: (16, {}), {1}: (17, {}), {2}: (18, {}), {3}: (19, {}),... | custom-call | flops 8589934592 | bytes 33554432 | tf_op jit(solution)/shard_map/forward_chunk/pallas_call | solution.py:309
  366.9 18.9 %collective-permute-done.28.refs_1_.refs_2_ = bf16[256,2048]{1,0:T(8,128)(2,1)S(1)} collective-permute-done((bf16[256,2048]{1,0:T(8,128)(2,1)S(1)}, bf16[256,2048]{1,0:T(8,128)(2,1)S(1)}, u32[]{:S(2)}, u32[]{:S(2)}) %collective-permute-start.28) | collective-permute-done | bytes 1048608 | tf_op jit(solution)/shard_map/ppermute | solution.py:635
  391.3 20.0 %backward_chunk.4 = (bf16[1024,2048]{1,0:T(8,128)(2,1)}, bf16[1024,2048]{1,0:T(8,128)(2,1)}, bf16[1024,2048]{1,0:T(8,128)(2,1)}, bf16[256,2048]{1,0:T(8,128)(2,1)}, f32[1,2048]{1,0:T(1,128)}) custom-call(s32[3]{0:T(128)} %pad_add_fusion.idx_ref, bf16[1024,2048]{1,0:T(8,128)(2,1)} %grad_ref.15, f32[1,2048]{1,0:T(1,128)} %bitcast.91, ...), custom_call_target="tpu_custom_call" | custom-call | flops 6442450944 | bytes 25165824 | tf_op jit(solution)/shard_map/backward_chunk/pallas_call | solution.py:407
  415.2 20.0 %backward_chunk.5 = (bf16[1024,2048]{1,0:T(8,128)(2,1)}, bf16[1024,2048]{1,0:T(8,128)(2,1)}, bf16[1024,2048]{1,0:T(8,128)(2,1)}, bf16[256,2048]{1,0:T(8,128)(2,1)}, f32[1,2048]{1,0:T(1,128)}) custom-call(s32[3]{0:T(128)} %pad_add_fusion.1.idx_ref, bf16[1024,2048]{1,0:T(8,128)(2,1)} %grad_ref.15, ...), custom_call_target="tpu_custom_call", output_to_operand_aliasing={{0}: (11, {}), {1}: (12, {}), {2}: (13, {})} | custom-call | flops 6442450944 | bytes 25165824 | tf_op jit(solution)/shard_map/backward_chunk/pallas_call | solution.py:407
  435.2 20.0 %backward_chunk.6 = (bf16[1024,2048]{1,0:T(8,128)(2,1)}, bf16[1024,2048]{1,0:T(8,128)(2,1)}, bf16[1024,2048]{1,0:T(8,128)(2,1)}, bf16[256,2048]{1,0:T(8,128)(2,1)}, f32[1,2048]{1,0:T(1,128)}) custom-call(s32[3]{0:T(128)} %get-tuple-element.436.idx_ref, bf16[1024,2048]{1,0:T(8,128)(2,1)} %grad_ref.15, ...), custom_call_target="tpu_custom_call", output_to_operand_aliasing={{0}: (13, {}), {1}: (14, {}), {2}: (15, {})} | custom-call | flops 6442450944 | bytes 25165824 | tf_op jit(solution)/shard_map/backward_chunk/pallas_call | solution.py:407
  456.5 20.4 %backward_chunk.7 = (bf16[1024,2048]{1,0:T(8,128)(2,1)}, bf16[1024,2048]{1,0:T(8,128)(2,1)}, bf16[1024,2048]{1,0:T(8,128)(2,1)}, bf16[256,2048]{1,0:T(8,128)(2,1)}, f32[1,2048]{1,0:T(1,128)}) custom-call(s32[3]{0:T(128)} %get-tuple-element.435.idx_ref, bf16[1024,2048]{1,0:T(8,128)(2,1)} %grad_ref.15, ...), custom_call_target="tpu_custom_call", output_to_operand_aliasing={{0}: (13, {}), {1}: (14, {}), {2}: (15, {})} | custom-call | flops 6442450944 | bytes 25165824 | tf_op jit(solution)/shard_map/backward_chunk/pallas_call | solution.py:407
  482.5 17.6 %collective-permute-done.34 = bf16[256,2048]{1,0:T(8,128)(2,1)S(1)} collective-permute-done((bf16[256,2048]{1,0:T(8,128)(2,1)}, bf16[256,2048]{1,0:T(8,128)(2,1)S(1)}, u32[]{:S(2)}, u32[]{:S(2)}) %collective-permute-start.34) | collective-permute-done | bytes 1048608 | tf_op jit(solution)/shard_map/ppermute | solution.py:640
  506.8 16.4 %collective-permute-done.35 = bf16[256,2048]{1,0:T(8,128)(2,1)S(1)} collective-permute-done((bf16[256,2048]{1,0:T(8,128)(2,1)S(1)}, bf16[256,2048]{1,0:T(8,128)(2,1)S(1)}, u32[]{:S(2)}, u32[]{:S(2)}) %collective-permute-start.35) | collective-permute-done | bytes 1048608 | tf_op jit(solution)/shard_map/ppermute | solution.py:640
  523.6 9.2 collective-permute-start.36
  534.1 15.2 %collective-permute-done.36 = bf16[256,2048]{1,0:T(8,128)(2,1)S(1)} collective-permute-done((bf16[256,2048]{1,0:T(8,128)(2,1)S(1)}, bf16[256,2048]{1,0:T(8,128)(2,1)S(1)}, u32[]{:S(2)}, u32[]{:S(2)}) %collective-permute-start.36) | collective-permute-done | bytes 1048608 | tf_op jit(solution)/shard_map/ppermute | solution.py:640
  557.6 14.4 %collective-permute-done.40.refs_1_.refs_2_ = bf16[256,2048]{1,0:T(8,128)(2,1)S(1)} collective-permute-done((bf16[256,2048]{1,0:T(8,128)(2,1)S(1)}, bf16[256,2048]{1,0:T(8,128)(2,1)S(1)}, u32[]{:S(2)}, u32[]{:S(2)}) %collective-permute-start.40) | collective-permute-done | bytes 1048608 | tf_op jit(solution)/shard_map/ppermute | solution.py:635
  582.4 20.3 %collective-permute-done.43.refs_0_.refs_1_ = bf16[256,2048]{1,0:T(8,128)(2,1)} collective-permute-done((bf16[256,2048]{1,0:T(8,128)(2,1)}, bf16[256,2048]{1,0:T(8,128)(2,1)}, u32[]{:S(2)}, u32[]{:S(2)}) %collective-permute-start.43) | collective-permute-done | bytes 1048608 | tf_op jit(solution)/shard_map/ppermute | solution.py:636
  604.4 9.5 convolution_convert_fusion.2
  640.0 18.1 %attend_backward.1 = (f32[1024,512]{1,0:T(8,128)}, f32[1024,512]{1,0:T(8,128)}, bf16[1024,512]{1,0:T(8,128)(2,1)}, f32[1024,1]{1,0:T(8,128)}, f32[1024,1]{1,0:T(...) custom-call(f32[1024,1536]{1,0:T(8,128)} %copy-done.3, f32[1024,1536]{1,0:T(8,128)} %copy-done.3, f32[1024,1]{1,0:T(8,128)} %copy.71.qs_ref, ...), custom_call_target="tpu_custom_call" | custom-call | flops 5368709120 | bytes 20971520 | tf_op jit(solution)/shard_map/attend_backward/pallas_call | solution.py:180
  660.6 12.2 %all-reduce = (f32[1024]{0:T(1024)S(1)}, f32[1024]{0:T(1024)S(1)}) all-reduce(f32[1024]{0:T(1024)S(1)} %reduce.1, f32[1024]{0:T(1024)S(1)} %reduce), channel_id=1, replica_groups=mesh['dp'=2,'row'=4,'col'=4] {'col'}, use_global_device_ids=true, to_apply=%region_5.6 | all-reduce | flops 2048 | bytes 16384 | tf_op jit(solution)/shard_map/psum | solution.py:873
  691.9 11.1 %collective-permute-done.46 = bf16[256,2048]{1,0:T(8,128)(2,1)S(1)} collective-permute-done((bf16[256,2048]{1,0:T(8,128)(2,1)S(1)}, bf16[256,2048]{1,0:T(8,128)(2,1)S(1)}, u32[]{:S(2)}, u32[]{:S(2)}) %collective-permute-start.46) | collective-permute-done | bytes 1048608 | tf_op jit(solution)/shard_map/ppermute | solution.py:640
  707.2 10.6 %add_convert_fusion.2 = bf16[2048,1024]{1,0:T(8,128)(2,1)} fusion(bf16[2048,1024]{1,0:T(8,128)(2,1)} %collective-permute-done.58, bf16[1024,2048]{1,0:T(8,128)(2,1)} %get-tuple-element.300, bf16[1024,2048]{1,0:T(8,128)(2,1)} %get-tuple-element.301, s32[]{:T(128)S(6)} %select_n.227), kind=kOutput, calls=%fused_computation.2 | convolution fusion | flops 4301258752 | bytes 14680068 | tf_op jit(solution)/shard_map/dot_general | solution.py:35
  781.0 15.1 %collective-permute-done.47 = bf16[256,2048]{1,0:T(8,128)(2,1)} collective-permute-done((bf16[256,2048]{1,0:T(8,128)(2,1)}, bf16[256,2048]{1,0:T(8,128)(2,1)}, u32[]{:S(2)}, u32[]{:S(2)}) %collective-permute-start.47) | collective-permute-done | bytes 1048608 | tf_op jit(solution)/shard_map/ppermute | solution.py:640
  808.1 20.5 %collective-permute-done.48 = bf16[256,2048]{1,0:T(8,128)(2,1)S(1)} collective-permute-done((bf16[256,2048]{1,0:T(8,128)(2,1)S(1)}, bf16[256,2048]{1,0:T(8,128)(2,1)S(1)}, u32[]{:S(2)}, u32[]{:S(2)}) %collective-permute-start.48) | collective-permute-done | bytes 1048608 | tf_op jit(solution)/shard_map/ppermute | solution.py:640
  879.7 18.7 %collective-permute-done.56.refs_0_.refs_1_ = bf16[256,2048]{1,0:T(8,128)(2,1)S(1)} collective-permute-done((bf16[256,2048]{1,0:T(8,128)(2,1)}, bf16[256,2048]{1,0:T(8,128)(2,1)S(1)}, u32[]{:S(2)}, u32[]{:S(2)}) %collective-permute-start.56) | collective-permute-done | bytes 1048608 | tf_op jit(solution)/shard_map/ppermute | solution.py:636
  923.2 26.6 %reduce-scatter.14.cloned.1.call-done = bf16[512,768]{1,0:T(8,128)(2,1)} async-done(((bf16[2048,768]{1,0:T(8,128)(2,1)}), bf16[512,768]{1,0:T(8,128)(2,1)}) %reduce-scatter.14.cloned.1.call-update) | async-done | bytes 786448 | tf_op jit(solution)/shard_map/reduce_scatter | solution.py:705
  (378 shorter events, 386.4 us)
Async XLA Ops:
  7.2 80.3 %all-gather.3.cloned.1.call-start = ((), (), s32[]{:S(2)}) async-start(), calls=%async_computation.5 | async-start | bytes 7077888 | tf_op jit(solution)/shard_map/all_gather | solution.py:632
  9.5 238.0 %all-gather.5.cloned.1.call-start = ((), (), s32[]{:S(2)}) async-start(), calls=%async_computation.6 | async-start | bytes 18874368 | tf_op jit(solution)/shard_map/all_gather | solution.py:632
  12.7 855.9 %reduce-scatter.12.cloned.1.call-start = ((), (), s32[]{:S(2)}) async-start(), calls=%async_computation.10 | async-start | bytes 1310720 | tf_op jit(solution)/shard_map/reduce_scatter | solution.py:705
  68.6 67.5 %collective-permute-start.13 = (bf16[256,2048]{1,0:T(8,128)(2,1)}, bf16[256,2048]{1,0:T(8,128)(2,1)}, u32[]{:S(2)}, u32[]{:S(2)}) collective-permute-start(bf16[256,2048]{1,0:T(8,128)(2,1)} %collective-permute-done.12), channel_id=1, source_target_pairs={{2,3},{6,7},{10,11},{14,15},{18,19},{22,23},{26,27},{30,31}} | collective-permute-start | bytes 3145736 | tf_op jit(solution)/shard_map/ppermute | solution.py:635
  86.2 54.5 %collective-permute-start.15 = (bf16[256,2048]{1,0:T(8,128)(2,1)}, bf16[256,2048]{1,0:T(8,128)(2,1)}, u32[]{:S(2)}, u32[]{:S(2)}) collective-permute-start(bf16[256,2048]{1,0:T(8,128)(2,1)} %collective-permute-done.14), channel_id=1, source_target_pairs={{1,0},{5,4},{9,8},{13,12},{17,16},{21,20},{25,24},{29,28}} | collective-permute-start | bytes 3145736 | tf_op jit(solution)/shard_map/ppermute | solution.py:636
  133.9 40.5 %collective-permute-start.17 = (bf16[1024,512]{1,0:T(8,128)(2,1)S(1)}, bf16[1024,512]{1,0:T(8,128)(2,1)}, u32[]{:S(2)}, u32[]{:S(2)}) collective-permute-start(bf16[1024,512]{1,0:T(8,128)(2,1)S(1)} %constant_dynamic-slice_fusion.9), channel_id=1, source_target_pairs={{0,4},{4,0},{8,12},{12,8},{1,5},{5,1},{9,13},{13,9},{2,6},{6,2},{1... | collective-permute-start | bytes 3145736 | tf_op jit(solution)/shard_map/ppermute | solution.py:713
  136.0 38.3 %collective-permute-start.18 = (bf16[1024,512]{1,0:T(8,128)(2,1)S(1)}, bf16[1024,512]{1,0:T(8,128)(2,1)}, u32[]{:S(2)}, u32[]{:S(2)}) collective-permute-start(bf16[1024,512]{1,0:T(8,128)(2,1)S(1)} %constant_dynamic-slice_fusion.9), channel_id=1, source_target_pairs={{0,8},{8,0},{4,12},{12,4},{1,9},{9,1},{5,13},{13,5},{2,10},{10,2},... | collective-permute-start | bytes 3145736 | tf_op jit(solution)/shard_map/ppermute | solution.py:713
  144.9 102.5 %collective-permute-start.16 = (bf16[1024,2048]{1,0:T(8,128)(2,1)}, bf16[1024,2048]{1,0:T(8,128)(2,1)}, u32[]{:S(2)}, u32[]{:S(2)}) collective-permute-start(bf16[1024,2048]{1,0:T(8,128)(2,1)} %pad_maximum_fusion.refs_7_.wo_own_ref), channel_id=1, source_target_pairs={{0,16},{16,0},{1,17},{17,1},{2,18},{18,2},{3,19},{19,3},{4,20},{20... | collective-permute-start | bytes 12582920 | tf_op jit(solution)/shard_map/ppermute | solution.py:789
  190.3 57.1 %collective-permute-start.21 = (bf16[4,1024,512]{2,1,0:T(8,128)(2,1)}, bf16[4,1024,512]{2,1,0:T(8,128)(2,1)}, u32[]{:S(2)}, u32[]{:S(2)}) collective-permute-start(bf16[4,1024,512]{2,1,0:T(8,128)(2,1)} %bitcast_dynamic-update-slice_fusion.3.refs_13_.wd_own_ref), channel_id=1, source_target_pairs={{0,16},{16,0},{1,17},{17,1},{2,18},{18,2},{3,19},{19,3},{4,20},{20... | collective-permute-start | bytes 12582920 | tf_op jit(solution)/shard_map/ppermute | solution.py:738
  191.0 29.6 %collective-permute-start.4 = (bf16[1024,512]{1,0:T(8,128)(2,1)S(1)}, bf16[1024,512]{1,0:T(8,128)(2,1)}, u32[]{:S(2)}, u32[]{:S(2)}) collective-permute-start(bf16[1024,512]{1,0:T(8,128)(2,1)S(1)} %collective-permute-done.3.refs_4_), channel_id=1, source_target_pairs={{1,0},{2,1},{5,4},{6,5},{9,8},{10,9},{13,12},{14,13},{17,16},{18,1... | collective-permute-start | bytes 3145736 | tf_op jit(solution)/shard_map/ppermute | solution.py:636
  192.3 30.2 %collective-permute-start.2 = (bf16[1024,512]{1,0:T(8,128)(2,1)S(1)}, bf16[1024,512]{1,0:T(8,128)(2,1)S(1)}, u32[]{:S(2)}, u32[]{:S(2)}) collective-permute-start(bf16[1024,512]{1,0:T(8,128)(2,1)S(1)} %collective-permute-done.1.refs_2_), channel_id=1, source_target_pairs={{2,3},{6,7},{10,11},{14,15},{18,19},{22,23},{26,27},{30,31}} | collective-permute-start | bytes 3145736 | tf_op jit(solution)/shard_map/ppermute | solution.py:635
  220.6 26.8 %collective-permute-start.5 = (bf16[1024,512]{1,0:T(8,128)(2,1)}, bf16[1024,512]{1,0:T(8,128)(2,1)S(1)}, u32[]{:S(2)}, u32[]{:S(2)}) collective-permute-start(bf16[1024,512]{1,0:T(8,128)(2,1)} %collective-permute-done.4.refs_5_), channel_id=1, source_target_pairs={{1,0},{5,4},{9,8},{13,12},{17,16},{21,20},{25,24},{29,28}} | collective-permute-start | bytes 3145736 | tf_op jit(solution)/shard_map/ppermute | solution.py:636
  301.3 27.3 %collective-permute-start.24 = (bf16[256,2048]{1,0:T(8,128)(2,1)}, bf16[256,2048]{1,0:T(8,128)(2,1)S(1)}, u32[]{:S(2)}, u32[]{:S(2)}) collective-permute-start(bf16[256,2048]{1,0:T(8,128)(2,1)} %get-tuple-element.406), channel_id=1, source_target_pairs={{0,1},{1,2},{4,5},{5,6},{8,9},{9,10},{12,13},{13,14},{16,17},{17,1... | collective-permute-start | bytes 3145736 | tf_op jit(solution)/shard_map/ppermute | solution.py:640
  331.3 27.3 %collective-permute-start.26 = (bf16[256,2048]{1,0:T(8,128)(2,1)}, bf16[256,2048]{1,0:T(8,128)(2,1)S(1)}, u32[]{:S(2)}, u32[]{:S(2)}) collective-permute-start(bf16[256,2048]{1,0:T(8,128)(2,1)} %get-tuple-element.404), channel_id=1, source_target_pairs={{0,1},{1,2},{2,3},{4,5},{5,6},{6,7},{8,9},{9,10},{10,11},{12,13},{... | collective-permute-start | bytes 3145736 | tf_op jit(solution)/shard_map/ppermute | solution.py:640
  411.3 43.8 %collective-permute-start.32 = (bf16[256,2048]{1,0:T(8,128)(2,1)S(1)}, bf16[256,2048]{1,0:T(8,128)(2,1)S(1)}, u32[]{:S(2)}, u32[]{:S(2)}) collective-permute-start(bf16[256,2048]{1,0:T(8,128)(2,1)S(1)} %collective-permute-done.29.refs_3_.refs_2_), channel_id=1, source_target_pairs={{2,3},{6,7},{10,11},{14,15},{18,19},{22,23},{26,27},{30,31}} | collective-permute-start | bytes 3145736 | tf_op jit(solution)/shard_map/ppermute | solution.py:635
  413.8 41.4 %collective-permute-start.33 = (bf16[256,2048]{1,0:T(8,128)(2,1)}, bf16[256,2048]{1,0:T(8,128)(2,1)S(1)}, u32[]{:S(2)}, u32[]{:S(2)}) collective-permute-start(bf16[256,2048]{1,0:T(8,128)(2,1)} %collective-permute-done.31.refs_0_.refs_1_), channel_id=1, source_target_pairs={{1,0},{5,4},{9,8},{13,12},{17,16},{21,20},{25,24},{29,28}} | collective-permute-start | bytes 3145736 | tf_op jit(solution)/shard_map/ppermute | solution.py:636
  580.7 52.8 %collective-permute-start.44 = (bf16[256,2048]{1,0:T(8,128)(2,1)S(1)}, bf16[256,2048]{1,0:T(8,128)(2,1)}, u32[]{:S(2)}, u32[]{:S(2)}) collective-permute-start(bf16[256,2048]{1,0:T(8,128)(2,1)S(1)} %collective-permute-done.41.refs_3_.refs_2_), channel_id=1, source_target_pairs={{2,3},{6,7},{10,11},{14,15},{18,19},{22,23},{26,27},{30,31}} | collective-permute-start | bytes 3145736 | tf_op jit(solution)/shard_map/ppermute | solution.py:635
  602.7 30.8 %collective-permute-start.45 = (bf16[256,2048]{1,0:T(8,128)(2,1)}, bf16[256,2048]{1,0:T(8,128)(2,1)}, u32[]{:S(2)}, u32[]{:S(2)}) collective-permute-start(bf16[256,2048]{1,0:T(8,128)(2,1)} %collective-permute-done.43.refs_0_.refs_1_), channel_id=1, source_target_pairs={{1,0},{5,4},{9,8},{13,12},{17,16},{21,20},{25,24},{29,28}} | collective-permute-start | bytes 3145736 | tf_op jit(solution)/shard_map/ppermute | solution.py:636
  613.9 93.2 %collective-permute-start.58 = (bf16[2048,1024]{1,0:T(8,128)(2,1)}, bf16[2048,1024]{1,0:T(8,128)(2,1)}, u32[]{:S(2)}, u32[]{:S(2)}) collective-permute-start(bf16[2048,1024]{1,0:T(8,128)(2,1)} %convolution_convert_fusion.2), channel_id=1, source_target_pairs={{0,16},{16,0},{1,17},{17,1},{2,18},{18,2},{3,19},{19,3},{4,20},{20... | collective-permute-start | bytes 12582920 | tf_op jit(solution)/shard_map/ppermute | solution.py:701
  706.9 163.8 %reduce-scatter.6.cloned.1.call-start = ((), (), s32[]{:S(2)}) async-start(), calls=%async_computation.7 | async-start | bytes 5242880 | tf_op jit(solution)/shard_map/reduce_scatter | solution.py:705
  717.8 158.5 %reduce-scatter.8.cloned.1.call-start = ((), (), s32[]{:S(2)}) async-start(), calls=%async_computation.8 | async-start | bytes 5242880 | tf_op jit(solution)/shard_map/reduce_scatter | solution.py:705
  739.3 163.6 %reduce-scatter.10.cloned.1.call-start = ((), (), s32[]{:S(2)}) async-start(), calls=%async_computation.9 | async-start | bytes 5242880 | tf_op jit(solution)/shard_map/reduce_scatter | solution.py:705
  761.0 188.7 %reduce-scatter.14.cloned.1.call-start = ((), (), s32[]{:S(2)}) async-start(), calls=%async_computation.11 | async-start | bytes 3932160 | tf_op jit(solution)/shard_map/reduce_scatter | solution.py:705
  768.6 27.5 %collective-permute-start.47 = (bf16[256,2048]{1,0:T(8,128)(2,1)}, bf16[256,2048]{1,0:T(8,128)(2,1)}, u32[]{:S(2)}, u32[]{:S(2)}) collective-permute-start(bf16[256,2048]{1,0:T(8,128)(2,1)} %get-tuple-element.385), channel_id=1, source_target_pairs={{0,1},{1,2},{4,5},{5,6},{8,9},{9,10},{12,13},{13,14},{16,17},{17,1... | collective-permute-start | bytes 3145736 | tf_op jit(solution)/shard_map/ppermute | solution.py:640
  798.9 29.7 %collective-permute-start.48 = (bf16[256,2048]{1,0:T(8,128)(2,1)S(1)}, bf16[256,2048]{1,0:T(8,128)(2,1)S(1)}, u32[]{:S(2)}, u32[]{:S(2)}) collective-permute-start(bf16[256,2048]{1,0:T(8,128)(2,1)S(1)} %get-tuple-element.389), channel_id=1, source_target_pairs={{0,1},{1,2},{2,3},{4,5},{5,6},{6,7},{8,9},{9,10},{10,11},{12,13},{... | collective-permute-start | bytes 3145736 | tf_op jit(solution)/shard_map/ppermute | solution.py:640
  834.9 33.7 %collective-permute-start.52 = (bf16[256,2048]{1,0:T(8,128)(2,1)S(1)}, bf16[256,2048]{1,0:T(8,128)(2,1)}, u32[]{:S(2)}, u32[]{:S(2)}) collective-permute-start(bf16[256,2048]{1,0:T(8,128)(2,1)S(1)} %add_convert_fusion.4.refs_0_), channel_id=1, source_target_pairs={{0,1},{1,2},{2,3},{4,5},{5,6},{6,7},{8,9},{9,10},{10,11},{12,13},{... | collective-permute-start | bytes 3145736 | tf_op jit(solution)/shard_map/ppermute | solution.py:635
  838.4 30.9 %collective-permute-start.55 = (bf16[256,2048]{1,0:T(8,128)(2,1)S(1)}, bf16[256,2048]{1,0:T(8,128)(2,1)}, u32[]{:S(2)}, u32[]{:S(2)}) collective-permute-start(bf16[256,2048]{1,0:T(8,128)(2,1)S(1)} %add_convert_fusion.4.refs_0_), channel_id=1, source_target_pairs={{1,0},{2,1},{3,2},{5,4},{6,5},{7,6},{9,8},{10,9},{11,10},{13,12},{... | collective-permute-start | bytes 3145736 | tf_op jit(solution)/shard_map/ppermute | solution.py:636
  869.4 28.9 %collective-permute-start.56 = (bf16[256,2048]{1,0:T(8,128)(2,1)}, bf16[256,2048]{1,0:T(8,128)(2,1)S(1)}, u32[]{:S(2)}, u32[]{:S(2)}) collective-permute-start(bf16[256,2048]{1,0:T(8,128)(2,1)} %collective-permute-done.55.refs_0_.refs_1_), channel_id=1, source_target_pairs={{1,0},{2,1},{5,4},{6,5},{9,8},{10,9},{13,12},{14,13},{17,16},{18,1... | collective-permute-start | bytes 3145736 | tf_op jit(solution)/shard_map/ppermute | solution.py:636
  870.7 32.1 %collective-permute-start.59 = (bf16[512,1024]{1,0:T(8,128)(2,1)}, bf16[512,1024]{1,0:T(8,128)(2,1)}, u32[]{:S(2)}, u32[]{:S(2)}) collective-permute-start(bf16[512,1024]{1,0:T(8,128)(2,1)} %reduce-scatter.6.cloned.1.call-done), channel_id=1, source_target_pairs={{0,16},{16,0},{1,17},{17,1},{2,18},{18,2},{3,19},{19,3},{4,20},{20... | collective-permute-start | bytes 3145736 | tf_op jit(solution)/shard_map/ppermute | solution.py:695
  876.4 36.1 %collective-permute-start.61 = (bf16[512,1024]{1,0:T(8,128)(2,1)}, bf16[512,1024]{1,0:T(8,128)(2,1)}, u32[]{:S(2)}, u32[]{:S(2)}) collective-permute-start(bf16[512,1024]{1,0:T(8,128)(2,1)} %reduce-scatter.8.cloned.1.call-done), channel_id=1, source_target_pairs={{0,16},{16,0},{1,17},{17,1},{2,18},{18,2},{3,19},{19,3},{4,20},{20... | collective-permute-start | bytes 3145736 | tf_op jit(solution)/shard_map/ppermute | solution.py:695
  878.0 86.3 %collective-permute-start.54 = (bf16[256,2048]{1,0:T(8,128)(2,1)S(1)}, bf16[256,2048]{1,0:T(8,128)(2,1)}, u32[]{:S(2)}, u32[]{:S(2)}) collective-permute-start(bf16[256,2048]{1,0:T(8,128)(2,1)S(1)} %collective-permute-done.53.refs_3_.refs_2_), channel_id=1, source_target_pairs={{2,3},{6,7},{10,11},{14,15},{18,19},{22,23},{26,27},{30,31}} | collective-permute-start | bytes 3145736 | tf_op jit(solution)/shard_map/ppermute | solution.py:635
  898.3 66.0 %collective-permute-start.57 = (bf16[256,2048]{1,0:T(8,128)(2,1)S(1)}, bf16[256,2048]{1,0:T(8,128)(2,1)}, u32[]{:S(2)}, u32[]{:S(2)}) collective-permute-start(bf16[256,2048]{1,0:T(8,128)(2,1)S(1)} %collective-permute-done.56.refs_0_.refs_1_), channel_id=1, source_target_pairs={{1,0},{5,4},{9,8},{13,12},{17,16},{21,20},{25,24},{29,28}} | collective-permute-start | bytes 3145736 | tf_op jit(solution)/shard_map/ppermute | solution.py:636
  (107 other events, 2052.2 us)
Sparse Core Ops, SparseCore 0:
  10.5 51.5 all-gather.2
  64.5 107.9 all-gather.4
  707.0 27.2 reduce-scatter.11
  737.7 52.5 reduce-scatter.5
  793.8 53.0 reduce-scatter.7
  850.2 52.5 reduce-scatter.9
  905.8 43.8 reduce-scatter.13

commit v13 on v12

--- a/solution.py
+++ b/solution.py
@@ -895,22 +895,14 @@
             return got["qkv"], got["out"], gain_pack
         if step == 2:
             blocks["out"] = sum_kept(left_out, own_half(right_out, 1), got["out"])
-            blocks["qkv"] = sum_kept(after(tokens_in, blocks["out"][0]), interleaved(own_half, pieces_in), got["qkv"]
-            )
             if rows == 4:
                 gain_pack = pack + lax.ppermute(pack, "row", by_x)
             return
+        blocks["qkv"] = sum_kept(tokens_in, interleaved(own_half, pieces_in), got["qkv"])
         gain_pack = pack + lax.ppermute(pack, "row", by_y) if rows == 4 else lax.psum(pack, "row")
 
-    rest = {}
-
     def input_work(slot, gate):
-        if slot == 0:
-            return times_transposed(slot_rows(grad_qkv, 0), full_qkv).astype(BF16)
-        if slot == 1:
-            others = jnp.concatenate([slot_rows(grad_qkv, one) for one in (1, 2, 3)], axis=0)
-            rest[0] = times_transposed(after(others, gate), full_qkv).astype(BF16)
-        return rest[0][(slot - 1) * chunk : slot * chunk]
+        return times_transposed(after(slot_rows(grad_qkv, slot), gate), full_qkv).astype(BF16)
 
     input_own = sum_slots(input_work, input_window)
 

time: 986 us -> 988 us (level)
  transfers between devices with their start and end apart: 80 -> 80, of which waited for: 34 -> 34; matrix products, arithmetic and copies ran while one was open for 16% -> 17% of each run, Pallas kernels for 23% -> 23%
where the time goes in v13:
time: 988 us; the launch traced here: 978 us
  waiting for transfers between devices  371 us (38%)
  Pallas kernels  273 us (28%)
  starting transfers between devices  109 us (11%)
  matrix products  88.9 us (9%)
  other arithmetic  59.1 us (6%)
  local copies, waits for them, and re-layouts  35.9 us (4%)
  blocking collectives  24.2 us (2%)
  between operations  16.2 us (2%)
    ppermute x15, waiting for transfers between devices, line_step(): lax.ppermute(from_right, 'col', [(i + 1, i) for i in range(cols - step)])  127 us
    ppermute x9, waiting for transfers between devices, sum_step(): up = lax.ppermute(up, 'col', [(i, i + 1) for i in range(step)])  96.8 us
    pallas_call x4, Pallas kernels, forward_chunk(): pl.pallas_call(functools.partial(forward_chunk_kernel, out_steps=out_step...  93.2 us
    pallas_call x4, Pallas kernels, backward_chunk(): pl.pallas_call(functools.partial(backward_chunk_kernel, tiles=tiles, choi...  80.2 us
    dot_general x10, matrix products, left_transposed(): lax.dot_general(left_mat, right_mat, (((0,), (0,)), ((), ())), preferred_...  63 us
    ppermute x15, waiting for transfers between devices, line_step(): lax.ppermute(from_left, 'col', [(i, i + 1) for i in range(step - 1, cols...  53.6 us
    ppermute x9, starting transfers between devices, sum_step(): up = lax.ppermute(up, 'col', [(i, i + 1) for i in range(step)])  37 us
    reduce_scatter x5, waiting for transfers between devices, sum_kept(): lax.psum_scatter(total, 'row', scatter_dimension=0, tiled=True)  29.5 us
  transfers between devices with their start and end apart: 80, of which 34 were waited for; matrix products, arithmetic and copies ran while one was open for 17% of the time, Pallas kernels for 23%

profile of v13, /device:TPU:0, one launch (start us, length us, event | category | flops | bytes accessed | tf_op | source)
XLA Modules:
  0.0 977.6 jit_solution(6666213371768194908)
XLA Ops:
  40.8 16.8 %collective-permute-done.11 = bf16[256,2048]{1,0:T(8,128)(2,1)} collective-permute-done((bf16[256,2048]{1,0:T(8,128)(2,1)}, bf16[256,2048]{1,0:T(8,128)(2,1)}, u32[]{:S(2)}, u32[]{:S(2)}) %collective-permute-start.11) | collective-permute-done | bytes 1048608 | tf_op jit(solution)/shard_map/ppermute | solution.py:635
  70.2 16.0 %collective-permute-done.14 = bf16[256,2048]{1,0:T(8,128)(2,1)} collective-permute-done((bf16[256,2048]{1,0:T(8,128)(2,1)}, bf16[256,2048]{1,0:T(8,128)(2,1)}, u32[]{:S(2)}, u32[]{:S(2)}) %collective-permute-start.14) | collective-permute-done | bytes 1048608 | tf_op jit(solution)/shard_map/ppermute | solution.py:636
  87.5 10.2 %convolution_bitcast_fusion.q_ref.k_ref.v_ref = f32[1024,1536]{1,0:T(8,128)S(1)} fusion(bf16[1024,2048]{1,0:T(8,128)(2,1)} %x_ref.7, bf16[2048,1536]{1,0:T(8,128)(2,1)} %all-gather.3.cloned.1.call-done), kind=kOutput, calls=%fused_computation.4 | convolution fusion | flops 6442450944 | bytes 16777216 | tf_op jit(solution)/shard_map/dot_general | solution.py:25
  100.7 12.1 %all-reduce.1 = (f32[1024]{0:T(1024)S(1)}, f32[1024]{0:T(1024)S(1)}) all-reduce(f32[1024]{0:T(1024)S(1)} %get-tuple-element.378, f32[1024]{0:T(1024)S(1)} %get-tuple-element.377), channel_id=1, replica_groups=mesh['dp'=2,'row'=4,'col'=4] {'col'}, use_global_device_ids=true, to_apply=%region_1.2 | all-reduce | flops 2048 | bytes 16384 | tf_op jit(solution)/shard_map/psum | solution.py:767
  115.0 16.2 %attend_forward.1 = (bf16[1024,512]{1,0:T(8,128)(2,1)}, bf16[1024,512]{1,0:T(8,128)(2,1)}, bf16[1024,512]{1,0:T(8,128)(2,1)}, bf16[1024,512]{1,0:T(8,128)(2,1)}, f32[4,1024,1]{2,1,0:T(8,128)}) custom-call(f32[1024,1536]{1,0:T(8,128)} %copy-done.3, f32[1024,1536]{1,0:T(8,128)} %copy-done.3, f32[1024,1536]{1,0:T(8,128)} %copy-done.3, f32[1024,1]{1,0:T(8,128)} %copy.71.qs_ref, ...), custom_call_target="tpu_custom_call" | custom-call | flops 2147483648 | bytes 10485760 | tf_op jit(solution)/shard_map/attend_forward/pallas_call | solution.py:156
  152.7 21.6 %collective-permute-done.17 = bf16[1024,512]{1,0:T(8,128)(2,1)} collective-permute-done((bf16[1024,512]{1,0:T(8,128)(2,1)S(1)}, bf16[1024,512]{1,0:T(8,128)(2,1)}, u32[]{:S(2)}, u32[]{:S(2)}) %collective-permute-start.17) | collective-permute-done | bytes 1048608 | tf_op jit(solution)/shard_map/ppermute | solution.py:713
  193.0 27.5 %collective-permute-done.4.refs_5_ = bf16[1024,512]{1,0:T(8,128)(2,1)} collective-permute-done((bf16[1024,512]{1,0:T(8,128)(2,1)S(1)}, bf16[1024,512]{1,0:T(8,128)(2,1)}, u32[]{:S(2)}, u32[]{:S(2)}) %collective-permute-start.4) | collective-permute-done | bytes 1048608 | tf_op jit(solution)/shard_map/ppermute | solution.py:636
  222.5 24.8 %collective-permute-done.5.refs_6_ = bf16[1024,512]{1,0:T(8,128)(2,1)S(1)} collective-permute-done((bf16[1024,512]{1,0:T(8,128)(2,1)}, bf16[1024,512]{1,0:T(8,128)(2,1)S(1)}, u32[]{:S(2)}, u32[]{:S(2)}) %collective-permute-start.5) | collective-permute-done | bytes 1048608 | tf_op jit(solution)/shard_map/ppermute | solution.py:636
  248.3 23.3 %forward_chunk.4 = (bf16[1024,2048]{1,0:T(8,128)(2,1)}, f32[1024,1]{1,0:T(8,128)}, bf16[1024,2048]{1,0:T(8,128)(2,1)}, bf16[1024,2048]{1,0:T(8,128)(2,1)}, bf16[...) custom-call(s32[3]{0:T(128)} %get-tuple-element.438.idx_ref, ...), custom_call_target="tpu_custom_call" | custom-call | flops 8589934592 | bytes 33554432 | tf_op jit(solution)/shard_map/forward_chunk/pallas_call | solution.py:309
  274.2 23.3 %forward_chunk.5 = (bf16[1024,2048]{1,0:T(8,128)(2,1)}, f32[1024,1]{1,0:T(8,128)}, bf16[1024,2048]{1,0:T(8,128)(2,1)}, bf16[1024,2048]{1,0:T(8,128)(2,1)}, bf16[...) custom-call(s32[3]{0:T(128)} %get-tuple-element.439.idx_ref, ...), custom_call_target="tpu_custom_call", output_to_operand_aliasing={{0}: (16, {}), {1}: (17, {}), {2}: (18, {}), {3}: (19, {}),... | custom-call | flops 8589934592 | bytes 33554432 | tf_op jit(solution)/shard_map/forward_chunk/pallas_call | solution.py:309
  305.2 23.4 %forward_chunk.6 = (bf16[1024,2048]{1,0:T(8,128)(2,1)}, f32[1024,1]{1,0:T(8,128)}, bf16[1024,2048]{1,0:T(8,128)(2,1)}, bf16[1024,2048]{1,0:T(8,128)(2,1)}, bf16[...) custom-call(s32[3]{0:T(128)} %pad_add_fusion.1.idx_ref, ...), custom_call_target="tpu_custom_call", output_to_operand_aliasing={{0}: (16, {}), {1}: (17, {}), {2}: (18, {}), {3}: (19, {}),... | custom-call | flops 8589934592 | bytes 33554432 | tf_op jit(solution)/shard_map/forward_chunk/pallas_call | solution.py:309
  335.4 23.2 %forward_chunk.7 = (bf16[1024,2048]{1,0:T(8,128)(2,1)}, f32[1024,1]{1,0:T(8,128)}, bf16[1024,2048]{1,0:T(8,128)(2,1)}, bf16[1024,2048]{1,0:T(8,128)(2,1)}, bf16[...) custom-call(s32[3]{0:T(128)} %pad_add_fusion.idx_ref, ...), custom_call_target="tpu_custom_call", output_to_operand_aliasing={{0}: (16, {}), {1}: (17, {}), {2}: (18, {}), {3}: (19, {}),... | custom-call | flops 8589934592 | bytes 33554432 | tf_op jit(solution)/shard_map/forward_chunk/pallas_call | solution.py:309
  367.0 18.8 %collective-permute-done.28.refs_1_.refs_2_ = bf16[256,2048]{1,0:T(8,128)(2,1)S(1)} collective-permute-done((bf16[256,2048]{1,0:T(8,128)(2,1)S(1)}, bf16[256,2048]{1,0:T(8,128)(2,1)S(1)}, u32[]{:S(2)}, u32[]{:S(2)}) %collective-permute-start.28) | collective-permute-done | bytes 1048608 | tf_op jit(solution)/shard_map/ppermute | solution.py:635
  391.2 20.0 %backward_chunk.4 = (bf16[1024,2048]{1,0:T(8,128)(2,1)}, bf16[1024,2048]{1,0:T(8,128)(2,1)}, bf16[1024,2048]{1,0:T(8,128)(2,1)}, bf16[256,2048]{1,0:T(8,128)(2,1)}, f32[1,2048]{1,0:T(1,128)}) custom-call(s32[3]{0:T(128)} %pad_add_fusion.idx_ref, bf16[1024,2048]{1,0:T(8,128)(2,1)} %grad_ref.15, f32[1,2048]{1,0:T(1,128)} %bitcast.96, ...), custom_call_target="tpu_custom_call" | custom-call | flops 6442450944 | bytes 25165824 | tf_op jit(solution)/shard_map/backward_chunk/pallas_call | solution.py:407
  414.9 20.0 %backward_chunk.5 = (bf16[1024,2048]{1,0:T(8,128)(2,1)}, bf16[1024,2048]{1,0:T(8,128)(2,1)}, bf16[1024,2048]{1,0:T(8,128)(2,1)}, bf16[256,2048]{1,0:T(8,128)(2,1)}, f32[1,2048]{1,0:T(1,128)}) custom-call(s32[3]{0:T(128)} %pad_add_fusion.1.idx_ref, bf16[1024,2048]{1,0:T(8,128)(2,1)} %grad_ref.15, ...), custom_call_target="tpu_custom_call", output_to_operand_aliasing={{0}: (11, {}), {1}: (12, {}), {2}: (13, {})} | custom-call | flops 6442450944 | bytes 25165824 | tf_op jit(solution)/shard_map/backward_chunk/pallas_call | solution.py:407
  434.9 20.0 %backward_chunk.6 = (bf16[1024,2048]{1,0:T(8,128)(2,1)}, bf16[1024,2048]{1,0:T(8,128)(2,1)}, bf16[1024,2048]{1,0:T(8,128)(2,1)}, bf16[256,2048]{1,0:T(8,128)(2,1)}, f32[1,2048]{1,0:T(1,128)}) custom-call(s32[3]{0:T(128)} %get-tuple-element.439.idx_ref, bf16[1024,2048]{1,0:T(8,128)(2,1)} %grad_ref.15, ...), custom_call_target="tpu_custom_call", output_to_operand_aliasing={{0}: (13, {}), {1}: (14, {}), {2}: (15, {})} | custom-call | flops 6442450944 | bytes 25165824 | tf_op jit(solution)/shard_map/backward_chunk/pallas_call | solution.py:407
  456.3 20.3 %backward_chunk.7 = (bf16[1024,2048]{1,0:T(8,128)(2,1)}, bf16[1024,2048]{1,0:T(8,128)(2,1)}, bf16[1024,2048]{1,0:T(8,128)(2,1)}, bf16[256,2048]{1,0:T(8,128)(2,1)}, f32[1,2048]{1,0:T(1,128)}) custom-call(s32[3]{0:T(128)} %get-tuple-element.438.idx_ref, bf16[1024,2048]{1,0:T(8,128)(2,1)} %grad_ref.15, ...), custom_call_target="tpu_custom_call", output_to_operand_aliasing={{0}: (13, {}), {1}: (14, {}), {2}: (15, {})} | custom-call | flops 6442450944 | bytes 25165824 | tf_op jit(solution)/shard_map/backward_chunk/pallas_call | solution.py:407
  482.1 17.4 %collective-permute-done.34 = bf16[256,2048]{1,0:T(8,128)(2,1)S(1)} collective-permute-done((bf16[256,2048]{1,0:T(8,128)(2,1)}, bf16[256,2048]{1,0:T(8,128)(2,1)S(1)}, u32[]{:S(2)}, u32[]{:S(2)}) %collective-permute-start.34) | collective-permute-done | bytes 1048608 | tf_op jit(solution)/shard_map/ppermute | solution.py:640
  506.4 16.3 %collective-permute-done.35 = bf16[256,2048]{1,0:T(8,128)(2,1)S(1)} collective-permute-done((bf16[256,2048]{1,0:T(8,128)(2,1)S(1)}, bf16[256,2048]{1,0:T(8,128)(2,1)S(1)}, u32[]{:S(2)}, u32[]{:S(2)}) %collective-permute-start.35) | collective-permute-done | bytes 1048608 | tf_op jit(solution)/shard_map/ppermute | solution.py:640
  523.0 9.5 collective-permute-start.36
  533.8 15.2 %collective-permute-done.36 = bf16[256,2048]{1,0:T(8,128)(2,1)S(1)} collective-permute-done((bf16[256,2048]{1,0:T(8,128)(2,1)S(1)}, bf16[256,2048]{1,0:T(8,128)(2,1)S(1)}, u32[]{:S(2)}, u32[]{:S(2)}) %collective-permute-start.36) | collective-permute-done | bytes 1048608 | tf_op jit(solution)/shard_map/ppermute | solution.py:640
  557.2 14.3 %collective-permute-done.40.refs_1_.refs_2_ = bf16[256,2048]{1,0:T(8,128)(2,1)S(1)} collective-permute-done((bf16[256,2048]{1,0:T(8,128)(2,1)S(1)}, bf16[256,2048]{1,0:T(8,128)(2,1)S(1)}, u32[]{:S(2)}, u32[]{:S(2)}) %collective-permute-start.40) | collective-permute-done | bytes 1048608 | tf_op jit(solution)/shard_map/ppermute | solution.py:635
  582.0 20.3 %collective-permute-done.43.refs_0_.refs_1_ = bf16[256,2048]{1,0:T(8,128)(2,1)} collective-permute-done((bf16[256,2048]{1,0:T(8,128)(2,1)}, bf16[256,2048]{1,0:T(8,128)(2,1)}, u32[]{:S(2)}, u32[]{:S(2)}) %collective-permute-start.43) | collective-permute-done | bytes 1048608 | tf_op jit(solution)/shard_map/ppermute | solution.py:636
  604.0 9.5 convolution_convert_fusion.2
  639.6 18.1 %attend_backward.1 = (f32[1024,512]{1,0:T(8,128)}, f32[1024,512]{1,0:T(8,128)}, bf16[1024,512]{1,0:T(8,128)(2,1)}, f32[1024,1]{1,0:T(8,128)}, f32[1024,1]{1,0:T(...) custom-call(f32[1024,1536]{1,0:T(8,128)} %copy-done.3, f32[1024,1536]{1,0:T(8,128)} %copy-done.3, f32[1024,1]{1,0:T(8,128)} %copy.71.qs_ref, ...), custom_call_target="tpu_custom_call" | custom-call | flops 5368709120 | bytes 20971520 | tf_op jit(solution)/shard_map/attend_backward/pallas_call | solution.py:180
  660.3 12.1 %all-reduce = (f32[1024]{0:T(1024)S(1)}, f32[1024]{0:T(1024)S(1)}) all-reduce(f32[1024]{0:T(1024)S(1)} %reduce.1, f32[1024]{0:T(1024)S(1)} %reduce), channel_id=1, replica_groups=mesh['dp'=2,'row'=4,'col'=4] {'col'}, use_global_device_ids=true, to_apply=%region_5.6 | all-reduce | flops 2048 | bytes 16384 | tf_op jit(solution)/shard_map/psum | solution.py:873
  687.0 16.2 %collective-permute-done.46 = bf16[256,2048]{1,0:T(8,128)(2,1)S(1)} collective-permute-done((bf16[256,2048]{1,0:T(8,128)(2,1)S(1)}, bf16[256,2048]{1,0:T(8,128)(2,1)S(1)}, u32[]{:S(2)}, u32[]{:S(2)}) %collective-permute-start.46) | collective-permute-done | bytes 1048608 | tf_op jit(solution)/shard_map/ppermute | solution.py:640
  709.4 10.6 %add_convert_fusion.2 = bf16[2048,1024]{1,0:T(8,128)(2,1)} fusion(bf16[2048,1024]{1,0:T(8,128)(2,1)} %collective-permute-done.58, bf16[1024,2048]{1,0:T(8,128)(2,1)} %get-tuple-element.303, bf16[1024,2048]{1,0:T(8,128)(2,1)} %get-tuple-element.304, s32[]{:T(128)S(6)} %select_n.227), kind=kOutput, calls=%fused_computation.2 | convolution fusion | flops 4301258752 | bytes 14680068 | tf_op jit(solution)/shard_map/dot_general | solution.py:35
  782.2 15.9 %collective-permute-done.48 = bf16[256,2048]{1,0:T(8,128)(2,1)S(1)} collective-permute-done((bf16[256,2048]{1,0:T(8,128)(2,1)S(1)}, bf16[256,2048]{1,0:T(8,128)(2,1)S(1)}, u32[]{:S(2)}, u32[]{:S(2)}) %collective-permute-start.48) | collective-permute-done | bytes 1048608 | tf_op jit(solution)/shard_map/ppermute | solution.py:640
  819.9 15.8 %collective-permute-done.50 = bf16[256,2048]{1,0:T(8,128)(2,1)S(1)} collective-permute-done((bf16[256,2048]{1,0:T(8,128)(2,1)S(1)}, bf16[256,2048]{1,0:T(8,128)(2,1)S(1)}, u32[]{:S(2)}, u32[]{:S(2)}) %collective-permute-start.50) | collective-permute-done | bytes 1048608 | tf_op jit(solution)/shard_map/ppermute | solution.py:640
  881.9 18.9 %collective-permute-done.56.refs_0_.refs_1_ = bf16[256,2048]{1,0:T(8,128)(2,1)S(1)} collective-permute-done((bf16[256,2048]{1,0:T(8,128)(2,1)}, bf16[256,2048]{1,0:T(8,128)(2,1)S(1)}, u32[]{:S(2)}, u32[]{:S(2)}) %collective-permute-start.56) | collective-permute-done | bytes 1048608 | tf_op jit(solution)/shard_map/ppermute | solution.py:636
  925.5 26.6 %reduce-scatter.14.cloned.1.call-done = bf16[512,768]{1,0:T(8,128)(2,1)} async-done(((bf16[2048,768]{1,0:T(8,128)(2,1)}), bf16[512,768]{1,0:T(8,128)(2,1)}) %reduce-scatter.14.cloned.1.call-update) | async-done | bytes 786448 | tf_op jit(solution)/shard_map/reduce_scatter | solution.py:705
  (388 shorter events, 387.2 us)
Async XLA Ops:
  7.2 80.3 %all-gather.3.cloned.1.call-start = ((), (), s32[]{:S(2)}) async-start(), calls=%async_computation.5 | async-start | bytes 7077888 | tf_op jit(solution)/shard_map/all_gather | solution.py:632
  9.5 237.9 %all-gather.5.cloned.1.call-start = ((), (), s32[]{:S(2)}) async-start(), calls=%async_computation.6 | async-start | bytes 18874368 | tf_op jit(solution)/shard_map/all_gather | solution.py:632
  12.7 858.2 %reduce-scatter.12.cloned.1.call-start = ((), (), s32[]{:S(2)}) async-start(), calls=%async_computation.10 | async-start | bytes 1310720 | tf_op jit(solution)/shard_map/reduce_scatter | solution.py:705
  68.5 67.5 %collective-permute-start.13 = (bf16[256,2048]{1,0:T(8,128)(2,1)}, bf16[256,2048]{1,0:T(8,128)(2,1)}, u32[]{:S(2)}, u32[]{:S(2)}) collective-permute-start(bf16[256,2048]{1,0:T(8,128)(2,1)} %collective-permute-done.12), channel_id=1, source_target_pairs={{2,3},{6,7},{10,11},{14,15},{18,19},{22,23},{26,27},{30,31}} | collective-permute-start | bytes 3145736 | tf_op jit(solution)/shard_map/ppermute | solution.py:635
  86.2 54.6 %collective-permute-start.15 = (bf16[256,2048]{1,0:T(8,128)(2,1)}, bf16[256,2048]{1,0:T(8,128)(2,1)}, u32[]{:S(2)}, u32[]{:S(2)}) collective-permute-start(bf16[256,2048]{1,0:T(8,128)(2,1)} %collective-permute-done.14), channel_id=1, source_target_pairs={{1,0},{5,4},{9,8},{13,12},{17,16},{21,20},{25,24},{29,28}} | collective-permute-start | bytes 3145736 | tf_op jit(solution)/shard_map/ppermute | solution.py:636
  134.0 40.3 %collective-permute-start.17 = (bf16[1024,512]{1,0:T(8,128)(2,1)S(1)}, bf16[1024,512]{1,0:T(8,128)(2,1)}, u32[]{:S(2)}, u32[]{:S(2)}) collective-permute-start(bf16[1024,512]{1,0:T(8,128)(2,1)S(1)} %constant_dynamic-slice_fusion.10), channel_id=1, source_target_pairs={{0,4},{4,0},{8,12},{12,8},{1,5},{5,1},{9,13},{13,9},{2,6},{6,2},{1... | collective-permute-start | bytes 3145736 | tf_op jit(solution)/shard_map/ppermute | solution.py:713
  136.1 38.3 %collective-permute-start.18 = (bf16[1024,512]{1,0:T(8,128)(2,1)S(1)}, bf16[1024,512]{1,0:T(8,128)(2,1)}, u32[]{:S(2)}, u32[]{:S(2)}) collective-permute-start(bf16[1024,512]{1,0:T(8,128)(2,1)S(1)} %constant_dynamic-slice_fusion.10), channel_id=1, source_target_pairs={{0,8},{8,0},{4,12},{12,4},{1,9},{9,1},{5,13},{13,5},{2,10},{10,2},... | collective-permute-start | bytes 3145736 | tf_op jit(solution)/shard_map/ppermute | solution.py:713
  145.0 102.3 %collective-permute-start.16 = (bf16[1024,2048]{1,0:T(8,128)(2,1)}, bf16[1024,2048]{1,0:T(8,128)(2,1)}, u32[]{:S(2)}, u32[]{:S(2)}) collective-permute-start(bf16[1024,2048]{1,0:T(8,128)(2,1)} %pad_maximum_fusion.refs_7_.wo_own_ref), channel_id=1, source_target_pairs={{0,16},{16,0},{1,17},{17,1},{2,18},{18,2},{3,19},{19,3},{4,20},{20... | collective-permute-start | bytes 12582920 | tf_op jit(solution)/shard_map/ppermute | solution.py:789
  190.2 57.1 %collective-permute-start.21 = (bf16[4,1024,512]{2,1,0:T(8,128)(2,1)}, bf16[4,1024,512]{2,1,0:T(8,128)(2,1)}, u32[]{:S(2)}, u32[]{:S(2)}) collective-permute-start(bf16[4,1024,512]{2,1,0:T(8,128)(2,1)} %bitcast_dynamic-update-slice_fusion.3.refs_13_.wd_own_ref), channel_id=1, source_target_pairs={{0,16},{16,0},{1,17},{17,1},{2,18},{18,2},{3,19},{19,3},{4,20},{20... | collective-permute-start | bytes 12582920 | tf_op jit(solution)/shard_map/ppermute | solution.py:738
  191.0 29.6 %collective-permute-start.4 = (bf16[1024,512]{1,0:T(8,128)(2,1)S(1)}, bf16[1024,512]{1,0:T(8,128)(2,1)}, u32[]{:S(2)}, u32[]{:S(2)}) collective-permute-start(bf16[1024,512]{1,0:T(8,128)(2,1)S(1)} %collective-permute-done.3.refs_4_), channel_id=1, source_target_pairs={{1,0},{2,1},{5,4},{6,5},{9,8},{10,9},{13,12},{14,13},{17,16},{18,1... | collective-permute-start | bytes 3145736 | tf_op jit(solution)/shard_map/ppermute | solution.py:636
  192.3 30.2 %collective-permute-start.2 = (bf16[1024,512]{1,0:T(8,128)(2,1)S(1)}, bf16[1024,512]{1,0:T(8,128)(2,1)S(1)}, u32[]{:S(2)}, u32[]{:S(2)}) collective-permute-start(bf16[1024,512]{1,0:T(8,128)(2,1)S(1)} %collective-permute-done.1.refs_2_), channel_id=1, source_target_pairs={{2,3},{6,7},{10,11},{14,15},{18,19},{22,23},{26,27},{30,31}} | collective-permute-start | bytes 3145736 | tf_op jit(solution)/shard_map/ppermute | solution.py:635
  220.5 26.8 %collective-permute-start.5 = (bf16[1024,512]{1,0:T(8,128)(2,1)}, bf16[1024,512]{1,0:T(8,128)(2,1)S(1)}, u32[]{:S(2)}, u32[]{:S(2)}) collective-permute-start(bf16[1024,512]{1,0:T(8,128)(2,1)} %collective-permute-done.4.refs_5_), channel_id=1, source_target_pairs={{1,0},{5,4},{9,8},{13,12},{17,16},{21,20},{25,24},{29,28}} | collective-permute-start | bytes 3145736 | tf_op jit(solution)/shard_map/ppermute | solution.py:636
  301.3 27.3 %collective-permute-start.24 = (bf16[256,2048]{1,0:T(8,128)(2,1)}, bf16[256,2048]{1,0:T(8,128)(2,1)S(1)}, u32[]{:S(2)}, u32[]{:S(2)}) collective-permute-start(bf16[256,2048]{1,0:T(8,128)(2,1)} %get-tuple-element.408), channel_id=1, source_target_pairs={{0,1},{1,2},{4,5},{5,6},{8,9},{9,10},{12,13},{13,14},{16,17},{17,1... | collective-permute-start | bytes 3145736 | tf_op jit(solution)/shard_map/ppermute | solution.py:640
  331.3 27.4 %collective-permute-start.26 = (bf16[256,2048]{1,0:T(8,128)(2,1)}, bf16[256,2048]{1,0:T(8,128)(2,1)S(1)}, u32[]{:S(2)}, u32[]{:S(2)}) collective-permute-start(bf16[256,2048]{1,0:T(8,128)(2,1)} %get-tuple-element.406), channel_id=1, source_target_pairs={{0,1},{1,2},{2,3},{4,5},{5,6},{6,7},{8,9},{9,10},{10,11},{12,13},{... | collective-permute-start | bytes 3145736 | tf_op jit(solution)/shard_map/ppermute | solution.py:640
  411.2 43.7 %collective-permute-start.32 = (bf16[256,2048]{1,0:T(8,128)(2,1)S(1)}, bf16[256,2048]{1,0:T(8,128)(2,1)S(1)}, u32[]{:S(2)}, u32[]{:S(2)}) collective-permute-start(bf16[256,2048]{1,0:T(8,128)(2,1)S(1)} %collective-permute-done.29.refs_3_.refs_2_), channel_id=1, source_target_pairs={{2,3},{6,7},{10,11},{14,15},{18,19},{22,23},{26,27},{30,31}} | collective-permute-start | bytes 3145736 | tf_op jit(solution)/shard_map/ppermute | solution.py:635
  413.5 41.5 %collective-permute-start.33 = (bf16[256,2048]{1,0:T(8,128)(2,1)}, bf16[256,2048]{1,0:T(8,128)(2,1)S(1)}, u32[]{:S(2)}, u32[]{:S(2)}) collective-permute-start(bf16[256,2048]{1,0:T(8,128)(2,1)} %collective-permute-done.31.refs_0_.refs_1_), channel_id=1, source_target_pairs={{1,0},{5,4},{9,8},{13,12},{17,16},{21,20},{25,24},{29,28}} | collective-permute-start | bytes 3145736 | tf_op jit(solution)/shard_map/ppermute | solution.py:636
  580.4 52.7 %collective-permute-start.44 = (bf16[256,2048]{1,0:T(8,128)(2,1)S(1)}, bf16[256,2048]{1,0:T(8,128)(2,1)}, u32[]{:S(2)}, u32[]{:S(2)}) collective-permute-start(bf16[256,2048]{1,0:T(8,128)(2,1)S(1)} %collective-permute-done.41.refs_3_.refs_2_), channel_id=1, source_target_pairs={{2,3},{6,7},{10,11},{14,15},{18,19},{22,23},{26,27},{30,31}} | collective-permute-start | bytes 3145736 | tf_op jit(solution)/shard_map/ppermute | solution.py:635
  602.4 30.8 %collective-permute-start.45 = (bf16[256,2048]{1,0:T(8,128)(2,1)}, bf16[256,2048]{1,0:T(8,128)(2,1)}, u32[]{:S(2)}, u32[]{:S(2)}) collective-permute-start(bf16[256,2048]{1,0:T(8,128)(2,1)} %collective-permute-done.43.refs_0_.refs_1_), channel_id=1, source_target_pairs={{1,0},{5,4},{9,8},{13,12},{17,16},{21,20},{25,24},{29,28}} | collective-permute-start | bytes 3145736 | tf_op jit(solution)/shard_map/ppermute | solution.py:636
  613.6 95.8 %collective-permute-start.58 = (bf16[2048,1024]{1,0:T(8,128)(2,1)}, bf16[2048,1024]{1,0:T(8,128)(2,1)}, u32[]{:S(2)}, u32[]{:S(2)}) collective-permute-start(bf16[2048,1024]{1,0:T(8,128)(2,1)} %convolution_convert_fusion.2), channel_id=1, source_target_pairs={{0,16},{16,0},{1,17},{17,1},{2,18},{18,2},{3,19},{19,3},{4,20},{20... | collective-permute-start | bytes 12582920 | tf_op jit(solution)/shard_map/ppermute | solution.py:701
  709.1 163.9 %reduce-scatter.6.cloned.1.call-start = ((), (), s32[]{:S(2)}) async-start(), calls=%async_computation.7 | async-start | bytes 5242880 | tf_op jit(solution)/shard_map/reduce_scatter | solution.py:705
  720.0 158.6 %reduce-scatter.8.cloned.1.call-start = ((), (), s32[]{:S(2)}) async-start(), calls=%async_computation.8 | async-start | bytes 5242880 | tf_op jit(solution)/shard_map/reduce_scatter | solution.py:705
  741.5 163.7 %reduce-scatter.10.cloned.1.call-start = ((), (), s32[]{:S(2)}) async-start(), calls=%async_computation.9 | async-start | bytes 5242880 | tf_op jit(solution)/shard_map/reduce_scatter | solution.py:705
  763.3 188.9 %reduce-scatter.14.cloned.1.call-start = ((), (), s32[]{:S(2)}) async-start(), calls=%async_computation.11 | async-start | bytes 3932160 | tf_op jit(solution)/shard_map/reduce_scatter | solution.py:705
  770.5 29.2 %collective-permute-start.68 = (bf16[2048,768]{1,0:T(8,128)(2,1)S(1)}, bf16[2048,768]{1,0:T(8,128)(2,1)S(1)}, u32[]{:S(2)}, u32[]{:S(2)}) collective-permute-start(bf16[2048,768]{1,0:T(8,128)(2,1)S(1)} %convolution_convert_fusion.3), channel_id=1, source_target_pairs={{0,16},{16,0},{1,17},{17,1},{2,18},{18,2},{3,19},{19,3},{4,20},{20... | collective-permute-start | bytes 9437192 | tf_op jit(solution)/shard_map/ppermute | solution.py:701
  770.8 27.2 %collective-permute-start.48 = (bf16[256,2048]{1,0:T(8,128)(2,1)S(1)}, bf16[256,2048]{1,0:T(8,128)(2,1)S(1)}, u32[]{:S(2)}, u32[]{:S(2)}) collective-permute-start(bf16[256,2048]{1,0:T(8,128)(2,1)S(1)} %copy-done.61), channel_id=1, source_target_pairs={{0,1},{1,2},{4,5},{5,6},{8,9},{9,10},{12,13},{13,14},{16,17},{17,1... | collective-permute-start | bytes 3145736 | tf_op jit(solution)/shard_map/ppermute | solution.py:640
  806.1 29.6 %collective-permute-start.50 = (bf16[256,2048]{1,0:T(8,128)(2,1)S(1)}, bf16[256,2048]{1,0:T(8,128)(2,1)S(1)}, u32[]{:S(2)}, u32[]{:S(2)}) collective-permute-start(bf16[256,2048]{1,0:T(8,128)(2,1)S(1)} %copy-done.38), channel_id=1, source_target_pairs={{0,1},{1,2},{2,3},{4,5},{5,6},{6,7},{8,9},{9,10},{10,11},{12,13},{... | collective-permute-start | bytes 3145736 | tf_op jit(solution)/shard_map/ppermute | solution.py:640
  842.1 28.8 %collective-permute-start.52 = (bf16[256,2048]{1,0:T(8,128)(2,1)S(1)}, bf16[256,2048]{1,0:T(8,128)(2,1)}, u32[]{:S(2)}, u32[]{:S(2)}) collective-permute-start(bf16[256,2048]{1,0:T(8,128)(2,1)S(1)} %add_convert_fusion.4.refs_0_), channel_id=1, source_target_pairs={{0,1},{1,2},{2,3},{4,5},{5,6},{6,7},{8,9},{9,10},{10,11},{12,13},{... | collective-permute-start | bytes 3145736 | tf_op jit(solution)/shard_map/ppermute | solution.py:635
  871.7 29.1 %collective-permute-start.56 = (bf16[256,2048]{1,0:T(8,128)(2,1)}, bf16[256,2048]{1,0:T(8,128)(2,1)S(1)}, u32[]{:S(2)}, u32[]{:S(2)}) collective-permute-start(bf16[256,2048]{1,0:T(8,128)(2,1)} %collective-permute-done.55.refs_0_.refs_1_), channel_id=1, source_target_pairs={{1,0},{2,1},{5,4},{6,5},{9,8},{10,9},{13,12},{14,13},{17,16},{18,1... | collective-permute-start | bytes 3145736 | tf_op jit(solution)/shard_map/ppermute | solution.py:636
  873.0 32.2 %collective-permute-start.59 = (bf16[512,1024]{1,0:T(8,128)(2,1)}, bf16[512,1024]{1,0:T(8,128)(2,1)}, u32[]{:S(2)}, u32[]{:S(2)}) collective-permute-start(bf16[512,1024]{1,0:T(8,128)(2,1)} %reduce-scatter.6.cloned.1.call-done), channel_id=1, source_target_pairs={{0,16},{16,0},{1,17},{17,1},{2,18},{18,2},{3,19},{19,3},{4,20},{20... | collective-permute-start | bytes 3145736 | tf_op jit(solution)/shard_map/ppermute | solution.py:695
  878.7 36.1 %collective-permute-start.61 = (bf16[512,1024]{1,0:T(8,128)(2,1)}, bf16[512,1024]{1,0:T(8,128)(2,1)}, u32[]{:S(2)}, u32[]{:S(2)}) collective-permute-start(bf16[512,1024]{1,0:T(8,128)(2,1)} %reduce-scatter.8.cloned.1.call-done), channel_id=1, source_target_pairs={{0,16},{16,0},{1,17},{17,1},{2,18},{18,2},{3,19},{19,3},{4,20},{20... | collective-permute-start | bytes 3145736 | tf_op jit(solution)/shard_map/ppermute | solution.py:695
  880.3 86.4 %collective-permute-start.54 = (bf16[256,2048]{1,0:T(8,128)(2,1)S(1)}, bf16[256,2048]{1,0:T(8,128)(2,1)}, u32[]{:S(2)}, u32[]{:S(2)}) collective-permute-start(bf16[256,2048]{1,0:T(8,128)(2,1)S(1)} %collective-permute-done.53.refs_3_.refs_2_), channel_id=1, source_target_pairs={{2,3},{6,7},{10,11},{14,15},{18,19},{22,23},{26,27},{30,31}} | collective-permute-start | bytes 3145736 | tf_op jit(solution)/shard_map/ppermute | solution.py:635
  900.8 65.8 %collective-permute-start.57 = (bf16[256,2048]{1,0:T(8,128)(2,1)S(1)}, bf16[256,2048]{1,0:T(8,128)(2,1)}, u32[]{:S(2)}, u32[]{:S(2)}) collective-permute-start(bf16[256,2048]{1,0:T(8,128)(2,1)S(1)} %collective-permute-done.56.refs_0_.refs_1_), channel_id=1, source_target_pairs={{1,0},{5,4},{9,8},{13,12},{17,16},{21,20},{25,24},{29,28}} | collective-permute-start | bytes 3145736 | tf_op jit(solution)/shard_map/ppermute | solution.py:636
  (112 other events, 2088.2 us)
Sparse Core Ops, SparseCore 0:
  10.5 51.5 all-gather.2
  64.5 107.9 all-gather.4
  709.2 27.4 reduce-scatter.11
  740.1 52.5 reduce-scatter.5
  796.1 52.5 reduce-scatter.7
  852.1 53.0 reduce-scatter.9
  908.2 43.8 reduce-scatter.13

commit v14 on v13

--- a/solution.py
+++ b/solution.py
@@ -559,9 +559,9 @@
         functools.partial(place_rows_kernel, choices=len(rows_in)),
         grid_spec=pltpu.PrefetchScalarGridSpec(
             num_scalar_prefetch=1,
-            grid=(4,),
+            grid=(2,),
             in_specs=[pl.BlockSpec(memory_space=pl.ANY)] * (len(rows_in) + len(before)),
-            out_specs=pl.BlockSpec((chunk // 4, width), lambda j, idx: (4 * idx[0] + j, 0)),
+            out_specs=pl.BlockSpec((chunk // 2, width), lambda j, idx: (2 * idx[0] + j, 0)),
             scratch_shapes=[pltpu.VMEM((chunk, width), BF16), pltpu.SemaphoreType.DMA(())],
         ),
         out_shape=jax.ShapeDtypeStruct((tokens, width), dtype),
@@ -679,10 +679,8 @@
         first = make(0, ())
         up, down = sum_step(first, first, 1)
         second = at(1, first)
-        up = jnp.where(col == 0, second, first) + up
-        down = jnp.where(col == 3, second, first) + down
-        gate = (up, down)
-        up, down = sum_step(up, down, 2)
+        gate = jnp.where((col == 0) | (col == 3), second, first) + (up + down)
+        up, down = sum_step(gate, gate, 2)
         third = at(2, gate)
         up = jnp.where(col == 1, second, third) + up
         down = jnp.where(col == 2, second, third) + down

time: 988 us -> 985 us (level)
  no operation moved by 1% of the time
where the time goes in v14:
time: 985 us; the launch traced here: 975 us
  waiting for transfers between devices  372 us (38%)
  Pallas kernels  271 us (28%)
  starting transfers between devices  110 us (11%)
  matrix products  88.6 us (9%)
  other arithmetic  56.9 us (6%)
  local copies, waits for them, and re-layouts  35.9 us (4%)
  blocking collectives  24.2 us (2%)
  between operations  16.2 us (2%)
    ppermute x15, waiting for transfers between devices, line_step(): lax.ppermute(from_right, 'col', [(i + 1, i) for i in range(cols - step)])  128 us
    ppermute x9, waiting for transfers between devices, sum_step(): up = lax.ppermute(up, 'col', [(i, i + 1) for i in range(step)])  96.7 us
    pallas_call x4, Pallas kernels, forward_chunk(): pl.pallas_call(functools.partial(forward_chunk_kernel, out_steps=out_step...  93.1 us
    pallas_call x4, Pallas kernels, backward_chunk(): pl.pallas_call(functools.partial(backward_chunk_kernel, tiles=tiles, choi...  80.2 us
    dot_general x10, matrix products, left_transposed(): lax.dot_general(left_mat, right_mat, (((0,), (0,)), ((), ())), preferred_...  63 us
    ppermute x15, waiting for transfers between devices, line_step(): lax.ppermute(from_left, 'col', [(i, i + 1) for i in range(step - 1, cols...  53.5 us
    ppermute x9, starting transfers between devices, sum_step(): up = lax.ppermute(up, 'col', [(i, i + 1) for i in range(step)])  37.8 us
    reduce_scatter x5, waiting for transfers between devices, sum_kept(): lax.psum_scatter(total, 'row', scatter_dimension=0, tiled=True)  30 us
  transfers between devices with their start and end apart: 80, of which 34 were waited for; matrix products, arithmetic and copies ran while one was open for 17% of the time, Pallas kernels for 23%

profile of v14, /device:TPU:0, one launch (start us, length us, event | category | flops | bytes accessed | tf_op | source)
XLA Modules:
  0.0 974.9 jit_solution(13354647053981791903)
XLA Ops:
  40.8 16.8 %collective-permute-done.11 = bf16[256,2048]{1,0:T(8,128)(2,1)} collective-permute-done((bf16[256,2048]{1,0:T(8,128)(2,1)}, bf16[256,2048]{1,0:T(8,128)(2,1)}, u32[]{:S(2)}, u32[]{:S(2)}) %collective-permute-start.11) | collective-permute-done | bytes 1048608 | tf_op jit(solution)/shard_map/ppermute | solution.py:635
  70.2 16.0 %collective-permute-done.14 = bf16[256,2048]{1,0:T(8,128)(2,1)} collective-permute-done((bf16[256,2048]{1,0:T(8,128)(2,1)}, bf16[256,2048]{1,0:T(8,128)(2,1)}, u32[]{:S(2)}, u32[]{:S(2)}) %collective-permute-start.14) | collective-permute-done | bytes 1048608 | tf_op jit(solution)/shard_map/ppermute | solution.py:636
  87.5 10.2 %convolution_bitcast_fusion.q_ref.k_ref.v_ref = f32[1024,1536]{1,0:T(8,128)S(1)} fusion(bf16[1024,2048]{1,0:T(8,128)(2,1)} %x_ref.7, bf16[2048,1536]{1,0:T(8,128)(2,1)} %all-gather.3.cloned.1.call-done), kind=kOutput, calls=%fused_computation.4 | convolution fusion | flops 6442450944 | bytes 16777216 | tf_op jit(solution)/shard_map/dot_general | solution.py:25
  100.7 12.1 %all-reduce.1 = (f32[1024]{0:T(1024)S(1)}, f32[1024]{0:T(1024)S(1)}) all-reduce(f32[1024]{0:T(1024)S(1)} %get-tuple-element.378, f32[1024]{0:T(1024)S(1)} %get-tuple-element.377), channel_id=1, replica_groups=mesh['dp'=2,'row'=4,'col'=4] {'col'}, use_global_device_ids=true, to_apply=%region_1.2 | all-reduce | flops 2048 | bytes 16384 | tf_op jit(solution)/shard_map/psum | solution.py:765
  115.0 16.1 %attend_forward.1 = (bf16[1024,512]{1,0:T(8,128)(2,1)}, bf16[1024,512]{1,0:T(8,128)(2,1)}, bf16[1024,512]{1,0:T(8,128)(2,1)}, bf16[1024,512]{1,0:T(8,128)(2,1)}, f32[4,1024,1]{2,1,0:T(8,128)}) custom-call(f32[1024,1536]{1,0:T(8,128)} %copy-done.3, f32[1024,1536]{1,0:T(8,128)} %copy-done.3, f32[1024,1536]{1,0:T(8,128)} %copy-done.3, f32[1024,1]{1,0:T(8,128)} %copy.71.qs_ref, ...), custom_call_target="tpu_custom_call" | custom-call | flops 2147483648 | bytes 10485760 | tf_op jit(solution)/shard_map/attend_forward/pallas_call | solution.py:156
  152.7 21.6 %collective-permute-done.17 = bf16[1024,512]{1,0:T(8,128)(2,1)} collective-permute-done((bf16[1024,512]{1,0:T(8,128)(2,1)S(1)}, bf16[1024,512]{1,0:T(8,128)(2,1)}, u32[]{:S(2)}, u32[]{:S(2)}) %collective-permute-start.17) | collective-permute-done | bytes 1048608 | tf_op jit(solution)/shard_map/ppermute | solution.py:711
  193.0 27.5 %collective-permute-done.4.refs_5_ = bf16[1024,512]{1,0:T(8,128)(2,1)} collective-permute-done((bf16[1024,512]{1,0:T(8,128)(2,1)S(1)}, bf16[1024,512]{1,0:T(8,128)(2,1)}, u32[]{:S(2)}, u32[]{:S(2)}) %collective-permute-start.4) | collective-permute-done | bytes 1048608 | tf_op jit(solution)/shard_map/ppermute | solution.py:636
  222.5 24.8 %collective-permute-done.5.refs_6_ = bf16[1024,512]{1,0:T(8,128)(2,1)S(1)} collective-permute-done((bf16[1024,512]{1,0:T(8,128)(2,1)}, bf16[1024,512]{1,0:T(8,128)(2,1)S(1)}, u32[]{:S(2)}, u32[]{:S(2)}) %collective-permute-start.5) | collective-permute-done | bytes 1048608 | tf_op jit(solution)/shard_map/ppermute | solution.py:636
  248.3 23.2 %forward_chunk.4 = (bf16[1024,2048]{1,0:T(8,128)(2,1)}, f32[1024,1]{1,0:T(8,128)}, bf16[1024,2048]{1,0:T(8,128)(2,1)}, bf16[1024,2048]{1,0:T(8,128)(2,1)}, bf16[...) custom-call(s32[3]{0:T(128)} %get-tuple-element.433.idx_ref, ...), custom_call_target="tpu_custom_call" | custom-call | flops 8589934592 | bytes 33554432 | tf_op jit(solution)/shard_map/forward_chunk/pallas_call | solution.py:309
  274.1 23.4 %forward_chunk.5 = (bf16[1024,2048]{1,0:T(8,128)(2,1)}, f32[1024,1]{1,0:T(8,128)}, bf16[1024,2048]{1,0:T(8,128)(2,1)}, bf16[1024,2048]{1,0:T(8,128)(2,1)}, bf16[...) custom-call(s32[3]{0:T(128)} %get-tuple-element.434.idx_ref, ...), custom_call_target="tpu_custom_call", output_to_operand_aliasing={{0}: (16, {}), {1}: (17, {}), {2}: (18, {}), {3}: (19, {}),... | custom-call | flops 8589934592 | bytes 33554432 | tf_op jit(solution)/shard_map/forward_chunk/pallas_call | solution.py:309
  303.9 23.3 %forward_chunk.6 = (bf16[1024,2048]{1,0:T(8,128)(2,1)}, f32[1024,1]{1,0:T(8,128)}, bf16[1024,2048]{1,0:T(8,128)(2,1)}, bf16[1024,2048]{1,0:T(8,128)(2,1)}, bf16[...) custom-call(s32[3]{0:T(128)} %pad_add_fusion.1.idx_ref, ...), custom_call_target="tpu_custom_call", output_to_operand_aliasing={{0}: (16, {}), {1}: (17, {}), {2}: (18, {}), {3}: (19, {}),... | custom-call | flops 8589934592 | bytes 33554432 | tf_op jit(solution)/shard_map/forward_chunk/pallas_call | solution.py:309
  334.2 23.2 %forward_chunk.7 = (bf16[1024,2048]{1,0:T(8,128)(2,1)}, f32[1024,1]{1,0:T(8,128)}, bf16[1024,2048]{1,0:T(8,128)(2,1)}, bf16[1024,2048]{1,0:T(8,128)(2,1)}, bf16[...) custom-call(s32[3]{0:T(128)} %pad_add_fusion.idx_ref, ...), custom_call_target="tpu_custom_call", output_to_operand_aliasing={{0}: (16, {}), {1}: (17, {}), {2}: (18, {}), {3}: (19, {}),... | custom-call | flops 8589934592 | bytes 33554432 | tf_op jit(solution)/shard_map/forward_chunk/pallas_call | solution.py:309
  365.7 18.8 %collective-permute-done.28.refs_1_.refs_2_ = bf16[256,2048]{1,0:T(8,128)(2,1)S(1)} collective-permute-done((bf16[256,2048]{1,0:T(8,128)(2,1)S(1)}, bf16[256,2048]{1,0:T(8,128)(2,1)S(1)}, u32[]{:S(2)}, u32[]{:S(2)}) %collective-permute-start.28) | collective-permute-done | bytes 1048608 | tf_op jit(solution)/shard_map/ppermute | solution.py:635
  390.0 19.9 %backward_chunk.4 = (bf16[1024,2048]{1,0:T(8,128)(2,1)}, bf16[1024,2048]{1,0:T(8,128)(2,1)}, bf16[1024,2048]{1,0:T(8,128)(2,1)}, bf16[256,2048]{1,0:T(8,128)(2,1)}, f32[1,2048]{1,0:T(1,128)}) custom-call(s32[3]{0:T(128)} %pad_add_fusion.idx_ref, bf16[1024,2048]{1,0:T(8,128)(2,1)} %grad_ref.15, f32[1,2048]{1,0:T(1,128)} %bitcast.96, ...), custom_call_target="tpu_custom_call" | custom-call | flops 6442450944 | bytes 25165824 | tf_op jit(solution)/shard_map/backward_chunk/pallas_call | solution.py:407
  413.7 20.0 %backward_chunk.5 = (bf16[1024,2048]{1,0:T(8,128)(2,1)}, bf16[1024,2048]{1,0:T(8,128)(2,1)}, bf16[1024,2048]{1,0:T(8,128)(2,1)}, bf16[256,2048]{1,0:T(8,128)(2,1)}, f32[1,2048]{1,0:T(1,128)}) custom-call(s32[3]{0:T(128)} %pad_add_fusion.1.idx_ref, bf16[1024,2048]{1,0:T(8,128)(2,1)} %grad_ref.15, ...), custom_call_target="tpu_custom_call", output_to_operand_aliasing={{0}: (11, {}), {1}: (12, {}), {2}: (13, {})} | custom-call | flops 6442450944 | bytes 25165824 | tf_op jit(solution)/shard_map/backward_chunk/pallas_call | solution.py:407
  433.7 20.0 %backward_chunk.6 = (bf16[1024,2048]{1,0:T(8,128)(2,1)}, bf16[1024,2048]{1,0:T(8,128)(2,1)}, bf16[1024,2048]{1,0:T(8,128)(2,1)}, bf16[256,2048]{1,0:T(8,128)(2,1)}, f32[1,2048]{1,0:T(1,128)}) custom-call(s32[3]{0:T(128)} %get-tuple-element.434.idx_ref, bf16[1024,2048]{1,0:T(8,128)(2,1)} %grad_ref.15, ...), custom_call_target="tpu_custom_call", output_to_operand_aliasing={{0}: (13, {}), {1}: (14, {}), {2}: (15, {})} | custom-call | flops 6442450944 | bytes 25165824 | tf_op jit(solution)/shard_map/backward_chunk/pallas_call | solution.py:407
  455.0 20.4 %backward_chunk.7 = (bf16[1024,2048]{1,0:T(8,128)(2,1)}, bf16[1024,2048]{1,0:T(8,128)(2,1)}, bf16[1024,2048]{1,0:T(8,128)(2,1)}, bf16[256,2048]{1,0:T(8,128)(2,1)}, f32[1,2048]{1,0:T(1,128)}) custom-call(s32[3]{0:T(128)} %get-tuple-element.433.idx_ref, bf16[1024,2048]{1,0:T(8,128)(2,1)} %grad_ref.15, ...), custom_call_target="tpu_custom_call", output_to_operand_aliasing={{0}: (13, {}), {1}: (14, {}), {2}: (15, {})} | custom-call | flops 6442450944 | bytes 25165824 | tf_op jit(solution)/shard_map/backward_chunk/pallas_call | solution.py:407
  481.0 17.4 %collective-permute-done.34 = bf16[256,2048]{1,0:T(8,128)(2,1)S(1)} collective-permute-done((bf16[256,2048]{1,0:T(8,128)(2,1)}, bf16[256,2048]{1,0:T(8,128)(2,1)S(1)}, u32[]{:S(2)}, u32[]{:S(2)}) %collective-permute-start.34) | collective-permute-done | bytes 1048608 | tf_op jit(solution)/shard_map/ppermute | solution.py:640
  505.1 16.3 %collective-permute-done.36 = bf16[256,2048]{1,0:T(8,128)(2,1)S(1)} collective-permute-done((bf16[256,2048]{1,0:T(8,128)(2,1)S(1)}, bf16[256,2048]{1,0:T(8,128)(2,1)S(1)}, u32[]{:S(2)}, u32[]{:S(2)}) %collective-permute-start.36) | collective-permute-done | bytes 1048608 | tf_op jit(solution)/shard_map/ppermute | solution.py:640
  521.7 9.3 collective-permute-start.37
  532.3 15.1 %collective-permute-done.37 = bf16[256,2048]{1,0:T(8,128)(2,1)S(1)} collective-permute-done((bf16[256,2048]{1,0:T(8,128)(2,1)S(1)}, bf16[256,2048]{1,0:T(8,128)(2,1)S(1)}, u32[]{:S(2)}, u32[]{:S(2)}) %collective-permute-start.37) | collective-permute-done | bytes 1048608 | tf_op jit(solution)/shard_map/ppermute | solution.py:640
  555.7 14.2 %collective-permute-done.40.refs_1_.refs_2_ = bf16[256,2048]{1,0:T(8,128)(2,1)S(1)} collective-permute-done((bf16[256,2048]{1,0:T(8,128)(2,1)S(1)}, bf16[256,2048]{1,0:T(8,128)(2,1)S(1)}, u32[]{:S(2)}, u32[]{:S(2)}) %collective-permute-start.40) | collective-permute-done | bytes 1048608 | tf_op jit(solution)/shard_map/ppermute | solution.py:635
  580.5 20.3 %collective-permute-done.43.refs_0_.refs_1_ = bf16[256,2048]{1,0:T(8,128)(2,1)} collective-permute-done((bf16[256,2048]{1,0:T(8,128)(2,1)}, bf16[256,2048]{1,0:T(8,128)(2,1)}, u32[]{:S(2)}, u32[]{:S(2)}) %collective-permute-start.43) | collective-permute-done | bytes 1048608 | tf_op jit(solution)/shard_map/ppermute | solution.py:636
  602.5 9.5 convolution_convert_fusion.2
  638.1 18.1 %attend_backward.1 = (f32[1024,512]{1,0:T(8,128)}, f32[1024,512]{1,0:T(8,128)}, bf16[1024,512]{1,0:T(8,128)(2,1)}, f32[1024,1]{1,0:T(8,128)}, f32[1024,1]{1,0:T(...) custom-call(f32[1024,1536]{1,0:T(8,128)} %copy-done.3, f32[1024,1536]{1,0:T(8,128)} %copy-done.3, f32[1024,1]{1,0:T(8,128)} %copy.71.qs_ref, ...), custom_call_target="tpu_custom_call" | custom-call | flops 5368709120 | bytes 20971520 | tf_op jit(solution)/shard_map/attend_backward/pallas_call | solution.py:180
  658.7 12.2 %all-reduce = (f32[1024]{0:T(1024)S(1)}, f32[1024]{0:T(1024)S(1)}) all-reduce(f32[1024]{0:T(1024)S(1)} %reduce.1, f32[1024]{0:T(1024)S(1)} %reduce), channel_id=1, replica_groups=mesh['dp'=2,'row'=4,'col'=4] {'col'}, use_global_device_ids=true, to_apply=%region_5.6 | all-reduce | flops 2048 | bytes 16384 | tf_op jit(solution)/shard_map/psum | solution.py:871
  685.4 16.2 %collective-permute-done.46 = bf16[256,2048]{1,0:T(8,128)(2,1)S(1)} collective-permute-done((bf16[256,2048]{1,0:T(8,128)(2,1)S(1)}, bf16[256,2048]{1,0:T(8,128)(2,1)S(1)}, u32[]{:S(2)}, u32[]{:S(2)}) %collective-permute-start.46) | collective-permute-done | bytes 1048608 | tf_op jit(solution)/shard_map/ppermute | solution.py:640
  707.4 10.6 %add_convert_fusion.2 = bf16[2048,1024]{1,0:T(8,128)(2,1)} fusion(bf16[2048,1024]{1,0:T(8,128)(2,1)} %collective-permute-done.58, bf16[1024,2048]{1,0:T(8,128)(2,1)} %get-tuple-element.303, bf16[1024,2048]{1,0:T(8,128)(2,1)} %get-tuple-element.304, s32[]{:T(128)S(6)} %select_n.213), kind=kOutput, calls=%fused_computation.2 | convolution fusion | flops 4301258752 | bytes 14680068 | tf_op jit(solution)/shard_map/dot_general | solution.py:35
  780.2 15.9 %collective-permute-done.48 = bf16[256,2048]{1,0:T(8,128)(2,1)S(1)} collective-permute-done((bf16[256,2048]{1,0:T(8,128)(2,1)S(1)}, bf16[256,2048]{1,0:T(8,128)(2,1)S(1)}, u32[]{:S(2)}, u32[]{:S(2)}) %collective-permute-start.48) | collective-permute-done | bytes 1048608 | tf_op jit(solution)/shard_map/ppermute | solution.py:640
  818.0 15.8 %collective-permute-done.50 = bf16[256,2048]{1,0:T(8,128)(2,1)S(1)} collective-permute-done((bf16[256,2048]{1,0:T(8,128)(2,1)S(1)}, bf16[256,2048]{1,0:T(8,128)(2,1)S(1)}, u32[]{:S(2)}, u32[]{:S(2)}) %collective-permute-start.50) | collective-permute-done | bytes 1048608 | tf_op jit(solution)/shard_map/ppermute | solution.py:640
  879.5 19.3 %collective-permute-done.56.refs_0_.refs_1_ = bf16[256,2048]{1,0:T(8,128)(2,1)S(1)} collective-permute-done((bf16[256,2048]{1,0:T(8,128)(2,1)}, bf16[256,2048]{1,0:T(8,128)(2,1)S(1)}, u32[]{:S(2)}, u32[]{:S(2)}) %collective-permute-start.56) | collective-permute-done | bytes 1048608 | tf_op jit(solution)/shard_map/ppermute | solution.py:636
  923.3 27.0 %reduce-scatter.14.cloned.1.call-done = bf16[512,768]{1,0:T(8,128)(2,1)} async-done(((bf16[2048,768]{1,0:T(8,128)(2,1)}), bf16[512,768]{1,0:T(8,128)(2,1)}) %reduce-scatter.14.cloned.1.call-update) | async-done | bytes 786448 | tf_op jit(solution)/shard_map/reduce_scatter | solution.py:703
  (386 shorter events, 384.0 us)
Async XLA Ops:
  7.2 80.3 %all-gather.3.cloned.1.call-start = ((), (), s32[]{:S(2)}) async-start(), calls=%async_computation.5 | async-start | bytes 7077888 | tf_op jit(solution)/shard_map/all_gather | solution.py:632
  9.5 237.9 %all-gather.5.cloned.1.call-start = ((), (), s32[]{:S(2)}) async-start(), calls=%async_computation.6 | async-start | bytes 18874368 | tf_op jit(solution)/shard_map/all_gather | solution.py:632
  12.7 856.2 %reduce-scatter.12.cloned.1.call-start = ((), (), s32[]{:S(2)}) async-start(), calls=%async_computation.10 | async-start | bytes 1310720 | tf_op jit(solution)/shard_map/reduce_scatter | solution.py:703
  68.5 67.5 %collective-permute-start.13 = (bf16[256,2048]{1,0:T(8,128)(2,1)}, bf16[256,2048]{1,0:T(8,128)(2,1)}, u32[]{:S(2)}, u32[]{:S(2)}) collective-permute-start(bf16[256,2048]{1,0:T(8,128)(2,1)} %collective-permute-done.12), channel_id=1, source_target_pairs={{2,3},{6,7},{10,11},{14,15},{18,19},{22,23},{26,27},{30,31}} | collective-permute-start | bytes 3145736 | tf_op jit(solution)/shard_map/ppermute | solution.py:635
  86.2 54.6 %collective-permute-start.15 = (bf16[256,2048]{1,0:T(8,128)(2,1)}, bf16[256,2048]{1,0:T(8,128)(2,1)}, u32[]{:S(2)}, u32[]{:S(2)}) collective-permute-start(bf16[256,2048]{1,0:T(8,128)(2,1)} %collective-permute-done.14), channel_id=1, source_target_pairs={{1,0},{5,4},{9,8},{13,12},{17,16},{21,20},{25,24},{29,28}} | collective-permute-start | bytes 3145736 | tf_op jit(solution)/shard_map/ppermute | solution.py:636
  134.0 40.4 %collective-permute-start.17 = (bf16[1024,512]{1,0:T(8,128)(2,1)S(1)}, bf16[1024,512]{1,0:T(8,128)(2,1)}, u32[]{:S(2)}, u32[]{:S(2)}) collective-permute-start(bf16[1024,512]{1,0:T(8,128)(2,1)S(1)} %constant_dynamic-slice_fusion.10), channel_id=1, source_target_pairs={{0,4},{4,0},{8,12},{12,8},{1,5},{5,1},{9,13},{13,9},{2,6},{6,2},{1... | collective-permute-start | bytes 3145736 | tf_op jit(solution)/shard_map/ppermute | solution.py:711
  136.0 38.3 %collective-permute-start.18 = (bf16[1024,512]{1,0:T(8,128)(2,1)S(1)}, bf16[1024,512]{1,0:T(8,128)(2,1)}, u32[]{:S(2)}, u32[]{:S(2)}) collective-permute-start(bf16[1024,512]{1,0:T(8,128)(2,1)S(1)} %constant_dynamic-slice_fusion.10), channel_id=1, source_target_pairs={{0,8},{8,0},{4,12},{12,4},{1,9},{9,1},{5,13},{13,5},{2,10},{10,2},... | collective-permute-start | bytes 3145736 | tf_op jit(solution)/shard_map/ppermute | solution.py:711
  145.0 102.3 %collective-permute-start.16 = (bf16[1024,2048]{1,0:T(8,128)(2,1)}, bf16[1024,2048]{1,0:T(8,128)(2,1)}, u32[]{:S(2)}, u32[]{:S(2)}) collective-permute-start(bf16[1024,2048]{1,0:T(8,128)(2,1)} %pad_maximum_fusion.refs_7_.wo_own_ref), channel_id=1, source_target_pairs={{0,16},{16,0},{1,17},{17,1},{2,18},{18,2},{3,19},{19,3},{4,20},{20... | collective-permute-start | bytes 12582920 | tf_op jit(solution)/shard_map/ppermute | solution.py:787
  190.2 57.1 %collective-permute-start.21 = (bf16[4,1024,512]{2,1,0:T(8,128)(2,1)}, bf16[4,1024,512]{2,1,0:T(8,128)(2,1)}, u32[]{:S(2)}, u32[]{:S(2)}) collective-permute-start(bf16[4,1024,512]{2,1,0:T(8,128)(2,1)} %bitcast_dynamic-update-slice_fusion.3.refs_13_.wd_own_ref), channel_id=1, source_target_pairs={{0,16},{16,0},{1,17},{17,1},{2,18},{18,2},{3,19},{19,3},{4,20},{20... | collective-permute-start | bytes 12582920 | tf_op jit(solution)/shard_map/ppermute | solution.py:736
  191.0 29.6 %collective-permute-start.4 = (bf16[1024,512]{1,0:T(8,128)(2,1)S(1)}, bf16[1024,512]{1,0:T(8,128)(2,1)}, u32[]{:S(2)}, u32[]{:S(2)}) collective-permute-start(bf16[1024,512]{1,0:T(8,128)(2,1)S(1)} %collective-permute-done.3.refs_4_), channel_id=1, source_target_pairs={{1,0},{2,1},{5,4},{6,5},{9,8},{10,9},{13,12},{14,13},{17,16},{18,1... | collective-permute-start | bytes 3145736 | tf_op jit(solution)/shard_map/ppermute | solution.py:636
  192.3 30.2 %collective-permute-start.2 = (bf16[1024,512]{1,0:T(8,128)(2,1)S(1)}, bf16[1024,512]{1,0:T(8,128)(2,1)S(1)}, u32[]{:S(2)}, u32[]{:S(2)}) collective-permute-start(bf16[1024,512]{1,0:T(8,128)(2,1)S(1)} %collective-permute-done.1.refs_2_), channel_id=1, source_target_pairs={{2,3},{6,7},{10,11},{14,15},{18,19},{22,23},{26,27},{30,31}} | collective-permute-start | bytes 3145736 | tf_op jit(solution)/shard_map/ppermute | solution.py:635
  220.5 26.8 %collective-permute-start.5 = (bf16[1024,512]{1,0:T(8,128)(2,1)}, bf16[1024,512]{1,0:T(8,128)(2,1)S(1)}, u32[]{:S(2)}, u32[]{:S(2)}) collective-permute-start(bf16[1024,512]{1,0:T(8,128)(2,1)} %collective-permute-done.4.refs_5_), channel_id=1, source_target_pairs={{1,0},{5,4},{9,8},{13,12},{17,16},{21,20},{25,24},{29,28}} | collective-permute-start | bytes 3145736 | tf_op jit(solution)/shard_map/ppermute | solution.py:636
  300.2 27.0 %collective-permute-start.24 = (bf16[256,2048]{1,0:T(8,128)(2,1)S(1)}, bf16[256,2048]{1,0:T(8,128)(2,1)S(1)}, u32[]{:S(2)}, u32[]{:S(2)}) collective-permute-start(bf16[256,2048]{1,0:T(8,128)(2,1)S(1)} %add_add_fusion.2), channel_id=1, source_target_pairs={{0,1},{1,2},{4,5},{5,6},{8,9},{9,10},{12,13},{13,14},{16,17},{17,1... | collective-permute-start | bytes 3145736 | tf_op jit(solution)/shard_map/ppermute | solution.py:640
  330.0 27.4 %collective-permute-start.26 = (bf16[256,2048]{1,0:T(8,128)(2,1)}, bf16[256,2048]{1,0:T(8,128)(2,1)S(1)}, u32[]{:S(2)}, u32[]{:S(2)}) collective-permute-start(bf16[256,2048]{1,0:T(8,128)(2,1)} %get-tuple-element.402), channel_id=1, source_target_pairs={{0,1},{1,2},{2,3},{4,5},{5,6},{6,7},{8,9},{9,10},{10,11},{12,13},{... | collective-permute-start | bytes 3145736 | tf_op jit(solution)/shard_map/ppermute | solution.py:640
  410.0 43.7 %collective-permute-start.32 = (bf16[256,2048]{1,0:T(8,128)(2,1)S(1)}, bf16[256,2048]{1,0:T(8,128)(2,1)S(1)}, u32[]{:S(2)}, u32[]{:S(2)}) collective-permute-start(bf16[256,2048]{1,0:T(8,128)(2,1)S(1)} %collective-permute-done.29.refs_3_.refs_2_), channel_id=1, source_target_pairs={{2,3},{6,7},{10,11},{14,15},{18,19},{22,23},{26,27},{30,31}} | collective-permute-start | bytes 3145736 | tf_op jit(solution)/shard_map/ppermute | solution.py:635
  412.2 41.4 %collective-permute-start.33 = (bf16[256,2048]{1,0:T(8,128)(2,1)}, bf16[256,2048]{1,0:T(8,128)(2,1)S(1)}, u32[]{:S(2)}, u32[]{:S(2)}) collective-permute-start(bf16[256,2048]{1,0:T(8,128)(2,1)} %collective-permute-done.31.refs_0_.refs_1_), channel_id=1, source_target_pairs={{1,0},{5,4},{9,8},{13,12},{17,16},{21,20},{25,24},{29,28}} | collective-permute-start | bytes 3145736 | tf_op jit(solution)/shard_map/ppermute | solution.py:636
  578.8 52.7 %collective-permute-start.44 = (bf16[256,2048]{1,0:T(8,128)(2,1)S(1)}, bf16[256,2048]{1,0:T(8,128)(2,1)}, u32[]{:S(2)}, u32[]{:S(2)}) collective-permute-start(bf16[256,2048]{1,0:T(8,128)(2,1)S(1)} %collective-permute-done.41.refs_3_.refs_2_), channel_id=1, source_target_pairs={{2,3},{6,7},{10,11},{14,15},{18,19},{22,23},{26,27},{30,31}} | collective-permute-start | bytes 3145736 | tf_op jit(solution)/shard_map/ppermute | solution.py:635
  600.8 30.8 %collective-permute-start.45 = (bf16[256,2048]{1,0:T(8,128)(2,1)}, bf16[256,2048]{1,0:T(8,128)(2,1)}, u32[]{:S(2)}, u32[]{:S(2)}) collective-permute-start(bf16[256,2048]{1,0:T(8,128)(2,1)} %collective-permute-done.43.refs_0_.refs_1_), channel_id=1, source_target_pairs={{1,0},{5,4},{9,8},{13,12},{17,16},{21,20},{25,24},{29,28}} | collective-permute-start | bytes 3145736 | tf_op jit(solution)/shard_map/ppermute | solution.py:636
  612.0 95.4 %collective-permute-start.58 = (bf16[2048,1024]{1,0:T(8,128)(2,1)}, bf16[2048,1024]{1,0:T(8,128)(2,1)}, u32[]{:S(2)}, u32[]{:S(2)}) collective-permute-start(bf16[2048,1024]{1,0:T(8,128)(2,1)} %convolution_convert_fusion.2), channel_id=1, source_target_pairs={{0,16},{16,0},{1,17},{17,1},{2,18},{18,2},{3,19},{19,3},{4,20},{20... | collective-permute-start | bytes 12582920 | tf_op jit(solution)/shard_map/ppermute | solution.py:699
  707.2 163.9 %reduce-scatter.6.cloned.1.call-start = ((), (), s32[]{:S(2)}) async-start(), calls=%async_computation.7 | async-start | bytes 5242880 | tf_op jit(solution)/shard_map/reduce_scatter | solution.py:703
  718.1 158.2 %reduce-scatter.8.cloned.1.call-start = ((), (), s32[]{:S(2)}) async-start(), calls=%async_computation.8 | async-start | bytes 5242880 | tf_op jit(solution)/shard_map/reduce_scatter | solution.py:703
  739.6 163.7 %reduce-scatter.10.cloned.1.call-start = ((), (), s32[]{:S(2)}) async-start(), calls=%async_computation.9 | async-start | bytes 5242880 | tf_op jit(solution)/shard_map/reduce_scatter | solution.py:703
  761.3 188.9 %reduce-scatter.14.cloned.1.call-start = ((), (), s32[]{:S(2)}) async-start(), calls=%async_computation.11 | async-start | bytes 3932160 | tf_op jit(solution)/shard_map/reduce_scatter | solution.py:703
  768.6 29.2 %collective-permute-start.68 = (bf16[2048,768]{1,0:T(8,128)(2,1)S(1)}, bf16[2048,768]{1,0:T(8,128)(2,1)S(1)}, u32[]{:S(2)}, u32[]{:S(2)}) collective-permute-start(bf16[2048,768]{1,0:T(8,128)(2,1)S(1)} %convolution_convert_fusion.3), channel_id=1, source_target_pairs={{0,16},{16,0},{1,17},{17,1},{2,18},{18,2},{3,19},{19,3},{4,20},{20... | collective-permute-start | bytes 9437192 | tf_op jit(solution)/shard_map/ppermute | solution.py:699
  768.9 27.2 %collective-permute-start.48 = (bf16[256,2048]{1,0:T(8,128)(2,1)S(1)}, bf16[256,2048]{1,0:T(8,128)(2,1)S(1)}, u32[]{:S(2)}, u32[]{:S(2)}) collective-permute-start(bf16[256,2048]{1,0:T(8,128)(2,1)S(1)} %copy-done.60), channel_id=1, source_target_pairs={{0,1},{1,2},{4,5},{5,6},{8,9},{9,10},{12,13},{13,14},{16,17},{17,1... | collective-permute-start | bytes 3145736 | tf_op jit(solution)/shard_map/ppermute | solution.py:640
  804.1 29.7 %collective-permute-start.50 = (bf16[256,2048]{1,0:T(8,128)(2,1)S(1)}, bf16[256,2048]{1,0:T(8,128)(2,1)S(1)}, u32[]{:S(2)}, u32[]{:S(2)}) collective-permute-start(bf16[256,2048]{1,0:T(8,128)(2,1)S(1)} %copy-done.38), channel_id=1, source_target_pairs={{0,1},{1,2},{2,3},{4,5},{5,6},{6,7},{8,9},{9,10},{10,11},{12,13},{... | collective-permute-start | bytes 3145736 | tf_op jit(solution)/shard_map/ppermute | solution.py:640
  840.2 28.8 %collective-permute-start.52 = (bf16[256,2048]{1,0:T(8,128)(2,1)S(1)}, bf16[256,2048]{1,0:T(8,128)(2,1)}, u32[]{:S(2)}, u32[]{:S(2)}) collective-permute-start(bf16[256,2048]{1,0:T(8,128)(2,1)S(1)} %add_convert_fusion.4.refs_0_), channel_id=1, source_target_pairs={{0,1},{1,2},{2,3},{4,5},{5,6},{6,7},{8,9},{9,10},{10,11},{12,13},{... | collective-permute-start | bytes 3145736 | tf_op jit(solution)/shard_map/ppermute | solution.py:635
  869.8 29.1 %collective-permute-start.56 = (bf16[256,2048]{1,0:T(8,128)(2,1)}, bf16[256,2048]{1,0:T(8,128)(2,1)S(1)}, u32[]{:S(2)}, u32[]{:S(2)}) collective-permute-start(bf16[256,2048]{1,0:T(8,128)(2,1)} %collective-permute-done.55.refs_0_.refs_1_), channel_id=1, source_target_pairs={{1,0},{2,1},{5,4},{6,5},{9,8},{10,9},{13,12},{14,13},{17,16},{18,1... | collective-permute-start | bytes 3145736 | tf_op jit(solution)/shard_map/ppermute | solution.py:636
  871.1 32.2 %collective-permute-start.59 = (bf16[512,1024]{1,0:T(8,128)(2,1)}, bf16[512,1024]{1,0:T(8,128)(2,1)}, u32[]{:S(2)}, u32[]{:S(2)}) collective-permute-start(bf16[512,1024]{1,0:T(8,128)(2,1)} %reduce-scatter.6.cloned.1.call-done), channel_id=1, source_target_pairs={{0,16},{16,0},{1,17},{17,1},{2,18},{18,2},{3,19},{19,3},{4,20},{20... | collective-permute-start | bytes 3145736 | tf_op jit(solution)/shard_map/ppermute | solution.py:693
  876.3 36.6 %collective-permute-start.61 = (bf16[512,1024]{1,0:T(8,128)(2,1)}, bf16[512,1024]{1,0:T(8,128)(2,1)}, u32[]{:S(2)}, u32[]{:S(2)}) collective-permute-start(bf16[512,1024]{1,0:T(8,128)(2,1)} %reduce-scatter.8.cloned.1.call-done), channel_id=1, source_target_pairs={{0,16},{16,0},{1,17},{17,1},{2,18},{18,2},{3,19},{19,3},{4,20},{20... | collective-permute-start | bytes 3145736 | tf_op jit(solution)/shard_map/ppermute | solution.py:693
  877.9 86.5 %collective-permute-start.54 = (bf16[256,2048]{1,0:T(8,128)(2,1)S(1)}, bf16[256,2048]{1,0:T(8,128)(2,1)}, u32[]{:S(2)}, u32[]{:S(2)}) collective-permute-start(bf16[256,2048]{1,0:T(8,128)(2,1)S(1)} %collective-permute-done.53.refs_3_.refs_2_), channel_id=1, source_target_pairs={{2,3},{6,7},{10,11},{14,15},{18,19},{22,23},{26,27},{30,31}} | collective-permute-start | bytes 3145736 | tf_op jit(solution)/shard_map/ppermute | solution.py:635
  898.9 65.5 %collective-permute-start.57 = (bf16[256,2048]{1,0:T(8,128)(2,1)S(1)}, bf16[256,2048]{1,0:T(8,128)(2,1)}, u32[]{:S(2)}, u32[]{:S(2)}) collective-permute-start(bf16[256,2048]{1,0:T(8,128)(2,1)S(1)} %collective-permute-done.56.refs_0_.refs_1_), channel_id=1, source_target_pairs={{1,0},{5,4},{9,8},{13,12},{17,16},{21,20},{25,24},{29,28}} | collective-permute-start | bytes 3145736 | tf_op jit(solution)/shard_map/ppermute | solution.py:636
  (111 other events, 2075.9 us)
Sparse Core Ops, SparseCore 0:
  10.5 51.5 all-gather.2
  64.5 107.9 all-gather.4
  707.3 27.4 reduce-scatter.11
  738.2 52.5 reduce-scatter.5
  794.2 52.5 reduce-scatter.7
  850.2 53.0 reduce-scatter.9
  906.3 43.8 reduce-scatter.13
